TPU v7x, 256 devices: a whole 4x4x8 slice. The times are simulated.
256 devices in a mesh: row: 16 (over y, x), col: 16 (over z, core).
Axes of the slice: x: 4, y: 4, z: 8, core: 2. Of those that a mesh axis runs over, the one named last changes fastest.
Arguments:
- features: bfloat16 [512, 512, 128], P('col')
- diag_inverse: bfloat16 [512, 128, 128], P('col')
- precision_tiles: float32 [16, 16, 32, 128, 128], P('row', 'col'), may hold values from -3 to 3
- inverse_tiles: float32 [16, 16, 32, 128, 128], P('row', 'col'), may hold values from -0.3125 to 0.3125
- slot_rows: int32 [16, 16, 32], replicated, may hold values from 0 to 511, as said below
- slot_columns: int32 [16, 16, 32], replicated, may hold values from 0 to 1, as said below
- owned_columns: int32 [16, 16, 2], replicated, may hold values from 0 to 511, as said below
- live_counts: int32 [16, 16], replicated, may hold values from 1 to 32, as said below
Outputs:
- direction: float32 [16, 16, 32, 128, 128], P('row', 'col')
Inputs may be any that keep to these rules, and one draw needn't show every extreme that they name: `slot_rows`: slot k of every owner names a block-row held by index k // 2 of col, that is one of feature blocks 32 * (k // 2) to 32 * (k // 2) + 31; no pair of block-row and block-column is named by two slots of the whole grid. `slot_columns`: some owner uses every entry of its list. `owned_columns`: an owner's 2 block-columns are distinct and lie among the feature blocks of its own index of col. The live slots of an owner are slots 0 to live_counts - 1; some owner has all 32 slots live.
All inputs are finite; a program needn't handle non-finite values.
Results may differ from a plain program's by a relative error of at most 0.0003.
Values may be sent and summed in bfloat16 or wider, within the bound.
No kernel may reach another device: no remote copies, remote signals or barrier semaphores. Data moves between devices by JAX's collectives and lax.ppermute only.
A program may use at most 128 MiB of HBM per device.

v0:
```python
import jax
import jax.numpy as jnp
from jax import lax
from jax.sharding import PartitionSpec as P

SWEEPS = 4


step_size = 0.3
penalty = 0.6
highest = lax.Precision.HIGHEST


def soft_update(precision_tile, direction, residual):
    shifted = precision_tile + direction - step_size * residual
    return (
        jnp.sign(shifted) * jnp.maximum(jnp.abs(shifted) - step_size * penalty, 0.0)
        - precision_tile
    )


def body(
    features,
    diag_inverse,
    precision_tiles,
    inverse_tiles,
    slot_rows,
    slot_columns,
    owned_columns,
    live_counts,
):
    col_count = lax.axis_size("col")
    row_index = lax.axis_index("row")
    col_index = lax.axis_index("col")
    block_count = features.shape[0]
    sample_count = features.shape[1]
    block_size = features.shape[2]
    slot_count = precision_tiles.shape[2]
    per_source = slot_count // col_count
    row_table = slot_rows[row_index]
    wanted = jnp.take(row_table.reshape(col_count, col_count, per_source), col_index, axis=1)
    local_rows = (wanted - col_index * block_count).reshape(-1)
    send_tiles = jnp.take(features, local_rows, axis=0).reshape(
        col_count, per_source, sample_count, block_size
    )
    send_diag = jnp.take(diag_inverse, local_rows, axis=0).reshape(
        col_count, per_source, block_size, block_size
    )
    row_tiles, row_diag = (
        lax.all_to_all(send_tiles, "col", split_axis=0, concat_axis=0, tiled=True),
        lax.all_to_all(send_diag, "col", split_axis=0, concat_axis=0, tiled=True),
    )
    row_tiles = row_tiles.reshape(slot_count, sample_count, block_size)
    row_diag = row_diag.reshape(slot_count, block_size, block_size).astype(jnp.float32)
    my_lists = slot_columns[row_index, col_index]
    my_owned = owned_columns[row_index, col_index]
    column_ids = jnp.take(my_owned, my_lists)
    local_cols = column_ids - col_index * block_count
    live_mask = (jnp.arange(slot_count) < live_counts[row_index, col_index]).astype(jnp.float32)
    col_tiles = jnp.take(features, local_cols, axis=0)
    covariance = (
        jnp.einsum("kna,knb->kab", row_tiles, col_tiles, preferred_element_type=jnp.float32)
        / sample_count
    )
    tiles_here = inverse_tiles[0, 0]
    theta_here = precision_tiles[0, 0]
    gradient = covariance - tiles_here
    col_diag = jnp.take(diag_inverse, local_cols, axis=0).astype(jnp.float32)
    direction = jnp.zeros_like(gradient)
    for sweep_index in range(SWEEPS):
        residual = gradient
        if sweep_index > 0:
            left_side = jnp.einsum("kab,kbc->kac", row_diag, direction, precision=highest)
            residual = residual + jnp.einsum("kac,kcd->kad", left_side, col_diag, precision=highest)
            products = (
                jnp.einsum("kba,kbc->kac", direction, tiles_here, precision=highest)
                * live_mask[:, None, None]
            )
            onehot = (local_cols[:, None] == jnp.arange(block_count)[None, :]).astype(jnp.float32)
            dense_sums = jnp.einsum("kf,kab->fab", onehot, products, precision=highest)
            summed = lax.psum(dense_sums, "row")
            residual = residual + jnp.einsum(
                "kab,kbc->kac",
                tiles_here,
                jnp.einsum("kf,fab->kab", onehot, summed, precision=highest),
                precision=highest,
            )
        direction = soft_update(theta_here, direction, residual)
    return (direction * live_mask[:, None, None]).reshape(precision_tiles.shape)


def solution(mesh):
    return jax.shard_map(
        body,
        mesh=mesh,
        in_specs=(
            P("col", None, None),
            P("col", None, None),
            P("row", "col", None, None, None),
            P("row", "col", None, None, None),
            P(),
            P(),
            P(),
            P(),
        ),
        out_specs=P("row", "col", None, None, None),
        check_vma=False,
    )
```

profile of v0, /device:TPU:32, one launch (start us, length us, event | category | flops | bytes accessed | tf_op | source)
XLA Modules:
  0.0 511.2 jit_solution(2454693895170861494)
XLA Ops:
  6.5 0.0 copy-start
  6.5 0.8 constant_dynamic-slice_fusion
  7.4 0.5 fusion.89
  7.9 0.7 constant_dynamic-slice_fusion.2
  8.6 0.1 copy.34
  8.7 0.1 copy.14
  8.8 0.1 sub.61
  8.9 2.0 compare_and_fusion
  10.9 5.2 %gather_fusion = bf16[32,512,128]{2,1,0:T(8,128)(2,1)} fusion(bf16[32,512,128]{2,1,0:T(8,128)(2,1)} %param.12, s32[1024]{0:T(1024)S(1)} %pad_clamp_fusion.1), kind=kCustom, calls=%fused_computation.clone | custom fusion | bytes 8388736 | tf_op jit(solution)/shard_map/jit(_take)/gather | solution.py:43
  16.1 4.6 broadcast_select_fusion
  20.7 6.5 %copy.15 = bf16[16,2,512,128]{2,3,1,0:T(8,128)(2,1)} copy(bf16[16,2,512,128]{3,2,1,0:T(8,128)(2,1)} %bitcast.129) | data formatting | bytes 8388608 | tf_op jit(solution)/shard_map/reshape | solution.py:43
  27.2 8.6 %all-to-all-start = ((bf16[16,2,512,128]{2,3,1,0:T(8,128)(2,1)}), bf16[16,2,512,128]{2,3,1,0:T(8,128)(2,1)}, u32[]{:S(2)}, u32[]{:S(2)}) async-start(bf16[16,2,512,128]{2,3,1,0:T(8,128)(2,1)} %copy.15), calls=%async_computation | async-start | bytes 8388608 | tf_op jit(solution)/shard_map/all_to_all | solution.py:50
  35.7 1.3 dynamic_slice.15
  37.0 0.0 copy-done
  37.0 1.6 gather_fusion.2
  38.7 5.2 %gather_fusion.1 = bf16[32,512,128]{2,1,0:T(8,128)(2,1)} fusion(bf16[32,512,128]{2,1,0:T(8,128)(2,1)} %param.12, s32[1024]{0:T(1024)S(1)} %pad_clamp_fusion), kind=kCustom, calls=%fused_computation.2.clone | custom fusion | bytes 8388736 | tf_op jit(solution)/shard_map/jit(_take)/gather | solution.py:60
  43.9 0.6 compare_convert_fusion
  44.5 0.0 copy-start.2
  44.5 2.5 broadcast_select_fusion.2
  47.1 81.1 %all-to-all-done = bf16[16,2,512,128]{2,3,1,0:T(8,128)(2,1)} async-done(((bf16[16,2,512,128]{2,3,1,0:T(8,128)(2,1)}), bf16[16,2,512,128]{2,3,1,0:T(8,128)(2,1)}, u32[]{:S(2)}, u32[]{:S(2)}) %all-to-all-start) | async-done | bytes 4194336 | tf_op jit(solution)/shard_map/all_to_all | solution.py:50
  128.2 6.7 %all-to-all-start.1 = ((bf16[16,2,128,128]{3,2,1,0:T(8,128)(2,1)}), bf16[16,2,128,128]{3,2,1,0:T(8,128)(2,1)}, u32[]{:S(2)}, u32[]{:S(2)}) async-start(bf16[16,2,128,128]{3,2,1,0:T(8,128)(2,1)} %bitcast.130), calls=%async_computation.1 | async-start | bytes 2097152 | tf_op jit(solution)/shard_map/all_to_all | solution.py:51
  134.9 0.6 all-reduce.4.cloned.1.call-start
  135.4 0.0 copy-done.2
  135.5 0.0 copy-start.3
  135.5 4.9 bitcast_subtract_fusion
  140.4 0.0 copy-done.3
  140.4 0.0 copy-start.7
  140.4 4.5 fusion.39
  144.9 0.0 copy-done.7
  144.9 2.5 fusion.36
  147.4 2.5 copy.20
  150.0 0.0 all-reduce.4.cloned.1.call-update
  150.0 0.2 all-reduce.6.cloned.1.call-start
  150.2 1.7 gather_fusion.3
  151.9 7.8 %all-to-all-done.1 = bf16[16,2,128,128]{3,2,1,0:T(8,128)(2,1)} async-done(((bf16[16,2,128,128]{3,2,1,0:T(8,128)(2,1)}), bf16[16,2,128,128]{3,2,1,0:T(8,128)(2,1)}, u32[]{:S(2)}, u32[]{:S(2)}) %all-to-all-start.1) | async-done | bytes 1048608 | tf_op jit(solution)/shard_map/all_to_all | solution.py:51
  159.7 4.9 fusion.62
  164.6 2.6 fusion.87
  167.2 84.6 %all-reduce.4.cloned.1.call-done = f32[32,128,128]{2,1,0:T(8,128)} async-done(((f32[32,128,128]{2,1,0:T(8,128)}), f32[32,128,128]{2,1,0:T(8,128)}) %all-reduce.4.cloned.1.call-update) | async-done | bytes 2097168 | tf_op jit(solution)/shard_map/psum | solution.py:81
  251.7 4.1 fusion.34
  255.8 6.9 %bitcast_subtract_fusion.3 = f32[32,128,128]{2,1,0:T(8,128)S(1)} fusion(f32[1,1,32,128,128]{4,3,2,1,0:T(8,128)S(1)} %copy-done.4, f32[32,128,128]{2,1,0:T(8,128)S(1)} %copy-done.8, f32[32,128,128]{2,1,0:T(8,128)} %fusion.87, f32[1,1,32,128,128]{4,3,2,1,0:T(8,128)S(1)} %copy-done.2, f32[32,128,128]{2,0,1:T(8,128)S(1)} %fusion.34), kind=kOutput, calls=%fused_computation.34 | convolution fusion | flops 815267840 | bytes 12582912 | tf_op jit(solution)/shard_map/kab,kbc->kac/dot_general | solution.py:82
  262.7 0.0 copy-start.12
  262.7 4.2 fusion.42
  267.0 2.5 fusion.31
  269.5 2.6 copy.25
  272.1 0.0 all-reduce.6.cloned.1.call-update
  272.1 0.0 all-reduce.8.cloned.1.call-start
  272.1 3.2 fusion.90
  275.3 2.5 fusion.86
  277.8 94.3 %all-reduce.6.cloned.1.call-done = f32[32,128,128]{2,1,0:T(8,128)} async-done(((f32[32,128,128]{2,1,0:T(8,128)}), f32[32,128,128]{2,1,0:T(8,128)}) %all-reduce.6.cloned.1.call-update) | async-done | bytes 2097168 | tf_op jit(solution)/shard_map/psum | solution.py:81
  372.1 4.1 fusion.29
  376.2 6.9 %bitcast_subtract_fusion.2 = f32[32,128,128]{2,1,0:T(8,128)S(1)} fusion(f32[1,1,32,128,128]{4,3,2,1,0:T(8,128)S(1)} %copy-done.5, f32[32,128,128]{2,1,0:T(8,128)} %copy-done.12, f32[32,128,128]{2,1,0:T(8,128)S(1)} %copy-done.9, f32[32,128,128]{2,1,0:T(8,128)} %fusion.86, f32[1,1,32,128,128]{4,3,2,1,0:T(8,128)S(1)} %copy-done.2, f32[32,128,128]{2,0,1:T(8,128)S(1)} %fusion.29), kind=kOutput, calls=%fused_computation.32 | convolution fusion | flops 811073536 | bytes 14680064 | tf_op jit(solution)/shard_map/kab,kbc->kac/dot_general | solution.py:82
  383.2 0.0 copy-start.11
  383.2 4.0 fusion.45
  387.2 2.5 fusion.26
  389.7 2.6 copy.30
  392.3 0.0 all-reduce.8.cloned.1.call-update
  392.3 3.2 fusion.91
  395.5 2.6 fusion.85
  398.0 94.2 %all-reduce.8.cloned.1.call-done = f32[32,128,128]{2,1,0:T(8,128)} async-done(((f32[32,128,128]{2,1,0:T(8,128)}), f32[32,128,128]{2,1,0:T(8,128)}) %all-reduce.8.cloned.1.call-update) | async-done | bytes 2097168 | tf_op jit(solution)/shard_map/psum | solution.py:81
  492.2 4.3 fusion.24
  496.6 0.0 copy-done.6
  496.6 0.0 copy-done.10
  496.6 0.0 copy-start.1
  496.6 7.8 %fusion.22 = f32[1,1,32,128,128]{4,3,2,1,0:T(8,128)} fusion(f32[1,1,32,128,128]{4,3,2,1,0:T(8,128)S(1)} %copy-done.6, f32[32,128,128]{2,1,0:T(8,128)} %copy-done.11, f32[32,128,128]{2,1,0:T(8,128)S(1)} %copy-done.10, f32[32,128,128]{2,1,0:T(8,128)} %fusion.85, f32[1,1,32,128,128]{4,3,2,1,0:T(8,128)S(1)} %copy-done.2, f32[32,128,128]{2,0,1:T(8,128)S(1)} %fusion.24, ...), kind=kOutput, calls=%fused_computation.39 | convolution fusion | flops 811597824 | bytes 14680192 | tf_op jit(solution)/shard_map/kab,kbc->kac/dot_general | solution.py:82
  (20 shorter events, 0.1 us)
Async XLA Ops:
  6.5 30.5 %copy-start = (bf16[32,128,128]{2,1,0:T(8,128)(2,1)S(1)}, bf16[32,128,128]{2,1,0:T(8,128)(2,1)}, u32[]{:S(2)}) copy-start(bf16[32,128,128]{2,1,0:T(8,128)(2,1)} %param.13) | copy-start | bytes 3145732
  27.2 101.1 %all-to-all-start = ((bf16[16,2,512,128]{2,3,1,0:T(8,128)(2,1)}), bf16[16,2,512,128]{2,3,1,0:T(8,128)(2,1)}, u32[]{:S(2)}, u32[]{:S(2)}) async-start(bf16[16,2,512,128]{2,3,1,0:T(8,128)(2,1)} %copy.15), calls=%async_computation | async-start | bytes 8388608 | tf_op jit(solution)/shard_map/all_to_all | solution.py:50
  44.5 90.9 %copy-start.2 = (f32[1,1,32,128,128]{4,3,2,1,0:T(8,128)S(1)}, f32[1,1,32,128,128]{4,3,2,1,0:T(8,128)}, u32[]{:S(2)}) copy-start(f32[1,1,32,128,128]{4,3,2,1,0:T(8,128)} %param.15) | copy-start | bytes 6291460
  128.2 31.5 %all-to-all-start.1 = ((bf16[16,2,128,128]{3,2,1,0:T(8,128)(2,1)}), bf16[16,2,128,128]{3,2,1,0:T(8,128)(2,1)}, u32[]{:S(2)}, u32[]{:S(2)}) async-start(bf16[16,2,128,128]{3,2,1,0:T(8,128)(2,1)} %bitcast.130), calls=%async_computation.1 | async-start | bytes 2097152 | tf_op jit(solution)/shard_map/all_to_all | solution.py:51
  134.9 116.9 %all-reduce.4.cloned.1.call-start = ((), (), s32[]{:S(2)}) async-start(), calls=%async_computation.2 | async-start | bytes 4194304 | tf_op jit(solution)/shard_map/psum | solution.py:81
  135.5 4.9 copy-start.3
  140.4 4.5 copy-start.7
  150.0 222.1 %all-reduce.6.cloned.1.call-start = ((), (), s32[]{:S(2)}) async-start(), calls=%async_computation.3 | async-start | bytes 4194304 | tf_op jit(solution)/shard_map/psum | solution.py:81
  159.7 4.9 copy-start.13
  251.7 4.1 copy-start.4
  251.7 4.1 copy-start.8
  262.7 4.2 copy-start.12
  272.1 220.1 %all-reduce.8.cloned.1.call-start = ((), (), s32[]{:S(2)}) async-start(), calls=%async_computation.4 | async-start | bytes 4194304 | tf_op jit(solution)/shard_map/psum | solution.py:81
  372.1 4.1 copy-start.5
  372.1 4.1 copy-start.9
  383.2 4.0 copy-start.11
  492.2 4.3 copy-start.6
  492.2 4.3 copy-start.10
  496.6 7.9 %copy-start.1 = (bf16[32,128,128]{2,1,0:T(8,128)(2,1)S(1)}, bf16[32,128,128]{2,1,0:T(8,128)(2,1)}, u32[]{:S(2)}) copy-start(bf16[32,128,128]{2,1,0:T(8,128)(2,1)} %param.13) | copy-start | bytes 3145732
Sparse Core Ops, SparseCore 0:
  150.1 101.5 all-reduce.3
  272.2 99.8 all-reduce.5
  392.4 99.7 all-reduce.7
where the time goes:
time: 515 us; the launch traced here: 511 us
  waiting for transfers between devices  362 us (70%)
  matrix products  78.1 us (15%)
  local copies, waits for them, and re-layouts  31.6 us (6%)
  starting transfers between devices  16.1 us (3%)
  between operations  13.6 us (3%)
  other arithmetic  9.75 us (2%)
    psum x3, waiting for transfers between devices, body(): summed = lax.psum(dense_sums, 'row')  273 us
    all_to_all x1, waiting for transfers between devices, body(): lax.all_to_all(send_tiles, 'col', split_axis=0, concat_axis=0, tiled=True)  81.1 us
    dot_general x3, matrix products, body(): jnp.einsum('kab,kbc->kac', tiles_here, jnp.einsum('kf,fab->kab', onehot,...  21.7 us
    dot_general x3, matrix products, body(): jnp.einsum('kba,kbc->kac', direction, tiles_here, precision=highest)  12.7 us
    dot_general x3, matrix products, body(): jnp.einsum('kf,fab->kab', onehot, summed, precision=highest)  12.4 us
    dot_general x3, matrix products, body(): jnp.einsum('kab,kbc->kac', row_diag, direction, precision=highest)  11.2 us
  transfers between devices with their start and end apart: 5, of which 5 were waited for; matrix products, arithmetic and copies ran while one was open for 9% of the time, Pallas kernels for 0%

commit v1 on v0

v1 whole, which is shorter than its diff:
```python
import functools

import jax
import jax.numpy as jnp
from jax import lax
from jax.experimental import pallas as pl
from jax.experimental.pallas import tpu as pltpu
from jax.sharding import PartitionSpec as P

SWEEPS = 4
STEP = 0.3
LAMBDA = 0.3 * 0.6
PER_STEP = 4

BF = jnp.bfloat16
F32 = jnp.float32
VMEM = pl.BlockSpec(memory_space=pltpu.VMEM)
SMEM = pl.BlockSpec(memory_space=pltpu.SMEM)
PARAMS = pltpu.CompilerParams(vmem_limit_bytes=20 * 1024 * 1024)


def split(x):
    high = x.astype(BF)
    low = (x - high.astype(F32)).astype(BF)
    return high, low


def dot(a, b):
    return jnp.dot(a, b, preferred_element_type=F32)


def shrink(x):
    return x - jnp.clip(x, -LAMBDA, LAMBDA)


def slice_kernel(group, features_ref, out_ref):
    r = lax.axis_index("row")
    variables = features_ref.shape[2]
    wanted = lax.broadcasted_iota(jnp.int32, (group, variables), 0) + r * group
    pick = (lax.broadcasted_iota(jnp.int32, (group, variables), 1) == wanted).astype(BF)
    for block in range(features_ref.shape[0]):
        rows = lax.dot_general(
            pick, features_ref[block], (((1,), (1,)), ((), ())), preferred_element_type=F32
        )
        out_ref[block] = rows.astype(BF)


def split_kernel(tiles_ref, out_ref):
    for s in range(tiles_ref.shape[0]):
        out_ref[s] = jnp.concatenate(split(tiles_ref[s]), axis=1)


def gather_kernel(wanted_ref, diag_ref, send_ref):
    for h in range(send_ref.shape[0]):
        for p in range(send_ref.shape[1]):
            send_ref[h, p] = diag_ref[wanted_ref[h, p]]


def covariance_kernel(
    rows_ref, lists_ref, owned_ref, slices_ref, features_ref, out_ref, left_ref,
):
    owners, slots = rows_ref.shape
    group = slices_ref.shape[1]
    samples = features_ref.shape[1]
    size = features_ref.shape[2]

    def owner_step(owner, carry):
        for k in range(slots):
            left_ref[k * group:(k + 1) * group, :] = slices_ref[rows_ref[owner, k]].astype(F32)
        left = left_ref[...].astype(BF)
        right = jnp.concatenate(
            [features_ref[owned_ref[owner, a]] for a in range(owned_ref.shape[1])], axis=1
        )
        both = dot(left, right) * (1.0 / samples)
        for k in range(slots):
            rows = both[k * group:(k + 1) * group]
            out_ref[owner, k] = jnp.where(
                lists_ref[owner, k] == 0, rows[:, :size], rows[:, size:]
            )
        return carry

    lax.fori_loop(0, owners, owner_step, 0)


def pair(x):
    size = x.shape[0]
    high = x[:, :size]
    return jnp.concatenate(
        [x, jnp.concatenate([high, jnp.zeros_like(high)], axis=1)], axis=0
    )


def add_product(s, d, column, tile, sums_ref):
    left = jnp.concatenate(split(d.T), axis=1)
    sums_ref[column] += dot(left, pair(tile))


def write_sums(sums_ref, out_ref):
    pieces, columns, group, size = out_ref.shape
    for a in range(columns):
        total = sums_ref[a][:, :size] + sums_ref[a][:, size:]
        out_ref[:, a] = total.reshape(pieces, group, size)


def first_kernel(
    list_ref, live_ref, cov_ref, theta_ref, tiles_ref, split_ref,
    base_ref, d_ref, out_ref, sums_ref,
):
    count, size, _ = theta_ref.shape
    step = pl.program_id(0)

    @pl.when(step == 0)
    def _():
        sums_ref[...] = jnp.zeros_like(sums_ref)

    for s in range(count):
        slot = step * count + s
        covariance = cov_ref[:, s].reshape(size, size)
        theta = theta_ref[s]
        base = theta - STEP * (covariance - tiles_ref[s])
        d = shrink(base) - theta
        d = jnp.where(slot < live_ref[0], d, 0.0)
        base_ref[s] = base
        d_ref[s] = d
        add_product(s, d, list_ref[slot], split_ref[s], sums_ref)

    @pl.when(step == pl.num_programs(0) - 1)
    def _():
        write_sums(sums_ref, out_ref)


def diagonal_kernel(list_ref, base_ref, d_ref, row_diag_ref, col_diag_ref, out_ref):
    count, size, _ = d_ref.shape
    step = pl.program_id(0)
    for s in range(count):
        d = d_ref[s]
        half = dot(row_diag_ref[s], jnp.concatenate(split(d), axis=1))
        half = half[:, :size] + half[:, size:]
        right = col_diag_ref[list_ref[step * count + s]]
        both = dot(
            jnp.concatenate(split(half), axis=1), jnp.concatenate([right, right], axis=0)
        )
        out_ref[s] = base_ref[s] + d - STEP * both


def sum_kernel(same_ref, in_ref, out_ref):
    same = same_ref[...].astype(BF)
    for g in range(in_ref.shape[1]):
        x = in_ref[:, g, :]
        x1, rest = x.astype(BF), x
        rest = rest - x1.astype(F32)
        x2 = rest.astype(BF)
        rest = rest - x2.astype(F32)
        x3 = rest.astype(BF)
        out_ref[:, g, :] = dot(
            jnp.concatenate([same, same, same], axis=1), jnp.concatenate([x1, x2, x3], axis=0)
        )


def sweep_kernel(last, list_ref, live_ref, t_ref, theta_ref, split_ref, q_ref, d_ref, *rest):
    count, size, _ = theta_ref.shape
    step = pl.program_id(0)
    if last:
        (right_ref,) = rest
    else:
        out_ref, right_ref, sums_ref = rest

    @pl.when(step == 0)
    def _():
        for a in range(q_ref.shape[1]):
            q = q_ref[:, a].reshape(size, size)
            right_ref[a] = pair(jnp.concatenate(split(q), axis=1))
        if not last:
            sums_ref[...] = jnp.zeros_like(sums_ref)

    for s in range(count):
        slot = step * count + s
        column = list_ref[slot]
        both = dot(split_ref[s], right_ref[column])
        product = both[:, :size] + both[:, size:]
        d = shrink(t_ref[s] - STEP * product) - theta_ref[s]
        d = jnp.where(slot < live_ref[0], d, 0.0)
        d_ref[s] = d
        if not last:
            add_product(s, d, column, split_ref[s], sums_ref)

    if not last:
        @pl.when(step == pl.num_programs(0) - 1)
        def _():
            write_sums(sums_ref, out_ref)


def shape(dims, dtype):
    return jax.ShapeDtypeStruct(dims, dtype)


def far(x):
    return pltpu.with_memory_space_constraint(x, pltpu.HBM)


def slot_blocks(*dims):
    return pl.BlockSpec((PER_STEP,) + dims, lambda i: (i,) + (0,) * len(dims))


def whole(*dims):
    return pl.BlockSpec(dims, lambda i: (0,) * len(dims))


def body(
    features,
    diag_inverse,
    precision_tiles,
    inverse_tiles,
    slot_rows,
    slot_columns,
    owned_columns,
    live_counts,
):
    row_count = lax.axis_size("row")
    col_count = lax.axis_size("col")
    r = lax.axis_index("row")
    c = lax.axis_index("col")
    blocks, samples, size = features.shape
    slots = precision_tiles.shape[2]
    columns = owned_columns.shape[2]
    per_source = slots // col_count
    group = size // row_count
    theta = precision_tiles[0, 0]
    tiles = inverse_tiles[0, 0]
    tile_shape = (slots, size, size)
    piece_shape = (row_count, columns, group, size)

    with jax.named_scope("slices"):
        per_step = 8
        mine = pl.pallas_call(
            functools.partial(slice_kernel, group),
            grid=(blocks // per_step,),
            in_specs=[pl.BlockSpec((per_step, samples, size), lambda i: (i, 0, 0))],
            out_specs=pl.BlockSpec((per_step, group, samples), lambda i: (i, 0, 0)),
            out_shape=shape((blocks, group, samples), BF),
        )(features)
        slices = lax.all_gather(mine, "col", axis=0, tiled=True)

    with jax.named_scope("tables"):
        rows_here = lax.dynamic_index_in_dim(slot_rows, c, 1, keepdims=False)
        lists_here = lax.dynamic_index_in_dim(slot_columns, c, 1, keepdims=False)
        owned_here = lax.dynamic_index_in_dim(owned_columns, c, 1, keepdims=False) - c * blocks
        my_list = lax.dynamic_index_in_dim(lists_here, r, 0, keepdims=False)
        live = lax.dynamic_slice(live_counts, (r, c), (1, 1)).reshape(1)
        wanted = lax.dynamic_slice(
            slot_rows, (r, 0, c * per_source), (1, col_count, per_source)
        ).reshape(col_count, per_source) - c * blocks
        flat = owned_here.reshape(-1)
        same = (flat[:, None] == flat[None, :]).astype(F32)
        my_owned = lax.dynamic_index_in_dim(owned_here, r, 0, keepdims=False)
        col_diag = jnp.take(diag_inverse, my_owned, axis=0)

    with jax.named_scope("diag"):
        send_diag = pl.pallas_call(
            gather_kernel,
            in_specs=[SMEM, VMEM],
            out_specs=VMEM,
            out_shape=shape((col_count, per_source, size, size), BF),
            compiler_params=PARAMS,
        )(wanted, diag_inverse)
        row_diag = lax.all_to_all(send_diag, "col", split_axis=0, concat_axis=0, tiled=True)
        row_diag = row_diag.reshape(tile_shape)

    steps = slots // PER_STEP
    tile_spec = slot_blocks(size, size)
    split_spec = slot_blocks(size, 2 * size)
    piece_spec = whole(*piece_shape)
    tile_out = pltpu.HBM(tile_shape, F32)
    sums = pltpu.VMEM((columns, size, 2 * size), F32)

    with jax.named_scope("split"):
        pairs = pl.pallas_call(
            split_kernel,
            grid=(steps,),
            in_specs=[tile_spec],
            out_specs=split_spec,
            out_shape=pltpu.HBM((slots, size, 2 * size), BF),
        )(tiles)

    with jax.named_scope("covariance"):
        partial = pl.pallas_call(
            covariance_kernel,
            in_specs=[SMEM, SMEM, SMEM, VMEM, VMEM],
            out_specs=VMEM,
            out_shape=shape((row_count, slots, group, size), F32),
            scratch_shapes=[pltpu.VMEM((slots * group, samples), F32)],
            compiler_params=PARAMS,
        )(rows_here, lists_here, owned_here, slices, features)
        partial, row_diag, pairs = lax.optimization_barrier((partial, row_diag, pairs))
        covariance = lax.all_to_all(partial, "row", split_axis=0, concat_axis=0, tiled=True)

    with jax.named_scope("first"):
        base, d, pieces = pl.pallas_call(
            first_kernel,
            grid=(steps,),
            in_specs=[
                SMEM,
                SMEM,
                pl.BlockSpec((row_count, PER_STEP, group, size), lambda i: (0, i, 0, 0)),
                tile_spec,
                tile_spec,
                split_spec,
            ],
            out_specs=[tile_spec, tile_spec, piece_spec],
            out_shape=[tile_out, tile_out, shape(piece_shape, F32)],
            scratch_shapes=[sums],
        )(my_list, live, covariance, far(theta), far(tiles), far(pairs))

    for sweep in range(1, SWEEPS):
        last = sweep == SWEEPS - 1
        with jax.named_scope("exchange"):
            got = lax.all_to_all(pieces, "row", split_axis=0, concat_axis=0, tiled=True)
            flat_shape = (row_count * columns, group, size)
            summed = pl.pallas_call(
                sum_kernel,
                in_specs=[VMEM, VMEM],
                out_specs=VMEM,
                out_shape=shape(flat_shape, F32),
            )(same, got.reshape(flat_shape))
            q = lax.all_to_all(
                summed.reshape(piece_shape), "row", split_axis=0, concat_axis=0, tiled=True
            )
        with jax.named_scope("diagonal"):
            t = pl.pallas_call(
                diagonal_kernel,
                grid=(steps,),
                in_specs=[
                    SMEM, tile_spec, tile_spec, tile_spec, whole(columns, size, size)
                ],
                out_specs=tile_spec,
                out_shape=tile_out,
            )(my_list, far(base), far(d), row_diag, col_diag)
        with jax.named_scope("sweep"):
            scratch = [pltpu.VMEM((columns, 2 * size, 2 * size), BF)]
            result = pl.pallas_call(
                functools.partial(sweep_kernel, last),
                grid=(steps,),
                in_specs=[SMEM, SMEM, tile_spec, tile_spec, split_spec, piece_spec],
                out_specs=[tile_spec] if last else [tile_spec, piece_spec],
                out_shape=[tile_out] if last else [tile_out, shape(piece_shape, F32)],
                scratch_shapes=scratch if last else scratch + [sums],
            )(my_list, live, far(t), far(theta), far(pairs), q)
            d = result[0]
            if not last:
                pieces = result[1]
    return d.reshape(precision_tiles.shape)


def solution(mesh):
    return jax.shard_map(
        body,
        mesh=mesh,
        in_specs=(
            P("col", None, None),
            P("col", None, None),
            P("row", "col", None, None, None),
            P("row", "col", None, None, None),
            P(),
            P(),
            P(),
            P(),
        ),
        out_specs=P("row", "col", None, None, None),
        check_vma=False,
    )
```

time: 515 us -> 257 us (0.50)
  waiting for transfers between devices: 362 us -> 81.5 us
  Pallas kernels: 0 us -> 83.2 us
  matrix products: 78.1 us -> 0 us
  blocking collectives: 0 us -> 30.3 us
  local copies, waits for them, and re-layouts: 31.6 us -> 12.5 us
  starting transfers between devices: 16.1 us -> 29.7 us
  other arithmetic: 9.75 us -> 2.58 us
    psum x3 -> x0, waiting for transfers between devices: 273 us -> none  [body(): summed = lax.psum(dense_sums, 'row')]
    pallas_call x0 -> x14, Pallas kernels: none -> 83.2 us  [the longest x3 26.3 us: body(): pl.pallas_call(functools.partial(sweep_kernel, last), grid=(steps,), in_s...]
    dot_general x19 -> x0, matrix products: 78.1 us -> none  [the longest x3 21.7 us: body(): jnp.einsum('kab,kbc->kac', tiles_here, jnp.einsum('kf,fab->kab', onehot,...]
    all_gather x0 -> x1, waiting for transfers between devices: none -> 43.7 us  [body(): slices = lax.all_gather(mine, 'col', axis=0, tiled=True)]
    all_to_all x1 -> x5, waiting for transfers between devices: 81.1 us -> 37.8 us  [the longest x1 29.4 us: body(): lax.all_to_all(partial, 'row', split_axis=0, concat_axis=0, tiled=True)]
    all_to_all x0 -> x2, blocking collectives: none -> 30.3 us  [body(): got = lax.all_to_all(pieces, 'row', split_axis=0, concat_axis=0, tiled=True)]
    gather x5 -> x1, local copies, waits for them, and re-layouts: 14.3 us -> 0.56 us  [body(): col_diag = jnp.take(diag_inverse, my_owned, axis=0)]
    all_to_all x1 -> x5, starting transfers between devices: 8.59 us -> 21.1 us  [the longest x3 10.5 us: body(): lax.all_to_all(summed.reshape(piece_shape), 'row', split_axis=0, concat_a...]
  transfers between devices with their start and end apart: 5 -> 7, of which waited for: 5 -> 5; matrix products, arithmetic and copies ran while one was open for 9% -> 3% of each run, Pallas kernels for 0% -> 14%
where the time goes in v1:
time: 257 us; the launch traced here: 253 us
  Pallas kernels  83.2 us (32%)
  waiting for transfers between devices  81.5 us (32%)
  blocking collectives  30.3 us (12%)
  starting transfers between devices  29.7 us (12%)
  between operations  13.5 us (5%)
  local copies, waits for them, and re-layouts  12.5 us (5%)
  other arithmetic  2.58 us (1%)
    all_gather x1, waiting for transfers between devices, body(): slices = lax.all_gather(mine, 'col', axis=0, tiled=True)  43.7 us
    all_to_all x2, blocking collectives, body(): got = lax.all_to_all(pieces, 'row', split_axis=0, concat_axis=0, tiled=True)  30.3 us
    all_to_all x1, waiting for transfers between devices, body(): lax.all_to_all(partial, 'row', split_axis=0, concat_axis=0, tiled=True)  29.4 us
    pallas_call x3, Pallas kernels, body(): pl.pallas_call(functools.partial(sweep_kernel, last), grid=(steps,), in_s...  26.3 us
    pallas_call x3, Pallas kernels, body(): pl.pallas_call(diagonal_kernel, grid=(steps,), in_specs=[SMEM, tile_spec,...  23.1 us
    all_to_all x3, starting transfers between devices, body(): lax.all_to_all(summed.reshape(piece_shape), 'row', split_axis=0, concat_a...  10.5 us
    pallas_call x1, Pallas kernels, body(): pl.pallas_call(first_kernel, grid=(steps,), in_specs=[SMEM, SMEM, pl.Bloc...  9.05 us
    all_to_all x1, starting transfers between devices, body(): lax.all_to_all(send_diag, 'col', split_axis=0, concat_axis=0, tiled=True)  8.59 us
  transfers between devices with their start and end apart: 7, of which 5 were waited for; matrix products, arithmetic and copies ran while one was open for 3% of the time, Pallas kernels for 14%

profile of v1, /device:TPU:32, one launch (start us, length us, event | category | flops | bytes accessed | tf_op | source)
XLA Modules:
  0.0 253.3 jit_solution(4777376697090125194)
XLA Ops:
  6.5 0.0 copy-start.2
  6.5 0.0 all-gather.2.cloned.1.call-start
  6.5 4.6 %slices.1 = bf16[32,8,512]{2,1,0:T(8,128)(2,1)} custom-call(bf16[32,512,128]{2,1,0:T(8,128)(2,1)} %features_ref.3), custom_call_target="tpu_custom_call" | custom-call | tf_op jit(solution)/shard_map/slices/pallas_call | solution.py:235
  11.2 0.0 all-gather.2.cloned.1.call-update
  11.2 0.8 dynamic-slice_subtract_fusion.1
  12.0 0.1 copy.26
  12.1 0.1 copy.24.wanted_ref
  12.2 0.0 copy-done.2
  12.2 0.0 copy-start.8
  12.2 1.7 diag.1
  13.9 8.6 %all-to-all-start = ((bf16[16,2,128,128]{3,2,1,0:T(8,128)(2,1)}), bf16[16,2,128,128]{3,2,1,0:T(8,128)(2,1)S(1)}, u32[]{:S(2)}, u32[]{:S(2)}) async-start(bf16[16,2,128,128]{3,2,1,0:T(8,128)(2,1)} %diag.1), calls=%async_computation | async-start | bytes 2097152 | tf_op jit(solution)/shard_map/diag/all_to_all | solution.py:266
  22.5 0.0 copy-done.8
  22.5 0.4 fusion.3
  22.9 0.1 copy.21
  23.0 0.1 copy.22.owned_ref
  23.1 5.7 %split.1.split_ref = bf16[32,128,256]{2,1,0:T(8,128)(2,1)} custom-call(f32[32,128,128]{2,1,0:T(8,128)} %bitcast.30), custom_call_target="tpu_custom_call" | custom-call | tf_op jit(solution)/shard_map/split/pallas_call | solution.py:277
  28.8 0.9 constant_dynamic-slice_fusion.1
  29.6 43.7 %all-gather.2.cloned.1.call-done.slices_ref = bf16[512,8,512]{2,1,0:T(8,128)(2,1)} async-done(((bf16[32,8,512]{2,1,0:T(8,128)(2,1)}), bf16[512,8,512]{2,1,0:T(8,128)(2,1)}) %all-gather.2.cloned.1.call-update) | async-done | bytes 4194320 | tf_op jit(solution)/shard_map/slices/all_gather | solution.py:242
  73.3 0.0 copy-start
  73.3 2.2 copy-done
  75.5 0.0 copy-start.1
  75.5 2.2 copy-done.1
  77.7 6.0 %covariance.1 = f32[16,32,8,128]{3,2,1,0:T(8,128)} custom-call(s32[16,32]{1,0:T(8,128)S(1)} %bitcast.22, s32[16,32]{1,0:T(8,128)S(1)} %bitcast.21, s32[16,2]{1,0:T(8,128)S(1)} %copy.22.owned_ref, bf16[512,8,512]{2,1,0:T(8,128)(2,1)S(1)} %copy-done.1, bf16[32,512,128]{2,1,0:T(8,128)(2,1)S(1)} %copy-done), custom_call_target="tpu_custom_call" | custom-call | tf_op jit(solution)/shard_map/covariance/pallas_call | solution.py:286
  83.7 0.0 all-to-all-done
  83.7 0.0 copy-start.3
  83.7 1.0 copy-done.3
  84.7 7.0 %all-to-all-start.1 = ((f32[16,32,8,128]{3,2,1,0:T(8,128)}), f32[16,32,8,128]{3,2,1,0:T(8,128)}, u32[]{:S(2)}, u32[]{:S(2)}) async-start(f32[16,32,8,128]{3,2,1,0:T(8,128)} %covariance.1), calls=%async_computation.1 | async-start | bytes 4194304 | tf_op jit(solution)/shard_map/covariance/all_to_all | solution.py:295
  91.8 0.1 fusion
  91.9 1.3 dynamic_slice.26
  93.2 0.1 sub.24
  93.3 0.6 gather_fusion
  93.8 1.3 fusion.1.list_ref
  95.1 0.7 compare_convert_fusion.same_ref
  95.8 29.4 %all-to-all-done.1.cov_ref = f32[16,32,8,128]{3,2,1,0:T(8,128)} async-done(((f32[16,32,8,128]{3,2,1,0:T(8,128)}), f32[16,32,8,128]{3,2,1,0:T(8,128)}, u32[]{:S(2)}, u32[]{:S(2)}) %all-to-all-start.1) | async-done | bytes 2097184 | tf_op jit(solution)/shard_map/covariance/all_to_all | solution.py:295
  125.2 9.0 %first.1 = (f32[32,128,128]{2,1,0:T(8,128)}, f32[32,128,128]{2,1,0:T(8,128)}, f32[16,2,8,128]{3,2,1,0:T(8,128)}) custom-call(s32[32]{0:T(128)} %fusion.1.list_ref, s32[1]{0:T(128)} %bitcast.1.live_ref, f32[16,32,8,128]{3,2,1,0:T(8,128)} %all-to-all-done.1.cov_ref, f32[32,128,128]{2,1,0:T(8,128)} %bitcast.23, f32[32,128,128]{2,1,0:T(8,128)} %bitcast.31, ...), custom_call_target="tpu_custom_call" | custom-call | tf_op jit(solution)/shard_map/first/pallas_call | solution.py:298
  134.2 3.6 %all-to-all-start.2 = ((f32[16,2,8,128]{3,2,1,0:T(8,128)}), f32[16,2,8,128]{3,2,1,0:T(8,128)S(1)}, u32[]{:S(2)}, u32[]{:S(2)}) async-start(f32[16,2,8,128]{3,2,1,0:T(8,128)} %get-tuple-element.20), calls=%async_computation.2 | async-start | bytes 262144 | tf_op jit(solution)/shard_map/exchange/all_to_all | solution.py:317
  137.8 8.0 %all-to-all-done.2 = f32[16,2,8,128]{3,2,1,0:T(8,128)S(1)} async-done(((f32[16,2,8,128]{3,2,1,0:T(8,128)}), f32[16,2,8,128]{3,2,1,0:T(8,128)S(1)}, u32[]{:S(2)}, u32[]{:S(2)}) %all-to-all-start.2) | async-done | bytes 131104 | tf_op jit(solution)/shard_map/exchange/all_to_all | solution.py:317
  145.8 0.0 copy-start.7
  145.8 0.7 copy-done.7
  146.4 2.2 exchange.3
  148.6 3.5 %all-to-all-start.3 = ((f32[16,2,8,128]{3,2,1,0:T(8,128)}), f32[16,2,8,128]{3,2,1,0:T(8,128)S(1)}, u32[]{:S(2)}, u32[]{:S(2)}) async-start(f32[16,2,8,128]{3,2,1,0:T(8,128)} %bitcast.34), calls=%async_computation.3 | async-start | bytes 262144 | tf_op jit(solution)/shard_map/exchange/all_to_all | solution.py:325
  152.2 0.7 broadcast_select_fusion.col_diag_ref
  152.9 7.7 %diagonal.3.t_ref = f32[32,128,128]{2,1,0:T(8,128)} custom-call(s32[32]{0:T(128)} %fusion.1.list_ref, f32[32,128,128]{2,1,0:T(8,128)} %get-tuple-element.17.base_ref, f32[32,128,128]{2,1,0:T(8,128)} %get-tuple-element.18.d_ref, bf16[32,128,128]{2,1,0:T(8,128)(2,1)} %bitcast.27, bf16[2,128,128]{2,1,0:T(8,128)(2,1)} %broadcast_select_fusion.col_diag_ref), custom_call_target="tpu_custom_call" | custom-call | tf_op jit(solution)/shard_map/diagonal/pallas_call | solution.py:329
  160.6 0.0 all-to-all-done.3.q_ref
  160.6 0.0 copy-start.5
  160.6 0.6 copy-done.5
  161.2 9.1 %sweep.3 = (f32[32,128,128]{2,1,0:T(8,128)}, f32[16,2,8,128]{3,2,1,0:T(8,128)}) custom-call(s32[32]{0:T(128)} %fusion.1.list_ref, s32[1]{0:T(128)} %bitcast.1.live_ref, f32[32,128,128]{2,1,0:T(8,128)} %diagonal.3.t_ref, f32[32,128,128]{2,1,0:T(8,128)} %bitcast.24, bf16[32,128,256]{2,1,0:T(8,128)(2,1)} %split.1.split_ref, f32[16,2,8,128]{3,2,1,0:T(8,128)} %copy-done.5), custom_call_target="tpu_custom_call" | custom-call | tf_op jit(solution)/shard_map/sweep/pallas_call | solution.py:340
  170.3 15.3 %all_to_all.40 = f32[16,2,8,128]{3,2,1,0:T(8,128)} all-to-all(f32[16,2,8,128]{3,2,1,0:T(8,128)} %get-tuple-element.22), channel_id=1, replica_groups=mesh['row'=16,'col'=16] {'row'}, dimensions={0} | all-to-all | bytes 262144 | tf_op jit(solution)/shard_map/exchange/all_to_all | solution.py:317
  185.6 2.2 exchange.4
  187.8 3.5 %all-to-all-start.5 = ((f32[16,2,8,128]{3,2,1,0:T(8,128)}), f32[16,2,8,128]{3,2,1,0:T(8,128)S(1)}, u32[]{:S(2)}, u32[]{:S(2)}) async-start(f32[16,2,8,128]{3,2,1,0:T(8,128)} %bitcast.35), calls=%async_computation.5 | async-start | bytes 262144 | tf_op jit(solution)/shard_map/exchange/all_to_all | solution.py:325
  191.3 7.7 %diagonal.4.t_ref = f32[32,128,128]{2,1,0:T(8,128)} custom-call(s32[32]{0:T(128)} %fusion.1.list_ref, f32[32,128,128]{2,1,0:T(8,128)} %get-tuple-element.17.base_ref, f32[32,128,128]{2,1,0:T(8,128)} %get-tuple-element.21.d_ref, bf16[32,128,128]{2,1,0:T(8,128)(2,1)} %bitcast.28, bf16[2,128,128]{2,1,0:T(8,128)(2,1)} %broadcast_select_fusion.col_diag_ref), custom_call_target="tpu_custom_call" | custom-call | tf_op jit(solution)/shard_map/diagonal/pallas_call | solution.py:329
  199.0 0.2 all-to-all-done.5.q_ref
  199.3 0.0 copy-start.6
  199.3 0.6 copy-done.6
  199.9 9.1 %sweep.4 = (f32[32,128,128]{2,1,0:T(8,128)}, f32[16,2,8,128]{3,2,1,0:T(8,128)}) custom-call(s32[32]{0:T(128)} %fusion.1.list_ref, s32[1]{0:T(128)} %bitcast.1.live_ref, f32[32,128,128]{2,1,0:T(8,128)} %diagonal.4.t_ref, f32[32,128,128]{2,1,0:T(8,128)} %bitcast.25, bf16[32,128,256]{2,1,0:T(8,128)(2,1)} %split.1.split_ref, f32[16,2,8,128]{3,2,1,0:T(8,128)} %copy-done.6), custom_call_target="tpu_custom_call" | custom-call | tf_op jit(solution)/shard_map/sweep/pallas_call | solution.py:340
  209.0 15.0 %all_to_all.41 = f32[16,2,8,128]{3,2,1,0:T(8,128)} all-to-all(f32[16,2,8,128]{3,2,1,0:T(8,128)} %get-tuple-element.24), channel_id=1, replica_groups=mesh['row'=16,'col'=16] {'row'}, dimensions={0} | all-to-all | bytes 262144 | tf_op jit(solution)/shard_map/exchange/all_to_all | solution.py:317
  224.0 2.2 exchange.5
  226.2 3.5 %all-to-all-start.7 = ((f32[16,2,8,128]{3,2,1,0:T(8,128)}), f32[16,2,8,128]{3,2,1,0:T(8,128)S(1)}, u32[]{:S(2)}, u32[]{:S(2)}) async-start(f32[16,2,8,128]{3,2,1,0:T(8,128)} %bitcast.32), calls=%async_computation.7 | async-start | bytes 262144 | tf_op jit(solution)/shard_map/exchange/all_to_all | solution.py:325
  229.7 7.7 %diagonal.5.t_ref = f32[32,128,128]{2,1,0:T(8,128)} custom-call(s32[32]{0:T(128)} %fusion.1.list_ref, f32[32,128,128]{2,1,0:T(8,128)} %get-tuple-element.17.base_ref, f32[32,128,128]{2,1,0:T(8,128)} %get-tuple-element.23.d_ref, bf16[32,128,128]{2,1,0:T(8,128)(2,1)} %bitcast.29, bf16[2,128,128]{2,1,0:T(8,128)(2,1)} %broadcast_select_fusion.col_diag_ref), custom_call_target="tpu_custom_call" | custom-call | tf_op jit(solution)/shard_map/diagonal/pallas_call | solution.py:329
  237.5 0.2 all-to-all-done.7.q_ref
  237.7 0.0 copy-start.4
  237.7 0.6 copy-done.4
  238.3 8.1 %sweep.5 = f32[32,128,128]{2,1,0:T(8,128)} custom-call(s32[32]{0:T(128)} %fusion.1.list_ref, s32[1]{0:T(128)} %bitcast.1.live_ref, f32[32,128,128]{2,1,0:T(8,128)} %diagonal.5.t_ref, f32[32,128,128]{2,1,0:T(8,128)} %bitcast.26, bf16[32,128,256]{2,1,0:T(8,128)(2,1)} %split.1.split_ref, f32[16,2,8,128]{3,2,1,0:T(8,128)} %copy-done.4), custom_call_target="tpu_custom_call" | custom-call | tf_op jit(solution)/shard_map/sweep/pallas_call | solution.py:340
  (3 shorter events, 0.0 us)
Async XLA Ops:
  6.5 5.6 %copy-start.2 = (bf16[32,128,128]{2,1,0:T(8,128)(2,1)S(1)}, bf16[32,128,128]{2,1,0:T(8,128)(2,1)}, u32[]{:S(2)}) copy-start(bf16[32,128,128]{2,1,0:T(8,128)(2,1)} %diag_ref.1) | copy-start | bytes 3145732
  6.5 66.8 %all-gather.2.cloned.1.call-start = ((), (), s32[]{:S(2)}) async-start(), calls=%async_computation.8 | async-start | bytes 4456448 | tf_op jit(solution)/shard_map/slices/all_gather | solution.py:242
  12.2 10.3 %copy-start.8 = (s32[16,16,2]{1,2,0:T(2,128)S(1)}, s32[16,16,2]{1,2,0:T(2,128)}, u32[]{:S(2)}) copy-start(s32[16,16,2]{1,2,0:T(2,128)} %param.14) | copy-start | bytes 6148
  13.9 69.8 %all-to-all-start = ((bf16[16,2,128,128]{3,2,1,0:T(8,128)(2,1)}), bf16[16,2,128,128]{3,2,1,0:T(8,128)(2,1)S(1)}, u32[]{:S(2)}, u32[]{:S(2)}) async-start(bf16[16,2,128,128]{3,2,1,0:T(8,128)(2,1)} %diag.1), calls=%async_computation | async-start | bytes 2097152 | tf_op jit(solution)/shard_map/diag/all_to_all | solution.py:266
  73.3 2.2 copy-start
  75.5 2.2 copy-start.1
  83.7 1.0 copy-start.3
  84.7 40.5 %all-to-all-start.1 = ((f32[16,32,8,128]{3,2,1,0:T(8,128)}), f32[16,32,8,128]{3,2,1,0:T(8,128)}, u32[]{:S(2)}, u32[]{:S(2)}) async-start(f32[16,32,8,128]{3,2,1,0:T(8,128)} %covariance.1), calls=%async_computation.1 | async-start | bytes 4194304 | tf_op jit(solution)/shard_map/covariance/all_to_all | solution.py:295
  134.2 11.6 %all-to-all-start.2 = ((f32[16,2,8,128]{3,2,1,0:T(8,128)}), f32[16,2,8,128]{3,2,1,0:T(8,128)S(1)}, u32[]{:S(2)}, u32[]{:S(2)}) async-start(f32[16,2,8,128]{3,2,1,0:T(8,128)} %get-tuple-element.20), calls=%async_computation.2 | async-start | bytes 262144 | tf_op jit(solution)/shard_map/exchange/all_to_all | solution.py:317
  145.8 0.7 copy-start.7
  148.6 11.9 %all-to-all-start.3 = ((f32[16,2,8,128]{3,2,1,0:T(8,128)}), f32[16,2,8,128]{3,2,1,0:T(8,128)S(1)}, u32[]{:S(2)}, u32[]{:S(2)}) async-start(f32[16,2,8,128]{3,2,1,0:T(8,128)} %bitcast.34), calls=%async_computation.3 | async-start | bytes 262144 | tf_op jit(solution)/shard_map/exchange/all_to_all | solution.py:325
  160.6 0.6 copy-start.5
  187.8 11.5 %all-to-all-start.5 = ((f32[16,2,8,128]{3,2,1,0:T(8,128)}), f32[16,2,8,128]{3,2,1,0:T(8,128)S(1)}, u32[]{:S(2)}, u32[]{:S(2)}) async-start(f32[16,2,8,128]{3,2,1,0:T(8,128)} %bitcast.35), calls=%async_computation.5 | async-start | bytes 262144 | tf_op jit(solution)/shard_map/exchange/all_to_all | solution.py:325
  199.3 0.6 copy-start.6
  226.2 11.5 %all-to-all-start.7 = ((f32[16,2,8,128]{3,2,1,0:T(8,128)}), f32[16,2,8,128]{3,2,1,0:T(8,128)S(1)}, u32[]{:S(2)}, u32[]{:S(2)}) async-start(f32[16,2,8,128]{3,2,1,0:T(8,128)} %bitcast.32), calls=%async_computation.7 | async-start | bytes 262144 | tf_op jit(solution)/shard_map/exchange/all_to_all | solution.py:325
  237.7 0.7 copy-start.4
Sparse Core Ops, SparseCore 0:
  11.3 61.9 all-gather.1

commit v2 on v1

v2 whole, which is shorter than its diff:
```python
import functools

import jax
import jax.numpy as jnp
from jax import lax
from jax.experimental import pallas as pl
from jax.experimental.pallas import tpu as pltpu
from jax.sharding import PartitionSpec as P

SWEEPS = 4
STEP = 0.3
LAMBDA = 0.3 * 0.6
PER_STEP = 8
CHUNK = 4

BF = jnp.bfloat16
F32 = jnp.float32
VMEM = pl.BlockSpec(memory_space=pltpu.VMEM)
HBM = pl.BlockSpec(memory_space=pltpu.HBM)
SMEM = pl.BlockSpec(memory_space=pltpu.SMEM)
PARAMS = pltpu.CompilerParams(vmem_limit_bytes=20 * 1024 * 1024)


def split(x):
    high = x.astype(BF)
    low = (x - high.astype(F32)).astype(BF)
    return high, low


def dot(a, b):
    return jnp.dot(a, b, preferred_element_type=F32)


def shrink(x):
    return x - jnp.clip(x, -LAMBDA, LAMBDA)


def slice_kernel(group, features_ref, out_ref):
    r = lax.axis_index("row")
    variables = features_ref.shape[2]
    wanted = lax.broadcasted_iota(jnp.int32, (group, variables), 0) + r * group
    pick = (lax.broadcasted_iota(jnp.int32, (group, variables), 1) == wanted).astype(BF)
    for block in range(features_ref.shape[0]):
        rows = lax.dot_general(
            pick, features_ref[block], (((1,), (1,)), ((), ())), preferred_element_type=F32
        )
        out_ref[block] = rows.astype(BF)


def split_kernel(tiles_ref, out_ref):
    for s in range(tiles_ref.shape[0]):
        out_ref[s] = jnp.concatenate(split(tiles_ref[s]), axis=1)


def gather_kernel(wanted_ref, diag_ref, *out_refs):
    c = lax.axis_index("col")
    for offset, out_ref in enumerate(out_refs):
        target = lax.rem(c + offset, len(out_refs))
        for p in range(out_ref.shape[0]):
            out_ref[p] = diag_ref[wanted_ref[target, p]]


class Tiles:
    def __init__(self, far_ref, near_ref, sem, back=False):
        self.refs = (near_ref, far_ref) if back else (far_ref, near_ref)
        self.near = near_ref
        self.sem = sem
        self.chunks = near_ref.shape[0] // CHUNK

    def copy(self, i):
        part = pl.ds(i * CHUNK, CHUNK)
        source, target = (ref.at[part] for ref in self.refs)
        return pltpu.make_async_copy(source, target, self.sem.at[i])

    def start(self, i):
        self.copy(i).start()

    def wait(self, i):
        self.copy(i).wait()


def start_all(arrays, chunks):
    for i in range(chunks):
        for array in arrays:
            array.start(i)


def each_slot(chunks, arrays, outs, slot_step):
    def step(i, carry):
        for array in arrays:
            array.wait(i)
        for s in range(CHUNK):
            slot_step(i * CHUNK + s)
        for out in outs:
            out.start(i)
        return carry

    lax.fori_loop(0, chunks, step, 0)
    for i in range(chunks):
        for out in outs:
            out.wait(i)


def covariance_kernel(
    rows_ref, lists_ref, owned_ref, far_slices, features, out_ref,
    slices_ref, right_ref, left_ref, slice_sem, right_sem,
):
    owners, slots = rows_ref.shape
    columns = owned_ref.shape[1]
    group = slices_ref.shape[1]
    samples = features.shape[1]
    size = features.shape[2]
    blocks = features.shape[0]
    parts = slices_ref.shape[0] // blocks

    def slice_copy(i):
        part = pl.ds(i * blocks, blocks)
        return pltpu.make_async_copy(far_slices.at[part], slices_ref.at[part], slice_sem.at[i])

    def right_copy(owner, a):
        return pltpu.make_async_copy(
            features.at[owned_ref[owner, a]], right_ref.at[owner, a], right_sem.at[owner, a]
        )

    for i in range(parts):
        slice_copy(i).start()
    for owner in range(owners):
        for a in range(columns):
            right_copy(owner, a).start()
    for i in range(parts):
        slice_copy(i).wait()

    def owner_step(owner, carry):
        for a in range(columns):
            right_copy(owner, a).wait()
        for k in range(slots):
            left_ref[k * group:(k + 1) * group, :] = slices_ref[rows_ref[owner, k]].astype(F32)
        left = left_ref[...].astype(BF)
        right = jnp.concatenate([right_ref[owner, a] for a in range(columns)], axis=1)
        both = dot(left, right) * (1.0 / samples)
        for k in range(slots):
            rows = both[k * group:(k + 1) * group]
            out_ref[owner, k] = jnp.where(
                lists_ref[owner, k] == 0, rows[:, :size], rows[:, size:]
            )
        return carry

    lax.fori_loop(0, owners, owner_step, 0)


def pair(x):
    size = x.shape[0]
    high = x[:, :size]
    return jnp.concatenate(
        [x, jnp.concatenate([high, jnp.zeros_like(high)], axis=1)], axis=0
    )


def add_product(d, column, tile, sums_ref):
    left = jnp.concatenate(split(d.T), axis=1)
    sums_ref[column] += dot(left, pair(tile))


def write_sums(sums_ref, out_ref):
    pieces, columns, group, size = out_ref.shape
    for a in range(columns):
        total = sums_ref[a][:, :size] + sums_ref[a][:, size:]
        out_ref[:, a] = total.reshape(pieces, group, size)


def first_kernel(
    list_ref, live_ref, cov_ref, far_theta, far_tiles, far_base, far_d, out_ref,
    theta_ref, tiles_ref, base_ref, d_ref, sums_ref, sems,
):
    slots, size, _ = theta_ref.shape
    chunks = slots // CHUNK
    arrays = [Tiles(far_theta, theta_ref, sems.at[0]), Tiles(far_tiles, tiles_ref, sems.at[1])]
    outs = [Tiles(far_base, base_ref, sems.at[2], True), Tiles(far_d, d_ref, sems.at[3], True)]
    start_all(arrays, chunks)
    sums_ref[...] = jnp.zeros_like(sums_ref)

    def slot_step(slot):
        covariance = cov_ref[:, slot].reshape(size, size)
        theta = theta_ref[slot]
        tile = tiles_ref[slot]
        base = theta - STEP * (covariance - tile)
        d = jnp.where(slot < live_ref[0], shrink(base) - theta, 0.0)
        base_ref[slot] = base
        d_ref[slot] = d
        halves = jnp.concatenate(split(tile), axis=1)
        add_product(d, list_ref[slot], halves, sums_ref)

    each_slot(chunks, arrays, outs, slot_step)
    write_sums(sums_ref, out_ref)


def diagonal_kernel(list_ref, far_base, far_d, col_diag_ref, *rest):
    far_diag = rest[:-7]
    far_out, base_ref, d_ref, diag_ref, out_ref, diag_sem, sems = rest[-7:]
    slots, size, _ = d_ref.shape
    chunks = slots // CHUNK
    c = lax.axis_index("col")
    per_source = slots // len(far_diag)
    arrays = [Tiles(far_base, base_ref, sems.at[0]), Tiles(far_d, d_ref, sems.at[1])]
    out = Tiles(far_out, out_ref, sems.at[2], True)

    def diag_copy(offset):
        source = lax.rem(c + len(far_diag) - offset, len(far_diag))
        return pltpu.make_async_copy(
            far_diag[offset], diag_ref.at[pl.ds(source * per_source, per_source)],
            diag_sem.at[offset],
        )

    for offset in range(len(far_diag)):
        diag_copy(offset).start()
    start_all(arrays, chunks)
    for offset in range(len(far_diag)):
        diag_copy(offset).wait()

    def slot_step(slot):
        d = d_ref[slot]
        half = dot(diag_ref[slot], jnp.concatenate(split(d), axis=1))
        half = half[:, :size] + half[:, size:]
        right = col_diag_ref[list_ref[slot]]
        both = dot(
            jnp.concatenate(split(half), axis=1), jnp.concatenate([right, right], axis=0)
        )
        out_ref[slot] = base_ref[slot] + d - STEP * both

    each_slot(chunks, arrays, [out], slot_step)


def sum_kernel(same_ref, in_ref, out_ref):
    same = same_ref[...].astype(BF)
    for g in range(in_ref.shape[1]):
        x = in_ref[:, g, :]
        x1, rest = x.astype(BF), x
        rest = rest - x1.astype(F32)
        x2 = rest.astype(BF)
        rest = rest - x2.astype(F32)
        x3 = rest.astype(BF)
        out_ref[:, g, :] = dot(
            jnp.concatenate([same, same, same], axis=1), jnp.concatenate([x1, x2, x3], axis=0)
        )


def sweep_kernel(
    last, list_ref, live_ref, far_t, far_theta, far_pairs, q_ref, far_d, *rest
):
    if last:
        t_ref, theta_ref, pairs_ref, d_ref, right_ref, sems = rest
    else:
        out_ref, t_ref, theta_ref, pairs_ref, d_ref, right_ref, sems, sums_ref = rest
    slots, size, _ = theta_ref.shape
    chunks = slots // CHUNK
    arrays = [
        Tiles(far_pairs, pairs_ref, sems.at[0]),
        Tiles(far_t, t_ref, sems.at[1]),
        Tiles(far_theta, theta_ref, sems.at[2]),
    ]
    out = Tiles(far_d, d_ref, sems.at[3], True)
    start_all(arrays, chunks)
    for a in range(q_ref.shape[1]):
        q = q_ref[:, a].reshape(size, size)
        right_ref[a] = pair(jnp.concatenate(split(q), axis=1))
    if not last:
        sums_ref[...] = jnp.zeros_like(sums_ref)

    def slot_step(slot):
        column = list_ref[slot]
        both = dot(pairs_ref[slot], right_ref[column])
        product = both[:, :size] + both[:, size:]
        d = shrink(t_ref[slot] - STEP * product) - theta_ref[slot]
        d = jnp.where(slot < live_ref[0], d, 0.0)
        d_ref[slot] = d
        if not last:
            add_product(d, column, pairs_ref[slot], sums_ref)

    each_slot(chunks, arrays, [out], slot_step)
    if not last:
        write_sums(sums_ref, out_ref)


def shape(dims, dtype):
    return jax.ShapeDtypeStruct(dims, dtype)


def far(x):
    return pltpu.with_memory_space_constraint(x, pltpu.HBM)


def slot_blocks(*dims):
    return pl.BlockSpec((PER_STEP,) + dims, lambda i: (i,) + (0,) * len(dims))


def body(
    features,
    diag_inverse,
    precision_tiles,
    inverse_tiles,
    slot_rows,
    slot_columns,
    owned_columns,
    live_counts,
):
    row_count = lax.axis_size("row")
    col_count = lax.axis_size("col")
    r = lax.axis_index("row")
    c = lax.axis_index("col")
    blocks, samples, size = features.shape
    slots = precision_tiles.shape[2]
    columns = owned_columns.shape[2]
    per_source = slots // col_count
    group = size // row_count
    theta = precision_tiles[0, 0]
    tiles = inverse_tiles[0, 0]
    tile_shape = (slots, size, size)
    piece_shape = (row_count, columns, group, size)

    with jax.named_scope("slices"):
        per_step = 8
        mine = pl.pallas_call(
            functools.partial(slice_kernel, group),
            grid=(blocks // per_step,),
            in_specs=[pl.BlockSpec((per_step, samples, size), lambda i: (i, 0, 0))],
            out_specs=pl.BlockSpec((per_step, group, samples), lambda i: (i, 0, 0)),
            out_shape=shape((blocks, group, samples), BF),
        )(features)
        slices = lax.all_gather(mine, "col", axis=0, tiled=True)

    with jax.named_scope("tables"):
        rows_here = lax.dynamic_index_in_dim(slot_rows, c, 1, keepdims=False)
        lists_here = lax.dynamic_index_in_dim(slot_columns, c, 1, keepdims=False)
        owned_here = lax.dynamic_index_in_dim(owned_columns, c, 1, keepdims=False) - c * blocks
        my_list = lax.dynamic_index_in_dim(lists_here, r, 0, keepdims=False)
        live = lax.dynamic_slice(live_counts, (r, c), (1, 1)).reshape(1)
        wanted = lax.dynamic_slice(
            slot_rows, (r, 0, c * per_source), (1, col_count, per_source)
        ).reshape(col_count, per_source) - c * blocks
        flat = owned_here.reshape(-1)
        same = (flat[:, None] == flat[None, :]).astype(F32)
        my_owned = lax.dynamic_index_in_dim(owned_here, r, 0, keepdims=False)
        col_diag = jnp.take(diag_inverse, my_owned, axis=0)

    tile_vmem = pltpu.VMEM(tile_shape, F32)
    tile_out = pltpu.HBM(tile_shape, F32)
    sums = pltpu.VMEM((columns, size, 2 * size), F32)
    chunks = slots // CHUNK

    def sems(*dims):
        return pltpu.SemaphoreType.DMA(dims)

    with jax.named_scope("split"):
        pairs = pl.pallas_call(
            split_kernel,
            grid=(slots // PER_STEP,),
            in_specs=[slot_blocks(size, size)],
            out_specs=slot_blocks(size, 2 * size),
            out_shape=pltpu.HBM((slots, size, 2 * size), BF),
        )(far(tiles))
        slices, pairs = lax.optimization_barrier((slices, pairs))

    with jax.named_scope("covariance"):
        partial = pl.pallas_call(
            covariance_kernel,
            in_specs=[SMEM, SMEM, SMEM, HBM, HBM],
            out_specs=VMEM,
            out_shape=pltpu.HBM((row_count, slots, group, size), F32),
            scratch_shapes=[
                pltpu.VMEM(slices.shape, BF),
                pltpu.VMEM((row_count, columns, samples, size), BF),
                pltpu.VMEM((slots * group, samples), F32),
                sems(col_count),
                sems(row_count, columns),
            ],
            compiler_params=PARAMS,
        )(rows_here, lists_here, owned_here, far(slices), far(features))
        covariance = lax.all_to_all(partial, "row", split_axis=0, concat_axis=0, tiled=True)

    with jax.named_scope("diag"):
        wanted, partial = lax.optimization_barrier((wanted, partial[0, 0]))
        send_diag = pl.pallas_call(
            gather_kernel,
            in_specs=[SMEM, VMEM],
            out_specs=[VMEM] * col_count,
            out_shape=[pltpu.HBM((per_source, size, size), BF)] * col_count,
            compiler_params=PARAMS,
        )(wanted, diag_inverse)
        row_diag = [
            lax.ppermute(
                block, "col", [(i, (i + offset) % col_count) for i in range(col_count)]
            ) if offset else block
            for offset, block in enumerate(send_diag)
        ]
        covariance, *row_diag = lax.optimization_barrier((covariance, *row_diag))

    with jax.named_scope("first"):
        base, d, pieces = pl.pallas_call(
            first_kernel,
            in_specs=[SMEM, SMEM, VMEM, HBM, HBM],
            out_specs=[HBM, HBM, VMEM],
            out_shape=[tile_out, tile_out, shape(piece_shape, F32)],
            scratch_shapes=[
                tile_vmem, tile_vmem, tile_vmem, tile_vmem, sums, sems(4, chunks),
            ],
            compiler_params=PARAMS,
        )(my_list, live, covariance, far(theta), far(tiles))

    for sweep in range(1, SWEEPS):
        last = sweep == SWEEPS - 1
        with jax.named_scope("exchange"):
            got = lax.all_to_all(pieces, "row", split_axis=0, concat_axis=0, tiled=True)
            flat_shape = (row_count * columns, group, size)
            summed = pl.pallas_call(
                sum_kernel,
                in_specs=[VMEM, VMEM],
                out_specs=VMEM,
                out_shape=shape(flat_shape, F32),
                compiler_params=PARAMS,
            )(same, got.reshape(flat_shape))
            q = lax.all_to_all(
                summed.reshape(piece_shape), "row", split_axis=0, concat_axis=0, tiled=True
            )
        with jax.named_scope("diagonal"):
            t = pl.pallas_call(
                diagonal_kernel,
                in_specs=[SMEM, HBM, HBM, VMEM] + [HBM] * col_count,
                out_specs=HBM,
                out_shape=tile_out,
                scratch_shapes=[
                    tile_vmem, tile_vmem, pltpu.VMEM(tile_shape, BF), tile_vmem,
                    sems(col_count), sems(3, chunks),
                ],
                compiler_params=PARAMS,
            )(my_list, far(base), far(d), col_diag, *[far(block) for block in row_diag])
        with jax.named_scope("sweep"):
            result = pl.pallas_call(
                functools.partial(sweep_kernel, last),
                in_specs=[SMEM, SMEM, HBM, HBM, HBM, VMEM],
                out_specs=[HBM] if last else [HBM, VMEM],
                out_shape=[tile_out] if last else [tile_out, shape(piece_shape, F32)],
                scratch_shapes=[
                    tile_vmem, tile_vmem, pltpu.VMEM((slots, size, 2 * size), BF), tile_vmem,
                    pltpu.VMEM((columns, 2 * size, 2 * size), BF), sems(4, chunks),
                ] + ([] if last else [sums]),
                compiler_params=PARAMS,
            )(my_list, live, far(t), far(theta), far(pairs), q)
            d = result[0]
            if not last:
                pieces = result[1]
    return d.reshape(precision_tiles.shape)


def solution(mesh):
    return jax.shard_map(
        body,
        mesh=mesh,
        in_specs=(
            P("col", None, None),
            P("col", None, None),
            P("row", "col", None, None, None),
            P("row", "col", None, None, None),
            P(),
            P(),
            P(),
            P(),
        ),
        out_specs=P("row", "col", None, None, None),
        check_vma=False,
    )
```

time: 257 us -> 231 us (0.90); the launches traced: 253 us -> 230 us
  waiting for transfers between devices: 81.5 us -> 57.9 us
  starting transfers between devices: 29.7 us -> 50.3 us
  Pallas kernels: 83.2 us -> 71.6 us
  local copies, waits for them, and re-layouts: 12.5 us -> 4.82 us
    all_to_all x1, waiting for transfers between devices: 29.4 us -> 0.01 us  [body(): lax.all_to_all(partial, 'row', split_axis=0, concat_axis=0, tiled=True)]
    ppermute x0 -> x15, starting transfers between devices: none -> 25.6 us  [body(): lax.ppermute(block, 'col', [(i, (i + offset) % col_count) for i in range(...]
    pallas_call x10, Pallas kernels: 71.9 us -> 63.1 us  [the longest x3 21.7 us: body(): pl.pallas_call(diagonal_kernel, in_specs=[SMEM, HBM, HBM, VMEM] + [HBM] *...]
    ppermute x0 -> x15, waiting for transfers between devices: none -> 8.64 us  [body(): lax.ppermute(block, 'col', [(i, (i + offset) % col_count) for i in range(...]
    all_to_all x1 -> x0, starting transfers between devices: 8.59 us -> none  [body(): lax.all_to_all(send_diag, 'col', split_axis=0, concat_axis=0, tiled=True)]
    unnamed x19 -> x33, local copies, waits for them, and re-layouts: 8 us -> 0.14 us
    all_gather x1, waiting for transfers between devices: 43.7 us -> 39.2 us  [body(): slices = lax.all_gather(mine, 'col', axis=0, tiled=True)]
    all_to_all x1, starting transfers between devices: 3.57 us -> 7.21 us  [body(): got = lax.all_to_all(pieces, 'row', split_axis=0, concat_axis=0, tiled=True)]
  transfers between devices with their start and end apart: 7 -> 21, of which waited for: 5 -> 9; matrix products, arithmetic and copies ran while one was open for 3% -> 3% of each run, Pallas kernels for 14% -> 12%
where the time goes in v2:
time: 231 us; the launch traced here: 230 us
  Pallas kernels  71.6 us (31%)
  waiting for transfers between devices  57.9 us (25%)
  starting transfers between devices  50.3 us (22%)
  blocking collectives  28.5 us (12%)
  between operations  13.7 us (6%)
  local copies, waits for them, and re-layouts  4.82 us (2%)
  other arithmetic  3.09 us (1%)
    all_gather x1, waiting for transfers between devices, body(): slices = lax.all_gather(mine, 'col', axis=0, tiled=True)  39.2 us
    all_to_all x2, blocking collectives, body(): got = lax.all_to_all(pieces, 'row', split_axis=0, concat_axis=0, tiled=True)  28.5 us
    ppermute x15, starting transfers between devices, body(): lax.ppermute(block, 'col', [(i, (i + offset) % col_count) for i in range(...  25.6 us
    pallas_call x3, Pallas kernels, body(): pl.pallas_call(diagonal_kernel, in_specs=[SMEM, HBM, HBM, VMEM] + [HBM] *...  21.7 us
    pallas_call x3, Pallas kernels, body(): pl.pallas_call(functools.partial(sweep_kernel, last), in_specs=[SMEM, SME...  19.7 us
    all_to_all x3, starting transfers between devices, body(): lax.all_to_all(summed.reshape(piece_shape), 'row', split_axis=0, concat_a...  10.5 us
    pallas_call x1, Pallas kernels, body(): pl.pallas_call(covariance_kernel, in_specs=[SMEM, SMEM, SMEM, HBM, HBM],...  9.87 us
    ppermute x15, waiting for transfers between devices, body(): lax.ppermute(block, 'col', [(i, (i + offset) % col_count) for i in range(...  8.64 us
  transfers between devices with their start and end apart: 21, of which 9 were waited for; matrix products, arithmetic and copies ran while one was open for 3% of the time, Pallas kernels for 12%

profile of v2, /device:TPU:32, one launch (start us, length us, event | category | flops | bytes accessed | tf_op | source)
XLA Modules:
  0.0 230.0 jit_solution(5751403397741719900)
XLA Ops:
  6.5 4.6 %slices.1 = bf16[32,8,512]{2,1,0:T(8,128)(2,1)} custom-call(bf16[32,512,128]{2,1,0:T(8,128)(2,1)} %features.1), custom_call_target="tpu_custom_call" | custom-call | tf_op jit(solution)/shard_map/slices/pallas_call | solution.py:322
  11.1 0.0 all-gather.2.cloned.1.call-update
  11.1 0.4 fusion.3
  11.6 0.1 copy.21
  11.7 0.1 copy.22.owned_ref
  11.8 3.9 %split.1.far_pairs = bf16[32,128,256]{2,1,0:T(8,128)(2,1)} custom-call(f32[32,128,128]{2,1,0:T(8,128)} %bitcast.29), custom_call_target="tpu_custom_call" | custom-call | tf_op jit(solution)/shard_map/split/pallas_call | solution.py:354
  15.6 0.9 constant_dynamic-slice_fusion.1
  16.5 39.2 %all-gather.2.cloned.1.call-done.far_slices = bf16[512,8,512]{2,1,0:T(8,128)(2,1)} async-done(((bf16[32,8,512]{2,1,0:T(8,128)(2,1)}), bf16[512,8,512]{2,1,0:T(8,128)(2,1)}) %all-gather.2.cloned.1.call-update) | async-done | bytes 4194320 | tf_op jit(solution)/shard_map/slices/all_gather | solution.py:329
  55.7 9.9 %covariance.1 = f32[16,32,8,128]{3,2,1,0:T(8,128)} custom-call(s32[16,32]{1,0:T(8,128)S(1)} %bitcast.24, s32[16,32]{1,0:T(8,128)S(1)} %bitcast.23, s32[16,2]{1,0:T(8,128)S(1)} %copy.22.owned_ref, bf16[512,8,512]{2,1,0:T(8,128)(2,1)} %all-gather.2.cloned.1.call-done.far_slices, bf16[32,512,128]{2,1,0:T(8,128)(2,1)} %features.1), custom_call_target="tpu_custom_call" | custom-call | tf_op jit(solution)/shard_map/covariance/pallas_call | solution.py:364
  65.6 0.0 copy-start
  65.6 7.0 %all-to-all-start = ((f32[16,32,8,128]{3,2,1,0:T(8,128)}), f32[16,32,8,128]{3,2,1,0:T(8,128)S(1)}, u32[]{:S(2)}, u32[]{:S(2)}) async-start(f32[16,32,8,128]{3,2,1,0:T(8,128)} %covariance.1), calls=%async_computation | async-start | bytes 4194304 | tf_op jit(solution)/shard_map/covariance/all_to_all | solution.py:378
  72.6 0.8 dynamic-slice_subtract_fusion.1
  73.3 0.1 copy.26
  73.4 0.1 copy.24.wanted_ref
  73.5 1.7 diag.1
  75.2 0.7 collective-permute-start.1
  75.9 2.3 %collective-permute-start.2 = (bf16[2,128,128]{2,1,0:T(8,128)(2,1)}, bf16[2,128,128]{2,1,0:T(8,128)(2,1)S(1)}, u32[]{:S(2)}, u32[]{:S(2)}) collective-permute-start(bf16[2,128,128]{2,1,0:T(8,128)(2,1)} %get-tuple-element.51), channel_id=1, source_target_pairs={{0,3},{1,4},{2,5},{3,6},{4,7},{5,8},{6,9},{7,10},{8,11},{9,12},{10... | collective-permute-start | bytes 196616 | tf_op jit(solution)/shard_map/diag/ppermute | solution.py:390
  78.2 1.4 collective-permute-start.3
  79.5 1.6 collective-permute-start.4
  81.1 0.1 fusion
  81.2 0.1 sub.25
  81.3 0.1 compare_convert_fusion.same_ref
  81.4 0.5 fusion.2
  81.9 1.3 dynamic_slice.26
  83.3 0.0 collective-permute-done.rest_1_
  83.3 2.8 %collective-permute-start.5 = (bf16[2,128,128]{2,1,0:T(8,128)(2,1)}, bf16[2,128,128]{2,1,0:T(8,128)(2,1)S(1)}, u32[]{:S(2)}, u32[]{:S(2)}) collective-permute-start(bf16[2,128,128]{2,1,0:T(8,128)(2,1)} %get-tuple-element.54), channel_id=1, source_target_pairs={{0,6},{1,7},{2,8},{3,9},{4,10},{5,11},{6,12},{7,13},{8,14},{9,15},... | collective-permute-start | bytes 196616 | tf_op jit(solution)/shard_map/diag/ppermute | solution.py:390
  86.1 2.4 %collective-permute-start.6 = (bf16[2,128,128]{2,1,0:T(8,128)(2,1)}, bf16[2,128,128]{2,1,0:T(8,128)(2,1)}, u32[]{:S(2)}, u32[]{:S(2)}) collective-permute-start(bf16[2,128,128]{2,1,0:T(8,128)(2,1)} %get-tuple-element.55), channel_id=1, source_target_pairs={{0,7},{1,8},{2,9},{3,10},{4,11},{5,12},{6,13},{7,14},{8,15},{9,0},... | collective-permute-start | bytes 196616 | tf_op jit(solution)/shard_map/diag/ppermute | solution.py:390
  88.5 0.0 collective-permute-done.2.rest_3_
  88.5 3.4 %collective-permute-start.7 = (bf16[2,128,128]{2,1,0:T(8,128)(2,1)}, bf16[2,128,128]{2,1,0:T(8,128)(2,1)}, u32[]{:S(2)}, u32[]{:S(2)}) collective-permute-start(bf16[2,128,128]{2,1,0:T(8,128)(2,1)} %get-tuple-element.56), channel_id=1, source_target_pairs={{0,8},{1,9},{2,10},{3,11},{4,12},{5,13},{6,14},{7,15},{8,0},{9,1},... | collective-permute-start | bytes 196616 | tf_op jit(solution)/shard_map/diag/ppermute | solution.py:390
  92.0 2.0 collective-permute-start.8
  94.0 2.9 %collective-permute-start.9 = (bf16[2,128,128]{2,1,0:T(8,128)(2,1)}, bf16[2,128,128]{2,1,0:T(8,128)(2,1)}, u32[]{:S(2)}, u32[]{:S(2)}) collective-permute-start(bf16[2,128,128]{2,1,0:T(8,128)(2,1)} %get-tuple-element.58), channel_id=1, source_target_pairs={{0,10},{1,11},{2,12},{3,13},{4,14},{5,15},{6,0},{7,1},{8,2},{9,3},... | collective-permute-start | bytes 196616 | tf_op jit(solution)/shard_map/diag/ppermute | solution.py:390
  96.9 1.2 pad_clamp_fusion
  98.1 1.3 gather_fusion
  99.4 0.5 collective-permute-start.10
  99.9 2.9 %collective-permute-start.11 = (bf16[2,128,128]{2,1,0:T(8,128)(2,1)}, bf16[2,128,128]{2,1,0:T(8,128)(2,1)S(1)}, u32[]{:S(2)}, u32[]{:S(2)}) collective-permute-start(bf16[2,128,128]{2,1,0:T(8,128)(2,1)} %get-tuple-element.60), channel_id=1, source_target_pairs={{0,12},{1,13},{2,14},{3,15},{4,0},{5,1},{6,2},{7,3},{8,4},{9,5},{1... | collective-permute-start | bytes 196616 | tf_op jit(solution)/shard_map/diag/ppermute | solution.py:390
  102.7 0.4 collective-permute-start.12
  103.1 2.4 %collective-permute-start.13 = (bf16[2,128,128]{2,1,0:T(8,128)(2,1)}, bf16[2,128,128]{2,1,0:T(8,128)(2,1)S(1)}, u32[]{:S(2)}, u32[]{:S(2)}) collective-permute-start(bf16[2,128,128]{2,1,0:T(8,128)(2,1)} %get-tuple-element.62), channel_id=1, source_target_pairs={{0,14},{1,15},{2,0},{3,1},{4,2},{5,3},{6,4},{7,5},{8,6},{9,7},{10,... | collective-permute-start | bytes 196616 | tf_op jit(solution)/shard_map/diag/ppermute | solution.py:390
  105.6 0.6 collective-permute-done.9.rest_10_
  106.2 0.7 fusion.1.list_ref
  106.9 0.0 collective-permute-done.10.rest_11_
  106.9 2.7 %collective-permute-done.11.rest_12_ = bf16[2,128,128]{2,1,0:T(8,128)(2,1)S(1)} collective-permute-done((bf16[2,128,128]{2,1,0:T(8,128)(2,1)}, bf16[2,128,128]{2,1,0:T(8,128)(2,1)S(1)}, u32[]{:S(2)}, u32[]{:S(2)}) %collective-permute-start.11) | collective-permute-done | bytes 65568 | tf_op jit(solution)/shard_map/diag/ppermute | solution.py:390
  109.6 3.8 %collective-permute-done.12.rest_13_ = bf16[2,128,128]{2,1,0:T(8,128)(2,1)S(1)} collective-permute-done((bf16[2,128,128]{2,1,0:T(8,128)(2,1)}, bf16[2,128,128]{2,1,0:T(8,128)(2,1)S(1)}, u32[]{:S(2)}, u32[]{:S(2)}) %collective-permute-start.12) | collective-permute-done | bytes 65568 | tf_op jit(solution)/shard_map/diag/ppermute | solution.py:390
  113.4 1.5 collective-permute-done.13.rest_14_
  114.9 6.3 %first.1 = (f32[32,128,128]{2,1,0:T(8,128)}, f32[32,128,128]{2,1,0:T(8,128)}, f32[16,2,8,128]{3,2,1,0:T(8,128)}) custom-call(s32[32]{0:T(128)S(1)} %fusion.1.list_ref, s32[1]{0:T(128)} %bitcast.1.live_ref, f32[16,32,8,128]{3,2,1,0:T(8,128)S(1)} %all-to-all-done.cov_ref, f32[32,128,128]{2,1,0:T(8,128)} %bitcast.25, f32[32,128,128]{2,1,0:T(8,128)} %bitcast.30), custom_call_target="tpu_custom_call" | custom-call | tf_op jit(solution)/shard_map/first/pallas_call | solution.py:398
  121.3 7.2 %all-to-all-start.1 = ((f32[16,2,8,128]{3,2,1,0:T(8,128)}), f32[16,2,8,128]{3,2,1,0:T(8,128)S(1)}, u32[]{:S(2)}, u32[]{:S(2)}) async-start(f32[16,2,8,128]{3,2,1,0:T(8,128)} %get-tuple-element.84), calls=%async_computation.1 | async-start | bytes 262144 | tf_op jit(solution)/shard_map/exchange/all_to_all | solution.py:412
  128.6 8.0 %all-to-all-done.1 = f32[16,2,8,128]{3,2,1,0:T(8,128)S(1)} async-done(((f32[16,2,8,128]{3,2,1,0:T(8,128)}), f32[16,2,8,128]{3,2,1,0:T(8,128)S(1)}, u32[]{:S(2)}, u32[]{:S(2)}) %all-to-all-start.1) | async-done | bytes 131104 | tf_op jit(solution)/shard_map/exchange/all_to_all | solution.py:412
  136.5 1.3 exchange.3
  137.9 3.5 %all-to-all-start.2 = ((f32[16,2,8,128]{3,2,1,0:T(8,128)}), f32[16,2,8,128]{3,2,1,0:T(8,128)S(1)}, u32[]{:S(2)}, u32[]{:S(2)}) async-start(f32[16,2,8,128]{3,2,1,0:T(8,128)} %bitcast.10), calls=%async_computation.2 | async-start | bytes 262144 | tf_op jit(solution)/shard_map/exchange/all_to_all | solution.py:421
  141.4 0.1 broadcast_select_fusion.col_diag_ref
  141.5 7.2 %diagonal.3.far_t = f32[32,128,128]{2,1,0:T(8,128)} custom-call(s32[32]{0:T(128)S(1)} %fusion.1.list_ref, f32[32,128,128]{2,1,0:T(8,128)} %get-tuple-element.65.far_base, f32[32,128,128]{2,1,0:T(8,128)} %get-tuple-element.66.far_d, bf16[2,128,128]{2,1,0:T(8,128)(2,1)S(1)} %broadcast_select_fusion.col_diag_ref, ...), custom_call_target="tpu_custom_call" | custom-call | tf_op jit(solution)/shard_map/diagonal/pallas_call | solution.py:425
  148.7 0.7 all-to-all-done.2.q_ref
  149.3 7.1 %sweep.3 = (f32[32,128,128]{2,1,0:T(8,128)}, f32[16,2,8,128]{3,2,1,0:T(8,128)S(1)}) custom-call(s32[32]{0:T(128)S(1)} %fusion.1.list_ref, s32[1]{0:T(128)} %bitcast.1.live_ref, f32[32,128,128]{2,1,0:T(8,128)} %diagonal.3.far_t, f32[32,128,128]{2,1,0:T(8,128)} %bitcast.26, bf16[32,128,256]{2,1,0:T(8,128)(2,1)} %split.1.far_pairs, ...), custom_call_target="tpu_custom_call" | custom-call | tf_op jit(solution)/shard_map/sweep/pallas_call | solution.py:437
  156.4 14.3 %all_to_all.35 = f32[16,2,8,128]{3,2,1,0:T(8,128)S(1)} all-to-all(f32[16,2,8,128]{3,2,1,0:T(8,128)S(1)} %get-tuple-element.86), channel_id=1, replica_groups=mesh['row'=16,'col'=16] {'row'}, dimensions={0} | all-to-all | bytes 262144 | tf_op jit(solution)/shard_map/exchange/all_to_all | solution.py:412
  170.7 1.3 exchange.4
  172.0 3.5 %all-to-all-start.4 = ((f32[16,2,8,128]{3,2,1,0:T(8,128)}), f32[16,2,8,128]{3,2,1,0:T(8,128)S(1)}, u32[]{:S(2)}, u32[]{:S(2)}) async-start(f32[16,2,8,128]{3,2,1,0:T(8,128)} %bitcast.12), calls=%async_computation.4 | async-start | bytes 262144 | tf_op jit(solution)/shard_map/exchange/all_to_all | solution.py:421
  175.5 7.3 %diagonal.4.far_t = f32[32,128,128]{2,1,0:T(8,128)} custom-call(s32[32]{0:T(128)S(1)} %fusion.1.list_ref, f32[32,128,128]{2,1,0:T(8,128)} %get-tuple-element.65.far_base, f32[32,128,128]{2,1,0:T(8,128)} %get-tuple-element.85.far_d, bf16[2,128,128]{2,1,0:T(8,128)(2,1)S(1)} %broadcast_select_fusion.col_diag_ref, ...), custom_call_target="tpu_custom_call" | custom-call | tf_op jit(solution)/shard_map/diagonal/pallas_call | solution.py:425
  182.8 0.7 all-to-all-done.4.q_ref
  183.5 7.1 %sweep.4 = (f32[32,128,128]{2,1,0:T(8,128)}, f32[16,2,8,128]{3,2,1,0:T(8,128)S(1)}) custom-call(s32[32]{0:T(128)S(1)} %fusion.1.list_ref, s32[1]{0:T(128)} %bitcast.1.live_ref, f32[32,128,128]{2,1,0:T(8,128)} %diagonal.4.far_t, f32[32,128,128]{2,1,0:T(8,128)} %bitcast.27, bf16[32,128,256]{2,1,0:T(8,128)(2,1)} %split.1.far_pairs, ...), custom_call_target="tpu_custom_call" | custom-call | tf_op jit(solution)/shard_map/sweep/pallas_call | solution.py:437
  190.6 14.2 %all_to_all.36 = f32[16,2,8,128]{3,2,1,0:T(8,128)S(1)} all-to-all(f32[16,2,8,128]{3,2,1,0:T(8,128)S(1)} %get-tuple-element.88), channel_id=1, replica_groups=mesh['row'=16,'col'=16] {'row'}, dimensions={0} | all-to-all | bytes 262144 | tf_op jit(solution)/shard_map/exchange/all_to_all | solution.py:412
  204.8 1.3 exchange.5
  206.1 3.5 %all-to-all-start.6 = ((f32[16,2,8,128]{3,2,1,0:T(8,128)}), f32[16,2,8,128]{3,2,1,0:T(8,128)S(1)}, u32[]{:S(2)}, u32[]{:S(2)}) async-start(f32[16,2,8,128]{3,2,1,0:T(8,128)} %bitcast.14), calls=%async_computation.6 | async-start | bytes 262144 | tf_op jit(solution)/shard_map/exchange/all_to_all | solution.py:421
  209.6 7.2 %diagonal.5.far_t = f32[32,128,128]{2,1,0:T(8,128)} custom-call(s32[32]{0:T(128)S(1)} %fusion.1.list_ref, f32[32,128,128]{2,1,0:T(8,128)} %get-tuple-element.65.far_base, f32[32,128,128]{2,1,0:T(8,128)} %get-tuple-element.87.far_d, bf16[2,128,128]{2,1,0:T(8,128)(2,1)S(1)} %broadcast_select_fusion.col_diag_ref, ...), custom_call_target="tpu_custom_call" | custom-call | tf_op jit(solution)/shard_map/diagonal/pallas_call | solution.py:425
  216.9 0.7 all-to-all-done.6.q_ref
  217.6 5.6 %sweep.5 = f32[32,128,128]{2,1,0:T(8,128)} custom-call(s32[32]{0:T(128)S(1)} %fusion.1.list_ref, s32[1]{0:T(128)} %bitcast.1.live_ref, f32[32,128,128]{2,1,0:T(8,128)} %diagonal.5.far_t, f32[32,128,128]{2,1,0:T(8,128)} %bitcast.28, bf16[32,128,256]{2,1,0:T(8,128)(2,1)} %split.1.far_pairs, f32[16,2,8,128]{3,2,1,0:T(8,128)S(1)} %all-to-all-done.6.q_ref), custom_call_target="tpu_custom_call" | custom-call | tf_op jit(solution)/shard_map/sweep/pallas_call | solution.py:437
  (44 shorter events, 0.1 us)
Async XLA Ops:
  6.5 4.6 %copy-start.13 = (s32[16,16,2]{1,2,0:T(2,128)S(1)}, s32[16,16,2]{1,2,0:T(2,128)}, u32[]{:S(2)}) copy-start(s32[16,16,2]{1,2,0:T(2,128)} %param.14) | copy-start | bytes 6148
  6.5 49.2 %all-gather.2.cloned.1.call-start = ((), (), s32[]{:S(2)}) async-start(), calls=%async_computation.7 | async-start | bytes 4456448 | tf_op jit(solution)/shard_map/slices/all_gather | solution.py:329
  65.6 7.9 %copy-start = (bf16[32,128,128]{2,1,0:T(8,128)(2,1)S(1)}, bf16[32,128,128]{2,1,0:T(8,128)(2,1)}, u32[]{:S(2)}) copy-start(bf16[32,128,128]{2,1,0:T(8,128)(2,1)} %diag_ref.1) | copy-start | bytes 3145732
  65.6 49.3 %all-to-all-start = ((f32[16,32,8,128]{3,2,1,0:T(8,128)}), f32[16,32,8,128]{3,2,1,0:T(8,128)S(1)}, u32[]{:S(2)}, u32[]{:S(2)}) async-start(f32[16,32,8,128]{3,2,1,0:T(8,128)} %covariance.1), calls=%async_computation | async-start | bytes 4194304 | tf_op jit(solution)/shard_map/covariance/all_to_all | solution.py:378
  75.2 8.0 %collective-permute-start = (bf16[2,128,128]{2,1,0:T(8,128)(2,1)}, bf16[2,128,128]{2,1,0:T(8,128)(2,1)S(1)}, u32[]{:S(2)}, u32[]{:S(2)}) collective-permute-start(bf16[2,128,128]{2,1,0:T(8,128)(2,1)} %get-tuple-element.49), channel_id=1, source_target_pairs={{0,1},{1,2},{2,3},{3,4},{4,5},{5,6},{6,7},{7,8},{8,9},{9,10},{10,1... | collective-permute-start | bytes 196616 | tf_op jit(solution)/shard_map/diag/ppermute | solution.py:390
  75.2 10.9 %collective-permute-start.1 = (bf16[2,128,128]{2,1,0:T(8,128)(2,1)}, bf16[2,128,128]{2,1,0:T(8,128)(2,1)S(1)}, u32[]{:S(2)}, u32[]{:S(2)}) collective-permute-start(bf16[2,128,128]{2,1,0:T(8,128)(2,1)} %get-tuple-element.50), channel_id=1, source_target_pairs={{0,2},{1,3},{2,4},{3,5},{4,6},{5,7},{6,8},{7,9},{8,10},{9,11},{10,... | collective-permute-start | bytes 196616 | tf_op jit(solution)/shard_map/diag/ppermute | solution.py:390
  75.9 12.6 %collective-permute-start.2 = (bf16[2,128,128]{2,1,0:T(8,128)(2,1)}, bf16[2,128,128]{2,1,0:T(8,128)(2,1)S(1)}, u32[]{:S(2)}, u32[]{:S(2)}) collective-permute-start(bf16[2,128,128]{2,1,0:T(8,128)(2,1)} %get-tuple-element.51), channel_id=1, source_target_pairs={{0,3},{1,4},{2,5},{3,6},{4,7},{5,8},{6,9},{7,10},{8,11},{9,12},{10... | collective-permute-start | bytes 196616 | tf_op jit(solution)/shard_map/diag/ppermute | solution.py:390
  78.2 13.8 %collective-permute-start.3 = (bf16[2,128,128]{2,1,0:T(8,128)(2,1)}, bf16[2,128,128]{2,1,0:T(8,128)(2,1)S(1)}, u32[]{:S(2)}, u32[]{:S(2)}) collective-permute-start(bf16[2,128,128]{2,1,0:T(8,128)(2,1)} %get-tuple-element.52), channel_id=1, source_target_pairs={{0,4},{1,5},{2,6},{3,7},{4,8},{5,9},{6,10},{7,11},{8,12},{9,13},{1... | collective-permute-start | bytes 196616 | tf_op jit(solution)/shard_map/diag/ppermute | solution.py:390
  79.5 14.5 %collective-permute-start.4 = (bf16[2,128,128]{2,1,0:T(8,128)(2,1)}, bf16[2,128,128]{2,1,0:T(8,128)(2,1)S(1)}, u32[]{:S(2)}, u32[]{:S(2)}) collective-permute-start(bf16[2,128,128]{2,1,0:T(8,128)(2,1)} %get-tuple-element.53), channel_id=1, source_target_pairs={{0,5},{1,6},{2,7},{3,8},{4,9},{5,10},{6,11},{7,12},{8,13},{9,14},{... | collective-permute-start | bytes 196616 | tf_op jit(solution)/shard_map/diag/ppermute | solution.py:390
  81.2 2.0 copy-start.14
  83.3 38.0 %copy-start.1 = (bf16[2,128,128]{2,1,0:T(8,128)(2,1)}, bf16[2,128,128]{2,1,0:T(8,128)(2,1)S(1)}, u32[]{:S(2)}) copy-start(bf16[2,128,128]{2,1,0:T(8,128)(2,1)S(1)} %collective-permute-done.rest_1_) | copy-start | bytes 196612
  83.3 16.1 %collective-permute-start.5 = (bf16[2,128,128]{2,1,0:T(8,128)(2,1)}, bf16[2,128,128]{2,1,0:T(8,128)(2,1)S(1)}, u32[]{:S(2)}, u32[]{:S(2)}) collective-permute-start(bf16[2,128,128]{2,1,0:T(8,128)(2,1)} %get-tuple-element.54), channel_id=1, source_target_pairs={{0,6},{1,7},{2,8},{3,9},{4,10},{5,11},{6,12},{7,13},{8,14},{9,15},... | collective-permute-start | bytes 196616 | tf_op jit(solution)/shard_map/diag/ppermute | solution.py:390
  86.1 35.1 %copy-start.2 = (bf16[2,128,128]{2,1,0:T(8,128)(2,1)}, bf16[2,128,128]{2,1,0:T(8,128)(2,1)S(1)}, u32[]{:S(2)}) copy-start(bf16[2,128,128]{2,1,0:T(8,128)(2,1)S(1)} %collective-permute-done.1.rest_2_) | copy-start | bytes 196612
  86.1 13.8 %collective-permute-start.6 = (bf16[2,128,128]{2,1,0:T(8,128)(2,1)}, bf16[2,128,128]{2,1,0:T(8,128)(2,1)}, u32[]{:S(2)}, u32[]{:S(2)}) collective-permute-start(bf16[2,128,128]{2,1,0:T(8,128)(2,1)} %get-tuple-element.55), channel_id=1, source_target_pairs={{0,7},{1,8},{2,9},{3,10},{4,11},{5,12},{6,13},{7,14},{8,15},{9,0},... | collective-permute-start | bytes 196616 | tf_op jit(solution)/shard_map/diag/ppermute | solution.py:390
  88.5 32.7 %copy-start.3 = (bf16[2,128,128]{2,1,0:T(8,128)(2,1)}, bf16[2,128,128]{2,1,0:T(8,128)(2,1)S(1)}, u32[]{:S(2)}) copy-start(bf16[2,128,128]{2,1,0:T(8,128)(2,1)S(1)} %collective-permute-done.2.rest_3_) | copy-start | bytes 196612
  88.5 14.2 %collective-permute-start.7 = (bf16[2,128,128]{2,1,0:T(8,128)(2,1)}, bf16[2,128,128]{2,1,0:T(8,128)(2,1)}, u32[]{:S(2)}, u32[]{:S(2)}) collective-permute-start(bf16[2,128,128]{2,1,0:T(8,128)(2,1)} %get-tuple-element.56), channel_id=1, source_target_pairs={{0,8},{1,9},{2,10},{3,11},{4,12},{5,13},{6,14},{7,15},{8,0},{9,1},... | collective-permute-start | bytes 196616 | tf_op jit(solution)/shard_map/diag/ppermute | solution.py:390
  92.0 29.3 %copy-start.4 = (bf16[2,128,128]{2,1,0:T(8,128)(2,1)}, bf16[2,128,128]{2,1,0:T(8,128)(2,1)S(1)}, u32[]{:S(2)}) copy-start(bf16[2,128,128]{2,1,0:T(8,128)(2,1)S(1)} %collective-permute-done.3.rest_4_) | copy-start | bytes 196612
  92.0 11.1 %collective-permute-start.8 = (bf16[2,128,128]{2,1,0:T(8,128)(2,1)}, bf16[2,128,128]{2,1,0:T(8,128)(2,1)}, u32[]{:S(2)}, u32[]{:S(2)}) collective-permute-start(bf16[2,128,128]{2,1,0:T(8,128)(2,1)} %get-tuple-element.57), channel_id=1, source_target_pairs={{0,9},{1,10},{2,11},{3,12},{4,13},{5,14},{6,15},{7,0},{8,1},{9,2},... | collective-permute-start | bytes 196616 | tf_op jit(solution)/shard_map/diag/ppermute | solution.py:390
  94.0 27.3 %copy-start.5 = (bf16[2,128,128]{2,1,0:T(8,128)(2,1)}, bf16[2,128,128]{2,1,0:T(8,128)(2,1)S(1)}, u32[]{:S(2)}) copy-start(bf16[2,128,128]{2,1,0:T(8,128)(2,1)S(1)} %collective-permute-done.4.rest_5_) | copy-start | bytes 196612
  94.0 12.2 %collective-permute-start.9 = (bf16[2,128,128]{2,1,0:T(8,128)(2,1)}, bf16[2,128,128]{2,1,0:T(8,128)(2,1)}, u32[]{:S(2)}, u32[]{:S(2)}) collective-permute-start(bf16[2,128,128]{2,1,0:T(8,128)(2,1)} %get-tuple-element.58), channel_id=1, source_target_pairs={{0,10},{1,11},{2,12},{3,13},{4,14},{5,15},{6,0},{7,1},{8,2},{9,3},... | collective-permute-start | bytes 196616 | tf_op jit(solution)/shard_map/diag/ppermute | solution.py:390
  99.4 21.9 %copy-start.6 = (bf16[2,128,128]{2,1,0:T(8,128)(2,1)}, bf16[2,128,128]{2,1,0:T(8,128)(2,1)S(1)}, u32[]{:S(2)}) copy-start(bf16[2,128,128]{2,1,0:T(8,128)(2,1)S(1)} %collective-permute-done.5.rest_6_) | copy-start | bytes 196612
  99.4 7.5 %collective-permute-start.10 = (bf16[2,128,128]{2,1,0:T(8,128)(2,1)}, bf16[2,128,128]{2,1,0:T(8,128)(2,1)S(1)}, u32[]{:S(2)}, u32[]{:S(2)}) collective-permute-start(bf16[2,128,128]{2,1,0:T(8,128)(2,1)} %get-tuple-element.59), channel_id=1, source_target_pairs={{0,11},{1,12},{2,13},{3,14},{4,15},{5,0},{6,1},{7,2},{8,3},{9,4},{... | collective-permute-start | bytes 196616 | tf_op jit(solution)/shard_map/diag/ppermute | solution.py:390
  99.9 9.7 %collective-permute-start.11 = (bf16[2,128,128]{2,1,0:T(8,128)(2,1)}, bf16[2,128,128]{2,1,0:T(8,128)(2,1)S(1)}, u32[]{:S(2)}, u32[]{:S(2)}) collective-permute-start(bf16[2,128,128]{2,1,0:T(8,128)(2,1)} %get-tuple-element.60), channel_id=1, source_target_pairs={{0,12},{1,13},{2,14},{3,15},{4,0},{5,1},{6,2},{7,3},{8,4},{9,5},{1... | collective-permute-start | bytes 196616 | tf_op jit(solution)/shard_map/diag/ppermute | solution.py:390
  102.7 10.6 %collective-permute-start.12 = (bf16[2,128,128]{2,1,0:T(8,128)(2,1)}, bf16[2,128,128]{2,1,0:T(8,128)(2,1)S(1)}, u32[]{:S(2)}, u32[]{:S(2)}) collective-permute-start(bf16[2,128,128]{2,1,0:T(8,128)(2,1)} %get-tuple-element.61), channel_id=1, source_target_pairs={{0,13},{1,14},{2,15},{3,0},{4,1},{5,2},{6,3},{7,4},{8,5},{9,6},{10... | collective-permute-start | bytes 196616 | tf_op jit(solution)/shard_map/diag/ppermute | solution.py:390
  103.1 11.8 %collective-permute-start.13 = (bf16[2,128,128]{2,1,0:T(8,128)(2,1)}, bf16[2,128,128]{2,1,0:T(8,128)(2,1)S(1)}, u32[]{:S(2)}, u32[]{:S(2)}) collective-permute-start(bf16[2,128,128]{2,1,0:T(8,128)(2,1)} %get-tuple-element.62), channel_id=1, source_target_pairs={{0,14},{1,15},{2,0},{3,1},{4,2},{5,3},{6,4},{7,5},{8,6},{9,7},{10,... | collective-permute-start | bytes 196616 | tf_op jit(solution)/shard_map/diag/ppermute | solution.py:390
  106.2 8.7 %collective-permute-start.14 = (bf16[2,128,128]{2,1,0:T(8,128)(2,1)}, bf16[2,128,128]{2,1,0:T(8,128)(2,1)S(1)}, u32[]{:S(2)}, u32[]{:S(2)}) collective-permute-start(bf16[2,128,128]{2,1,0:T(8,128)(2,1)} %get-tuple-element.63), channel_id=1, source_target_pairs={{0,15},{1,0},{2,1},{3,2},{4,3},{5,4},{6,5},{7,6},{8,7},{9,8},{10,9... | collective-permute-start | bytes 196616 | tf_op jit(solution)/shard_map/diag/ppermute | solution.py:390
  106.9 14.4 %copy-start.7 = (bf16[2,128,128]{2,1,0:T(8,128)(2,1)}, bf16[2,128,128]{2,1,0:T(8,128)(2,1)S(1)}, u32[]{:S(2)}) copy-start(bf16[2,128,128]{2,1,0:T(8,128)(2,1)S(1)} %collective-permute-done.10.rest_11_) | copy-start | bytes 196612
  109.6 11.7 %copy-start.8 = (bf16[2,128,128]{2,1,0:T(8,128)(2,1)}, bf16[2,128,128]{2,1,0:T(8,128)(2,1)S(1)}, u32[]{:S(2)}) copy-start(bf16[2,128,128]{2,1,0:T(8,128)(2,1)S(1)} %collective-permute-done.11.rest_12_) | copy-start | bytes 196612
  113.4 7.9 %copy-start.9 = (bf16[2,128,128]{2,1,0:T(8,128)(2,1)}, bf16[2,128,128]{2,1,0:T(8,128)(2,1)S(1)}, u32[]{:S(2)}) copy-start(bf16[2,128,128]{2,1,0:T(8,128)(2,1)S(1)} %collective-permute-done.12.rest_13_) | copy-start | bytes 196612
  114.9 6.4 %copy-start.10 = (bf16[2,128,128]{2,1,0:T(8,128)(2,1)}, bf16[2,128,128]{2,1,0:T(8,128)(2,1)S(1)}, u32[]{:S(2)}) copy-start(bf16[2,128,128]{2,1,0:T(8,128)(2,1)S(1)} %collective-permute-done.13.rest_14_) | copy-start | bytes 196612
  114.9 6.4 %copy-start.11 = (bf16[2,128,128]{2,1,0:T(8,128)(2,1)}, bf16[2,128,128]{2,1,0:T(8,128)(2,1)S(1)}, u32[]{:S(2)}) copy-start(bf16[2,128,128]{2,1,0:T(8,128)(2,1)S(1)} %collective-permute-done.14.rest_15_) | copy-start | bytes 196612
  114.9 13.7 %copy-start.15 = (s32[2]{0:T(128)S(1)}, s32[2]{0:T(128)}, u32[]{:S(2)}) copy-start(s32[2]{0:T(128)} %copy-done.14) | copy-start | bytes 28
  114.9 26.5 %copy-start.12 = (bf16[2,128,128]{2,1,0:T(8,128)(2,1)S(1)}, bf16[2,128,128]{2,1,0:T(8,128)(2,1)}, u32[]{:S(2)}) copy-start(bf16[2,128,128]{2,1,0:T(8,128)(2,1)} %gather_fusion) | copy-start | bytes 196612
  121.3 15.2 %all-to-all-start.1 = ((f32[16,2,8,128]{3,2,1,0:T(8,128)}), f32[16,2,8,128]{3,2,1,0:T(8,128)S(1)}, u32[]{:S(2)}, u32[]{:S(2)}) async-start(f32[16,2,8,128]{3,2,1,0:T(8,128)} %get-tuple-element.84), calls=%async_computation.1 | async-start | bytes 262144 | tf_op jit(solution)/shard_map/exchange/all_to_all | solution.py:412
  137.9 11.5 %all-to-all-start.2 = ((f32[16,2,8,128]{3,2,1,0:T(8,128)}), f32[16,2,8,128]{3,2,1,0:T(8,128)S(1)}, u32[]{:S(2)}, u32[]{:S(2)}) async-start(f32[16,2,8,128]{3,2,1,0:T(8,128)} %bitcast.10), calls=%async_computation.2 | async-start | bytes 262144 | tf_op jit(solution)/shard_map/exchange/all_to_all | solution.py:421
  172.0 11.5 %all-to-all-start.4 = ((f32[16,2,8,128]{3,2,1,0:T(8,128)}), f32[16,2,8,128]{3,2,1,0:T(8,128)S(1)}, u32[]{:S(2)}, u32[]{:S(2)}) async-start(f32[16,2,8,128]{3,2,1,0:T(8,128)} %bitcast.12), calls=%async_computation.4 | async-start | bytes 262144 | tf_op jit(solution)/shard_map/exchange/all_to_all | solution.py:421
  206.1 11.5 %all-to-all-start.6 = ((f32[16,2,8,128]{3,2,1,0:T(8,128)}), f32[16,2,8,128]{3,2,1,0:T(8,128)S(1)}, u32[]{:S(2)}, u32[]{:S(2)}) async-start(f32[16,2,8,128]{3,2,1,0:T(8,128)} %bitcast.14), calls=%async_computation.6 | async-start | bytes 262144 | tf_op jit(solution)/shard_map/exchange/all_to_all | solution.py:421
Sparse Core Ops, SparseCore 0:
  11.3 44.4 all-gather.1

commit v3 on v2

--- a/solution.py
+++ b/solution.py
@@ -12,6 +12,7 @@
 LAMBDA = 0.3 * 0.6
 PER_STEP = 8
 CHUNK = 4
+CORES = 2
 
 BF = jnp.bfloat16
 F32 = jnp.float32
@@ -52,12 +53,38 @@
         out_ref[s] = jnp.concatenate(split(tiles_ref[s]), axis=1)
 
 
-def gather_kernel(wanted_ref, diag_ref, *out_refs):
+def gather_kernel(steps, wanted_ref, features, diag, *rest):
+    outs, sems = rest[:-1], rest[-1]
     c = lax.axis_index("col")
-    for offset, out_ref in enumerate(out_refs):
-        target = lax.rem(c + offset, len(out_refs))
-        for p in range(out_ref.shape[0]):
-            out_ref[p] = diag_ref[wanted_ref[target, p]]
+    samples = features.shape[1]
+    copies = []
+    for n, ((dz, dk), out) in enumerate(zip(steps, outs)):
+        target = holder(c, -dz, dk, wanted_ref.shape[0])
+        for p in range(out.shape[0]):
+            block = wanted_ref[target, p]
+            begin = 0
+            if out.shape[1] > diag.shape[1]:
+                copies.append(pltpu.make_async_copy(
+                    features.at[block], out.at[p, pl.ds(0, samples)], sems.at[n, p, 0]
+                ))
+                begin = samples
+            copies.append(pltpu.make_async_copy(
+                diag.at[block], out.at[p, pl.ds(begin, diag.shape[1])], sems.at[n, p, 1]
+            ))
+    for copy in copies:
+        copy.start()
+    for copy in copies:
+        copy.wait()
+
+
+def holder(c, dz, dk, col_count):
+    chips = col_count // CORES
+    z = lax.rem(c // CORES + dz + chips, chips)
+    return z * CORES + lax.rem(c + dk, CORES)
+
+
+def chip_at(dz, col_count):
+    return lax.rem(lax.axis_index("col") // CORES + dz, col_count // CORES)
 
 
 class Tiles:
@@ -102,47 +129,56 @@
 
 
 def covariance_kernel(
-    rows_ref, lists_ref, owned_ref, far_slices, features, out_ref,
+    far, col_count, rows_ref, lists_ref, owned_ref, far_slices, features, out_ref,
     slices_ref, right_ref, left_ref, slice_sem, right_sem,
 ):
-    owners, slots = rows_ref.shape
+    owners = rows_ref.shape[0]
     columns = owned_ref.shape[1]
     group = slices_ref.shape[1]
     samples = features.shape[1]
     size = features.shape[2]
-    blocks = features.shape[0]
-    parts = slices_ref.shape[0] // blocks
-
-    def slice_copy(i):
-        part = pl.ds(i * blocks, blocks)
-        return pltpu.make_async_copy(far_slices.at[part], slices_ref.at[part], slice_sem.at[i])
+    part = far_slices.shape[0] * CORES // col_count
+
+    def slice_copy(n):
+        here = pl.ds(chip_at(far[n], col_count) * part, part)
+        return pltpu.make_async_copy(
+            far_slices.at[here], slices_ref.at[here], slice_sem.at[n]
+        )
 
     def right_copy(owner, a):
         return pltpu.make_async_copy(
             features.at[owned_ref[owner, a]], right_ref.at[owner, a], right_sem.at[owner, a]
         )
 
-    for i in range(parts):
-        slice_copy(i).start()
+    for n in range(len(far)):
+        slice_copy(n).start()
     for owner in range(owners):
         for a in range(columns):
             right_copy(owner, a).start()
-    for i in range(parts):
-        slice_copy(i).wait()
+    for n in range(len(far)):
+        slice_copy(n).wait()
 
     def owner_step(owner, carry):
         for a in range(columns):
             right_copy(owner, a).wait()
-        for k in range(slots):
-            left_ref[k * group:(k + 1) * group, :] = slices_ref[rows_ref[owner, k]].astype(F32)
+        for n, dz in enumerate(far):
+            first = chip_at(dz, col_count) * CHUNK
+            for s in range(CHUNK):
+                k = n * CHUNK + s
+                left_ref[k * group:(k + 1) * group, :] = slices_ref[
+                    rows_ref[owner, first + s]
+                ].astype(F32)
         left = left_ref[...].astype(BF)
         right = jnp.concatenate([right_ref[owner, a] for a in range(columns)], axis=1)
         both = dot(left, right) * (1.0 / samples)
-        for k in range(slots):
-            rows = both[k * group:(k + 1) * group]
-            out_ref[owner, k] = jnp.where(
-                lists_ref[owner, k] == 0, rows[:, :size], rows[:, size:]
-            )
+        for n, dz in enumerate(far):
+            first = chip_at(dz, col_count) * CHUNK
+            for s in range(CHUNK):
+                k = n * CHUNK + s
+                rows = both[k * group:(k + 1) * group]
+                out_ref[owner, k] = jnp.where(
+                    lists_ref[owner, first + s] == 0, rows[:, :size], rows[:, size:]
+                )
         return carry
 
     lax.fori_loop(0, owners, owner_step, 0)
@@ -168,33 +204,113 @@
         out_ref[:, a] = total.reshape(pieces, group, size)
 
 
+def first_step(slot, covariance, list_ref, live_ref, theta_ref, tiles_ref, base_ref, d_ref, sums_ref):
+    theta = theta_ref[slot]
+    tile = tiles_ref[slot]
+    base = theta - STEP * (covariance - tile)
+    d = jnp.where(slot < live_ref[0], shrink(base) - theta, 0.0)
+    base_ref[slot] = base
+    d_ref[slot] = d
+    halves = jnp.concatenate(split(tile), axis=1)
+    add_product(d, list_ref[slot], halves, sums_ref)
+
+
+def near_kernel(near, col_count, list_ref, live_ref, owned_ref, features, far_theta, far_tiles, *rest):
+    count = len(near) * CORES
+    blocks = rest[:count]
+    (
+        far_base, far_d, sums_ref, left_ref, right_ref, theta_ref, tiles_ref, base_ref, d_ref,
+        left_sem, right_sem, sems,
+    ) = rest[count:]
+    slots, size, _ = theta_ref.shape
+    samples = features.shape[1]
+    per_source = CHUNK // CORES
+    core = lax.rem(lax.axis_index("col"), CORES)
+    arrays = [Tiles(far_theta, theta_ref, sems.at[0]), Tiles(far_tiles, tiles_ref, sems.at[1])]
+    outs = [Tiles(far_base, base_ref, sems.at[2], True), Tiles(far_d, d_ref, sems.at[3], True)]
+
+    def left_copy(n):
+        place = n // CORES * CHUNK + lax.rem(core + n % CORES, CORES) * per_source
+        return pltpu.make_async_copy(
+            blocks[n].at[:, pl.ds(0, samples)], left_ref.at[pl.ds(place, per_source)],
+            left_sem.at[n],
+        )
+
+    def right_copy(a):
+        return pltpu.make_async_copy(
+            features.at[owned_ref[a]], right_ref.at[a], right_sem.at[a]
+        )
+
+    for a in range(right_ref.shape[0]):
+        right_copy(a).start()
+    for n in range(count):
+        left_copy(n).start()
+    for dz in near:
+        for array in arrays:
+            array.start(chip_at(dz, col_count))
+    sums_ref[...] = jnp.zeros_like(sums_ref)
+    for a in range(right_ref.shape[0]):
+        right_copy(a).wait()
+    for n in range(count):
+        left_copy(n).wait()
+    for n, dz in enumerate(near):
+        chip = chip_at(dz, col_count)
+        for array in arrays:
+            array.wait(chip)
+        for s in range(CHUNK):
+            slot = chip * CHUNK + s
+            covariance = lax.dot_general(
+                left_ref[n * CHUNK + s], right_ref[list_ref[slot]],
+                (((0,), (0,)), ((), ())), preferred_element_type=F32,
+            ) * (1.0 / samples)
+            first_step(
+                slot, covariance, list_ref, live_ref, theta_ref, tiles_ref, base_ref, d_ref,
+                sums_ref,
+            )
+        for out in outs:
+            out.start(chip)
+    for dz in near:
+        for out in outs:
+            out.wait(chip_at(dz, col_count))
+
+
 def first_kernel(
-    list_ref, live_ref, cov_ref, far_theta, far_tiles, far_base, far_d, out_ref,
-    theta_ref, tiles_ref, base_ref, d_ref, sums_ref, sems,
+    far, col_count, list_ref, live_ref, cov_ref, near_sums, far_theta, far_tiles, in_base, in_d,
+    far_base, far_d, out_ref, theta_ref, tiles_ref, base_ref, d_ref, sums_ref, sum_sem, sems,
 ):
     slots, size, _ = theta_ref.shape
-    chunks = slots // CHUNK
     arrays = [Tiles(far_theta, theta_ref, sems.at[0]), Tiles(far_tiles, tiles_ref, sems.at[1])]
     outs = [Tiles(far_base, base_ref, sems.at[2], True), Tiles(far_d, d_ref, sems.at[3], True)]
-    start_all(arrays, chunks)
-    sums_ref[...] = jnp.zeros_like(sums_ref)
-
-    def slot_step(slot):
-        covariance = cov_ref[:, slot].reshape(size, size)
-        theta = theta_ref[slot]
-        tile = tiles_ref[slot]
-        base = theta - STEP * (covariance - tile)
-        d = jnp.where(slot < live_ref[0], shrink(base) - theta, 0.0)
-        base_ref[slot] = base
-        d_ref[slot] = d
-        halves = jnp.concatenate(split(tile), axis=1)
-        add_product(d, list_ref[slot], halves, sums_ref)
-
-    each_slot(chunks, arrays, outs, slot_step)
+    bring = pltpu.make_async_copy(near_sums, sums_ref, sum_sem.at[0])
+    bring.start()
+    for dz in far:
+        for array in arrays:
+            array.start(chip_at(dz, col_count))
+    bring.wait()
+
+    def step(n, carry):
+        chip = chip_at(n + far[0], col_count)
+        for array in arrays:
+            array.wait(chip)
+        for s in range(CHUNK):
+            slot = chip * CHUNK + s
+            covariance = cov_ref[:, n * CHUNK + s].reshape(size, size)
+            first_step(
+                slot, covariance, list_ref, live_ref, theta_ref, tiles_ref, base_ref, d_ref,
+                sums_ref,
+            )
+        for out in outs:
+            out.start(chip)
+        return carry
+
+    lax.fori_loop(0, len(far), step, 0)
     write_sums(sums_ref, out_ref)
-
-
-def diagonal_kernel(list_ref, far_base, far_d, col_diag_ref, *rest):
+    for dz in far:
+        for out in outs:
+            out.wait(chip_at(dz, col_count))
+
+
+def diagonal_kernel(steps, list_ref, far_base, far_d, col_diag_ref, *rest):
     far_diag = rest[:-7]
     far_out, base_ref, d_ref, diag_ref, out_ref, diag_sem, sems = rest[-7:]
     slots, size, _ = d_ref.shape
@@ -204,18 +320,20 @@
     arrays = [Tiles(far_base, base_ref, sems.at[0]), Tiles(far_d, d_ref, sems.at[1])]
     out = Tiles(far_out, out_ref, sems.at[2], True)
 
-    def diag_copy(offset):
-        source = lax.rem(c + len(far_diag) - offset, len(far_diag))
+    def diag_copy(n):
+        block = far_diag[n]
+        place = holder(c, *steps[n], len(far_diag)) * per_source
         return pltpu.make_async_copy(
-            far_diag[offset], diag_ref.at[pl.ds(source * per_source, per_source)],
-            diag_sem.at[offset],
-        )
-
-    for offset in range(len(far_diag)):
-        diag_copy(offset).start()
+            block.at[:, pl.ds(block.shape[1] - size, size)],
+            diag_ref.at[pl.ds(place, per_source)],
+            diag_sem.at[n],
+        )
+
+    for n in range(len(far_diag)):
+        diag_copy(n).start()
     start_all(arrays, chunks)
-    for offset in range(len(far_diag)):
-        diag_copy(offset).wait()
+    for n in range(len(far_diag)):
+        diag_copy(n).wait()
 
     def slot_step(slot):
         d = d_ref[slot]
@@ -358,53 +476,100 @@
             out_specs=slot_blocks(size, 2 * size),
             out_shape=pltpu.HBM((slots, size, 2 * size), BF),
         )(far(tiles))
-        slices, pairs = lax.optimization_barrier((slices, pairs))
-
+
+    with jax.named_scope("blocks"):
+        chips = col_count // CORES
+        near = [0, 1, chips - 1]
+        far_chips = list(range(2, chips - 1))
+        cores = range(CORES)
+        steps = [(dz, dk) for dz in near for dk in cores]
+        steps += [(dz, dk) for dz in (2, chips - 2) for dk in cores]
+        early = len(steps)
+        steps += [(dz, dk) for dz in far_chips[1:-1] for dk in cores]
+        near_count = len(near) * CORES
+        block_shapes = [
+            (per_source, samples + size if n < near_count else size, size)
+            for n in range(len(steps))
+        ]
+        mine, wanted = lax.optimization_barrier((mine, wanted))
+        blocks_out = list(pl.pallas_call(
+            functools.partial(gather_kernel, steps),
+            in_specs=[SMEM, HBM, HBM],
+            out_specs=[HBM] * len(steps),
+            out_shape=[pltpu.HBM(dims, BF) for dims in block_shapes],
+            scratch_shapes=[sems(len(steps), per_source, 2)],
+        )(wanted, far(features), far(diag_inverse)))
+
+        def send(n):
+            dz, dk = steps[n]
+            if dz == 0 and dk == 0:
+                return blocks_out[n]
+            pairs_of = [
+                (h, (h // CORES - dz) % chips * CORES + (h + dk) % CORES)
+                for h in range(col_count)
+            ]
+            return lax.ppermute(blocks_out[n], "col", pairs_of)
+
+        got_blocks = [send(n) for n in range(early)]
+        slices, pairs, *got_blocks = lax.optimization_barrier((slices, pairs, *got_blocks))
+
+    far_slots = len(far_chips) * CHUNK
     with jax.named_scope("covariance"):
         partial = pl.pallas_call(
-            covariance_kernel,
+            functools.partial(covariance_kernel, far_chips, col_count),
             in_specs=[SMEM, SMEM, SMEM, HBM, HBM],
             out_specs=VMEM,
-            out_shape=pltpu.HBM((row_count, slots, group, size), F32),
+            out_shape=pltpu.HBM((row_count, far_slots, group, size), F32),
             scratch_shapes=[
                 pltpu.VMEM(slices.shape, BF),
                 pltpu.VMEM((row_count, columns, samples, size), BF),
-                pltpu.VMEM((slots * group, samples), F32),
-                sems(col_count),
+                pltpu.VMEM((far_slots * group, samples), F32),
+                sems(len(far_chips)),
                 sems(row_count, columns),
             ],
             compiler_params=PARAMS,
         )(rows_here, lists_here, owned_here, far(slices), far(features))
         covariance = lax.all_to_all(partial, "row", split_axis=0, concat_axis=0, tiled=True)
 
-    with jax.named_scope("diag"):
-        wanted, partial = lax.optimization_barrier((wanted, partial[0, 0]))
-        send_diag = pl.pallas_call(
-            gather_kernel,
-            in_specs=[SMEM, VMEM],
-            out_specs=[VMEM] * col_count,
-            out_shape=[pltpu.HBM((per_source, size, size), BF)] * col_count,
+    with jax.named_scope("near"):
+        blocks_out[early:], got_blocks, _ = lax.optimization_barrier(
+            (blocks_out[early:], got_blocks, partial[0, 0])
+        )
+        got_blocks = got_blocks + [send(n) for n in range(early, len(steps))]
+        base, d, near_sums = pl.pallas_call(
+            functools.partial(near_kernel, near, col_count),
+            in_specs=[SMEM, SMEM, SMEM] + [HBM] * (3 + near_count),
+            out_specs=[HBM] * 2 + [VMEM],
+            out_shape=[tile_out, tile_out, pltpu.HBM((columns, size, 2 * size), F32)],
+            scratch_shapes=[
+                pltpu.VMEM((len(near) * CHUNK, samples, size), BF),
+                pltpu.VMEM((columns, samples, size), BF),
+                tile_vmem, tile_vmem, tile_vmem, tile_vmem,
+                sems(near_count), sems(columns), sems(4, chunks),
+            ],
             compiler_params=PARAMS,
-        )(wanted, diag_inverse)
-        row_diag = [
-            lax.ppermute(
-                block, "col", [(i, (i + offset) % col_count) for i in range(col_count)]
-            ) if offset else block
-            for offset, block in enumerate(send_diag)
-        ]
-        covariance, *row_diag = lax.optimization_barrier((covariance, *row_diag))
+        )(
+            my_list, live, my_owned, far(features), far(theta), far(tiles),
+            *[far(block) for block in got_blocks[:near_count]],
+        )
+        covariance, got_blocks, base, d, near_sums = lax.optimization_barrier(
+            (covariance, got_blocks, base, d, near_sums)
+        )
 
     with jax.named_scope("first"):
         base, d, pieces = pl.pallas_call(
-            first_kernel,
-            in_specs=[SMEM, SMEM, VMEM, HBM, HBM],
+            functools.partial(first_kernel, far_chips, col_count),
+            in_specs=[SMEM, SMEM, VMEM] + [HBM] * 5,
             out_specs=[HBM, HBM, VMEM],
             out_shape=[tile_out, tile_out, shape(piece_shape, F32)],
             scratch_shapes=[
-                tile_vmem, tile_vmem, tile_vmem, tile_vmem, sums, sems(4, chunks),
+                tile_vmem, tile_vmem, tile_vmem, tile_vmem, sums, sems(1), sems(4, chunks),
             ],
+            input_output_aliases={6: 0, 7: 1},
             compiler_params=PARAMS,
-        )(my_list, live, covariance, far(theta), far(tiles))
+        )(
+            my_list, live, covariance, far(near_sums), far(theta), far(tiles), far(base), far(d)
+        )
 
     for sweep in range(1, SWEEPS):
         last = sweep == SWEEPS - 1
@@ -423,7 +588,7 @@
             )
         with jax.named_scope("diagonal"):
             t = pl.pallas_call(
-                diagonal_kernel,
+                functools.partial(diagonal_kernel, steps),
                 in_specs=[SMEM, HBM, HBM, VMEM] + [HBM] * col_count,
                 out_specs=HBM,
                 out_shape=tile_out,
@@ -432,7 +597,7 @@
                     sems(col_count), sems(3, chunks),
                 ],
                 compiler_params=PARAMS,
-            )(my_list, far(base), far(d), col_diag, *[far(block) for block in row_diag])
+            )(my_list, far(base), far(d), col_diag, *[far(block) for block in got_blocks])
         with jax.named_scope("sweep"):
             result = pl.pallas_call(
                 functools.partial(sweep_kernel, last),

time: 231 us -> 286 us (1.24)
  Pallas kernels: 71.6 us -> 158 us
  waiting for transfers between devices: 57.9 us -> 23.1 us
  starting transfers between devices: 50.3 us -> 53.3 us
    pallas_call x6 -> x7, Pallas kernels: 39.6 us -> 126 us  [the longest x1 81.9 us: body(): pl.pallas_call(functools.partial(gather_kernel, steps), in_specs=[SMEM, H...]
    all_gather x1, waiting for transfers between devices: 39.2 us -> 0.01 us  [body(): slices = lax.all_gather(mine, 'col', axis=0, tiled=True)]
    ppermute x15, waiting for transfers between devices: 8.64 us -> 12.9 us  [send(): return lax.ppermute(blocks_out[n], 'col', pairs_of)]
    ppermute x15, starting transfers between devices: 25.6 us -> 28.7 us  [send(): return lax.ppermute(blocks_out[n], 'col', pairs_of)]
  transfers between devices with their start and end apart: 21 -> 21, of which waited for: 9 -> 10; matrix products, arithmetic and copies ran while one was open for 3% -> 3% of each run, Pallas kernels for 12% -> 41%
where the time goes in v3:
time: 286 us; the launch traced here: 284 us
  Pallas kernels  158 us (55%)
  starting transfers between devices  53.3 us (19%)
  blocking collectives  28.4 us (10%)
  waiting for transfers between devices  23.1 us (8%)
  between operations  13.9 us (5%)
  local copies, waits for them, and re-layouts  5.9 us (2%)
    pallas_call x1, Pallas kernels, body(): pl.pallas_call(functools.partial(gather_kernel, steps), in_specs=[SMEM, H...  81.9 us
    ppermute x15, starting transfers between devices, send(): return lax.ppermute(blocks_out[n], 'col', pairs_of)  28.7 us
    all_to_all x2, blocking collectives, body(): got = lax.all_to_all(pieces, 'row', split_axis=0, concat_axis=0, tiled=True)  28.4 us
    pallas_call x3, Pallas kernels, body(): pl.pallas_call(functools.partial(diagonal_kernel, steps), in_specs=[SMEM,...  21.5 us
    pallas_call x3, Pallas kernels, body(): pl.pallas_call(functools.partial(sweep_kernel, last), in_specs=[SMEM, SME...  19.6 us
    ppermute x15, waiting for transfers between devices, send(): return lax.ppermute(blocks_out[n], 'col', pairs_of)  12.9 us
    all_to_all x3, starting transfers between devices, body(): lax.all_to_all(summed.reshape(piece_shape), 'row', split_axis=0, concat_a...  10.5 us
    pallas_call x1, Pallas kernels, body(): pl.pallas_call(functools.partial(covariance_kernel, far_chips, col_count)...  8.71 us
  transfers between devices with their start and end apart: 21, of which 10 were waited for; matrix products, arithmetic and copies ran while one was open for 3% of the time, Pallas kernels for 41%

profile of v3, /device:TPU:32, one launch (start us, length us, event | category | flops | bytes accessed | tf_op | source)
XLA Modules:
  0.0 283.6 jit_solution(3412370588062412050)
XLA Ops:
  6.5 4.5 %slices.1 = bf16[32,8,512]{2,1,0:T(8,128)(2,1)} custom-call(bf16[32,512,128]{2,1,0:T(8,128)(2,1)} %features.5), custom_call_target="tpu_custom_call" | custom-call | tf_op jit(solution)/shard_map/slices/pallas_call | solution.py:440
  11.1 0.0 all-gather.2.cloned.1.call-update
  11.1 0.8 dynamic-slice_subtract_fusion.1
  11.9 0.1 copy.28
  12.0 0.7 copy.25.wanted_ref
  12.6 81.9 %blocks.1 = (bf16[2,640,128]{2,1,0:T(8,128)(2,1)}, bf16[2,640,128]{2,1,0:T(8,128)(2,1)}, bf16[2,640,128]{2,1,0:T(8,128)(2,1)}, bf16[2,640,128]{2,1,0:T(8,128)(2,...) custom-call(s32[16,2]{1,0:T(8,128)} %copy.25.wanted_ref, ...), custom_call_target="tpu_custom_call" | custom-call | tf_op jit(solution)/shard_map/blocks/pallas_call | solution.py:495
  94.6 5.5 %collective-permute-start.5 = (bf16[2,128,128]{2,1,0:T(8,128)(2,1)}, bf16[2,128,128]{2,1,0:T(8,128)(2,1)S(1)}, u32[]{:S(2)}, u32[]{:S(2)}) collective-permute-start(bf16[2,128,128]{2,1,0:T(8,128)(2,1)} %get-tuple-element.87), channel_id=1, source_target_pairs={{0,12},{1,13},{2,14},{3,15},{4,0},{5,1},{6,2},{7,3},{8,4},{9,5},{1... | collective-permute-start | bytes 196616 | tf_op jit(solution)/shard_map/blocks/ppermute | solution.py:511
  100.1 0.6 collective-permute-start.6
  100.7 1.5 collective-permute-start.7
  102.1 0.6 collective-permute-start.8
  102.7 0.1 collective-permute-start
  102.8 2.2 collective-permute-start.1
  105.0 2.2 collective-permute-done.6.rest_7_
  107.2 0.9 collective-permute-done.7.rest_8_
  108.1 0.7 collective-permute-start.3
  108.8 0.8 collective-permute-done.8.rest_9_
  109.6 2.1 collective-permute-start.4
  111.7 3.9 %split.1.far_pairs = bf16[32,128,256]{2,1,0:T(8,128)(2,1)} custom-call(f32[32,128,128]{2,1,0:T(8,128)} %bitcast.30), custom_call_target="tpu_custom_call" | custom-call | tf_op jit(solution)/shard_map/split/pallas_call | solution.py:472
  115.6 0.4 fusion.3
  116.0 0.1 copy.23
  116.1 0.1 copy.26.owned_ref
  116.2 0.9 constant_dynamic-slice_fusion.1
  117.1 0.0 collective-permute-done.rest_1_
  117.1 0.0 collective-permute-done.1.rest_2_
  117.2 2.0 collective-permute-done.2.rest_3_
  119.1 1.0 collective-permute-done.3.rest_4_
  120.1 6.0 %collective-permute-done.4.rest_5_ = bf16[2,640,128]{2,1,0:T(8,128)(2,1)S(1)} collective-permute-done((bf16[2,640,128]{2,1,0:T(8,128)(2,1)}, bf16[2,640,128]{2,1,0:T(8,128)(2,1)S(1)}, u32[]{:S(2)}, u32[]{:S(2)}) %collective-permute-start.4) | collective-permute-done | bytes 327712 | tf_op jit(solution)/shard_map/blocks/ppermute | solution.py:511
  126.1 8.7 %covariance.1 = f32[16,20,8,128]{3,2,1,0:T(8,128)} custom-call(s32[16,32]{1,0:T(8,128)S(1)} %bitcast.24, s32[16,32]{1,0:T(8,128)S(1)} %bitcast.23, s32[16,2]{1,0:T(8,128)S(1)} %copy.26.owned_ref, bf16[512,8,512]{2,1,0:T(8,128)(2,1)} %all-gather.2.cloned.1.call-done.far_slices, bf16[32,512,128]{2,1,0:T(8,128)(2,1)} %features.5), custom_call_target="tpu_custom_call" | custom-call | tf_op jit(solution)/shard_map/covariance/pallas_call | solution.py:518
  134.9 7.2 %all-to-all-start = ((f32[16,20,8,128]{3,2,1,0:T(8,128)}), f32[16,20,8,128]{3,2,1,0:T(8,128)S(1)}, u32[]{:S(2)}, u32[]{:S(2)}) async-start(f32[16,20,8,128]{3,2,1,0:T(8,128)} %covariance.1), calls=%async_computation | async-start | bytes 2621440 | tf_op jit(solution)/shard_map/covariance/all_to_all | solution.py:532
  142.1 0.1 fusion.owned_ref
  142.2 1.3 dynamic_slice.26
  143.5 0.1 sub.25
  143.6 0.1 compare_convert_fusion.same_ref
  143.7 0.9 collective-permute-start.10
  144.6 1.8 gather_fusion
  146.4 3.1 %collective-permute-start.11 = (bf16[2,128,128]{2,1,0:T(8,128)(2,1)S(1)}, bf16[2,128,128]{2,1,0:T(8,128)(2,1)S(1)}, u32[]{:S(2)}, u32[]{:S(2)}) collective-permute-start(bf16[2,128,128]{2,1,0:T(8,128)(2,1)S(1)} %copy-done.20), channel_id=1, source_target_pairs={{0,8},{1,9},{2,10},{3,11},{4,12},{5,13},{6,14},{7,15},{8,0},{9,1},... | collective-permute-start | bytes 196616 | tf_op jit(solution)/shard_map/near/ppermute | solution.py:511
  149.5 2.8 collective-permute-start.12
  152.3 3.7 %collective-permute-start.13 = (bf16[2,128,128]{2,1,0:T(8,128)(2,1)S(1)}, bf16[2,128,128]{2,1,0:T(8,128)(2,1)S(1)}, u32[]{:S(2)}, u32[]{:S(2)}) collective-permute-start(bf16[2,128,128]{2,1,0:T(8,128)(2,1)S(1)} %copy-done.18), channel_id=1, source_target_pairs={{0,6},{1,7},{2,8},{3,9},{4,10},{5,11},{6,12},{7,13},{8,14},{9,15},... | collective-permute-start | bytes 196616 | tf_op jit(solution)/shard_map/near/ppermute | solution.py:511
  156.0 0.1 collective-permute-start.14
  156.1 0.0 collective-permute-done.10.rest_11_
  156.1 4.9 %collective-permute-start.9 = (bf16[2,128,128]{2,1,0:T(8,128)(2,1)S(1)}, bf16[2,128,128]{2,1,0:T(8,128)(2,1)S(1)}, u32[]{:S(2)}, u32[]{:S(2)}) collective-permute-start(bf16[2,128,128]{2,1,0:T(8,128)(2,1)S(1)} %copy-done.16), channel_id=1, source_target_pairs={{0,10},{1,11},{2,12},{3,13},{4,14},{5,15},{6,0},{7,1},{8,2},{9,3},... | collective-permute-start | bytes 196616 | tf_op jit(solution)/shard_map/near/ppermute | solution.py:511
  161.0 0.7 fusion.1.list_ref
  161.7 8.2 %near.1 = (f32[32,128,128]{2,1,0:T(8,128)}, f32[32,128,128]{2,1,0:T(8,128)}, f32[2,128,256]{2,1,0:T(8,128)}) custom-call(s32[32]{0:T(128)S(1)} %fusion.1.list_ref, s32[1]{0:T(128)} %bitcast.1.live_ref, s32[2]{0:T(128)S(1)} %fusion.owned_ref, bf16[32,512,128]{2,1,0:T(8,128)(2,1)} %features.5, f32[32,128,128]{2,1,0:T(8,128)} %bitcast.25, ...), custom_call_target="tpu_custom_call" | custom-call | tf_op jit(solution)/shard_map/near/pallas_call | solution.py:539
  170.1 5.4 %first.1 = (f32[32,128,128]{2,1,0:T(8,128)}, f32[32,128,128]{2,1,0:T(8,128)}, f32[16,2,8,128]{3,2,1,0:T(8,128)}) custom-call(s32[32]{0:T(128)S(1)} %fusion.1.list_ref, s32[1]{0:T(128)} %bitcast.1.live_ref, f32[16,20,8,128]{3,2,1,0:T(8,128)S(1)} %all-to-all-done.cov_ref, ...), custom_call_target="tpu_custom_call", output_to_operand_aliasing={{0}: (6, {}), {1}: (7, {})} | custom-call | tf_op jit(solution)/shard_map/first/pallas_call | solution.py:560
  175.5 6.9 %all-to-all-start.1 = ((f32[16,2,8,128]{3,2,1,0:T(8,128)}), f32[16,2,8,128]{3,2,1,0:T(8,128)S(1)}, u32[]{:S(2)}, u32[]{:S(2)}) async-start(f32[16,2,8,128]{3,2,1,0:T(8,128)} %get-tuple-element.150), calls=%async_computation.1 | async-start | bytes 262144 | tf_op jit(solution)/shard_map/exchange/all_to_all | solution.py:577
  182.5 8.0 %all-to-all-done.1 = f32[16,2,8,128]{3,2,1,0:T(8,128)S(1)} async-done(((f32[16,2,8,128]{3,2,1,0:T(8,128)}), f32[16,2,8,128]{3,2,1,0:T(8,128)S(1)}, u32[]{:S(2)}, u32[]{:S(2)}) %all-to-all-start.1) | async-done | bytes 131104 | tf_op jit(solution)/shard_map/exchange/all_to_all | solution.py:577
  190.4 1.3 exchange.3
  191.7 3.5 %all-to-all-start.2 = ((f32[16,2,8,128]{3,2,1,0:T(8,128)}), f32[16,2,8,128]{3,2,1,0:T(8,128)S(1)}, u32[]{:S(2)}, u32[]{:S(2)}) async-start(f32[16,2,8,128]{3,2,1,0:T(8,128)} %bitcast.10), calls=%async_computation.2 | async-start | bytes 262144 | tf_op jit(solution)/shard_map/exchange/all_to_all | solution.py:586
  195.3 0.1 broadcast_select_fusion.col_diag_ref
  195.3 7.1 %diagonal.3.far_t = f32[32,128,128]{2,1,0:T(8,128)} custom-call(s32[32]{0:T(128)S(1)} %fusion.1.list_ref, f32[32,128,128]{2,1,0:T(8,128)} %get-tuple-element.131.far_base, f32[32,128,128]{2,1,0:T(8,128)} %get-tuple-element.132.far_d, bf16[2,128,128]{2,1,0:T(8,128)(2,1)S(1)} %broadcast_select_fusion.col_diag_ref, ...), custom_call_target="tpu_custom_call" | custom-call | tf_op jit(solution)/shard_map/diagonal/pallas_call | solution.py:590
  202.5 0.7 all-to-all-done.2.q_ref
  203.2 7.0 %sweep.3 = (f32[32,128,128]{2,1,0:T(8,128)}, f32[16,2,8,128]{3,2,1,0:T(8,128)S(1)}) custom-call(s32[32]{0:T(128)S(1)} %fusion.1.list_ref, s32[1]{0:T(128)} %bitcast.1.live_ref, f32[32,128,128]{2,1,0:T(8,128)} %diagonal.3.far_t, f32[32,128,128]{2,1,0:T(8,128)} %bitcast.27, bf16[32,128,256]{2,1,0:T(8,128)(2,1)} %split.1.far_pairs, ...), custom_call_target="tpu_custom_call" | custom-call | tf_op jit(solution)/shard_map/sweep/pallas_call | solution.py:602
  210.2 14.2 %all_to_all.35 = f32[16,2,8,128]{3,2,1,0:T(8,128)S(1)} all-to-all(f32[16,2,8,128]{3,2,1,0:T(8,128)S(1)} %get-tuple-element.152), channel_id=1, replica_groups=mesh['row'=16,'col'=16] {'row'}, dimensions={0} | all-to-all | bytes 262144 | tf_op jit(solution)/shard_map/exchange/all_to_all | solution.py:577
  224.5 1.3 exchange.4
  225.8 3.5 %all-to-all-start.4 = ((f32[16,2,8,128]{3,2,1,0:T(8,128)}), f32[16,2,8,128]{3,2,1,0:T(8,128)S(1)}, u32[]{:S(2)}, u32[]{:S(2)}) async-start(f32[16,2,8,128]{3,2,1,0:T(8,128)} %bitcast.12), calls=%async_computation.4 | async-start | bytes 262144 | tf_op jit(solution)/shard_map/exchange/all_to_all | solution.py:586
  229.3 7.2 %diagonal.4.far_t = f32[32,128,128]{2,1,0:T(8,128)} custom-call(s32[32]{0:T(128)S(1)} %fusion.1.list_ref, f32[32,128,128]{2,1,0:T(8,128)} %get-tuple-element.131.far_base, f32[32,128,128]{2,1,0:T(8,128)} %get-tuple-element.151.far_d, bf16[2,128,128]{2,1,0:T(8,128)(2,1)S(1)} %broadcast_select_fusion.col_diag_ref, ...), custom_call_target="tpu_custom_call" | custom-call | tf_op jit(solution)/shard_map/diagonal/pallas_call | solution.py:590
  236.5 0.8 all-to-all-done.4.q_ref
  237.3 7.0 %sweep.4 = (f32[32,128,128]{2,1,0:T(8,128)}, f32[16,2,8,128]{3,2,1,0:T(8,128)S(1)}) custom-call(s32[32]{0:T(128)S(1)} %fusion.1.list_ref, s32[1]{0:T(128)} %bitcast.1.live_ref, f32[32,128,128]{2,1,0:T(8,128)} %diagonal.4.far_t, f32[32,128,128]{2,1,0:T(8,128)} %bitcast.28, bf16[32,128,256]{2,1,0:T(8,128)(2,1)} %split.1.far_pairs, ...), custom_call_target="tpu_custom_call" | custom-call | tf_op jit(solution)/shard_map/sweep/pallas_call | solution.py:602
  244.3 14.2 %all_to_all.36 = f32[16,2,8,128]{3,2,1,0:T(8,128)S(1)} all-to-all(f32[16,2,8,128]{3,2,1,0:T(8,128)S(1)} %get-tuple-element.154), channel_id=1, replica_groups=mesh['row'=16,'col'=16] {'row'}, dimensions={0} | all-to-all | bytes 262144 | tf_op jit(solution)/shard_map/exchange/all_to_all | solution.py:577
  258.5 1.3 exchange.5
  259.8 3.5 %all-to-all-start.6 = ((f32[16,2,8,128]{3,2,1,0:T(8,128)}), f32[16,2,8,128]{3,2,1,0:T(8,128)S(1)}, u32[]{:S(2)}, u32[]{:S(2)}) async-start(f32[16,2,8,128]{3,2,1,0:T(8,128)} %bitcast.14), calls=%async_computation.6 | async-start | bytes 262144 | tf_op jit(solution)/shard_map/exchange/all_to_all | solution.py:586
  263.3 7.2 %diagonal.5.far_t = f32[32,128,128]{2,1,0:T(8,128)} custom-call(s32[32]{0:T(128)S(1)} %fusion.1.list_ref, f32[32,128,128]{2,1,0:T(8,128)} %get-tuple-element.131.far_base, f32[32,128,128]{2,1,0:T(8,128)} %get-tuple-element.153.far_d, bf16[2,128,128]{2,1,0:T(8,128)(2,1)S(1)} %broadcast_select_fusion.col_diag_ref, ...), custom_call_target="tpu_custom_call" | custom-call | tf_op jit(solution)/shard_map/diagonal/pallas_call | solution.py:590
  270.5 0.8 all-to-all-done.6.q_ref
  271.3 5.5 %sweep.5 = f32[32,128,128]{2,1,0:T(8,128)} custom-call(s32[32]{0:T(128)S(1)} %fusion.1.list_ref, s32[1]{0:T(128)} %bitcast.1.live_ref, f32[32,128,128]{2,1,0:T(8,128)} %diagonal.5.far_t, f32[32,128,128]{2,1,0:T(8,128)} %bitcast.29, bf16[32,128,256]{2,1,0:T(8,128)(2,1)} %split.1.far_pairs, f32[16,2,8,128]{3,2,1,0:T(8,128)S(1)} %all-to-all-done.6.q_ref), custom_call_target="tpu_custom_call" | custom-call | tf_op jit(solution)/shard_map/sweep/pallas_call | solution.py:602
  (57 shorter events, 0.1 us)
Async XLA Ops:
  6.5 119.6 %all-gather.2.cloned.1.call-start = ((), (), s32[]{:S(2)}) async-start(), calls=%async_computation.7 | async-start | bytes 4456448 | tf_op jit(solution)/shard_map/slices/all_gather | solution.py:447
  94.6 8.2 %collective-permute-start.5 = (bf16[2,128,128]{2,1,0:T(8,128)(2,1)}, bf16[2,128,128]{2,1,0:T(8,128)(2,1)S(1)}, u32[]{:S(2)}, u32[]{:S(2)}) collective-permute-start(bf16[2,128,128]{2,1,0:T(8,128)(2,1)} %get-tuple-element.87), channel_id=1, source_target_pairs={{0,12},{1,13},{2,14},{3,15},{4,0},{5,1},{6,2},{7,3},{8,4},{9,5},{1... | collective-permute-start | bytes 196616 | tf_op jit(solution)/shard_map/blocks/ppermute | solution.py:511
  100.1 7.1 %collective-permute-start.6 = (bf16[2,128,128]{2,1,0:T(8,128)(2,1)}, bf16[2,128,128]{2,1,0:T(8,128)(2,1)S(1)}, u32[]{:S(2)}, u32[]{:S(2)}) collective-permute-start(bf16[2,128,128]{2,1,0:T(8,128)(2,1)} %get-tuple-element.88), channel_id=1, source_target_pairs={{0,13},{1,12},{2,15},{3,14},{4,1},{5,0},{6,3},{7,2},{8,5},{9,4},{1... | collective-permute-start | bytes 196616 | tf_op jit(solution)/shard_map/blocks/ppermute | solution.py:511
  100.7 7.4 %collective-permute-start.7 = (bf16[2,128,128]{2,1,0:T(8,128)(2,1)}, bf16[2,128,128]{2,1,0:T(8,128)(2,1)S(1)}, u32[]{:S(2)}, u32[]{:S(2)}) collective-permute-start(bf16[2,128,128]{2,1,0:T(8,128)(2,1)} %get-tuple-element.89), channel_id=1, source_target_pairs={{0,4},{1,5},{2,6},{3,7},{4,8},{5,9},{6,10},{7,11},{8,12},{9,13},{1... | collective-permute-start | bytes 196616 | tf_op jit(solution)/shard_map/blocks/ppermute | solution.py:511
  102.1 7.5 %collective-permute-start.8 = (bf16[2,128,128]{2,1,0:T(8,128)(2,1)}, bf16[2,128,128]{2,1,0:T(8,128)(2,1)S(1)}, u32[]{:S(2)}, u32[]{:S(2)}) collective-permute-start(bf16[2,128,128]{2,1,0:T(8,128)(2,1)} %get-tuple-element.90), channel_id=1, source_target_pairs={{0,5},{1,4},{2,7},{3,6},{4,9},{5,8},{6,11},{7,10},{8,13},{9,12},{1... | collective-permute-start | bytes 196616 | tf_op jit(solution)/shard_map/blocks/ppermute | solution.py:511
  102.7 14.4 %collective-permute-start = (bf16[2,640,128]{2,1,0:T(8,128)(2,1)}, bf16[2,640,128]{2,1,0:T(8,128)(2,1)S(1)}, u32[]{:S(2)}, u32[]{:S(2)}) collective-permute-start(bf16[2,640,128]{2,1,0:T(8,128)(2,1)} %get-tuple-element.82), channel_id=1, source_target_pairs={{0,1},{1,0},{2,3},{3,2},{4,5},{5,4},{6,7},{7,6},{8,9},{9,8},{10,11... | collective-permute-start | bytes 983048 | tf_op jit(solution)/shard_map/blocks/ppermute | solution.py:511
  102.8 12.8 %copy-start.5 = (bf16[2,128,128]{2,1,0:T(8,128)(2,1)}, bf16[2,128,128]{2,1,0:T(8,128)(2,1)S(1)}, u32[]{:S(2)}) copy-start(bf16[2,128,128]{2,1,0:T(8,128)(2,1)S(1)} %collective-permute-done.5.rest_6_) | copy-start | bytes 196612
  102.8 14.3 %collective-permute-start.1 = (bf16[2,640,128]{2,1,0:T(8,128)(2,1)}, bf16[2,640,128]{2,1,0:T(8,128)(2,1)S(1)}, u32[]{:S(2)}, u32[]{:S(2)}) collective-permute-start(bf16[2,640,128]{2,1,0:T(8,128)(2,1)} %get-tuple-element.83), channel_id=1, source_target_pairs={{0,14},{1,15},{2,0},{3,1},{4,2},{5,3},{6,4},{7,5},{8,6},{9,7},{10,... | collective-permute-start | bytes 983048 | tf_op jit(solution)/shard_map/blocks/ppermute | solution.py:511
  107.2 8.4 %copy-start.6 = (bf16[2,128,128]{2,1,0:T(8,128)(2,1)}, bf16[2,128,128]{2,1,0:T(8,128)(2,1)S(1)}, u32[]{:S(2)}) copy-start(bf16[2,128,128]{2,1,0:T(8,128)(2,1)S(1)} %collective-permute-done.6.rest_7_) | copy-start | bytes 196612
  107.2 11.9 %collective-permute-start.2 = (bf16[2,640,128]{2,1,0:T(8,128)(2,1)}, bf16[2,640,128]{2,1,0:T(8,128)(2,1)S(1)}, u32[]{:S(2)}, u32[]{:S(2)}) collective-permute-start(bf16[2,640,128]{2,1,0:T(8,128)(2,1)} %get-tuple-element.84), channel_id=1, source_target_pairs={{0,15},{1,14},{2,1},{3,0},{4,3},{5,2},{6,5},{7,4},{8,7},{9,6},{10,... | collective-permute-start | bytes 983048 | tf_op jit(solution)/shard_map/blocks/ppermute | solution.py:511
  108.1 7.5 %copy-start.7 = (bf16[2,128,128]{2,1,0:T(8,128)(2,1)}, bf16[2,128,128]{2,1,0:T(8,128)(2,1)S(1)}, u32[]{:S(2)}) copy-start(bf16[2,128,128]{2,1,0:T(8,128)(2,1)S(1)} %collective-permute-done.7.rest_8_) | copy-start | bytes 196612
  108.1 12.0 %collective-permute-start.3 = (bf16[2,640,128]{2,1,0:T(8,128)(2,1)}, bf16[2,640,128]{2,1,0:T(8,128)(2,1)S(1)}, u32[]{:S(2)}, u32[]{:S(2)}) collective-permute-start(bf16[2,640,128]{2,1,0:T(8,128)(2,1)} %get-tuple-element.85), channel_id=1, source_target_pairs={{0,2},{1,3},{2,4},{3,5},{4,6},{5,7},{6,8},{7,9},{8,10},{9,11},{10,... | collective-permute-start | bytes 983048 | tf_op jit(solution)/shard_map/blocks/ppermute | solution.py:511
  109.6 6.0 %copy-start.8 = (bf16[2,128,128]{2,1,0:T(8,128)(2,1)}, bf16[2,128,128]{2,1,0:T(8,128)(2,1)S(1)}, u32[]{:S(2)}) copy-start(bf16[2,128,128]{2,1,0:T(8,128)(2,1)S(1)} %collective-permute-done.8.rest_9_) | copy-start | bytes 196612
  109.6 16.5 %collective-permute-start.4 = (bf16[2,640,128]{2,1,0:T(8,128)(2,1)}, bf16[2,640,128]{2,1,0:T(8,128)(2,1)S(1)}, u32[]{:S(2)}, u32[]{:S(2)}) collective-permute-start(bf16[2,640,128]{2,1,0:T(8,128)(2,1)} %get-tuple-element.86), channel_id=1, source_target_pairs={{0,3},{1,2},{2,5},{3,4},{4,7},{5,6},{6,9},{7,8},{8,11},{9,10},{10,... | collective-permute-start | bytes 983048 | tf_op jit(solution)/shard_map/blocks/ppermute | solution.py:511
  111.7 3.9 %copy-start.15 = (s32[16,16,2]{1,2,0:T(2,128)S(1)}, s32[16,16,2]{1,2,0:T(2,128)}, u32[]{:S(2)}) copy-start(s32[16,16,2]{1,2,0:T(2,128)} %param.14) | copy-start | bytes 6148
  117.1 17.7 %copy-start = (bf16[2,640,128]{2,1,0:T(8,128)(2,1)}, bf16[2,640,128]{2,1,0:T(8,128)(2,1)S(1)}, u32[]{:S(2)}) copy-start(bf16[2,640,128]{2,1,0:T(8,128)(2,1)S(1)} %collective-permute-done.rest_1_) | copy-start | bytes 983044
  117.1 17.7 %copy-start.1 = (bf16[2,640,128]{2,1,0:T(8,128)(2,1)}, bf16[2,640,128]{2,1,0:T(8,128)(2,1)S(1)}, u32[]{:S(2)}) copy-start(bf16[2,640,128]{2,1,0:T(8,128)(2,1)S(1)} %collective-permute-done.1.rest_2_) | copy-start | bytes 983044
  119.1 15.7 %copy-start.2 = (bf16[2,640,128]{2,1,0:T(8,128)(2,1)}, bf16[2,640,128]{2,1,0:T(8,128)(2,1)S(1)}, u32[]{:S(2)}) copy-start(bf16[2,640,128]{2,1,0:T(8,128)(2,1)S(1)} %collective-permute-done.2.rest_3_) | copy-start | bytes 983044
  120.1 14.7 %copy-start.3 = (bf16[2,640,128]{2,1,0:T(8,128)(2,1)}, bf16[2,640,128]{2,1,0:T(8,128)(2,1)S(1)}, u32[]{:S(2)}) copy-start(bf16[2,640,128]{2,1,0:T(8,128)(2,1)S(1)} %collective-permute-done.3.rest_4_) | copy-start | bytes 983044
  126.1 8.8 %copy-start.4 = (bf16[2,640,128]{2,1,0:T(8,128)(2,1)}, bf16[2,640,128]{2,1,0:T(8,128)(2,1)S(1)}, u32[]{:S(2)}) copy-start(bf16[2,640,128]{2,1,0:T(8,128)(2,1)S(1)} %collective-permute-done.4.rest_5_) | copy-start | bytes 983044
  134.9 8.8 %copy-start.21 = (bf16[2,128,128]{2,1,0:T(8,128)(2,1)S(1)}, bf16[2,128,128]{2,1,0:T(8,128)(2,1)}, u32[]{:S(2)}) copy-start(bf16[2,128,128]{2,1,0:T(8,128)(2,1)} %get-tuple-element.119) | copy-start | bytes 196612
  134.9 11.5 %copy-start.20 = (bf16[2,128,128]{2,1,0:T(8,128)(2,1)S(1)}, bf16[2,128,128]{2,1,0:T(8,128)(2,1)}, u32[]{:S(2)}) copy-start(bf16[2,128,128]{2,1,0:T(8,128)(2,1)} %get-tuple-element.120) | copy-start | bytes 196612
  134.9 14.6 %copy-start.19 = (bf16[2,128,128]{2,1,0:T(8,128)(2,1)S(1)}, bf16[2,128,128]{2,1,0:T(8,128)(2,1)}, u32[]{:S(2)}) copy-start(bf16[2,128,128]{2,1,0:T(8,128)(2,1)} %get-tuple-element.121) | copy-start | bytes 196612
  134.9 17.4 %copy-start.18 = (bf16[2,128,128]{2,1,0:T(8,128)(2,1)S(1)}, bf16[2,128,128]{2,1,0:T(8,128)(2,1)}, u32[]{:S(2)}) copy-start(bf16[2,128,128]{2,1,0:T(8,128)(2,1)} %get-tuple-element.122) | copy-start | bytes 196612
  134.9 21.1 %copy-start.17 = (bf16[2,128,128]{2,1,0:T(8,128)(2,1)S(1)}, bf16[2,128,128]{2,1,0:T(8,128)(2,1)}, u32[]{:S(2)}) copy-start(bf16[2,128,128]{2,1,0:T(8,128)(2,1)} %get-tuple-element.123) | copy-start | bytes 196612
  134.9 21.2 %copy-start.16 = (bf16[2,128,128]{2,1,0:T(8,128)(2,1)S(1)}, bf16[2,128,128]{2,1,0:T(8,128)(2,1)}, u32[]{:S(2)}) copy-start(bf16[2,128,128]{2,1,0:T(8,128)(2,1)} %get-tuple-element.118) | copy-start | bytes 196612
  134.9 35.1 %all-to-all-start = ((f32[16,20,8,128]{3,2,1,0:T(8,128)}), f32[16,20,8,128]{3,2,1,0:T(8,128)S(1)}, u32[]{:S(2)}, u32[]{:S(2)}) async-start(f32[16,20,8,128]{3,2,1,0:T(8,128)} %covariance.1), calls=%async_computation | async-start | bytes 2621440 | tf_op jit(solution)/shard_map/covariance/all_to_all | solution.py:532
  143.7 12.4 %collective-permute-start.10 = (bf16[2,128,128]{2,1,0:T(8,128)(2,1)S(1)}, bf16[2,128,128]{2,1,0:T(8,128)(2,1)S(1)}, u32[]{:S(2)}, u32[]{:S(2)}) collective-permute-start(bf16[2,128,128]{2,1,0:T(8,128)(2,1)S(1)} %copy-done.21), channel_id=1, source_target_pairs={{0,11},{1,10},{2,13},{3,12},{4,15},{5,14},{6,1},{7,0},{8,3},{9,2},... | collective-permute-start | bytes 196616 | tf_op jit(solution)/shard_map/near/ppermute | solution.py:511
  146.4 23.5 %collective-permute-start.11 = (bf16[2,128,128]{2,1,0:T(8,128)(2,1)S(1)}, bf16[2,128,128]{2,1,0:T(8,128)(2,1)S(1)}, u32[]{:S(2)}, u32[]{:S(2)}) collective-permute-start(bf16[2,128,128]{2,1,0:T(8,128)(2,1)S(1)} %copy-done.20), channel_id=1, source_target_pairs={{0,8},{1,9},{2,10},{3,11},{4,12},{5,13},{6,14},{7,15},{8,0},{9,1},... | collective-permute-start | bytes 196616 | tf_op jit(solution)/shard_map/near/ppermute | solution.py:511
  149.5 20.5 %collective-permute-start.12 = (bf16[2,128,128]{2,1,0:T(8,128)(2,1)S(1)}, bf16[2,128,128]{2,1,0:T(8,128)(2,1)S(1)}, u32[]{:S(2)}, u32[]{:S(2)}) collective-permute-start(bf16[2,128,128]{2,1,0:T(8,128)(2,1)S(1)} %copy-done.19), channel_id=1, source_target_pairs={{0,9},{1,8},{2,11},{3,10},{4,13},{5,12},{6,15},{7,14},{8,1},{9,0},... | collective-permute-start | bytes 196616 | tf_op jit(solution)/shard_map/near/ppermute | solution.py:511
  152.3 17.7 %collective-permute-start.13 = (bf16[2,128,128]{2,1,0:T(8,128)(2,1)S(1)}, bf16[2,128,128]{2,1,0:T(8,128)(2,1)S(1)}, u32[]{:S(2)}, u32[]{:S(2)}) collective-permute-start(bf16[2,128,128]{2,1,0:T(8,128)(2,1)S(1)} %copy-done.18), channel_id=1, source_target_pairs={{0,6},{1,7},{2,8},{3,9},{4,10},{5,11},{6,12},{7,13},{8,14},{9,15},... | collective-permute-start | bytes 196616 | tf_op jit(solution)/shard_map/near/ppermute | solution.py:511
  156.0 14.0 %collective-permute-start.14 = (bf16[2,128,128]{2,1,0:T(8,128)(2,1)S(1)}, bf16[2,128,128]{2,1,0:T(8,128)(2,1)S(1)}, u32[]{:S(2)}, u32[]{:S(2)}) collective-permute-start(bf16[2,128,128]{2,1,0:T(8,128)(2,1)S(1)} %copy-done.17), channel_id=1, source_target_pairs={{0,7},{1,6},{2,9},{3,8},{4,11},{5,10},{6,13},{7,12},{8,15},{9,14},... | collective-permute-start | bytes 196616 | tf_op jit(solution)/shard_map/near/ppermute | solution.py:511
  156.1 13.8 %copy-start.9 = (bf16[2,128,128]{2,1,0:T(8,128)(2,1)}, bf16[2,128,128]{2,1,0:T(8,128)(2,1)S(1)}, u32[]{:S(2)}) copy-start(bf16[2,128,128]{2,1,0:T(8,128)(2,1)S(1)} %collective-permute-done.10.rest_11_) | copy-start | bytes 196612
  156.1 13.9 %collective-permute-start.9 = (bf16[2,128,128]{2,1,0:T(8,128)(2,1)S(1)}, bf16[2,128,128]{2,1,0:T(8,128)(2,1)S(1)}, u32[]{:S(2)}, u32[]{:S(2)}) collective-permute-start(bf16[2,128,128]{2,1,0:T(8,128)(2,1)S(1)} %copy-done.16), channel_id=1, source_target_pairs={{0,10},{1,11},{2,12},{3,13},{4,14},{5,15},{6,0},{7,1},{8,2},{9,3},... | collective-permute-start | bytes 196616 | tf_op jit(solution)/shard_map/near/ppermute | solution.py:511
  170.0 5.5 %copy-start.10 = (bf16[2,128,128]{2,1,0:T(8,128)(2,1)}, bf16[2,128,128]{2,1,0:T(8,128)(2,1)S(1)}, u32[]{:S(2)}) copy-start(bf16[2,128,128]{2,1,0:T(8,128)(2,1)S(1)} %collective-permute-done.11.rest_12_) | copy-start | bytes 196612
  170.0 5.5 %copy-start.11 = (bf16[2,128,128]{2,1,0:T(8,128)(2,1)}, bf16[2,128,128]{2,1,0:T(8,128)(2,1)S(1)}, u32[]{:S(2)}) copy-start(bf16[2,128,128]{2,1,0:T(8,128)(2,1)S(1)} %collective-permute-done.12.rest_13_) | copy-start | bytes 196612
  170.0 5.5 %copy-start.12 = (bf16[2,128,128]{2,1,0:T(8,128)(2,1)}, bf16[2,128,128]{2,1,0:T(8,128)(2,1)S(1)}, u32[]{:S(2)}) copy-start(bf16[2,128,128]{2,1,0:T(8,128)(2,1)S(1)} %collective-permute-done.13.rest_14_) | copy-start | bytes 196612
  170.0 5.5 %copy-start.13 = (bf16[2,128,128]{2,1,0:T(8,128)(2,1)}, bf16[2,128,128]{2,1,0:T(8,128)(2,1)S(1)}, u32[]{:S(2)}) copy-start(bf16[2,128,128]{2,1,0:T(8,128)(2,1)S(1)} %collective-permute-done.14.rest_15_) | copy-start | bytes 196612
  170.0 5.4 %copy-start.14 = (bf16[2,128,128]{2,1,0:T(8,128)(2,1)}, bf16[2,128,128]{2,1,0:T(8,128)(2,1)S(1)}, u32[]{:S(2)}) copy-start(bf16[2,128,128]{2,1,0:T(8,128)(2,1)S(1)} %collective-permute-done.9.rest_10_) | copy-start | bytes 196612
  175.5 14.9 %all-to-all-start.1 = ((f32[16,2,8,128]{3,2,1,0:T(8,128)}), f32[16,2,8,128]{3,2,1,0:T(8,128)S(1)}, u32[]{:S(2)}, u32[]{:S(2)}) async-start(f32[16,2,8,128]{3,2,1,0:T(8,128)} %get-tuple-element.150), calls=%async_computation.1 | async-start | bytes 262144 | tf_op jit(solution)/shard_map/exchange/all_to_all | solution.py:577
  191.7 11.5 %all-to-all-start.2 = ((f32[16,2,8,128]{3,2,1,0:T(8,128)}), f32[16,2,8,128]{3,2,1,0:T(8,128)S(1)}, u32[]{:S(2)}, u32[]{:S(2)}) async-start(f32[16,2,8,128]{3,2,1,0:T(8,128)} %bitcast.10), calls=%async_computation.2 | async-start | bytes 262144 | tf_op jit(solution)/shard_map/exchange/all_to_all | solution.py:586
  225.8 11.5 %all-to-all-start.4 = ((f32[16,2,8,128]{3,2,1,0:T(8,128)}), f32[16,2,8,128]{3,2,1,0:T(8,128)S(1)}, u32[]{:S(2)}, u32[]{:S(2)}) async-start(f32[16,2,8,128]{3,2,1,0:T(8,128)} %bitcast.12), calls=%async_computation.4 | async-start | bytes 262144 | tf_op jit(solution)/shard_map/exchange/all_to_all | solution.py:586
  259.8 11.5 %all-to-all-start.6 = ((f32[16,2,8,128]{3,2,1,0:T(8,128)}), f32[16,2,8,128]{3,2,1,0:T(8,128)S(1)}, u32[]{:S(2)}, u32[]{:S(2)}) async-start(f32[16,2,8,128]{3,2,1,0:T(8,128)} %bitcast.14), calls=%async_computation.6 | async-start | bytes 262144 | tf_op jit(solution)/shard_map/exchange/all_to_all | solution.py:586
Sparse Core Ops, SparseCore 0:
  11.2 91.0 all-gather.1

commit v4 on v3

--- a/solution.py
+++ b/solution.py
@@ -54,27 +54,37 @@
 
 
 def gather_kernel(steps, wanted_ref, features, diag, *rest):
-    outs, sems = rest[:-1], rest[-1]
+    outs, (near_ref, far_ref, sems, out_sems) = rest[:-4], rest[-4:]
     c = lax.axis_index("col")
     samples = features.shape[1]
+    size = diag.shape[1]
+    near_count = near_ref.shape[0]
     copies = []
+    backs = []
     for n, ((dz, dk), out) in enumerate(zip(steps, outs)):
         target = holder(c, -dz, dk, wanted_ref.shape[0])
+        place = near_ref.at[n] if n < near_count else far_ref.at[n - near_count]
+        begin = samples if n < near_count else 0
+        mine = []
         for p in range(out.shape[0]):
             block = wanted_ref[target, p]
-            begin = 0
-            if out.shape[1] > diag.shape[1]:
-                copies.append(pltpu.make_async_copy(
-                    features.at[block], out.at[p, pl.ds(0, samples)], sems.at[n, p, 0]
+            if n < near_count:
+                mine.append(pltpu.make_async_copy(
+                    features.at[block], place.at[p, pl.ds(0, samples)], sems.at[n, p, 0]
                 ))
-                begin = samples
-            copies.append(pltpu.make_async_copy(
-                diag.at[block], out.at[p, pl.ds(begin, diag.shape[1])], sems.at[n, p, 1]
+            mine.append(pltpu.make_async_copy(
+                diag.at[block], place.at[p, pl.ds(begin, size)], sems.at[n, p, 1]
             ))
-    for copy in copies:
-        copy.start()
-    for copy in copies:
-        copy.wait()
+        for copy in mine:
+            copy.start()
+        copies.append(mine)
+        backs.append(pltpu.make_async_copy(place, out, out_sems.at[n]))
+    for mine, back in zip(copies, backs):
+        for copy in mine:
+            copy.wait()
+        back.start()
+    for back in backs:
+        back.wait()
 
 
 def holder(c, dz, dk, col_count):
@@ -130,7 +140,7 @@
 
 def covariance_kernel(
     far, col_count, rows_ref, lists_ref, owned_ref, far_slices, features, out_ref,
-    slices_ref, right_ref, left_ref, slice_sem, right_sem,
+    slices_ref, right_ref, slice_sem, right_sem,
 ):
     owners = rows_ref.shape[0]
     columns = owned_ref.shape[1]
@@ -161,14 +171,13 @@
     def owner_step(owner, carry):
         for a in range(columns):
             right_copy(owner, a).wait()
-        for n, dz in enumerate(far):
-            first = chip_at(dz, col_count) * CHUNK
-            for s in range(CHUNK):
-                k = n * CHUNK + s
-                left_ref[k * group:(k + 1) * group, :] = slices_ref[
-                    rows_ref[owner, first + s]
-                ].astype(F32)
-        left = left_ref[...].astype(BF)
+        left = jnp.concatenate(
+            [
+                slices_ref[rows_ref[owner, chip_at(dz, col_count) * CHUNK + s]].astype(F32)
+                for dz in far for s in range(CHUNK)
+            ],
+            axis=0,
+        ).astype(BF)
         right = jnp.concatenate([right_ref[owner, a] for a in range(columns)], axis=1)
         both = dot(left, right) * (1.0 / samples)
         for n, dz in enumerate(far):
@@ -497,7 +506,13 @@
             in_specs=[SMEM, HBM, HBM],
             out_specs=[HBM] * len(steps),
             out_shape=[pltpu.HBM(dims, BF) for dims in block_shapes],
-            scratch_shapes=[sems(len(steps), per_source, 2)],
+            scratch_shapes=[
+                pltpu.VMEM((near_count,) + block_shapes[0], BF),
+                pltpu.VMEM((len(steps) - near_count,) + block_shapes[-1], BF),
+                sems(len(steps), per_source, 2),
+                sems(len(steps)),
+            ],
+            compiler_params=PARAMS,
         )(wanted, far(features), far(diag_inverse)))
 
         def send(n):
@@ -511,31 +526,6 @@
             return lax.ppermute(blocks_out[n], "col", pairs_of)
 
         got_blocks = [send(n) for n in range(early)]
-        slices, pairs, *got_blocks = lax.optimization_barrier((slices, pairs, *got_blocks))
-
-    far_slots = len(far_chips) * CHUNK
-    with jax.named_scope("covariance"):
-        partial = pl.pallas_call(
-            functools.partial(covariance_kernel, far_chips, col_count),
-            in_specs=[SMEM, SMEM, SMEM, HBM, HBM],
-            out_specs=VMEM,
-            out_shape=pltpu.HBM((row_count, far_slots, group, size), F32),
-            scratch_shapes=[
-                pltpu.VMEM(slices.shape, BF),
-                pltpu.VMEM((row_count, columns, samples, size), BF),
-                pltpu.VMEM((far_slots * group, samples), F32),
-                sems(len(far_chips)),
-                sems(row_count, columns),
-            ],
-            compiler_params=PARAMS,
-        )(rows_here, lists_here, owned_here, far(slices), far(features))
-        covariance = lax.all_to_all(partial, "row", split_axis=0, concat_axis=0, tiled=True)
-
-    with jax.named_scope("near"):
-        blocks_out[early:], got_blocks, _ = lax.optimization_barrier(
-            (blocks_out[early:], got_blocks, partial[0, 0])
-        )
-        got_blocks = got_blocks + [send(n) for n in range(early, len(steps))]
         base, d, near_sums = pl.pallas_call(
             functools.partial(near_kernel, near, col_count),
             in_specs=[SMEM, SMEM, SMEM] + [HBM] * (3 + near_count),
@@ -552,9 +542,31 @@
             my_list, live, my_owned, far(features), far(theta), far(tiles),
             *[far(block) for block in got_blocks[:near_count]],
         )
-        covariance, got_blocks, base, d, near_sums = lax.optimization_barrier(
-            (covariance, got_blocks, base, d, near_sums)
-        )
+        slices, pairs, got_blocks, base, d, near_sums = lax.optimization_barrier(
+            (slices, pairs, got_blocks, base, d, near_sums)
+        )
+
+    far_slots = len(far_chips) * CHUNK
+    with jax.named_scope("covariance"):
+        partial = pl.pallas_call(
+            functools.partial(covariance_kernel, far_chips, col_count),
+            in_specs=[SMEM, SMEM, SMEM, HBM, HBM],
+            out_specs=VMEM,
+            out_shape=pltpu.HBM((row_count, far_slots, group, size), F32),
+            scratch_shapes=[
+                pltpu.VMEM(slices.shape, BF),
+                pltpu.VMEM((row_count, columns, samples, size), BF),
+                sems(len(far_chips)),
+                sems(row_count, columns),
+            ],
+            compiler_params=PARAMS,
+        )(rows_here, lists_here, owned_here, far(slices), far(features))
+        covariance = lax.all_to_all(partial, "row", split_axis=0, concat_axis=0, tiled=True)
+
+    with jax.named_scope("diag"):
+        blocks_out[early:], _ = lax.optimization_barrier((blocks_out[early:], partial[0, 0]))
+        got_blocks = got_blocks + [send(n) for n in range(early, len(steps))]
+        covariance, got_blocks = lax.optimization_barrier((covariance, got_blocks))
 
     with jax.named_scope("first"):
         base, d, pieces = pl.pallas_call(

time: 286 us -> 223 us (0.78)
  Pallas kernels: 158 us -> 80.9 us
  starting transfers between devices: 53.3 us -> 61.9 us
  waiting for transfers between devices: 23.1 us -> 28.9 us
    pallas_call x1, Pallas kernels: 81.9 us -> 4.8 us  [body(): pl.pallas_call(functools.partial(gather_kernel, steps), in_specs=[SMEM, H...]
    ppermute x15, starting transfers between devices: 28.7 us -> 36.1 us  [send(): return lax.ppermute(blocks_out[n], 'col', pairs_of)]
    all_gather x1, waiting for transfers between devices: 0.01 us -> 3.62 us  [body(): slices = lax.all_gather(mine, 'col', axis=0, tiled=True)]
  transfers between devices with their start and end apart: 21 -> 21, of which waited for: 10 -> 11; matrix products, arithmetic and copies ran while one was open for 3% -> 3% of each run, Pallas kernels for 41% -> 17%
where the time goes in v4:
time: 223 us; the launch traced here: 221 us
  Pallas kernels  80.9 us (36%)
  starting transfers between devices  61.9 us (28%)
  waiting for transfers between devices  28.9 us (13%)
  blocking collectives  28.4 us (13%)
  between operations  13.9 us (6%)
  local copies, waits for them, and re-layouts  6.05 us (3%)
    ppermute x15, starting transfers between devices, send(): return lax.ppermute(blocks_out[n], 'col', pairs_of)  36.1 us
    all_to_all x2, blocking collectives, body(): got = lax.all_to_all(pieces, 'row', split_axis=0, concat_axis=0, tiled=True)  28.4 us
    pallas_call x3, Pallas kernels, body(): pl.pallas_call(functools.partial(diagonal_kernel, steps), in_specs=[SMEM,...  21.5 us
    pallas_call x3, Pallas kernels, body(): pl.pallas_call(functools.partial(sweep_kernel, last), in_specs=[SMEM, SME...  19.8 us
    ppermute x15, waiting for transfers between devices, send(): return lax.ppermute(blocks_out[n], 'col', pairs_of)  15 us
    all_to_all x3, starting transfers between devices, body(): lax.all_to_all(summed.reshape(piece_shape), 'row', split_axis=0, concat_a...  10.5 us
    pallas_call x1, Pallas kernels, body(): pl.pallas_call(functools.partial(covariance_kernel, far_chips, col_count)...  8.67 us
    pallas_call x1, Pallas kernels, body(): pl.pallas_call(functools.partial(near_kernel, near, col_count), in_specs=...  8.35 us
  transfers between devices with their start and end apart: 21, of which 11 were waited for; matrix products, arithmetic and copies ran while one was open for 3% of the time, Pallas kernels for 17%

profile of v4, /device:TPU:32, one launch (start us, length us, event | category | flops | bytes accessed | tf_op | source)
XLA Modules:
  0.0 221.4 jit_solution(3819312036429665059)
XLA Ops:
  6.5 4.5 %slices.1 = bf16[32,8,512]{2,1,0:T(8,128)(2,1)} custom-call(bf16[32,512,128]{2,1,0:T(8,128)(2,1)} %features.5), custom_call_target="tpu_custom_call" | custom-call | tf_op jit(solution)/shard_map/slices/pallas_call | solution.py:449
  11.1 0.0 all-gather.2.cloned.1.call-update
  11.1 0.8 dynamic-slice_subtract_fusion.1
  11.9 0.1 copy.28
  12.0 0.1 copy.25.wanted_ref
  12.1 4.8 %blocks.2 = (bf16[2,640,128]{2,1,0:T(8,128)(2,1)}, bf16[2,640,128]{2,1,0:T(8,128)(2,1)}, bf16[2,640,128]{2,1,0:T(8,128)(2,1)}, bf16[2,640,128]{2,1,0:T(8,128)(2,...) custom-call(s32[16,2]{1,0:T(8,128)S(1)} %copy.25.wanted_ref, ...), custom_call_target="tpu_custom_call" | custom-call | tf_op jit(solution)/shard_map/blocks/pallas_call | solution.py:504
  16.9 0.1 collective-permute-start
  17.0 1.8 collective-permute-start.1
  18.8 3.9 %collective-permute-start.2 = (bf16[2,640,128]{2,1,0:T(8,128)(2,1)}, bf16[2,640,128]{2,1,0:T(8,128)(2,1)S(1)}, u32[]{:S(2)}, u32[]{:S(2)}) collective-permute-start(bf16[2,640,128]{2,1,0:T(8,128)(2,1)} %get-tuple-element.74), channel_id=1, source_target_pairs={{0,15},{1,14},{2,1},{3,0},{4,3},{5,2},{6,5},{7,4},{8,7},{9,6},{10,... | collective-permute-start | bytes 983048 | tf_op jit(solution)/shard_map/blocks/ppermute | solution.py:526
  22.7 0.0 collective-permute-start.4
  22.7 0.4 fusion.3
  23.1 0.1 fusion.owned_ref
  23.3 0.1 copy.23
  23.4 1.3 dynamic_slice.26
  24.7 3.9 %split.1.far_pairs = bf16[32,128,256]{2,1,0:T(8,128)(2,1)} custom-call(f32[32,128,128]{2,1,0:T(8,128)} %bitcast.30), custom_call_target="tpu_custom_call" | custom-call | tf_op jit(solution)/shard_map/split/pallas_call | solution.py:481
  28.6 0.1 copy.26.owned_ref
  28.7 0.9 constant_dynamic-slice_fusion.1
  29.6 4.5 %collective-permute-start.5 = (bf16[2,128,128]{2,1,0:T(8,128)(2,1)S(1)}, bf16[2,128,128]{2,1,0:T(8,128)(2,1)S(1)}, u32[]{:S(2)}, u32[]{:S(2)}) collective-permute-start(bf16[2,128,128]{2,1,0:T(8,128)(2,1)S(1)} %copy-done.25), channel_id=1, source_target_pairs={{0,12},{1,13},{2,14},{3,15},{4,0},{5,1},{6,2},{7,3},{8,4},{9,5},{1... | collective-permute-start | bytes 196616 | tf_op jit(solution)/shard_map/blocks/ppermute | solution.py:526
  34.0 0.0 collective-permute-done.1.rest_2_
  34.1 3.2 %collective-permute-start.6 = (bf16[2,128,128]{2,1,0:T(8,128)(2,1)S(1)}, bf16[2,128,128]{2,1,0:T(8,128)(2,1)S(1)}, u32[]{:S(2)}, u32[]{:S(2)}) collective-permute-start(bf16[2,128,128]{2,1,0:T(8,128)(2,1)S(1)} %copy-done.24), channel_id=1, source_target_pairs={{0,13},{1,12},{2,15},{3,14},{4,1},{5,0},{6,3},{7,2},{8,5},{9,4},{1... | collective-permute-start | bytes 196616 | tf_op jit(solution)/shard_map/blocks/ppermute | solution.py:526
  37.3 6.3 %collective-permute-done.2.rest_3_ = bf16[2,640,128]{2,1,0:T(8,128)(2,1)S(1)} collective-permute-done((bf16[2,640,128]{2,1,0:T(8,128)(2,1)}, bf16[2,640,128]{2,1,0:T(8,128)(2,1)S(1)}, u32[]{:S(2)}, u32[]{:S(2)}) %collective-permute-start.2) | collective-permute-done | bytes 327712 | tf_op jit(solution)/shard_map/blocks/ppermute | solution.py:526
  43.6 2.7 %collective-permute-start.7 = (bf16[2,128,128]{2,1,0:T(8,128)(2,1)S(1)}, bf16[2,128,128]{2,1,0:T(8,128)(2,1)S(1)}, u32[]{:S(2)}, u32[]{:S(2)}) collective-permute-start(bf16[2,128,128]{2,1,0:T(8,128)(2,1)S(1)} %copy-done.23), channel_id=1, source_target_pairs={{0,4},{1,5},{2,6},{3,7},{4,8},{5,9},{6,10},{7,11},{8,12},{9,13},{1... | collective-permute-start | bytes 196616 | tf_op jit(solution)/shard_map/blocks/ppermute | solution.py:526
  46.3 5.7 %collective-permute-start.8 = (bf16[2,128,128]{2,1,0:T(8,128)(2,1)S(1)}, bf16[2,128,128]{2,1,0:T(8,128)(2,1)S(1)}, u32[]{:S(2)}, u32[]{:S(2)}) collective-permute-start(bf16[2,128,128]{2,1,0:T(8,128)(2,1)S(1)} %copy-done.22), channel_id=1, source_target_pairs={{0,5},{1,4},{2,7},{3,6},{4,9},{5,8},{6,11},{7,10},{8,13},{9,12},{1... | collective-permute-start | bytes 196616 | tf_op jit(solution)/shard_map/blocks/ppermute | solution.py:526
  51.9 0.7 fusion.1.list_ref
  52.7 0.7 copy-done.4
  53.4 8.3 %blocks.3 = (f32[32,128,128]{2,1,0:T(8,128)}, f32[32,128,128]{2,1,0:T(8,128)}, f32[2,128,256]{2,1,0:T(8,128)}) custom-call(s32[32]{0:T(128)S(1)} %fusion.1.list_ref, s32[1]{0:T(128)} %bitcast.1.live_ref, s32[2]{0:T(128)S(1)} %fusion.owned_ref, bf16[32,512,128]{2,1,0:T(8,128)(2,1)} %features.5, f32[32,128,128]{2,1,0:T(8,128)} %bitcast.25, ...), custom_call_target="tpu_custom_call" | custom-call | tf_op jit(solution)/shard_map/blocks/pallas_call | solution.py:529
  61.8 2.7 %collective-permute-done.8.rest_9_ = bf16[2,128,128]{2,1,0:T(8,128)(2,1)S(1)} collective-permute-done((bf16[2,128,128]{2,1,0:T(8,128)(2,1)S(1)}, bf16[2,128,128]{2,1,0:T(8,128)(2,1)S(1)}, u32[]{:S(2)}, u32[]{:S(2)}) %collective-permute-start.8) | collective-permute-done | bytes 65568 | tf_op jit(solution)/shard_map/blocks/ppermute | solution.py:526
  64.4 3.6 %all-gather.2.cloned.1.call-done.far_slices = bf16[512,8,512]{2,1,0:T(8,128)(2,1)} async-done(((bf16[32,8,512]{2,1,0:T(8,128)(2,1)}), bf16[512,8,512]{2,1,0:T(8,128)(2,1)}) %all-gather.2.cloned.1.call-update) | async-done | bytes 4194320 | tf_op jit(solution)/shard_map/slices/all_gather | solution.py:456
  68.1 8.7 %covariance.1 = f32[16,20,8,128]{3,2,1,0:T(8,128)} custom-call(s32[16,32]{1,0:T(8,128)S(1)} %bitcast.24, s32[16,32]{1,0:T(8,128)S(1)} %bitcast.23, s32[16,2]{1,0:T(8,128)S(1)} %copy.26.owned_ref, bf16[512,8,512]{2,1,0:T(8,128)(2,1)} %all-gather.2.cloned.1.call-done.far_slices, bf16[32,512,128]{2,1,0:T(8,128)(2,1)} %features.5), custom_call_target="tpu_custom_call" | custom-call | tf_op jit(solution)/shard_map/covariance/pallas_call | solution.py:551
  76.8 7.8 %all-to-all-start = ((f32[16,20,8,128]{3,2,1,0:T(8,128)}), f32[16,20,8,128]{3,2,1,0:T(8,128)S(1)}, u32[]{:S(2)}, u32[]{:S(2)}) async-start(f32[16,20,8,128]{3,2,1,0:T(8,128)} %covariance.1), calls=%async_computation | async-start | bytes 2621440 | tf_op jit(solution)/shard_map/covariance/all_to_all | solution.py:564
  84.6 0.6 collective-permute-start.10
  85.2 1.9 collective-permute-start.11
  87.1 3.9 %collective-permute-start.12 = (bf16[2,128,128]{2,1,0:T(8,128)(2,1)S(1)}, bf16[2,128,128]{2,1,0:T(8,128)(2,1)S(1)}, u32[]{:S(2)}, u32[]{:S(2)}) collective-permute-start(bf16[2,128,128]{2,1,0:T(8,128)(2,1)S(1)} %copy-done.19), channel_id=1, source_target_pairs={{0,9},{1,8},{2,11},{3,10},{4,13},{5,12},{6,15},{7,14},{8,1},{9,0},... | collective-permute-start | bytes 196616 | tf_op jit(solution)/shard_map/diag/ppermute | solution.py:526
  91.0 4.1 %collective-permute-start.13 = (bf16[2,128,128]{2,1,0:T(8,128)(2,1)S(1)}, bf16[2,128,128]{2,1,0:T(8,128)(2,1)S(1)}, u32[]{:S(2)}, u32[]{:S(2)}) collective-permute-start(bf16[2,128,128]{2,1,0:T(8,128)(2,1)S(1)} %copy-done.18), channel_id=1, source_target_pairs={{0,6},{1,7},{2,8},{3,9},{4,10},{5,11},{6,12},{7,13},{8,14},{9,15},... | collective-permute-start | bytes 196616 | tf_op jit(solution)/shard_map/diag/ppermute | solution.py:526
  95.1 0.2 collective-permute-start.14
  95.3 0.1 sub.25
  95.4 0.1 compare_convert_fusion.same_ref
  95.4 0.9 collective-permute-done.10.rest_11_
  96.3 3.7 %collective-permute-start.9 = (bf16[2,128,128]{2,1,0:T(8,128)(2,1)S(1)}, bf16[2,128,128]{2,1,0:T(8,128)(2,1)S(1)}, u32[]{:S(2)}, u32[]{:S(2)}) collective-permute-start(bf16[2,128,128]{2,1,0:T(8,128)(2,1)S(1)} %copy-done.16), channel_id=1, source_target_pairs={{0,10},{1,11},{2,12},{3,13},{4,14},{5,15},{6,0},{7,1},{8,2},{9,3},... | collective-permute-start | bytes 196616 | tf_op jit(solution)/shard_map/diag/ppermute | solution.py:526
  100.0 1.8 gather_fusion
  101.8 0.5 collective-permute-done.13.rest_14_
  102.3 3.5 %collective-permute-done.14.rest_15_ = bf16[2,128,128]{2,1,0:T(8,128)(2,1)S(1)} collective-permute-done((bf16[2,128,128]{2,1,0:T(8,128)(2,1)S(1)}, bf16[2,128,128]{2,1,0:T(8,128)(2,1)S(1)}, u32[]{:S(2)}, u32[]{:S(2)}) %collective-permute-start.14) | collective-permute-done | bytes 65568 | tf_op jit(solution)/shard_map/diag/ppermute | solution.py:526
  105.8 1.1 collective-permute-done.9.rest_10_
  107.0 5.5 %first.1 = (f32[32,128,128]{2,1,0:T(8,128)}, f32[32,128,128]{2,1,0:T(8,128)}, f32[16,2,8,128]{3,2,1,0:T(8,128)}) custom-call(s32[32]{0:T(128)S(1)} %fusion.1.list_ref, s32[1]{0:T(128)} %bitcast.1.live_ref, f32[16,20,8,128]{3,2,1,0:T(8,128)S(1)} %all-to-all-done.cov_ref, ...), custom_call_target="tpu_custom_call", output_to_operand_aliasing={{0}: (6, {}), {1}: (7, {})} | custom-call | tf_op jit(solution)/shard_map/first/pallas_call | solution.py:572
  112.5 7.4 %all-to-all-start.1 = ((f32[16,2,8,128]{3,2,1,0:T(8,128)}), f32[16,2,8,128]{3,2,1,0:T(8,128)S(1)}, u32[]{:S(2)}, u32[]{:S(2)}) async-start(f32[16,2,8,128]{3,2,1,0:T(8,128)} %get-tuple-element.130), calls=%async_computation.1 | async-start | bytes 262144 | tf_op jit(solution)/shard_map/exchange/all_to_all | solution.py:589
  119.9 8.0 %all-to-all-done.1 = f32[16,2,8,128]{3,2,1,0:T(8,128)S(1)} async-done(((f32[16,2,8,128]{3,2,1,0:T(8,128)}), f32[16,2,8,128]{3,2,1,0:T(8,128)S(1)}, u32[]{:S(2)}, u32[]{:S(2)}) %all-to-all-start.1) | async-done | bytes 131104 | tf_op jit(solution)/shard_map/exchange/all_to_all | solution.py:589
  127.9 1.3 exchange.3
  129.2 3.5 %all-to-all-start.2 = ((f32[16,2,8,128]{3,2,1,0:T(8,128)}), f32[16,2,8,128]{3,2,1,0:T(8,128)S(1)}, u32[]{:S(2)}, u32[]{:S(2)}) async-start(f32[16,2,8,128]{3,2,1,0:T(8,128)} %bitcast.10), calls=%async_computation.2 | async-start | bytes 262144 | tf_op jit(solution)/shard_map/exchange/all_to_all | solution.py:598
  132.8 0.1 broadcast_select_fusion.col_diag_ref
  132.8 7.2 %diagonal.3.far_t = f32[32,128,128]{2,1,0:T(8,128)} custom-call(s32[32]{0:T(128)S(1)} %fusion.1.list_ref, f32[32,128,128]{2,1,0:T(8,128)} %get-tuple-element.111.far_base, f32[32,128,128]{2,1,0:T(8,128)} %get-tuple-element.112.far_d, bf16[2,128,128]{2,1,0:T(8,128)(2,1)S(1)} %broadcast_select_fusion.col_diag_ref, ...), custom_call_target="tpu_custom_call" | custom-call | tf_op jit(solution)/shard_map/diagonal/pallas_call | solution.py:602
  140.0 0.7 all-to-all-done.2.q_ref
  140.7 7.1 %sweep.3 = (f32[32,128,128]{2,1,0:T(8,128)}, f32[16,2,8,128]{3,2,1,0:T(8,128)S(1)}) custom-call(s32[32]{0:T(128)S(1)} %fusion.1.list_ref, s32[1]{0:T(128)} %bitcast.1.live_ref, f32[32,128,128]{2,1,0:T(8,128)} %diagonal.3.far_t, f32[32,128,128]{2,1,0:T(8,128)} %bitcast.27, bf16[32,128,256]{2,1,0:T(8,128)(2,1)} %split.1.far_pairs, ...), custom_call_target="tpu_custom_call" | custom-call | tf_op jit(solution)/shard_map/sweep/pallas_call | solution.py:614
  147.8 14.2 %all_to_all.35 = f32[16,2,8,128]{3,2,1,0:T(8,128)S(1)} all-to-all(f32[16,2,8,128]{3,2,1,0:T(8,128)S(1)} %get-tuple-element.132), channel_id=1, replica_groups=mesh['row'=16,'col'=16] {'row'}, dimensions={0} | all-to-all | bytes 262144 | tf_op jit(solution)/shard_map/exchange/all_to_all | solution.py:589
  162.1 1.3 exchange.4
  163.4 3.5 %all-to-all-start.4 = ((f32[16,2,8,128]{3,2,1,0:T(8,128)}), f32[16,2,8,128]{3,2,1,0:T(8,128)S(1)}, u32[]{:S(2)}, u32[]{:S(2)}) async-start(f32[16,2,8,128]{3,2,1,0:T(8,128)} %bitcast.12), calls=%async_computation.4 | async-start | bytes 262144 | tf_op jit(solution)/shard_map/exchange/all_to_all | solution.py:598
  166.9 7.2 %diagonal.4.far_t = f32[32,128,128]{2,1,0:T(8,128)} custom-call(s32[32]{0:T(128)S(1)} %fusion.1.list_ref, f32[32,128,128]{2,1,0:T(8,128)} %get-tuple-element.111.far_base, f32[32,128,128]{2,1,0:T(8,128)} %get-tuple-element.131.far_d, bf16[2,128,128]{2,1,0:T(8,128)(2,1)S(1)} %broadcast_select_fusion.col_diag_ref, ...), custom_call_target="tpu_custom_call" | custom-call | tf_op jit(solution)/shard_map/diagonal/pallas_call | solution.py:602
  174.1 0.8 all-to-all-done.4.q_ref
  174.9 7.1 %sweep.4 = (f32[32,128,128]{2,1,0:T(8,128)}, f32[16,2,8,128]{3,2,1,0:T(8,128)S(1)}) custom-call(s32[32]{0:T(128)S(1)} %fusion.1.list_ref, s32[1]{0:T(128)} %bitcast.1.live_ref, f32[32,128,128]{2,1,0:T(8,128)} %diagonal.4.far_t, f32[32,128,128]{2,1,0:T(8,128)} %bitcast.28, bf16[32,128,256]{2,1,0:T(8,128)(2,1)} %split.1.far_pairs, ...), custom_call_target="tpu_custom_call" | custom-call | tf_op jit(solution)/shard_map/sweep/pallas_call | solution.py:614
  182.0 14.2 %all_to_all.36 = f32[16,2,8,128]{3,2,1,0:T(8,128)S(1)} all-to-all(f32[16,2,8,128]{3,2,1,0:T(8,128)S(1)} %get-tuple-element.134), channel_id=1, replica_groups=mesh['row'=16,'col'=16] {'row'}, dimensions={0} | all-to-all | bytes 262144 | tf_op jit(solution)/shard_map/exchange/all_to_all | solution.py:589
  196.1 1.3 exchange.5
  197.4 3.5 %all-to-all-start.6 = ((f32[16,2,8,128]{3,2,1,0:T(8,128)}), f32[16,2,8,128]{3,2,1,0:T(8,128)S(1)}, u32[]{:S(2)}, u32[]{:S(2)}) async-start(f32[16,2,8,128]{3,2,1,0:T(8,128)} %bitcast.14), calls=%async_computation.6 | async-start | bytes 262144 | tf_op jit(solution)/shard_map/exchange/all_to_all | solution.py:598
  201.0 7.2 %diagonal.5.far_t = f32[32,128,128]{2,1,0:T(8,128)} custom-call(s32[32]{0:T(128)S(1)} %fusion.1.list_ref, f32[32,128,128]{2,1,0:T(8,128)} %get-tuple-element.111.far_base, f32[32,128,128]{2,1,0:T(8,128)} %get-tuple-element.133.far_d, bf16[2,128,128]{2,1,0:T(8,128)(2,1)S(1)} %broadcast_select_fusion.col_diag_ref, ...), custom_call_target="tpu_custom_call" | custom-call | tf_op jit(solution)/shard_map/diagonal/pallas_call | solution.py:602
  208.1 0.8 all-to-all-done.6.q_ref
  208.9 5.6 %sweep.5 = f32[32,128,128]{2,1,0:T(8,128)} custom-call(s32[32]{0:T(128)S(1)} %fusion.1.list_ref, s32[1]{0:T(128)} %bitcast.1.live_ref, f32[32,128,128]{2,1,0:T(8,128)} %diagonal.5.far_t, f32[32,128,128]{2,1,0:T(8,128)} %bitcast.29, bf16[32,128,256]{2,1,0:T(8,128)(2,1)} %split.1.far_pairs, f32[16,2,8,128]{3,2,1,0:T(8,128)S(1)} %all-to-all-done.6.q_ref), custom_call_target="tpu_custom_call" | custom-call | tf_op jit(solution)/shard_map/sweep/pallas_call | solution.py:614
  (65 shorter events, 0.1 us)
Async XLA Ops:
  6.5 61.5 %all-gather.2.cloned.1.call-start = ((), (), s32[]{:S(2)}) async-start(), calls=%async_computation.7 | async-start | bytes 4456448 | tf_op jit(solution)/shard_map/slices/all_gather | solution.py:456
  12.0 10.7 %copy-start.15 = (s32[16,16,2]{1,2,0:T(2,128)S(1)}, s32[16,16,2]{1,2,0:T(2,128)}, u32[]{:S(2)}) copy-start(s32[16,16,2]{1,2,0:T(2,128)} %param.14) | copy-start | bytes 6148
  16.9 12.7 %collective-permute-start = (bf16[2,640,128]{2,1,0:T(8,128)(2,1)}, bf16[2,640,128]{2,1,0:T(8,128)(2,1)S(1)}, u32[]{:S(2)}, u32[]{:S(2)}) collective-permute-start(bf16[2,640,128]{2,1,0:T(8,128)(2,1)} %get-tuple-element.72), channel_id=1, source_target_pairs={{0,1},{1,0},{2,3},{3,2},{4,5},{5,4},{6,7},{7,6},{8,9},{9,8},{10,11... | collective-permute-start | bytes 983048 | tf_op jit(solution)/shard_map/blocks/ppermute | solution.py:526
  17.0 17.1 %collective-permute-start.1 = (bf16[2,640,128]{2,1,0:T(8,128)(2,1)}, bf16[2,640,128]{2,1,0:T(8,128)(2,1)S(1)}, u32[]{:S(2)}, u32[]{:S(2)}) collective-permute-start(bf16[2,640,128]{2,1,0:T(8,128)(2,1)} %get-tuple-element.73), channel_id=1, source_target_pairs={{0,14},{1,15},{2,0},{3,1},{4,2},{5,3},{6,4},{7,5},{8,6},{9,7},{10,... | collective-permute-start | bytes 983048 | tf_op jit(solution)/shard_map/blocks/ppermute | solution.py:526
  18.8 24.8 %collective-permute-start.2 = (bf16[2,640,128]{2,1,0:T(8,128)(2,1)}, bf16[2,640,128]{2,1,0:T(8,128)(2,1)S(1)}, u32[]{:S(2)}, u32[]{:S(2)}) collective-permute-start(bf16[2,640,128]{2,1,0:T(8,128)(2,1)} %get-tuple-element.74), channel_id=1, source_target_pairs={{0,15},{1,14},{2,1},{3,0},{4,3},{5,2},{6,5},{7,4},{8,7},{9,6},{10,... | collective-permute-start | bytes 983048 | tf_op jit(solution)/shard_map/blocks/ppermute | solution.py:526
  22.7 23.6 %collective-permute-start.3 = (bf16[2,640,128]{2,1,0:T(8,128)(2,1)}, bf16[2,640,128]{2,1,0:T(8,128)(2,1)S(1)}, u32[]{:S(2)}, u32[]{:S(2)}) collective-permute-start(bf16[2,640,128]{2,1,0:T(8,128)(2,1)} %get-tuple-element.75), channel_id=1, source_target_pairs={{0,2},{1,3},{2,4},{3,5},{4,6},{5,7},{6,8},{7,9},{8,10},{9,11},{10,... | collective-permute-start | bytes 983048 | tf_op jit(solution)/shard_map/blocks/ppermute | solution.py:526
  22.7 29.9 %collective-permute-start.4 = (bf16[2,640,128]{2,1,0:T(8,128)(2,1)}, bf16[2,640,128]{2,1,0:T(8,128)(2,1)S(1)}, u32[]{:S(2)}, u32[]{:S(2)}) collective-permute-start(bf16[2,640,128]{2,1,0:T(8,128)(2,1)} %get-tuple-element.76), channel_id=1, source_target_pairs={{0,3},{1,2},{2,5},{3,4},{4,7},{5,6},{6,9},{7,8},{8,11},{9,10},{10,... | collective-permute-start | bytes 983048 | tf_op jit(solution)/shard_map/blocks/ppermute | solution.py:526
  24.7 4.9 %copy-start.25 = (bf16[2,128,128]{2,1,0:T(8,128)(2,1)S(1)}, bf16[2,128,128]{2,1,0:T(8,128)(2,1)}, u32[]{:S(2)}) copy-start(bf16[2,128,128]{2,1,0:T(8,128)(2,1)} %get-tuple-element.77) | copy-start | bytes 196612
  24.7 9.4 %copy-start.24 = (bf16[2,128,128]{2,1,0:T(8,128)(2,1)S(1)}, bf16[2,128,128]{2,1,0:T(8,128)(2,1)}, u32[]{:S(2)}) copy-start(bf16[2,128,128]{2,1,0:T(8,128)(2,1)} %get-tuple-element.78) | copy-start | bytes 196612
  24.7 18.9 %copy-start.23 = (bf16[2,128,128]{2,1,0:T(8,128)(2,1)S(1)}, bf16[2,128,128]{2,1,0:T(8,128)(2,1)}, u32[]{:S(2)}) copy-start(bf16[2,128,128]{2,1,0:T(8,128)(2,1)} %get-tuple-element.79) | copy-start | bytes 196612
  24.7 21.6 %copy-start.22 = (bf16[2,128,128]{2,1,0:T(8,128)(2,1)S(1)}, bf16[2,128,128]{2,1,0:T(8,128)(2,1)}, u32[]{:S(2)}) copy-start(bf16[2,128,128]{2,1,0:T(8,128)(2,1)} %get-tuple-element.80) | copy-start | bytes 196612
  29.6 23.0 %copy-start = (bf16[2,640,128]{2,1,0:T(8,128)(2,1)}, bf16[2,640,128]{2,1,0:T(8,128)(2,1)S(1)}, u32[]{:S(2)}) copy-start(bf16[2,640,128]{2,1,0:T(8,128)(2,1)S(1)} %collective-permute-done.rest_1_) | copy-start | bytes 983044
  29.6 32.1 %collective-permute-start.5 = (bf16[2,128,128]{2,1,0:T(8,128)(2,1)S(1)}, bf16[2,128,128]{2,1,0:T(8,128)(2,1)S(1)}, u32[]{:S(2)}, u32[]{:S(2)}) collective-permute-start(bf16[2,128,128]{2,1,0:T(8,128)(2,1)S(1)} %copy-done.25), channel_id=1, source_target_pairs={{0,12},{1,13},{2,14},{3,15},{4,0},{5,1},{6,2},{7,3},{8,4},{9,5},{1... | collective-permute-start | bytes 196616 | tf_op jit(solution)/shard_map/blocks/ppermute | solution.py:526
  34.1 18.6 %copy-start.1 = (bf16[2,640,128]{2,1,0:T(8,128)(2,1)}, bf16[2,640,128]{2,1,0:T(8,128)(2,1)S(1)}, u32[]{:S(2)}) copy-start(bf16[2,640,128]{2,1,0:T(8,128)(2,1)S(1)} %collective-permute-done.1.rest_2_) | copy-start | bytes 983044
  34.1 27.7 %collective-permute-start.6 = (bf16[2,128,128]{2,1,0:T(8,128)(2,1)S(1)}, bf16[2,128,128]{2,1,0:T(8,128)(2,1)S(1)}, u32[]{:S(2)}, u32[]{:S(2)}) collective-permute-start(bf16[2,128,128]{2,1,0:T(8,128)(2,1)S(1)} %copy-done.24), channel_id=1, source_target_pairs={{0,13},{1,12},{2,15},{3,14},{4,1},{5,0},{6,3},{7,2},{8,5},{9,4},{1... | collective-permute-start | bytes 196616 | tf_op jit(solution)/shard_map/blocks/ppermute | solution.py:526
  43.6 9.0 %copy-start.2 = (bf16[2,640,128]{2,1,0:T(8,128)(2,1)}, bf16[2,640,128]{2,1,0:T(8,128)(2,1)S(1)}, u32[]{:S(2)}) copy-start(bf16[2,640,128]{2,1,0:T(8,128)(2,1)S(1)} %collective-permute-done.2.rest_3_) | copy-start | bytes 983044
  43.6 18.2 %collective-permute-start.7 = (bf16[2,128,128]{2,1,0:T(8,128)(2,1)S(1)}, bf16[2,128,128]{2,1,0:T(8,128)(2,1)S(1)}, u32[]{:S(2)}, u32[]{:S(2)}) collective-permute-start(bf16[2,128,128]{2,1,0:T(8,128)(2,1)S(1)} %copy-done.23), channel_id=1, source_target_pairs={{0,4},{1,5},{2,6},{3,7},{4,8},{5,9},{6,10},{7,11},{8,12},{9,13},{1... | collective-permute-start | bytes 196616 | tf_op jit(solution)/shard_map/blocks/ppermute | solution.py:526
  46.3 6.4 %copy-start.3 = (bf16[2,640,128]{2,1,0:T(8,128)(2,1)}, bf16[2,640,128]{2,1,0:T(8,128)(2,1)S(1)}, u32[]{:S(2)}) copy-start(bf16[2,640,128]{2,1,0:T(8,128)(2,1)S(1)} %collective-permute-done.3.rest_4_) | copy-start | bytes 983044
  46.3 18.2 %collective-permute-start.8 = (bf16[2,128,128]{2,1,0:T(8,128)(2,1)S(1)}, bf16[2,128,128]{2,1,0:T(8,128)(2,1)S(1)}, u32[]{:S(2)}, u32[]{:S(2)}) collective-permute-start(bf16[2,128,128]{2,1,0:T(8,128)(2,1)S(1)} %copy-done.22), channel_id=1, source_target_pairs={{0,5},{1,4},{2,7},{3,6},{4,9},{5,8},{6,11},{7,10},{8,13},{9,12},{1... | collective-permute-start | bytes 196616 | tf_op jit(solution)/shard_map/blocks/ppermute | solution.py:526
  52.6 0.7 copy-start.4
  61.7 15.0 %copy-start.5 = (bf16[2,128,128]{2,1,0:T(8,128)(2,1)}, bf16[2,128,128]{2,1,0:T(8,128)(2,1)S(1)}, u32[]{:S(2)}) copy-start(bf16[2,128,128]{2,1,0:T(8,128)(2,1)S(1)} %collective-permute-done.5.rest_6_) | copy-start | bytes 196612
  61.7 15.0 %copy-start.6 = (bf16[2,128,128]{2,1,0:T(8,128)(2,1)}, bf16[2,128,128]{2,1,0:T(8,128)(2,1)S(1)}, u32[]{:S(2)}) copy-start(bf16[2,128,128]{2,1,0:T(8,128)(2,1)S(1)} %collective-permute-done.6.rest_7_) | copy-start | bytes 196612
  61.8 15.0 %copy-start.7 = (bf16[2,128,128]{2,1,0:T(8,128)(2,1)}, bf16[2,128,128]{2,1,0:T(8,128)(2,1)S(1)}, u32[]{:S(2)}) copy-start(bf16[2,128,128]{2,1,0:T(8,128)(2,1)S(1)} %collective-permute-done.7.rest_8_) | copy-start | bytes 196612
  64.4 12.3 %copy-start.8 = (bf16[2,128,128]{2,1,0:T(8,128)(2,1)}, bf16[2,128,128]{2,1,0:T(8,128)(2,1)S(1)}, u32[]{:S(2)}) copy-start(bf16[2,128,128]{2,1,0:T(8,128)(2,1)S(1)} %collective-permute-done.8.rest_9_) | copy-start | bytes 196612
  76.8 7.8 %copy-start.21 = (bf16[2,128,128]{2,1,0:T(8,128)(2,1)S(1)}, bf16[2,128,128]{2,1,0:T(8,128)(2,1)}, u32[]{:S(2)}) copy-start(bf16[2,128,128]{2,1,0:T(8,128)(2,1)} %get-tuple-element.102) | copy-start | bytes 196612
  76.8 8.4 %copy-start.20 = (bf16[2,128,128]{2,1,0:T(8,128)(2,1)S(1)}, bf16[2,128,128]{2,1,0:T(8,128)(2,1)}, u32[]{:S(2)}) copy-start(bf16[2,128,128]{2,1,0:T(8,128)(2,1)} %get-tuple-element.103) | copy-start | bytes 196612
  76.8 10.3 %copy-start.19 = (bf16[2,128,128]{2,1,0:T(8,128)(2,1)S(1)}, bf16[2,128,128]{2,1,0:T(8,128)(2,1)}, u32[]{:S(2)}) copy-start(bf16[2,128,128]{2,1,0:T(8,128)(2,1)} %get-tuple-element.104) | copy-start | bytes 196612
  76.8 14.2 %copy-start.18 = (bf16[2,128,128]{2,1,0:T(8,128)(2,1)S(1)}, bf16[2,128,128]{2,1,0:T(8,128)(2,1)}, u32[]{:S(2)}) copy-start(bf16[2,128,128]{2,1,0:T(8,128)(2,1)} %get-tuple-element.105) | copy-start | bytes 196612
  76.8 18.3 %copy-start.17 = (bf16[2,128,128]{2,1,0:T(8,128)(2,1)S(1)}, bf16[2,128,128]{2,1,0:T(8,128)(2,1)}, u32[]{:S(2)}) copy-start(bf16[2,128,128]{2,1,0:T(8,128)(2,1)} %get-tuple-element.106) | copy-start | bytes 196612
  76.8 19.5 %copy-start.16 = (bf16[2,128,128]{2,1,0:T(8,128)(2,1)S(1)}, bf16[2,128,128]{2,1,0:T(8,128)(2,1)}, u32[]{:S(2)}) copy-start(bf16[2,128,128]{2,1,0:T(8,128)(2,1)} %get-tuple-element.101) | copy-start | bytes 196612
  76.8 30.1 %all-to-all-start = ((f32[16,20,8,128]{3,2,1,0:T(8,128)}), f32[16,20,8,128]{3,2,1,0:T(8,128)S(1)}, u32[]{:S(2)}, u32[]{:S(2)}) async-start(f32[16,20,8,128]{3,2,1,0:T(8,128)} %covariance.1), calls=%async_computation | async-start | bytes 2621440 | tf_op jit(solution)/shard_map/covariance/all_to_all | solution.py:564
  84.6 11.7 %collective-permute-start.10 = (bf16[2,128,128]{2,1,0:T(8,128)(2,1)S(1)}, bf16[2,128,128]{2,1,0:T(8,128)(2,1)S(1)}, u32[]{:S(2)}, u32[]{:S(2)}) collective-permute-start(bf16[2,128,128]{2,1,0:T(8,128)(2,1)S(1)} %copy-done.21), channel_id=1, source_target_pairs={{0,11},{1,10},{2,13},{3,12},{4,15},{5,14},{6,1},{7,0},{8,3},{9,2},... | collective-permute-start | bytes 196616 | tf_op jit(solution)/shard_map/diag/ppermute | solution.py:526
  85.2 16.6 %collective-permute-start.11 = (bf16[2,128,128]{2,1,0:T(8,128)(2,1)S(1)}, bf16[2,128,128]{2,1,0:T(8,128)(2,1)S(1)}, u32[]{:S(2)}, u32[]{:S(2)}) collective-permute-start(bf16[2,128,128]{2,1,0:T(8,128)(2,1)S(1)} %copy-done.20), channel_id=1, source_target_pairs={{0,8},{1,9},{2,10},{3,11},{4,12},{5,13},{6,14},{7,15},{8,0},{9,1},... | collective-permute-start | bytes 196616 | tf_op jit(solution)/shard_map/diag/ppermute | solution.py:526
  87.1 14.7 %collective-permute-start.12 = (bf16[2,128,128]{2,1,0:T(8,128)(2,1)S(1)}, bf16[2,128,128]{2,1,0:T(8,128)(2,1)S(1)}, u32[]{:S(2)}, u32[]{:S(2)}) collective-permute-start(bf16[2,128,128]{2,1,0:T(8,128)(2,1)S(1)} %copy-done.19), channel_id=1, source_target_pairs={{0,9},{1,8},{2,11},{3,10},{4,13},{5,12},{6,15},{7,14},{8,1},{9,0},... | collective-permute-start | bytes 196616 | tf_op jit(solution)/shard_map/diag/ppermute | solution.py:526
  91.0 11.3 %collective-permute-start.13 = (bf16[2,128,128]{2,1,0:T(8,128)(2,1)S(1)}, bf16[2,128,128]{2,1,0:T(8,128)(2,1)S(1)}, u32[]{:S(2)}, u32[]{:S(2)}) collective-permute-start(bf16[2,128,128]{2,1,0:T(8,128)(2,1)S(1)} %copy-done.18), channel_id=1, source_target_pairs={{0,6},{1,7},{2,8},{3,9},{4,10},{5,11},{6,12},{7,13},{8,14},{9,15},... | collective-permute-start | bytes 196616 | tf_op jit(solution)/shard_map/diag/ppermute | solution.py:526
  95.1 10.7 %collective-permute-start.14 = (bf16[2,128,128]{2,1,0:T(8,128)(2,1)S(1)}, bf16[2,128,128]{2,1,0:T(8,128)(2,1)S(1)}, u32[]{:S(2)}, u32[]{:S(2)}) collective-permute-start(bf16[2,128,128]{2,1,0:T(8,128)(2,1)S(1)} %copy-done.17), channel_id=1, source_target_pairs={{0,7},{1,6},{2,9},{3,8},{4,11},{5,10},{6,13},{7,12},{8,15},{9,14},... | collective-permute-start | bytes 196616 | tf_op jit(solution)/shard_map/diag/ppermute | solution.py:526
  96.3 16.1 %copy-start.9 = (bf16[2,128,128]{2,1,0:T(8,128)(2,1)}, bf16[2,128,128]{2,1,0:T(8,128)(2,1)S(1)}, u32[]{:S(2)}) copy-start(bf16[2,128,128]{2,1,0:T(8,128)(2,1)S(1)} %collective-permute-done.10.rest_11_) | copy-start | bytes 196612
  96.3 10.6 %collective-permute-start.9 = (bf16[2,128,128]{2,1,0:T(8,128)(2,1)S(1)}, bf16[2,128,128]{2,1,0:T(8,128)(2,1)S(1)}, u32[]{:S(2)}, u32[]{:S(2)}) collective-permute-start(bf16[2,128,128]{2,1,0:T(8,128)(2,1)S(1)} %copy-done.16), channel_id=1, source_target_pairs={{0,10},{1,11},{2,12},{3,13},{4,14},{5,15},{6,0},{7,1},{8,2},{9,3},... | collective-permute-start | bytes 196616 | tf_op jit(solution)/shard_map/diag/ppermute | solution.py:526
  101.8 10.6 %copy-start.10 = (bf16[2,128,128]{2,1,0:T(8,128)(2,1)}, bf16[2,128,128]{2,1,0:T(8,128)(2,1)S(1)}, u32[]{:S(2)}) copy-start(bf16[2,128,128]{2,1,0:T(8,128)(2,1)S(1)} %collective-permute-done.11.rest_12_) | copy-start | bytes 196612
  101.8 10.6 %copy-start.11 = (bf16[2,128,128]{2,1,0:T(8,128)(2,1)}, bf16[2,128,128]{2,1,0:T(8,128)(2,1)S(1)}, u32[]{:S(2)}) copy-start(bf16[2,128,128]{2,1,0:T(8,128)(2,1)S(1)} %collective-permute-done.12.rest_13_) | copy-start | bytes 196612
  102.3 10.2 %copy-start.12 = (bf16[2,128,128]{2,1,0:T(8,128)(2,1)}, bf16[2,128,128]{2,1,0:T(8,128)(2,1)S(1)}, u32[]{:S(2)}) copy-start(bf16[2,128,128]{2,1,0:T(8,128)(2,1)S(1)} %collective-permute-done.13.rest_14_) | copy-start | bytes 196612
  105.8 6.7 %copy-start.13 = (bf16[2,128,128]{2,1,0:T(8,128)(2,1)}, bf16[2,128,128]{2,1,0:T(8,128)(2,1)S(1)}, u32[]{:S(2)}) copy-start(bf16[2,128,128]{2,1,0:T(8,128)(2,1)S(1)} %collective-permute-done.14.rest_15_) | copy-start | bytes 196612
  107.0 5.5 %copy-start.14 = (bf16[2,128,128]{2,1,0:T(8,128)(2,1)}, bf16[2,128,128]{2,1,0:T(8,128)(2,1)S(1)}, u32[]{:S(2)}) copy-start(bf16[2,128,128]{2,1,0:T(8,128)(2,1)S(1)} %collective-permute-done.9.rest_10_) | copy-start | bytes 196612
  112.5 15.4 %all-to-all-start.1 = ((f32[16,2,8,128]{3,2,1,0:T(8,128)}), f32[16,2,8,128]{3,2,1,0:T(8,128)S(1)}, u32[]{:S(2)}, u32[]{:S(2)}) async-start(f32[16,2,8,128]{3,2,1,0:T(8,128)} %get-tuple-element.130), calls=%async_computation.1 | async-start | bytes 262144 | tf_op jit(solution)/shard_map/exchange/all_to_all | solution.py:589
  129.2 11.5 %all-to-all-start.2 = ((f32[16,2,8,128]{3,2,1,0:T(8,128)}), f32[16,2,8,128]{3,2,1,0:T(8,128)S(1)}, u32[]{:S(2)}, u32[]{:S(2)}) async-start(f32[16,2,8,128]{3,2,1,0:T(8,128)} %bitcast.10), calls=%async_computation.2 | async-start | bytes 262144 | tf_op jit(solution)/shard_map/exchange/all_to_all | solution.py:598
  163.4 11.5 %all-to-all-start.4 = ((f32[16,2,8,128]{3,2,1,0:T(8,128)}), f32[16,2,8,128]{3,2,1,0:T(8,128)S(1)}, u32[]{:S(2)}, u32[]{:S(2)}) async-start(f32[16,2,8,128]{3,2,1,0:T(8,128)} %bitcast.12), calls=%async_computation.4 | async-start | bytes 262144 | tf_op jit(solution)/shard_map/exchange/all_to_all | solution.py:598
  197.4 11.5 %all-to-all-start.6 = ((f32[16,2,8,128]{3,2,1,0:T(8,128)}), f32[16,2,8,128]{3,2,1,0:T(8,128)S(1)}, u32[]{:S(2)}, u32[]{:S(2)}) async-start(f32[16,2,8,128]{3,2,1,0:T(8,128)} %bitcast.14), calls=%async_computation.6 | async-start | bytes 262144 | tf_op jit(solution)/shard_map/exchange/all_to_all | solution.py:598
Sparse Core Ops, SparseCore 0:
  11.2 56.7 all-gather.1

commit v5 on v4

--- a/solution.py
+++ b/solution.py
@@ -13,6 +13,7 @@
 PER_STEP = 8
 CHUNK = 4
 CORES = 2
+MANY = 8
 
 BF = jnp.bfloat16
 F32 = jnp.float32
@@ -36,16 +37,32 @@
     return x - jnp.clip(x, -LAMBDA, LAMBDA)
 
 
-def slice_kernel(group, features_ref, out_ref):
+def slice_kernel(group, features, out_ref, near_ref, sems):
     r = lax.axis_index("row")
-    variables = features_ref.shape[2]
+    blocks, _, variables = features.shape
+    parts = sems.shape[0]
+    count = blocks // parts
+
+    def copy(i):
+        part = pl.ds(i * count, count)
+        return pltpu.make_async_copy(features.at[part], near_ref.at[part], sems.at[i])
+
+    for i in range(parts):
+        copy(i).start()
     wanted = lax.broadcasted_iota(jnp.int32, (group, variables), 0) + r * group
     pick = (lax.broadcasted_iota(jnp.int32, (group, variables), 1) == wanted).astype(BF)
-    for block in range(features_ref.shape[0]):
-        rows = lax.dot_general(
-            pick, features_ref[block], (((1,), (1,)), ((), ())), preferred_element_type=F32
-        )
-        out_ref[block] = rows.astype(BF)
+
+    def step(i, carry):
+        copy(i).wait()
+        for b in range(count):
+            rows = lax.dot_general(
+                pick, near_ref[i * count + b], (((1,), (1,)), ((), ())),
+                preferred_element_type=F32,
+            )
+            out_ref[i * count + b] = rows.astype(BF)
+        return carry
+
+    lax.fori_loop(0, parts, step, 0)
 
 
 def split_kernel(tiles_ref, out_ref):
@@ -98,14 +115,13 @@
 
 
 class Tiles:
-    def __init__(self, far_ref, near_ref, sem, back=False):
+    def __init__(self, far_ref, near_ref, sem, back=False, count=CHUNK):
         self.refs = (near_ref, far_ref) if back else (far_ref, near_ref)
-        self.near = near_ref
         self.sem = sem
-        self.chunks = near_ref.shape[0] // CHUNK
+        self.count = count
 
     def copy(self, i):
-        part = pl.ds(i * CHUNK, CHUNK)
+        part = pl.ds(i * self.count, self.count)
         source, target = (ref.at[part] for ref in self.refs)
         return pltpu.make_async_copy(source, target, self.sem.at[i])
 
@@ -139,15 +155,15 @@
 
 
 def covariance_kernel(
-    far, col_count, rows_ref, lists_ref, owned_ref, far_slices, features, out_ref,
-    slices_ref, right_ref, slice_sem, right_sem,
+    far, col_count, rows_ref, lists_ref, owned_ref, far_slices, features, far_out,
+    slices_ref, right_ref, out_ref, slice_sem, right_sem, out_sem,
 ):
     owners = rows_ref.shape[0]
     columns = owned_ref.shape[1]
     group = slices_ref.shape[1]
-    samples = features.shape[1]
-    size = features.shape[2]
+    _, samples, size = features.shape
     part = far_slices.shape[0] * CORES // col_count
+    slots = [chip_at(dz, col_count) * CHUNK + s for dz in far for s in range(CHUNK)]
 
     def slice_copy(n):
         here = pl.ds(chip_at(far[n], col_count) * part, part)
@@ -159,6 +175,9 @@
         return pltpu.make_async_copy(
             features.at[owned_ref[owner, a]], right_ref.at[owner, a], right_sem.at[owner, a]
         )
+
+    def out_copy(owner):
+        return pltpu.make_async_copy(out_ref.at[owner], far_out.at[owner], out_sem.at[owner])
 
     for n in range(len(far)):
         slice_copy(n).start()
@@ -172,25 +191,21 @@
         for a in range(columns):
             right_copy(owner, a).wait()
         left = jnp.concatenate(
-            [
-                slices_ref[rows_ref[owner, chip_at(dz, col_count) * CHUNK + s]].astype(F32)
-                for dz in far for s in range(CHUNK)
-            ],
-            axis=0,
+            [slices_ref[rows_ref[owner, slot]].astype(F32) for slot in slots], axis=0
         ).astype(BF)
         right = jnp.concatenate([right_ref[owner, a] for a in range(columns)], axis=1)
         both = dot(left, right) * (1.0 / samples)
-        for n, dz in enumerate(far):
-            first = chip_at(dz, col_count) * CHUNK
-            for s in range(CHUNK):
-                k = n * CHUNK + s
-                rows = both[k * group:(k + 1) * group]
-                out_ref[owner, k] = jnp.where(
-                    lists_ref[owner, first + s] == 0, rows[:, :size], rows[:, size:]
-                )
+        for k, slot in enumerate(slots):
+            rows = both[k * group:(k + 1) * group]
+            out_ref[owner, k] = jnp.where(
+                lists_ref[owner, slot] == 0, rows[:, :size], rows[:, size:]
+            )
+        out_copy(owner).start()
         return carry
 
-    lax.fori_loop(0, owners, owner_step, 0)
+    lax.fori_loop(0, owners, owner_step, 0, unroll=2)
+    for owner in range(owners):
+        out_copy(owner).wait()
 
 
 def pair(x):
@@ -201,9 +216,11 @@
     )
 
 
-def add_product(d, column, tile, sums_ref):
-    left = jnp.concatenate(split(d.T), axis=1)
-    sums_ref[column] += dot(left, pair(tile))
+def add_products(slots, ds, tiles, list_ref, sums_ref):
+    lefts = [jnp.concatenate(split(d.T), axis=1) for d in ds]
+    products = [dot(left, pair(tile)) for left, tile in zip(lefts, tiles)]
+    for slot, product in zip(slots, products):
+        sums_ref[list_ref[slot]] += product
 
 
 def write_sums(sums_ref, out_ref):
@@ -213,15 +230,21 @@
         out_ref[:, a] = total.reshape(pieces, group, size)
 
 
-def first_step(slot, covariance, list_ref, live_ref, theta_ref, tiles_ref, base_ref, d_ref, sums_ref):
-    theta = theta_ref[slot]
-    tile = tiles_ref[slot]
-    base = theta - STEP * (covariance - tile)
-    d = jnp.where(slot < live_ref[0], shrink(base) - theta, 0.0)
-    base_ref[slot] = base
-    d_ref[slot] = d
-    halves = jnp.concatenate(split(tile), axis=1)
-    add_product(d, list_ref[slot], halves, sums_ref)
+def first_steps(
+    slots, covariances, list_ref, live_ref, theta_ref, tiles_ref, base_ref, d_ref, sums_ref
+):
+    ds = []
+    tiles = []
+    for slot, covariance in zip(slots, covariances):
+        theta = theta_ref[slot]
+        tile = tiles_ref[slot]
+        base = theta - STEP * (covariance - tile)
+        base_ref[slot] = base
+        ds.append(jnp.where(slot < live_ref[0], shrink(base) - theta, 0.0))
+        tiles.append(jnp.concatenate(split(tile), axis=1))
+    for slot, d in zip(slots, ds):
+        d_ref[slot] = d
+    add_products(slots, ds, tiles, list_ref, sums_ref)
 
 
 def near_kernel(near, col_count, list_ref, live_ref, owned_ref, features, far_theta, far_tiles, *rest):
@@ -266,16 +289,18 @@
         chip = chip_at(dz, col_count)
         for array in arrays:
             array.wait(chip)
-        for s in range(CHUNK):
-            slot = chip * CHUNK + s
-            covariance = lax.dot_general(
+        slots_here = [chip * CHUNK + s for s in range(CHUNK)]
+        covariances = [
+            lax.dot_general(
                 left_ref[n * CHUNK + s], right_ref[list_ref[slot]],
                 (((0,), (0,)), ((), ())), preferred_element_type=F32,
             ) * (1.0 / samples)
-            first_step(
-                slot, covariance, list_ref, live_ref, theta_ref, tiles_ref, base_ref, d_ref,
-                sums_ref,
-            )
+            for s, slot in enumerate(slots_here)
+        ]
+        first_steps(
+            slots_here, covariances, list_ref, live_ref, theta_ref, tiles_ref, base_ref, d_ref,
+            sums_ref,
+        )
         for out in outs:
             out.start(chip)
     for dz in near:
@@ -296,23 +321,23 @@
         for array in arrays:
             array.start(chip_at(dz, col_count))
     bring.wait()
-
-    def step(n, carry):
-        chip = chip_at(n + far[0], col_count)
-        for array in arrays:
-            array.wait(chip)
-        for s in range(CHUNK):
-            slot = chip * CHUNK + s
-            covariance = cov_ref[:, n * CHUNK + s].reshape(size, size)
-            first_step(
-                slot, covariance, list_ref, live_ref, theta_ref, tiles_ref, base_ref, d_ref,
-                sums_ref,
-            )
-        for out in outs:
-            out.start(chip)
-        return carry
-
-    lax.fori_loop(0, len(far), step, 0)
+    for begin in range(0, len(far), 2):
+        part = range(begin, min(begin + 2, len(far)))
+        chips = [chip_at(far[n], col_count) for n in part]
+        for chip in chips:
+            for array in arrays:
+                array.wait(chip)
+        first_steps(
+            [chip * CHUNK + s for chip in chips for s in range(CHUNK)],
+            [
+                cov_ref[:, n * CHUNK + s].reshape(size, size)
+                for n in part for s in range(CHUNK)
+            ],
+            list_ref, live_ref, theta_ref, tiles_ref, base_ref, d_ref, sums_ref,
+        )
+        for chip in chips:
+            for out in outs:
+                out.start(chip)
     write_sums(sums_ref, out_ref)
     for dz in far:
         for out in outs:
@@ -379,13 +404,13 @@
     else:
         out_ref, t_ref, theta_ref, pairs_ref, d_ref, right_ref, sems, sums_ref = rest
     slots, size, _ = theta_ref.shape
-    chunks = slots // CHUNK
+    chunks = slots // MANY
     arrays = [
-        Tiles(far_pairs, pairs_ref, sems.at[0]),
-        Tiles(far_t, t_ref, sems.at[1]),
-        Tiles(far_theta, theta_ref, sems.at[2]),
+        Tiles(far_pairs, pairs_ref, sems.at[0], count=MANY),
+        Tiles(far_t, t_ref, sems.at[1], count=MANY),
+        Tiles(far_theta, theta_ref, sems.at[2], count=MANY),
     ]
-    out = Tiles(far_d, d_ref, sems.at[3], True)
+    out = Tiles(far_d, d_ref, sems.at[3], True, count=MANY)
     start_all(arrays, chunks)
     for a in range(q_ref.shape[1]):
         q = q_ref[:, a].reshape(size, size)
@@ -393,19 +418,29 @@
     if not last:
         sums_ref[...] = jnp.zeros_like(sums_ref)
 
-    def slot_step(slot):
-        column = list_ref[slot]
-        both = dot(pairs_ref[slot], right_ref[column])
-        product = both[:, :size] + both[:, size:]
-        d = shrink(t_ref[slot] - STEP * product) - theta_ref[slot]
-        d = jnp.where(slot < live_ref[0], d, 0.0)
-        d_ref[slot] = d
+    def step(i, carry):
+        for array in arrays:
+            array.wait(i)
+        slots_here = [i * MANY + s for s in range(MANY)]
+        both = [dot(pairs_ref[slot], right_ref[list_ref[slot]]) for slot in slots_here]
+        ds = []
+        for slot, x in zip(slots_here, both):
+            product = x[:, :size] + x[:, size:]
+            d = shrink(t_ref[slot] - STEP * product) - theta_ref[slot]
+            ds.append(jnp.where(slot < live_ref[0], d, 0.0))
+        for slot, d in zip(slots_here, ds):
+            d_ref[slot] = d
         if not last:
-            add_product(d, column, pairs_ref[slot], sums_ref)
-
-    each_slot(chunks, arrays, [out], slot_step)
+            tiles = [pairs_ref[slot] for slot in slots_here]
+            add_products(slots_here, ds, tiles, list_ref, sums_ref)
+        out.start(i)
+        return carry
+
+    lax.fori_loop(0, chunks, step, 0)
     if not last:
         write_sums(sums_ref, out_ref)
+    for i in range(chunks):
+        out.wait(i)
 
 
 def shape(dims, dtype):
@@ -445,14 +480,16 @@
     piece_shape = (row_count, columns, group, size)
 
     with jax.named_scope("slices"):
-        per_step = 8
         mine = pl.pallas_call(
             functools.partial(slice_kernel, group),
-            grid=(blocks // per_step,),
-            in_specs=[pl.BlockSpec((per_step, samples, size), lambda i: (i, 0, 0))],
-            out_specs=pl.BlockSpec((per_step, group, samples), lambda i: (i, 0, 0)),
+            in_specs=[HBM],
+            out_specs=VMEM,
             out_shape=shape((blocks, group, samples), BF),
-        )(features)
+            scratch_shapes=[
+                pltpu.VMEM(features.shape, BF), pltpu.SemaphoreType.DMA((4,))
+            ],
+            compiler_params=PARAMS,
+        )(far(features))
         slices = lax.all_gather(mine, "col", axis=0, tiled=True)
 
     with jax.named_scope("tables"):
@@ -488,11 +525,11 @@
 
     with jax.named_scope("blocks"):
         chips = col_count // CORES
-        near = [0, 1, chips - 1]
-        far_chips = list(range(2, chips - 1))
+        near = [0]
+        far_chips = list(range(1, chips))
         cores = range(CORES)
         steps = [(dz, dk) for dz in near for dk in cores]
-        steps += [(dz, dk) for dz in (2, chips - 2) for dk in cores]
+        steps += [(dz, dk) for dz in (1, chips - 1) for dk in cores]
         early = len(steps)
         steps += [(dz, dk) for dz in far_chips[1:-1] for dk in cores]
         near_count = len(near) * CORES
@@ -551,13 +588,15 @@
         partial = pl.pallas_call(
             functools.partial(covariance_kernel, far_chips, col_count),
             in_specs=[SMEM, SMEM, SMEM, HBM, HBM],
-            out_specs=VMEM,
+            out_specs=HBM,
             out_shape=pltpu.HBM((row_count, far_slots, group, size), F32),
             scratch_shapes=[
                 pltpu.VMEM(slices.shape, BF),
                 pltpu.VMEM((row_count, columns, samples, size), BF),
+                pltpu.VMEM((row_count, far_slots, group, size), F32),
                 sems(len(far_chips)),
                 sems(row_count, columns),
+                sems(row_count),
             ],
             compiler_params=PARAMS,
         )(rows_here, lists_here, owned_here, far(slices), far(features))
@@ -618,7 +657,7 @@
                 out_shape=[tile_out] if last else [tile_out, shape(piece_shape, F32)],
                 scratch_shapes=[
                     tile_vmem, tile_vmem, pltpu.VMEM((slots, size, 2 * size), BF), tile_vmem,
-                    pltpu.VMEM((columns, 2 * size, 2 * size), BF), sems(4, chunks),
+                    pltpu.VMEM((columns, 2 * size, 2 * size), BF), sems(4, slots // MANY),
                 ] + ([] if last else [sums]),
                 compiler_params=PARAMS,
             )(my_list, live, far(t), far(theta), far(pairs), q)

time: 223 us -> 218 us (0.978)
  waiting for transfers between devices: 28.9 us -> 41.2 us
  starting transfers between devices: 61.9 us -> 52.3 us
  Pallas kernels: 80.9 us -> 73.7 us
    all_gather x1, waiting for transfers between devices: 3.62 us -> 20.8 us  [body(): slices = lax.all_gather(mine, 'col', axis=0, tiled=True)]
    ppermute x15, starting transfers between devices: 36.1 us -> 28.4 us  [send(): return lax.ppermute(blocks_out[n], 'col', pairs_of)]
    ppermute x15, waiting for transfers between devices: 15 us -> 10.2 us  [send(): return lax.ppermute(blocks_out[n], 'col', pairs_of)]
    pallas_call x1, Pallas kernels: 8.35 us -> 4.69 us  [body(): pl.pallas_call(functools.partial(near_kernel, near, col_count), in_specs=...]
    pallas_call x3, Pallas kernels: 19.8 us -> 16.5 us  [body(): pl.pallas_call(functools.partial(sweep_kernel, last), in_specs=[SMEM, SME...]
  transfers between devices with their start and end apart: 21 -> 21, of which waited for: 11 -> 10; matrix products, arithmetic and copies ran while one was open for 3% -> 3% of each run, Pallas kernels for 17% -> 16%
where the time goes in v5:
time: 218 us; the launch traced here: 217 us
  Pallas kernels  73.7 us (34%)
  starting transfers between devices  52.3 us (24%)
  waiting for transfers between devices  41.2 us (19%)
  blocking collectives  28.4 us (13%)
  between operations  13.9 us (6%)
  local copies, waits for them, and re-layouts  6.07 us (3%)
    ppermute x15, starting transfers between devices, send(): return lax.ppermute(blocks_out[n], 'col', pairs_of)  28.4 us
    all_to_all x2, blocking collectives, body(): got = lax.all_to_all(pieces, 'row', split_axis=0, concat_axis=0, tiled=True)  28.4 us
    pallas_call x3, Pallas kernels, body(): pl.pallas_call(functools.partial(diagonal_kernel, steps), in_specs=[SMEM,...  21.5 us
    all_gather x1, waiting for transfers between devices, body(): slices = lax.all_gather(mine, 'col', axis=0, tiled=True)  20.8 us
    pallas_call x3, Pallas kernels, body(): pl.pallas_call(functools.partial(sweep_kernel, last), in_specs=[SMEM, SME...  16.5 us
    all_to_all x3, starting transfers between devices, body(): lax.all_to_all(summed.reshape(piece_shape), 'row', split_axis=0, concat_a...  10.5 us
    ppermute x15, waiting for transfers between devices, send(): return lax.ppermute(blocks_out[n], 'col', pairs_of)  10.2 us
    pallas_call x1, Pallas kernels, body(): pl.pallas_call(functools.partial(covariance_kernel, far_chips, col_count)...  9.72 us
  transfers between devices with their start and end apart: 21, of which 10 were waited for; matrix products, arithmetic and copies ran while one was open for 3% of the time, Pallas kernels for 16%

profile of v5, /device:TPU:32, one launch (start us, length us, event | category | flops | bytes accessed | tf_op | source)
XLA Modules:
  0.0 216.9 jit_solution(4600945100555052697)
XLA Ops:
  6.5 3.5 %slices.1 = bf16[32,8,512]{2,1,0:T(8,128)(2,1)} custom-call(bf16[32,512,128]{2,1,0:T(8,128)(2,1)} %features.7), custom_call_target="tpu_custom_call" | custom-call | tf_op jit(solution)/shard_map/slices/pallas_call | solution.py:483
  10.1 0.0 all-gather.2.cloned.1.call-update
  10.1 0.8 dynamic-slice_subtract_fusion.1
  10.9 0.1 copy.28
  11.0 0.1 copy.25.wanted_ref
  11.1 4.1 %blocks.2 = (bf16[2,640,128]{2,1,0:T(8,128)(2,1)}, bf16[2,640,128]{2,1,0:T(8,128)(2,1)}, bf16[2,128,128]{2,1,0:T(8,128)(2,1)}, bf16[2,128,128]{2,1,0:T(8,128)(2,...) custom-call(s32[16,2]{1,0:T(8,128)S(1)} %copy.25.wanted_ref, ...), custom_call_target="tpu_custom_call" | custom-call | tf_op jit(solution)/shard_map/blocks/pallas_call | solution.py:541
  15.2 0.1 collective-permute-start
  15.3 1.9 collective-permute-start.1
  17.2 3.8 %collective-permute-start.2 = (bf16[2,128,128]{2,1,0:T(8,128)(2,1)}, bf16[2,128,128]{2,1,0:T(8,128)(2,1)S(1)}, u32[]{:S(2)}, u32[]{:S(2)}) collective-permute-start(bf16[2,128,128]{2,1,0:T(8,128)(2,1)} %get-tuple-element.74), channel_id=1, source_target_pairs={{0,15},{1,14},{2,1},{3,0},{4,3},{5,2},{6,5},{7,4},{8,7},{9,6},{10,... | collective-permute-start | bytes 196616 | tf_op jit(solution)/shard_map/blocks/ppermute | solution.py:563
  21.0 0.0 collective-permute-start.4
  21.0 0.4 fusion.3
  21.4 0.1 fusion.owned_ref
  21.6 0.1 copy.23
  21.7 1.3 dynamic_slice.26
  23.0 3.8 %split.1.far_pairs = bf16[32,128,256]{2,1,0:T(8,128)(2,1)} custom-call(f32[32,128,128]{2,1,0:T(8,128)} %bitcast.30), custom_call_target="tpu_custom_call" | custom-call | tf_op jit(solution)/shard_map/split/pallas_call | solution.py:518
  26.8 0.1 copy.26.owned_ref
  26.9 0.9 constant_dynamic-slice_fusion.1
  27.8 0.7 fusion.1.list_ref
  28.5 0.0 collective-permute-done.rest_1_
  28.5 0.7 copy-done
  29.2 4.7 %blocks.3 = (f32[32,128,128]{2,1,0:T(8,128)}, f32[32,128,128]{2,1,0:T(8,128)}, f32[2,128,256]{2,1,0:T(8,128)}) custom-call(s32[32]{0:T(128)S(1)} %fusion.1.list_ref, s32[1]{0:T(128)} %bitcast.1.live_ref, s32[2]{0:T(128)S(1)} %fusion.owned_ref, bf16[32,512,128]{2,1,0:T(8,128)(2,1)} %features.7, f32[32,128,128]{2,1,0:T(8,128)} %bitcast.25, ...), custom_call_target="tpu_custom_call" | custom-call | tf_op jit(solution)/shard_map/blocks/pallas_call | solution.py:566
  34.0 20.8 %all-gather.2.cloned.1.call-done.far_slices = bf16[512,8,512]{2,1,0:T(8,128)(2,1)} async-done(((bf16[32,8,512]{2,1,0:T(8,128)(2,1)}), bf16[512,8,512]{2,1,0:T(8,128)(2,1)}) %all-gather.2.cloned.1.call-update) | async-done | bytes 4194320 | tf_op jit(solution)/shard_map/slices/all_gather | solution.py:493
  54.8 9.7 %covariance.1 = f32[16,28,8,128]{3,2,1,0:T(8,128)} custom-call(s32[16,32]{1,0:T(8,128)S(1)} %bitcast.24, s32[16,32]{1,0:T(8,128)S(1)} %bitcast.23, s32[16,2]{1,0:T(8,128)S(1)} %copy.26.owned_ref, bf16[512,8,512]{2,1,0:T(8,128)(2,1)} %all-gather.2.cloned.1.call-done.far_slices, bf16[32,512,128]{2,1,0:T(8,128)(2,1)} %features.7), custom_call_target="tpu_custom_call" | custom-call | tf_op jit(solution)/shard_map/covariance/pallas_call | solution.py:588
  64.6 6.9 %all-to-all-start = ((f32[16,28,8,128]{3,2,1,0:T(8,128)}), f32[16,28,8,128]{3,2,1,0:T(8,128)S(1)}, u32[]{:S(2)}, u32[]{:S(2)}) async-start(f32[16,28,8,128]{3,2,1,0:T(8,128)} %covariance.1), calls=%async_computation | async-start | bytes 3670016 | tf_op jit(solution)/shard_map/covariance/all_to_all | solution.py:603
  71.5 2.6 %collective-permute-start.10 = (bf16[2,128,128]{2,1,0:T(8,128)(2,1)S(1)}, bf16[2,128,128]{2,1,0:T(8,128)(2,1)S(1)}, u32[]{:S(2)}, u32[]{:S(2)}) collective-permute-start(bf16[2,128,128]{2,1,0:T(8,128)(2,1)S(1)} %copy-done.25), channel_id=1, source_target_pairs={{0,9},{1,8},{2,11},{3,10},{4,13},{5,12},{6,15},{7,14},{8,1},{9,0},... | collective-permute-start | bytes 196616 | tf_op jit(solution)/shard_map/diag/ppermute | solution.py:563
  74.2 2.4 %collective-permute-start.11 = (bf16[2,128,128]{2,1,0:T(8,128)(2,1)S(1)}, bf16[2,128,128]{2,1,0:T(8,128)(2,1)S(1)}, u32[]{:S(2)}, u32[]{:S(2)}) collective-permute-start(bf16[2,128,128]{2,1,0:T(8,128)(2,1)S(1)} %copy-done.24), channel_id=1, source_target_pairs={{0,6},{1,7},{2,8},{3,9},{4,10},{5,11},{6,12},{7,13},{8,14},{9,15},... | collective-permute-start | bytes 196616 | tf_op jit(solution)/shard_map/diag/ppermute | solution.py:563
  76.6 2.5 %collective-permute-start.12 = (bf16[2,128,128]{2,1,0:T(8,128)(2,1)S(1)}, bf16[2,128,128]{2,1,0:T(8,128)(2,1)S(1)}, u32[]{:S(2)}, u32[]{:S(2)}) collective-permute-start(bf16[2,128,128]{2,1,0:T(8,128)(2,1)S(1)} %copy-done.23), channel_id=1, source_target_pairs={{0,7},{1,6},{2,9},{3,8},{4,11},{5,10},{6,13},{7,12},{8,15},{9,14},... | collective-permute-start | bytes 196616 | tf_op jit(solution)/shard_map/diag/ppermute | solution.py:563
  79.1 1.5 collective-permute-start.13
  80.5 1.3 collective-permute-start.14
  81.8 0.1 sub.25
  81.9 0.1 compare_convert_fusion.same_ref
  82.0 0.0 collective-permute-done.10.rest_11_
  82.0 2.5 %collective-permute-start.5 = (bf16[2,128,128]{2,1,0:T(8,128)(2,1)S(1)}, bf16[2,128,128]{2,1,0:T(8,128)(2,1)S(1)}, u32[]{:S(2)}, u32[]{:S(2)}) collective-permute-start(bf16[2,128,128]{2,1,0:T(8,128)(2,1)S(1)} %copy-done.20), channel_id=1, source_target_pairs={{0,12},{1,13},{2,14},{3,15},{4,0},{5,1},{6,2},{7,3},{8,4},{9,5},{1... | collective-permute-start | bytes 196616 | tf_op jit(solution)/shard_map/diag/ppermute | solution.py:563
  84.5 1.4 collective-permute-start.6
  85.9 3.1 %collective-permute-done.12.rest_13_ = bf16[2,128,128]{2,1,0:T(8,128)(2,1)S(1)} collective-permute-done((bf16[2,128,128]{2,1,0:T(8,128)(2,1)S(1)}, bf16[2,128,128]{2,1,0:T(8,128)(2,1)S(1)}, u32[]{:S(2)}, u32[]{:S(2)}) %collective-permute-start.12) | collective-permute-done | bytes 65568 | tf_op jit(solution)/shard_map/diag/ppermute | solution.py:563
  89.0 4.4 %collective-permute-start.7 = (bf16[2,128,128]{2,1,0:T(8,128)(2,1)S(1)}, bf16[2,128,128]{2,1,0:T(8,128)(2,1)S(1)}, u32[]{:S(2)}, u32[]{:S(2)}) collective-permute-start(bf16[2,128,128]{2,1,0:T(8,128)(2,1)S(1)} %copy-done.18), channel_id=1, source_target_pairs={{0,10},{1,11},{2,12},{3,13},{4,14},{5,15},{6,0},{7,1},{8,2},{9,3},... | collective-permute-start | bytes 196616 | tf_op jit(solution)/shard_map/diag/ppermute | solution.py:563
  93.5 0.1 collective-permute-done.13.rest_14_
  93.6 0.7 collective-permute-start.8
  94.3 0.6 collective-permute-done.14.rest_15_
  95.0 3.3 %collective-permute-start.9 = (bf16[2,128,128]{2,1,0:T(8,128)(2,1)S(1)}, bf16[2,128,128]{2,1,0:T(8,128)(2,1)S(1)}, u32[]{:S(2)}, u32[]{:S(2)}) collective-permute-start(bf16[2,128,128]{2,1,0:T(8,128)(2,1)S(1)} %copy-done.16), channel_id=1, source_target_pairs={{0,8},{1,9},{2,10},{3,11},{4,12},{5,13},{6,14},{7,15},{8,0},{9,1},... | collective-permute-start | bytes 196616 | tf_op jit(solution)/shard_map/diag/ppermute | solution.py:563
  98.3 1.8 gather_fusion
  100.1 1.9 collective-permute-done.8.rest_9_
  102.0 4.4 %collective-permute-done.9.rest_10_ = bf16[2,128,128]{2,1,0:T(8,128)(2,1)S(1)} collective-permute-done((bf16[2,128,128]{2,1,0:T(8,128)(2,1)S(1)}, bf16[2,128,128]{2,1,0:T(8,128)(2,1)S(1)}, u32[]{:S(2)}, u32[]{:S(2)}) %collective-permute-start.9) | collective-permute-done | bytes 65568 | tf_op jit(solution)/shard_map/diag/ppermute | solution.py:563
  106.4 5.8 %first.1 = (f32[32,128,128]{2,1,0:T(8,128)}, f32[32,128,128]{2,1,0:T(8,128)}, f32[16,2,8,128]{3,2,1,0:T(8,128)}) custom-call(s32[32]{0:T(128)S(1)} %fusion.1.list_ref, s32[1]{0:T(128)} %bitcast.1.live_ref, f32[16,28,8,128]{3,2,1,0:T(8,128)S(1)} %all-to-all-done.cov_ref, ...), custom_call_target="tpu_custom_call", output_to_operand_aliasing={{0}: (6, {}), {1}: (7, {})} | custom-call | tf_op jit(solution)/shard_map/first/pallas_call | solution.py:611
  112.3 6.4 %all-to-all-start.1 = ((f32[16,2,8,128]{3,2,1,0:T(8,128)}), f32[16,2,8,128]{3,2,1,0:T(8,128)S(1)}, u32[]{:S(2)}, u32[]{:S(2)}) async-start(f32[16,2,8,128]{3,2,1,0:T(8,128)} %get-tuple-element.130), calls=%async_computation.1 | async-start | bytes 262144 | tf_op jit(solution)/shard_map/exchange/all_to_all | solution.py:628
  118.7 8.0 %all-to-all-done.1 = f32[16,2,8,128]{3,2,1,0:T(8,128)S(1)} async-done(((f32[16,2,8,128]{3,2,1,0:T(8,128)}), f32[16,2,8,128]{3,2,1,0:T(8,128)S(1)}, u32[]{:S(2)}, u32[]{:S(2)}) %all-to-all-start.1) | async-done | bytes 131104 | tf_op jit(solution)/shard_map/exchange/all_to_all | solution.py:628
  126.7 1.3 exchange.3
  128.0 3.5 %all-to-all-start.2 = ((f32[16,2,8,128]{3,2,1,0:T(8,128)}), f32[16,2,8,128]{3,2,1,0:T(8,128)S(1)}, u32[]{:S(2)}, u32[]{:S(2)}) async-start(f32[16,2,8,128]{3,2,1,0:T(8,128)} %bitcast.10), calls=%async_computation.2 | async-start | bytes 262144 | tf_op jit(solution)/shard_map/exchange/all_to_all | solution.py:637
  131.5 0.1 broadcast_select_fusion.col_diag_ref
  131.6 7.2 %diagonal.3.far_t = f32[32,128,128]{2,1,0:T(8,128)} custom-call(s32[32]{0:T(128)S(1)} %fusion.1.list_ref, f32[32,128,128]{2,1,0:T(8,128)} %get-tuple-element.111.far_base, f32[32,128,128]{2,1,0:T(8,128)} %get-tuple-element.112.far_d, bf16[2,128,128]{2,1,0:T(8,128)(2,1)S(1)} %broadcast_select_fusion.col_diag_ref, ...), custom_call_target="tpu_custom_call" | custom-call | tf_op jit(solution)/shard_map/diagonal/pallas_call | solution.py:641
  138.8 0.7 all-to-all-done.2.q_ref
  139.5 5.6 %sweep.3 = (f32[32,128,128]{2,1,0:T(8,128)}, f32[16,2,8,128]{3,2,1,0:T(8,128)S(1)}) custom-call(s32[32]{0:T(128)S(1)} %fusion.1.list_ref, s32[1]{0:T(128)} %bitcast.1.live_ref, f32[32,128,128]{2,1,0:T(8,128)} %diagonal.3.far_t, f32[32,128,128]{2,1,0:T(8,128)} %bitcast.27, bf16[32,128,256]{2,1,0:T(8,128)(2,1)} %split.1.far_pairs, ...), custom_call_target="tpu_custom_call" | custom-call | tf_op jit(solution)/shard_map/sweep/pallas_call | solution.py:653
  145.0 14.2 %all_to_all.35 = f32[16,2,8,128]{3,2,1,0:T(8,128)S(1)} all-to-all(f32[16,2,8,128]{3,2,1,0:T(8,128)S(1)} %get-tuple-element.132), channel_id=1, replica_groups=mesh['row'=16,'col'=16] {'row'}, dimensions={0} | all-to-all | bytes 262144 | tf_op jit(solution)/shard_map/exchange/all_to_all | solution.py:628
  159.3 1.3 exchange.4
  160.6 3.5 %all-to-all-start.4 = ((f32[16,2,8,128]{3,2,1,0:T(8,128)}), f32[16,2,8,128]{3,2,1,0:T(8,128)S(1)}, u32[]{:S(2)}, u32[]{:S(2)}) async-start(f32[16,2,8,128]{3,2,1,0:T(8,128)} %bitcast.12), calls=%async_computation.4 | async-start | bytes 262144 | tf_op jit(solution)/shard_map/exchange/all_to_all | solution.py:637
  164.1 7.2 %diagonal.4.far_t = f32[32,128,128]{2,1,0:T(8,128)} custom-call(s32[32]{0:T(128)S(1)} %fusion.1.list_ref, f32[32,128,128]{2,1,0:T(8,128)} %get-tuple-element.111.far_base, f32[32,128,128]{2,1,0:T(8,128)} %get-tuple-element.131.far_d, bf16[2,128,128]{2,1,0:T(8,128)(2,1)S(1)} %broadcast_select_fusion.col_diag_ref, ...), custom_call_target="tpu_custom_call" | custom-call | tf_op jit(solution)/shard_map/diagonal/pallas_call | solution.py:641
  171.3 0.8 all-to-all-done.4.q_ref
  172.1 5.6 %sweep.4 = (f32[32,128,128]{2,1,0:T(8,128)}, f32[16,2,8,128]{3,2,1,0:T(8,128)S(1)}) custom-call(s32[32]{0:T(128)S(1)} %fusion.1.list_ref, s32[1]{0:T(128)} %bitcast.1.live_ref, f32[32,128,128]{2,1,0:T(8,128)} %diagonal.4.far_t, f32[32,128,128]{2,1,0:T(8,128)} %bitcast.28, bf16[32,128,256]{2,1,0:T(8,128)(2,1)} %split.1.far_pairs, ...), custom_call_target="tpu_custom_call" | custom-call | tf_op jit(solution)/shard_map/sweep/pallas_call | solution.py:653
  177.6 14.2 %all_to_all.36 = f32[16,2,8,128]{3,2,1,0:T(8,128)S(1)} all-to-all(f32[16,2,8,128]{3,2,1,0:T(8,128)S(1)} %get-tuple-element.134), channel_id=1, replica_groups=mesh['row'=16,'col'=16] {'row'}, dimensions={0} | all-to-all | bytes 262144 | tf_op jit(solution)/shard_map/exchange/all_to_all | solution.py:628
  191.8 1.3 exchange.5
  193.1 3.5 %all-to-all-start.6 = ((f32[16,2,8,128]{3,2,1,0:T(8,128)}), f32[16,2,8,128]{3,2,1,0:T(8,128)S(1)}, u32[]{:S(2)}, u32[]{:S(2)}) async-start(f32[16,2,8,128]{3,2,1,0:T(8,128)} %bitcast.14), calls=%async_computation.6 | async-start | bytes 262144 | tf_op jit(solution)/shard_map/exchange/all_to_all | solution.py:637
  196.6 7.2 %diagonal.5.far_t = f32[32,128,128]{2,1,0:T(8,128)} custom-call(s32[32]{0:T(128)S(1)} %fusion.1.list_ref, f32[32,128,128]{2,1,0:T(8,128)} %get-tuple-element.111.far_base, f32[32,128,128]{2,1,0:T(8,128)} %get-tuple-element.133.far_d, bf16[2,128,128]{2,1,0:T(8,128)(2,1)S(1)} %broadcast_select_fusion.col_diag_ref, ...), custom_call_target="tpu_custom_call" | custom-call | tf_op jit(solution)/shard_map/diagonal/pallas_call | solution.py:641
  203.8 0.8 all-to-all-done.6.q_ref
  204.6 5.4 %sweep.5 = f32[32,128,128]{2,1,0:T(8,128)} custom-call(s32[32]{0:T(128)S(1)} %fusion.1.list_ref, s32[1]{0:T(128)} %bitcast.1.live_ref, f32[32,128,128]{2,1,0:T(8,128)} %diagonal.5.far_t, f32[32,128,128]{2,1,0:T(8,128)} %bitcast.29, bf16[32,128,256]{2,1,0:T(8,128)(2,1)} %split.1.far_pairs, f32[16,2,8,128]{3,2,1,0:T(8,128)S(1)} %all-to-all-done.6.q_ref), custom_call_target="tpu_custom_call" | custom-call | tf_op jit(solution)/shard_map/sweep/pallas_call | solution.py:653
  (65 shorter events, 0.1 us)
Async XLA Ops:
  6.5 48.2 %all-gather.2.cloned.1.call-start = ((), (), s32[]{:S(2)}) async-start(), calls=%async_computation.7 | async-start | bytes 4456448 | tf_op jit(solution)/shard_map/slices/all_gather | solution.py:493
  11.1 10.0 %copy-start.15 = (s32[16,16,2]{1,2,0:T(2,128)S(1)}, s32[16,16,2]{1,2,0:T(2,128)}, u32[]{:S(2)}) copy-start(s32[16,16,2]{1,2,0:T(2,128)} %param.14) | copy-start | bytes 6148
  15.2 13.3 %collective-permute-start = (bf16[2,640,128]{2,1,0:T(8,128)(2,1)}, bf16[2,640,128]{2,1,0:T(8,128)(2,1)S(1)}, u32[]{:S(2)}, u32[]{:S(2)}) collective-permute-start(bf16[2,640,128]{2,1,0:T(8,128)(2,1)} %get-tuple-element.72), channel_id=1, source_target_pairs={{0,1},{1,0},{2,3},{3,2},{4,5},{5,4},{6,7},{7,6},{8,9},{9,8},{10,11... | collective-permute-start | bytes 983048 | tf_op jit(solution)/shard_map/blocks/ppermute | solution.py:563
  15.3 18.6 %collective-permute-start.1 = (bf16[2,128,128]{2,1,0:T(8,128)(2,1)}, bf16[2,128,128]{2,1,0:T(8,128)(2,1)S(1)}, u32[]{:S(2)}, u32[]{:S(2)}) collective-permute-start(bf16[2,128,128]{2,1,0:T(8,128)(2,1)} %get-tuple-element.73), channel_id=1, source_target_pairs={{0,14},{1,15},{2,0},{3,1},{4,2},{5,3},{6,4},{7,5},{8,6},{9,7},{10,... | collective-permute-start | bytes 196616 | tf_op jit(solution)/shard_map/blocks/ppermute | solution.py:563
  17.2 16.8 %collective-permute-start.2 = (bf16[2,128,128]{2,1,0:T(8,128)(2,1)}, bf16[2,128,128]{2,1,0:T(8,128)(2,1)S(1)}, u32[]{:S(2)}, u32[]{:S(2)}) collective-permute-start(bf16[2,128,128]{2,1,0:T(8,128)(2,1)} %get-tuple-element.74), channel_id=1, source_target_pairs={{0,15},{1,14},{2,1},{3,0},{4,3},{5,2},{6,5},{7,4},{8,7},{9,6},{10,... | collective-permute-start | bytes 196616 | tf_op jit(solution)/shard_map/blocks/ppermute | solution.py:563
  21.0 12.9 %collective-permute-start.3 = (bf16[2,128,128]{2,1,0:T(8,128)(2,1)}, bf16[2,128,128]{2,1,0:T(8,128)(2,1)S(1)}, u32[]{:S(2)}, u32[]{:S(2)}) collective-permute-start(bf16[2,128,128]{2,1,0:T(8,128)(2,1)} %get-tuple-element.75), channel_id=1, source_target_pairs={{0,2},{1,3},{2,4},{3,5},{4,6},{5,7},{6,8},{7,9},{8,10},{9,11},{10,... | collective-permute-start | bytes 196616 | tf_op jit(solution)/shard_map/blocks/ppermute | solution.py:563
  21.0 13.0 %collective-permute-start.4 = (bf16[2,128,128]{2,1,0:T(8,128)(2,1)}, bf16[2,128,128]{2,1,0:T(8,128)(2,1)S(1)}, u32[]{:S(2)}, u32[]{:S(2)}) collective-permute-start(bf16[2,128,128]{2,1,0:T(8,128)(2,1)} %get-tuple-element.76), channel_id=1, source_target_pairs={{0,3},{1,2},{2,5},{3,4},{4,7},{5,6},{6,9},{7,8},{8,11},{9,10},{10,... | collective-permute-start | bytes 196616 | tf_op jit(solution)/shard_map/blocks/ppermute | solution.py:563
  28.5 0.7 copy-start
  33.9 30.6 %copy-start.1 = (bf16[2,128,128]{2,1,0:T(8,128)(2,1)}, bf16[2,128,128]{2,1,0:T(8,128)(2,1)S(1)}, u32[]{:S(2)}) copy-start(bf16[2,128,128]{2,1,0:T(8,128)(2,1)S(1)} %collective-permute-done.1.rest_2_) | copy-start | bytes 196612
  33.9 30.6 %copy-start.2 = (bf16[2,128,128]{2,1,0:T(8,128)(2,1)}, bf16[2,128,128]{2,1,0:T(8,128)(2,1)S(1)}, u32[]{:S(2)}) copy-start(bf16[2,128,128]{2,1,0:T(8,128)(2,1)S(1)} %collective-permute-done.2.rest_3_) | copy-start | bytes 196612
  34.0 30.5 %copy-start.3 = (bf16[2,128,128]{2,1,0:T(8,128)(2,1)}, bf16[2,128,128]{2,1,0:T(8,128)(2,1)S(1)}, u32[]{:S(2)}) copy-start(bf16[2,128,128]{2,1,0:T(8,128)(2,1)S(1)} %collective-permute-done.3.rest_4_) | copy-start | bytes 196612
  34.0 30.5 %copy-start.4 = (bf16[2,128,128]{2,1,0:T(8,128)(2,1)}, bf16[2,128,128]{2,1,0:T(8,128)(2,1)S(1)}, u32[]{:S(2)}) copy-start(bf16[2,128,128]{2,1,0:T(8,128)(2,1)S(1)} %collective-permute-done.4.rest_5_) | copy-start | bytes 196612
  64.5 7.0 %copy-start.25 = (bf16[2,128,128]{2,1,0:T(8,128)(2,1)S(1)}, bf16[2,128,128]{2,1,0:T(8,128)(2,1)}, u32[]{:S(2)}) copy-start(bf16[2,128,128]{2,1,0:T(8,128)(2,1)} %get-tuple-element.102) | copy-start | bytes 196612
  64.5 9.6 %copy-start.24 = (bf16[2,128,128]{2,1,0:T(8,128)(2,1)S(1)}, bf16[2,128,128]{2,1,0:T(8,128)(2,1)}, u32[]{:S(2)}) copy-start(bf16[2,128,128]{2,1,0:T(8,128)(2,1)} %get-tuple-element.103) | copy-start | bytes 196612
  64.5 12.0 %copy-start.23 = (bf16[2,128,128]{2,1,0:T(8,128)(2,1)S(1)}, bf16[2,128,128]{2,1,0:T(8,128)(2,1)}, u32[]{:S(2)}) copy-start(bf16[2,128,128]{2,1,0:T(8,128)(2,1)} %get-tuple-element.104) | copy-start | bytes 196612
  64.6 14.5 %copy-start.22 = (bf16[2,128,128]{2,1,0:T(8,128)(2,1)S(1)}, bf16[2,128,128]{2,1,0:T(8,128)(2,1)}, u32[]{:S(2)}) copy-start(bf16[2,128,128]{2,1,0:T(8,128)(2,1)} %get-tuple-element.105) | copy-start | bytes 196612
  64.6 16.0 %copy-start.21 = (bf16[2,128,128]{2,1,0:T(8,128)(2,1)S(1)}, bf16[2,128,128]{2,1,0:T(8,128)(2,1)}, u32[]{:S(2)}) copy-start(bf16[2,128,128]{2,1,0:T(8,128)(2,1)} %get-tuple-element.106) | copy-start | bytes 196612
  64.6 17.4 %copy-start.20 = (bf16[2,128,128]{2,1,0:T(8,128)(2,1)S(1)}, bf16[2,128,128]{2,1,0:T(8,128)(2,1)}, u32[]{:S(2)}) copy-start(bf16[2,128,128]{2,1,0:T(8,128)(2,1)} %get-tuple-element.97) | copy-start | bytes 196612
  64.6 19.9 %copy-start.19 = (bf16[2,128,128]{2,1,0:T(8,128)(2,1)S(1)}, bf16[2,128,128]{2,1,0:T(8,128)(2,1)}, u32[]{:S(2)}) copy-start(bf16[2,128,128]{2,1,0:T(8,128)(2,1)} %get-tuple-element.98) | copy-start | bytes 196612
  64.6 24.4 %copy-start.18 = (bf16[2,128,128]{2,1,0:T(8,128)(2,1)S(1)}, bf16[2,128,128]{2,1,0:T(8,128)(2,1)}, u32[]{:S(2)}) copy-start(bf16[2,128,128]{2,1,0:T(8,128)(2,1)} %get-tuple-element.99) | copy-start | bytes 196612
  64.6 29.0 %copy-start.17 = (bf16[2,128,128]{2,1,0:T(8,128)(2,1)S(1)}, bf16[2,128,128]{2,1,0:T(8,128)(2,1)}, u32[]{:S(2)}) copy-start(bf16[2,128,128]{2,1,0:T(8,128)(2,1)} %get-tuple-element.100) | copy-start | bytes 196612
  64.6 30.3 %copy-start.16 = (bf16[2,128,128]{2,1,0:T(8,128)(2,1)S(1)}, bf16[2,128,128]{2,1,0:T(8,128)(2,1)}, u32[]{:S(2)}) copy-start(bf16[2,128,128]{2,1,0:T(8,128)(2,1)} %get-tuple-element.101) | copy-start | bytes 196612
  64.6 41.8 %all-to-all-start = ((f32[16,28,8,128]{3,2,1,0:T(8,128)}), f32[16,28,8,128]{3,2,1,0:T(8,128)S(1)}, u32[]{:S(2)}, u32[]{:S(2)}) async-start(f32[16,28,8,128]{3,2,1,0:T(8,128)} %covariance.1), calls=%async_computation | async-start | bytes 3670016 | tf_op jit(solution)/shard_map/covariance/all_to_all | solution.py:603
  71.5 10.5 %collective-permute-start.10 = (bf16[2,128,128]{2,1,0:T(8,128)(2,1)S(1)}, bf16[2,128,128]{2,1,0:T(8,128)(2,1)S(1)}, u32[]{:S(2)}, u32[]{:S(2)}) collective-permute-start(bf16[2,128,128]{2,1,0:T(8,128)(2,1)S(1)} %copy-done.25), channel_id=1, source_target_pairs={{0,9},{1,8},{2,11},{3,10},{4,13},{5,12},{6,15},{7,14},{8,1},{9,0},... | collective-permute-start | bytes 196616 | tf_op jit(solution)/shard_map/diag/ppermute | solution.py:563
  74.2 10.4 %collective-permute-start.11 = (bf16[2,128,128]{2,1,0:T(8,128)(2,1)S(1)}, bf16[2,128,128]{2,1,0:T(8,128)(2,1)S(1)}, u32[]{:S(2)}, u32[]{:S(2)}) collective-permute-start(bf16[2,128,128]{2,1,0:T(8,128)(2,1)S(1)} %copy-done.24), channel_id=1, source_target_pairs={{0,6},{1,7},{2,8},{3,9},{4,10},{5,11},{6,12},{7,13},{8,14},{9,15},... | collective-permute-start | bytes 196616 | tf_op jit(solution)/shard_map/diag/ppermute | solution.py:563
  76.6 12.4 %collective-permute-start.12 = (bf16[2,128,128]{2,1,0:T(8,128)(2,1)S(1)}, bf16[2,128,128]{2,1,0:T(8,128)(2,1)S(1)}, u32[]{:S(2)}, u32[]{:S(2)}) collective-permute-start(bf16[2,128,128]{2,1,0:T(8,128)(2,1)S(1)} %copy-done.23), channel_id=1, source_target_pairs={{0,7},{1,6},{2,9},{3,8},{4,11},{5,10},{6,13},{7,12},{8,15},{9,14},... | collective-permute-start | bytes 196616 | tf_op jit(solution)/shard_map/diag/ppermute | solution.py:563
  79.1 14.5 %collective-permute-start.13 = (bf16[2,128,128]{2,1,0:T(8,128)(2,1)S(1)}, bf16[2,128,128]{2,1,0:T(8,128)(2,1)S(1)}, u32[]{:S(2)}, u32[]{:S(2)}) collective-permute-start(bf16[2,128,128]{2,1,0:T(8,128)(2,1)S(1)} %copy-done.22), channel_id=1, source_target_pairs={{0,4},{1,5},{2,6},{3,7},{4,8},{5,9},{6,10},{7,11},{8,12},{9,13},{1... | collective-permute-start | bytes 196616 | tf_op jit(solution)/shard_map/diag/ppermute | solution.py:563
  80.5 14.4 %collective-permute-start.14 = (bf16[2,128,128]{2,1,0:T(8,128)(2,1)S(1)}, bf16[2,128,128]{2,1,0:T(8,128)(2,1)S(1)}, u32[]{:S(2)}, u32[]{:S(2)}) collective-permute-start(bf16[2,128,128]{2,1,0:T(8,128)(2,1)S(1)} %copy-done.21), channel_id=1, source_target_pairs={{0,5},{1,4},{2,7},{3,6},{4,9},{5,8},{6,11},{7,10},{8,13},{9,12},{1... | collective-permute-start | bytes 196616 | tf_op jit(solution)/shard_map/diag/ppermute | solution.py:563
  82.0 30.1 %copy-start.5 = (bf16[2,128,128]{2,1,0:T(8,128)(2,1)}, bf16[2,128,128]{2,1,0:T(8,128)(2,1)S(1)}, u32[]{:S(2)}) copy-start(bf16[2,128,128]{2,1,0:T(8,128)(2,1)S(1)} %collective-permute-done.10.rest_11_) | copy-start | bytes 196612
  82.0 18.0 %collective-permute-start.5 = (bf16[2,128,128]{2,1,0:T(8,128)(2,1)S(1)}, bf16[2,128,128]{2,1,0:T(8,128)(2,1)S(1)}, u32[]{:S(2)}, u32[]{:S(2)}) collective-permute-start(bf16[2,128,128]{2,1,0:T(8,128)(2,1)S(1)} %copy-done.20), channel_id=1, source_target_pairs={{0,12},{1,13},{2,14},{3,15},{4,0},{5,1},{6,2},{7,3},{8,4},{9,5},{1... | collective-permute-start | bytes 196616 | tf_op jit(solution)/shard_map/diag/ppermute | solution.py:563
  84.5 27.7 %copy-start.6 = (bf16[2,128,128]{2,1,0:T(8,128)(2,1)}, bf16[2,128,128]{2,1,0:T(8,128)(2,1)S(1)}, u32[]{:S(2)}) copy-start(bf16[2,128,128]{2,1,0:T(8,128)(2,1)S(1)} %collective-permute-done.11.rest_12_) | copy-start | bytes 196612
  84.5 15.5 %collective-permute-start.6 = (bf16[2,128,128]{2,1,0:T(8,128)(2,1)S(1)}, bf16[2,128,128]{2,1,0:T(8,128)(2,1)S(1)}, u32[]{:S(2)}, u32[]{:S(2)}) collective-permute-start(bf16[2,128,128]{2,1,0:T(8,128)(2,1)S(1)} %copy-done.19), channel_id=1, source_target_pairs={{0,13},{1,12},{2,15},{3,14},{4,1},{5,0},{6,3},{7,2},{8,5},{9,4},{1... | collective-permute-start | bytes 196616 | tf_op jit(solution)/shard_map/diag/ppermute | solution.py:563
  89.0 23.2 %copy-start.7 = (bf16[2,128,128]{2,1,0:T(8,128)(2,1)}, bf16[2,128,128]{2,1,0:T(8,128)(2,1)S(1)}, u32[]{:S(2)}) copy-start(bf16[2,128,128]{2,1,0:T(8,128)(2,1)S(1)} %collective-permute-done.12.rest_13_) | copy-start | bytes 196612
  89.0 11.1 %collective-permute-start.7 = (bf16[2,128,128]{2,1,0:T(8,128)(2,1)S(1)}, bf16[2,128,128]{2,1,0:T(8,128)(2,1)S(1)}, u32[]{:S(2)}, u32[]{:S(2)}) collective-permute-start(bf16[2,128,128]{2,1,0:T(8,128)(2,1)S(1)} %copy-done.18), channel_id=1, source_target_pairs={{0,10},{1,11},{2,12},{3,13},{4,14},{5,15},{6,0},{7,1},{8,2},{9,3},... | collective-permute-start | bytes 196616 | tf_op jit(solution)/shard_map/diag/ppermute | solution.py:563
  93.6 18.6 %copy-start.8 = (bf16[2,128,128]{2,1,0:T(8,128)(2,1)}, bf16[2,128,128]{2,1,0:T(8,128)(2,1)S(1)}, u32[]{:S(2)}) copy-start(bf16[2,128,128]{2,1,0:T(8,128)(2,1)S(1)} %collective-permute-done.13.rest_14_) | copy-start | bytes 196612
  93.6 8.4 %collective-permute-start.8 = (bf16[2,128,128]{2,1,0:T(8,128)(2,1)S(1)}, bf16[2,128,128]{2,1,0:T(8,128)(2,1)S(1)}, u32[]{:S(2)}, u32[]{:S(2)}) collective-permute-start(bf16[2,128,128]{2,1,0:T(8,128)(2,1)S(1)} %copy-done.17), channel_id=1, source_target_pairs={{0,11},{1,10},{2,13},{3,12},{4,15},{5,14},{6,1},{7,0},{8,3},{9,2},... | collective-permute-start | bytes 196616 | tf_op jit(solution)/shard_map/diag/ppermute | solution.py:563
  95.0 17.3 %copy-start.9 = (bf16[2,128,128]{2,1,0:T(8,128)(2,1)}, bf16[2,128,128]{2,1,0:T(8,128)(2,1)S(1)}, u32[]{:S(2)}) copy-start(bf16[2,128,128]{2,1,0:T(8,128)(2,1)S(1)} %collective-permute-done.14.rest_15_) | copy-start | bytes 196612
  95.0 11.4 %collective-permute-start.9 = (bf16[2,128,128]{2,1,0:T(8,128)(2,1)S(1)}, bf16[2,128,128]{2,1,0:T(8,128)(2,1)S(1)}, u32[]{:S(2)}, u32[]{:S(2)}) collective-permute-start(bf16[2,128,128]{2,1,0:T(8,128)(2,1)S(1)} %copy-done.16), channel_id=1, source_target_pairs={{0,8},{1,9},{2,10},{3,11},{4,12},{5,13},{6,14},{7,15},{8,0},{9,1},... | collective-permute-start | bytes 196616 | tf_op jit(solution)/shard_map/diag/ppermute | solution.py:563
  100.1 12.2 %copy-start.10 = (bf16[2,128,128]{2,1,0:T(8,128)(2,1)}, bf16[2,128,128]{2,1,0:T(8,128)(2,1)S(1)}, u32[]{:S(2)}) copy-start(bf16[2,128,128]{2,1,0:T(8,128)(2,1)S(1)} %collective-permute-done.5.rest_6_) | copy-start | bytes 196612
  100.1 12.1 %copy-start.11 = (bf16[2,128,128]{2,1,0:T(8,128)(2,1)}, bf16[2,128,128]{2,1,0:T(8,128)(2,1)S(1)}, u32[]{:S(2)}) copy-start(bf16[2,128,128]{2,1,0:T(8,128)(2,1)S(1)} %collective-permute-done.6.rest_7_) | copy-start | bytes 196612
  100.1 12.1 %copy-start.12 = (bf16[2,128,128]{2,1,0:T(8,128)(2,1)}, bf16[2,128,128]{2,1,0:T(8,128)(2,1)S(1)}, u32[]{:S(2)}) copy-start(bf16[2,128,128]{2,1,0:T(8,128)(2,1)S(1)} %collective-permute-done.7.rest_8_) | copy-start | bytes 196612
  102.0 10.3 %copy-start.13 = (bf16[2,128,128]{2,1,0:T(8,128)(2,1)}, bf16[2,128,128]{2,1,0:T(8,128)(2,1)S(1)}, u32[]{:S(2)}) copy-start(bf16[2,128,128]{2,1,0:T(8,128)(2,1)S(1)} %collective-permute-done.8.rest_9_) | copy-start | bytes 196612
  106.4 5.9 %copy-start.14 = (bf16[2,128,128]{2,1,0:T(8,128)(2,1)}, bf16[2,128,128]{2,1,0:T(8,128)(2,1)S(1)}, u32[]{:S(2)}) copy-start(bf16[2,128,128]{2,1,0:T(8,128)(2,1)S(1)} %collective-permute-done.9.rest_10_) | copy-start | bytes 196612
  112.3 14.4 %all-to-all-start.1 = ((f32[16,2,8,128]{3,2,1,0:T(8,128)}), f32[16,2,8,128]{3,2,1,0:T(8,128)S(1)}, u32[]{:S(2)}, u32[]{:S(2)}) async-start(f32[16,2,8,128]{3,2,1,0:T(8,128)} %get-tuple-element.130), calls=%async_computation.1 | async-start | bytes 262144 | tf_op jit(solution)/shard_map/exchange/all_to_all | solution.py:628
  128.0 11.5 %all-to-all-start.2 = ((f32[16,2,8,128]{3,2,1,0:T(8,128)}), f32[16,2,8,128]{3,2,1,0:T(8,128)S(1)}, u32[]{:S(2)}, u32[]{:S(2)}) async-start(f32[16,2,8,128]{3,2,1,0:T(8,128)} %bitcast.10), calls=%async_computation.2 | async-start | bytes 262144 | tf_op jit(solution)/shard_map/exchange/all_to_all | solution.py:637
  160.6 11.5 %all-to-all-start.4 = ((f32[16,2,8,128]{3,2,1,0:T(8,128)}), f32[16,2,8,128]{3,2,1,0:T(8,128)S(1)}, u32[]{:S(2)}, u32[]{:S(2)}) async-start(f32[16,2,8,128]{3,2,1,0:T(8,128)} %bitcast.12), calls=%async_computation.4 | async-start | bytes 262144 | tf_op jit(solution)/shard_map/exchange/all_to_all | solution.py:637
  193.1 11.5 %all-to-all-start.6 = ((f32[16,2,8,128]{3,2,1,0:T(8,128)}), f32[16,2,8,128]{3,2,1,0:T(8,128)S(1)}, u32[]{:S(2)}, u32[]{:S(2)}) async-start(f32[16,2,8,128]{3,2,1,0:T(8,128)} %bitcast.14), calls=%async_computation.6 | async-start | bytes 262144 | tf_op jit(solution)/shard_map/exchange/all_to_all | solution.py:637
Sparse Core Ops, SparseCore 0:
  10.2 44.4 all-gather.1

commit v6 on v5

--- a/solution.py
+++ b/solution.py
@@ -344,42 +344,55 @@
             out.wait(chip_at(dz, col_count))
 
 
-def diagonal_kernel(steps, list_ref, far_base, far_d, col_diag_ref, *rest):
-    far_diag = rest[:-7]
+def diagonal_kernel(steps, half, list_ref, far_base, far_d, col_diag_ref, *rest):
+    far_diag = rest[:len(steps)]
     far_out, base_ref, d_ref, diag_ref, out_ref, diag_sem, sems = rest[-7:]
     slots, size, _ = d_ref.shape
-    chunks = slots // CHUNK
+    chunks = slots // MANY
+    mine = range(half * chunks // 2, (half + 1) * chunks // 2)
     c = lax.axis_index("col")
     per_source = slots // len(far_diag)
-    arrays = [Tiles(far_base, base_ref, sems.at[0]), Tiles(far_d, d_ref, sems.at[1])]
-    out = Tiles(far_out, out_ref, sems.at[2], True)
-
-    def diag_copy(n):
+    arrays = [
+        Tiles(far_d, d_ref, sems.at[1], count=MANY),
+        Tiles(far_base, base_ref, sems.at[0], count=MANY),
+    ]
+    out = Tiles(far_out, out_ref, sems.at[2], True, count=MANY)
+
+    def with_diag(n, use):
         block = far_diag[n]
         place = holder(c, *steps[n], len(far_diag)) * per_source
-        return pltpu.make_async_copy(
-            block.at[:, pl.ds(block.shape[1] - size, size)],
-            diag_ref.at[pl.ds(place, per_source)],
-            diag_sem.at[n],
-        )
+
+        @pl.when(place // (slots // 2) == half)
+        def _():
+            use(pltpu.make_async_copy(
+                block.at[:, pl.ds(block.shape[1] - size, size)],
+                diag_ref.at[pl.ds(place, per_source)],
+                diag_sem.at[n],
+            ))
 
     for n in range(len(far_diag)):
-        diag_copy(n).start()
-    start_all(arrays, chunks)
+        with_diag(n, lambda copy: copy.start())
+    for i in mine:
+        for array in arrays:
+            array.start(i)
     for n in range(len(far_diag)):
-        diag_copy(n).wait()
-
-    def slot_step(slot):
-        d = d_ref[slot]
-        half = dot(diag_ref[slot], jnp.concatenate(split(d), axis=1))
-        half = half[:, :size] + half[:, size:]
-        right = col_diag_ref[list_ref[slot]]
-        both = dot(
-            jnp.concatenate(split(half), axis=1), jnp.concatenate([right, right], axis=0)
-        )
-        out_ref[slot] = base_ref[slot] + d - STEP * both
-
-    each_slot(chunks, arrays, [out], slot_step)
+        with_diag(n, lambda copy: copy.wait())
+    for i in mine:
+        for array in arrays:
+            array.wait(i)
+        slots_here = [i * MANY + s for s in range(MANY)]
+        halves = [
+            dot(diag_ref[slot], jnp.concatenate(split(d_ref[slot]), axis=1))
+            for slot in slots_here
+        ]
+        for slot, x in zip(slots_here, halves):
+            left = jnp.concatenate(split(x[:, :size] + x[:, size:]), axis=1)
+            right = col_diag_ref[list_ref[slot]]
+            both = dot(left, jnp.concatenate([right, right], axis=0))
+            out_ref[slot] = base_ref[slot] + d_ref[slot] - STEP * both
+        out.start(i)
+    for i in mine:
+        out.wait(i)
 
 
 def sum_kernel(same_ref, in_ref, out_ref):
@@ -529,9 +542,9 @@
         far_chips = list(range(1, chips))
         cores = range(CORES)
         steps = [(dz, dk) for dz in near for dk in cores]
-        steps += [(dz, dk) for dz in (1, chips - 1) for dk in cores]
+        steps += [(dz, dk) for dz in (1, chips - 1, 2, chips - 2) for dk in cores]
         early = len(steps)
-        steps += [(dz, dk) for dz in far_chips[1:-1] for dk in cores]
+        steps += [(dz, dk) for dz in far_chips[2:-2] for dk in cores]
         near_count = len(near) * CORES
         block_shapes = [
             (per_source, samples + size if n < near_count else size, size)
@@ -622,11 +635,30 @@
             my_list, live, covariance, far(near_sums), far(theta), far(tiles), far(base), far(d)
         )
 
+    def diagonal(half, base, d, col_diag, before=()):
+        operands = [my_list, far(base), far(d), col_diag]
+        operands += [far(block) for block in got_blocks] + [far(x) for x in before]
+        with jax.named_scope("diagonal"):
+            return pl.pallas_call(
+                functools.partial(diagonal_kernel, steps, half),
+                in_specs=[SMEM, HBM, HBM, VMEM] + [HBM] * (len(operands) - 4),
+                out_specs=HBM,
+                out_shape=tile_out,
+                scratch_shapes=[
+                    tile_vmem, tile_vmem, pltpu.VMEM(tile_shape, BF), tile_vmem,
+                    sems(col_count), sems(3, slots // MANY),
+                ],
+                input_output_aliases={len(operands) - 1: 0} if before else {},
+                compiler_params=PARAMS,
+            )(*operands)
+
     for sweep in range(1, SWEEPS):
         last = sweep == SWEEPS - 1
         with jax.named_scope("exchange"):
+            flat_shape = (row_count * columns, group, size)
             got = lax.all_to_all(pieces, "row", split_axis=0, concat_axis=0, tiled=True)
-            flat_shape = (row_count * columns, group, size)
+            t = diagonal(0, base, d, col_diag)
+            got, t = lax.optimization_barrier((got, t))
             summed = pl.pallas_call(
                 sum_kernel,
                 in_specs=[VMEM, VMEM],
@@ -637,18 +669,8 @@
             q = lax.all_to_all(
                 summed.reshape(piece_shape), "row", split_axis=0, concat_axis=0, tiled=True
             )
-        with jax.named_scope("diagonal"):
-            t = pl.pallas_call(
-                functools.partial(diagonal_kernel, steps),
-                in_specs=[SMEM, HBM, HBM, VMEM] + [HBM] * col_count,
-                out_specs=HBM,
-                out_shape=tile_out,
-                scratch_shapes=[
-                    tile_vmem, tile_vmem, pltpu.VMEM(tile_shape, BF), tile_vmem,
-                    sems(col_count), sems(3, chunks),
-                ],
-                compiler_params=PARAMS,
-            )(my_list, far(base), far(d), col_diag, *[far(block) for block in got_blocks])
+            d, t, _ = lax.optimization_barrier((d, t, summed[0]))
+            t = diagonal(1, base, d, col_diag, (t,))
         with jax.named_scope("sweep"):
             result = pl.pallas_call(
                 functools.partial(sweep_kernel, last),

time: 218 us -> 210 us (0.963)
  blocking collectives: 28.4 us -> 0 us
  waiting for transfers between devices: 41.2 us -> 53.5 us
  starting transfers between devices: 52.3 us -> 56.7 us
  Pallas kernels: 73.7 us -> 77.5 us
    all_to_all x2 -> x0, blocking collectives: 28.4 us -> none  [body(): got = lax.all_to_all(pieces, 'row', split_axis=0, concat_axis=0, tiled=True)]
    all_to_all x3, waiting for transfers between devices: 2.26 us -> 11.1 us  [body(): lax.all_to_all(summed.reshape(piece_shape), 'row', split_axis=0, concat_a...]
    all_to_all x1, waiting for transfers between devices: 0.01 us -> 6.57 us  [body(): lax.all_to_all(partial, 'row', split_axis=0, concat_axis=0, tiled=True)]
    all_gather x1, waiting for transfers between devices: 20.8 us -> 14.2 us  [body(): slices = lax.all_gather(mine, 'col', axis=0, tiled=True)]
    all_to_all x1 -> x3, starting transfers between devices: 6.42 us -> 10.8 us  [body(): got = lax.all_to_all(pieces, 'row', split_axis=0, concat_axis=0, tiled=True)]
    all_to_all x1 -> x3, waiting for transfers between devices: 7.98 us -> 11.6 us  [body(): got = lax.all_to_all(pieces, 'row', split_axis=0, concat_axis=0, tiled=True)]
    pallas_call x3 -> x6, Pallas kernels: 21.5 us -> 24.6 us  [diagonal(): pl.pallas_call(functools.partial(diagonal_kernel, steps, half), in_specs=...]
  transfers between devices with their start and end apart: 21 -> 23, of which waited for: 10 -> 13; matrix products, arithmetic and copies ran while one was open for 3% -> 3% of each run, Pallas kernels for 16% -> 18%
where the time goes in v6:
time: 210 us; the launch traced here: 208 us
  Pallas kernels  77.5 us (37%)
  starting transfers between devices  56.7 us (27%)
  waiting for transfers between devices  53.5 us (25%)
  between operations  13.9 us (7%)
  local copies, waits for them, and re-layouts  5.33 us (3%)
    ppermute x15, starting transfers between devices, send(): return lax.ppermute(blocks_out[n], 'col', pairs_of)  28.4 us
    pallas_call x6, Pallas kernels, diagonal(): pl.pallas_call(functools.partial(diagonal_kernel, steps, half), in_specs=...  24.6 us
    pallas_call x3, Pallas kernels, body(): pl.pallas_call(functools.partial(sweep_kernel, last), in_specs=[SMEM, SME...  17.5 us
    all_gather x1, waiting for transfers between devices, body(): slices = lax.all_gather(mine, 'col', axis=0, tiled=True)  14.2 us
    all_to_all x3, waiting for transfers between devices, body(): got = lax.all_to_all(pieces, 'row', split_axis=0, concat_axis=0, tiled=True)  11.6 us
    all_to_all x3, waiting for transfers between devices, body(): lax.all_to_all(summed.reshape(piece_shape), 'row', split_axis=0, concat_a...  11.1 us
    all_to_all x3, starting transfers between devices, body(): got = lax.all_to_all(pieces, 'row', split_axis=0, concat_axis=0, tiled=True)  10.8 us
    all_to_all x3, starting transfers between devices, body(): lax.all_to_all(summed.reshape(piece_shape), 'row', split_axis=0, concat_a...  10.5 us
  transfers between devices with their start and end apart: 23, of which 13 were waited for; matrix products, arithmetic and copies ran while one was open for 3% of the time, Pallas kernels for 18%

profile of v6, /device:TPU:32, one launch (start us, length us, event | category | flops | bytes accessed | tf_op | source)
XLA Modules:
  0.0 208.3 jit_solution(13312113409947490303)
XLA Ops:
  6.5 3.5 %slices.1 = bf16[32,8,512]{2,1,0:T(8,128)(2,1)} custom-call(bf16[32,512,128]{2,1,0:T(8,128)(2,1)} %features.7), custom_call_target="tpu_custom_call" | custom-call | tf_op jit(solution)/shard_map/slices/pallas_call | solution.py:496
  10.1 0.8 dynamic-slice_subtract_fusion.1
  10.9 0.1 copy.31
  11.0 0.1 copy.28.wanted_ref
  11.0 4.1 %blocks.2 = (bf16[2,640,128]{2,1,0:T(8,128)(2,1)}, bf16[2,640,128]{2,1,0:T(8,128)(2,1)}, bf16[2,128,128]{2,1,0:T(8,128)(2,1)}, bf16[2,128,128]{2,1,0:T(8,128)(2,...) custom-call(s32[16,2]{1,0:T(8,128)S(1)} %copy.28.wanted_ref, ...), custom_call_target="tpu_custom_call" | custom-call | tf_op jit(solution)/shard_map/blocks/pallas_call | solution.py:554
  15.2 0.1 collective-permute-start
  15.3 1.9 collective-permute-start.1
  17.2 3.9 %collective-permute-start.2 = (bf16[2,128,128]{2,1,0:T(8,128)(2,1)}, bf16[2,128,128]{2,1,0:T(8,128)(2,1)S(1)}, u32[]{:S(2)}, u32[]{:S(2)}) collective-permute-start(bf16[2,128,128]{2,1,0:T(8,128)(2,1)} %get-tuple-element.86), channel_id=1, source_target_pairs={{0,15},{1,14},{2,1},{3,0},{4,3},{5,2},{6,5},{7,4},{8,7},{9,6},{10,... | collective-permute-start | bytes 196616 | tf_op jit(solution)/shard_map/blocks/ppermute | solution.py:576
  21.1 0.4 fusion.3
  21.5 0.1 fusion.owned_ref
  21.6 0.1 copy.26
  21.7 1.3 dynamic_slice.26
  23.0 3.9 %split.1.far_pairs = bf16[32,128,256]{2,1,0:T(8,128)(2,1)} custom-call(f32[32,128,128]{2,1,0:T(8,128)} %bitcast.30), custom_call_target="tpu_custom_call" | custom-call | tf_op jit(solution)/shard_map/split/pallas_call | solution.py:531
  26.9 0.1 copy.29.owned_ref
  27.0 0.9 constant_dynamic-slice_fusion.1
  27.9 4.4 %collective-permute-start.5 = (bf16[2,128,128]{2,1,0:T(8,128)(2,1)S(1)}, bf16[2,128,128]{2,1,0:T(8,128)(2,1)S(1)}, u32[]{:S(2)}, u32[]{:S(2)}) collective-permute-start(bf16[2,128,128]{2,1,0:T(8,128)(2,1)S(1)} %copy-done.25), channel_id=1, source_target_pairs={{0,12},{1,13},{2,14},{3,15},{4,0},{5,1},{6,2},{7,3},{8,4},{9,5},{1... | collective-permute-start | bytes 196616 | tf_op jit(solution)/shard_map/blocks/ppermute | solution.py:576
  32.3 0.2 collective-permute-start.6
  32.5 2.7 %collective-permute-start.7 = (bf16[2,128,128]{2,1,0:T(8,128)(2,1)S(1)}, bf16[2,128,128]{2,1,0:T(8,128)(2,1)S(1)}, u32[]{:S(2)}, u32[]{:S(2)}) collective-permute-start(bf16[2,128,128]{2,1,0:T(8,128)(2,1)S(1)} %copy-done.23), channel_id=1, source_target_pairs={{0,4},{1,5},{2,6},{3,7},{4,8},{5,9},{6,10},{7,11},{8,12},{9,13},{1... | collective-permute-start | bytes 196616 | tf_op jit(solution)/shard_map/blocks/ppermute | solution.py:576
  35.2 0.1 collective-permute-start.8
  35.3 0.7 fusion.1.list_ref
  36.0 4.6 %blocks.3 = (f32[32,128,128]{2,1,0:T(8,128)}, f32[32,128,128]{2,1,0:T(8,128)}, f32[2,128,256]{2,1,0:T(8,128)}) custom-call(s32[32]{0:T(128)S(1)} %fusion.1.list_ref, s32[1]{0:T(128)} %bitcast.1.live_ref, s32[2]{0:T(128)S(1)} %fusion.owned_ref, bf16[32,512,128]{2,1,0:T(8,128)(2,1)} %features.7, f32[32,128,128]{2,1,0:T(8,128)} %bitcast.25, ...), custom_call_target="tpu_custom_call" | custom-call | tf_op jit(solution)/shard_map/blocks/pallas_call | solution.py:579
  40.6 0.1 collective-permute-done.6.rest_7_
  40.8 0.9 collective-permute-done.7.rest_8_
  41.7 3.4 %collective-permute-done.8.rest_9_ = bf16[2,128,128]{2,1,0:T(8,128)(2,1)S(1)} collective-permute-done((bf16[2,128,128]{2,1,0:T(8,128)(2,1)S(1)}, bf16[2,128,128]{2,1,0:T(8,128)(2,1)S(1)}, u32[]{:S(2)}, u32[]{:S(2)}) %collective-permute-start.8) | collective-permute-done | bytes 65568 | tf_op jit(solution)/shard_map/blocks/ppermute | solution.py:576
  45.1 14.2 %all-gather.2.cloned.1.call-done.far_slices = bf16[512,8,512]{2,1,0:T(8,128)(2,1)} async-done(((bf16[32,8,512]{2,1,0:T(8,128)(2,1)}), bf16[512,8,512]{2,1,0:T(8,128)(2,1)}) %all-gather.2.cloned.1.call-update) | async-done | bytes 4194320 | tf_op jit(solution)/shard_map/slices/all_gather | solution.py:506
  59.4 9.7 %covariance.1 = f32[16,28,8,128]{3,2,1,0:T(8,128)} custom-call(s32[16,32]{1,0:T(8,128)S(1)} %bitcast.24, s32[16,32]{1,0:T(8,128)S(1)} %bitcast.23, s32[16,2]{1,0:T(8,128)S(1)} %copy.29.owned_ref, bf16[512,8,512]{2,1,0:T(8,128)(2,1)} %all-gather.2.cloned.1.call-done.far_slices, bf16[32,512,128]{2,1,0:T(8,128)(2,1)} %features.7), custom_call_target="tpu_custom_call" | custom-call | tf_op jit(solution)/shard_map/covariance/pallas_call | solution.py:601
  69.2 7.0 %all-to-all-start = ((f32[16,28,8,128]{3,2,1,0:T(8,128)}), f32[16,28,8,128]{3,2,1,0:T(8,128)S(1)}, u32[]{:S(2)}, u32[]{:S(2)}) async-start(f32[16,28,8,128]{3,2,1,0:T(8,128)} %covariance.1), calls=%async_computation | async-start | bytes 3670016 | tf_op jit(solution)/shard_map/covariance/all_to_all | solution.py:616
  76.2 2.1 collective-permute-start.10
  78.3 3.1 %collective-permute-start.11 = (bf16[2,128,128]{2,1,0:T(8,128)(2,1)S(1)}, bf16[2,128,128]{2,1,0:T(8,128)(2,1)S(1)}, u32[]{:S(2)}, u32[]{:S(2)}) collective-permute-start(bf16[2,128,128]{2,1,0:T(8,128)(2,1)S(1)} %copy-done.20), channel_id=1, source_target_pairs={{0,8},{1,9},{2,10},{3,11},{4,12},{5,13},{6,14},{7,15},{8,0},{9,1},... | collective-permute-start | bytes 196616 | tf_op jit(solution)/shard_map/diag/ppermute | solution.py:576
  81.4 2.7 %collective-permute-start.12 = (bf16[2,128,128]{2,1,0:T(8,128)(2,1)S(1)}, bf16[2,128,128]{2,1,0:T(8,128)(2,1)S(1)}, u32[]{:S(2)}, u32[]{:S(2)}) collective-permute-start(bf16[2,128,128]{2,1,0:T(8,128)(2,1)S(1)} %copy-done.19), channel_id=1, source_target_pairs={{0,9},{1,8},{2,11},{3,10},{4,13},{5,12},{6,15},{7,14},{8,1},{9,0},... | collective-permute-start | bytes 196616 | tf_op jit(solution)/shard_map/diag/ppermute | solution.py:576
  84.1 2.6 %collective-permute-start.13 = (bf16[2,128,128]{2,1,0:T(8,128)(2,1)S(1)}, bf16[2,128,128]{2,1,0:T(8,128)(2,1)S(1)}, u32[]{:S(2)}, u32[]{:S(2)}) collective-permute-start(bf16[2,128,128]{2,1,0:T(8,128)(2,1)S(1)} %copy-done.18), channel_id=1, source_target_pairs={{0,6},{1,7},{2,8},{3,9},{4,10},{5,11},{6,12},{7,13},{8,14},{9,15},... | collective-permute-start | bytes 196616 | tf_op jit(solution)/shard_map/diag/ppermute | solution.py:576
  86.7 0.7 collective-permute-start.14
  87.4 1.8 gather_fusion
  89.3 4.0 %collective-permute-start.9 = (bf16[2,128,128]{2,1,0:T(8,128)(2,1)S(1)}, bf16[2,128,128]{2,1,0:T(8,128)(2,1)S(1)}, u32[]{:S(2)}, u32[]{:S(2)}) collective-permute-start(bf16[2,128,128]{2,1,0:T(8,128)(2,1)S(1)} %copy-done.16), channel_id=1, source_target_pairs={{0,10},{1,11},{2,12},{3,13},{4,14},{5,15},{6,0},{7,1},{8,2},{9,3},... | collective-permute-start | bytes 196616 | tf_op jit(solution)/shard_map/diag/ppermute | solution.py:576
  93.3 0.1 broadcast_select_fusion.col_diag_ref
  93.3 0.1 sub.25
  93.5 1.1 collective-permute-done.13.rest_14_
  94.6 4.3 %collective-permute-done.14.rest_15_ = bf16[2,128,128]{2,1,0:T(8,128)(2,1)S(1)} collective-permute-done((bf16[2,128,128]{2,1,0:T(8,128)(2,1)S(1)}, bf16[2,128,128]{2,1,0:T(8,128)(2,1)S(1)}, u32[]{:S(2)}, u32[]{:S(2)}) %collective-permute-start.14) | collective-permute-done | bytes 65568 | tf_op jit(solution)/shard_map/diag/ppermute | solution.py:576
  98.9 6.6 %all-to-all-done.cov_ref = f32[16,28,8,128]{3,2,1,0:T(8,128)S(1)} async-done(((f32[16,28,8,128]{3,2,1,0:T(8,128)}), f32[16,28,8,128]{3,2,1,0:T(8,128)S(1)}, u32[]{:S(2)}, u32[]{:S(2)}) %all-to-all-start) | async-done | bytes 1835040 | tf_op jit(solution)/shard_map/covariance/all_to_all | solution.py:616
  105.5 5.6 %first.1 = (f32[32,128,128]{2,1,0:T(8,128)}, f32[32,128,128]{2,1,0:T(8,128)}, f32[16,2,8,128]{3,2,1,0:T(8,128)}) custom-call(s32[32]{0:T(128)S(1)} %fusion.1.list_ref, s32[1]{0:T(128)} %bitcast.1.live_ref, f32[16,28,8,128]{3,2,1,0:T(8,128)S(1)} %all-to-all-done.cov_ref, ...), custom_call_target="tpu_custom_call", output_to_operand_aliasing={{0}: (6, {}), {1}: (7, {})} | custom-call | tf_op jit(solution)/shard_map/first/pallas_call | solution.py:624
  111.1 3.5 %all-to-all-start.1 = ((f32[16,2,8,128]{3,2,1,0:T(8,128)}), f32[16,2,8,128]{3,2,1,0:T(8,128)S(1)}, u32[]{:S(2)}, u32[]{:S(2)}) async-start(f32[16,2,8,128]{3,2,1,0:T(8,128)} %get-tuple-element.125), calls=%async_computation.1 | async-start | bytes 262144 | tf_op jit(solution)/shard_map/exchange/all_to_all | solution.py:659
  114.7 4.0 %diagonal.6.rest_16_ = f32[32,128,128]{2,1,0:T(8,128)} custom-call(s32[32]{0:T(128)S(1)} %fusion.1.list_ref, f32[32,128,128]{2,1,0:T(8,128)} %get-tuple-element.123.far_base, f32[32,128,128]{2,1,0:T(8,128)} %get-tuple-element.143.far_d, bf16[2,128,128]{2,1,0:T(8,128)(2,1)S(1)} %broadcast_select_fusion.col_diag_ref, ...), custom_call_target="tpu_custom_call" | custom-call | tf_op jit(solution)/shard_map/exchange/diagonal/pallas_call | solution.py:642
  118.7 3.9 %all-to-all-done.1 = f32[16,2,8,128]{3,2,1,0:T(8,128)S(1)} async-done(((f32[16,2,8,128]{3,2,1,0:T(8,128)}), f32[16,2,8,128]{3,2,1,0:T(8,128)S(1)}, u32[]{:S(2)}, u32[]{:S(2)}) %all-to-all-start.1) | async-done | bytes 131104 | tf_op jit(solution)/shard_map/exchange/all_to_all | solution.py:659
  122.6 1.3 exchange.3
  123.9 3.5 %all-to-all-start.2 = ((f32[16,2,8,128]{3,2,1,0:T(8,128)}), f32[16,2,8,128]{3,2,1,0:T(8,128)S(1)}, u32[]{:S(2)}, u32[]{:S(2)}) async-start(f32[16,2,8,128]{3,2,1,0:T(8,128)} %bitcast.10), calls=%async_computation.2 | async-start | bytes 262144 | tf_op jit(solution)/shard_map/exchange/all_to_all | solution.py:669
  127.5 4.2 %diagonal.7.far_t = f32[32,128,128]{2,1,0:T(8,128)} custom-call(s32[32]{0:T(128)S(1)} %fusion.1.list_ref, f32[32,128,128]{2,1,0:T(8,128)} %get-tuple-element.123.far_base, f32[32,128,128]{2,1,0:T(8,128)} %get-tuple-element.143.far_d, bf16[2,128,128]{2,1,0:T(8,128)(2,1)S(1)} %broadcast_select_fusion.col_diag_ref, ...), custom_call_target="tpu_custom_call", output_to_operand_aliasing={{}: (20, {})} | custom-call | tf_op jit(solution)/shard_map/exchange/diagonal/pallas_call | solution.py:642
  131.7 3.7 %all-to-all-done.2.q_ref = f32[16,2,8,128]{3,2,1,0:T(8,128)S(1)} async-done(((f32[16,2,8,128]{3,2,1,0:T(8,128)}), f32[16,2,8,128]{3,2,1,0:T(8,128)S(1)}, u32[]{:S(2)}, u32[]{:S(2)}) %all-to-all-start.2) | async-done | bytes 131104 | tf_op jit(solution)/shard_map/exchange/all_to_all | solution.py:669
  135.4 6.1 %sweep.3 = (f32[32,128,128]{2,1,0:T(8,128)}, f32[16,2,8,128]{3,2,1,0:T(8,128)}) custom-call(s32[32]{0:T(128)S(1)} %fusion.1.list_ref, s32[1]{0:T(128)} %bitcast.1.live_ref, f32[32,128,128]{2,1,0:T(8,128)} %diagonal.7.far_t, f32[32,128,128]{2,1,0:T(8,128)} %bitcast.27, bf16[32,128,256]{2,1,0:T(8,128)(2,1)} %split.1.far_pairs, ...), custom_call_target="tpu_custom_call" | custom-call | tf_op jit(solution)/shard_map/sweep/pallas_call | solution.py:675
  141.5 3.5 %all-to-all-start.3 = ((f32[16,2,8,128]{3,2,1,0:T(8,128)}), f32[16,2,8,128]{3,2,1,0:T(8,128)S(1)}, u32[]{:S(2)}, u32[]{:S(2)}) async-start(f32[16,2,8,128]{3,2,1,0:T(8,128)} %get-tuple-element.148), calls=%async_computation.3 | async-start | bytes 262144 | tf_op jit(solution)/shard_map/exchange/all_to_all | solution.py:659
  145.0 4.0 %diagonal.8.rest_16_ = f32[32,128,128]{2,1,0:T(8,128)} custom-call(s32[32]{0:T(128)S(1)} %fusion.1.list_ref, f32[32,128,128]{2,1,0:T(8,128)} %get-tuple-element.123.far_base, f32[32,128,128]{2,1,0:T(8,128)} %get-tuple-element.150.far_d, bf16[2,128,128]{2,1,0:T(8,128)(2,1)S(1)} %broadcast_select_fusion.col_diag_ref, ...), custom_call_target="tpu_custom_call" | custom-call | tf_op jit(solution)/shard_map/exchange/diagonal/pallas_call | solution.py:642
  149.0 4.0 %all-to-all-done.3 = f32[16,2,8,128]{3,2,1,0:T(8,128)S(1)} async-done(((f32[16,2,8,128]{3,2,1,0:T(8,128)}), f32[16,2,8,128]{3,2,1,0:T(8,128)S(1)}, u32[]{:S(2)}, u32[]{:S(2)}) %all-to-all-start.3) | async-done | bytes 131104 | tf_op jit(solution)/shard_map/exchange/all_to_all | solution.py:659
  153.0 1.3 exchange.4
  154.3 3.5 %all-to-all-start.4 = ((f32[16,2,8,128]{3,2,1,0:T(8,128)}), f32[16,2,8,128]{3,2,1,0:T(8,128)S(1)}, u32[]{:S(2)}, u32[]{:S(2)}) async-start(f32[16,2,8,128]{3,2,1,0:T(8,128)} %bitcast.12), calls=%async_computation.4 | async-start | bytes 262144 | tf_op jit(solution)/shard_map/exchange/all_to_all | solution.py:669
  157.8 4.2 %diagonal.9.far_t = f32[32,128,128]{2,1,0:T(8,128)} custom-call(s32[32]{0:T(128)S(1)} %fusion.1.list_ref, f32[32,128,128]{2,1,0:T(8,128)} %get-tuple-element.123.far_base, f32[32,128,128]{2,1,0:T(8,128)} %get-tuple-element.150.far_d, bf16[2,128,128]{2,1,0:T(8,128)(2,1)S(1)} %broadcast_select_fusion.col_diag_ref, ...), custom_call_target="tpu_custom_call", output_to_operand_aliasing={{}: (20, {})} | custom-call | tf_op jit(solution)/shard_map/exchange/diagonal/pallas_call | solution.py:642
  162.1 3.7 %all-to-all-done.4.q_ref = f32[16,2,8,128]{3,2,1,0:T(8,128)S(1)} async-done(((f32[16,2,8,128]{3,2,1,0:T(8,128)}), f32[16,2,8,128]{3,2,1,0:T(8,128)S(1)}, u32[]{:S(2)}, u32[]{:S(2)}) %all-to-all-start.4) | async-done | bytes 131104 | tf_op jit(solution)/shard_map/exchange/all_to_all | solution.py:669
  165.8 6.1 %sweep.4 = (f32[32,128,128]{2,1,0:T(8,128)}, f32[16,2,8,128]{3,2,1,0:T(8,128)}) custom-call(s32[32]{0:T(128)S(1)} %fusion.1.list_ref, s32[1]{0:T(128)} %bitcast.1.live_ref, f32[32,128,128]{2,1,0:T(8,128)} %diagonal.9.far_t, f32[32,128,128]{2,1,0:T(8,128)} %bitcast.28, bf16[32,128,256]{2,1,0:T(8,128)(2,1)} %split.1.far_pairs, ...), custom_call_target="tpu_custom_call" | custom-call | tf_op jit(solution)/shard_map/sweep/pallas_call | solution.py:675
  171.9 3.7 %all-to-all-start.5 = ((f32[16,2,8,128]{3,2,1,0:T(8,128)}), f32[16,2,8,128]{3,2,1,0:T(8,128)S(1)}, u32[]{:S(2)}, u32[]{:S(2)}) async-start(f32[16,2,8,128]{3,2,1,0:T(8,128)} %get-tuple-element.154), calls=%async_computation.5 | async-start | bytes 262144 | tf_op jit(solution)/shard_map/exchange/all_to_all | solution.py:659
  175.6 4.0 %diagonal.10.rest_16_ = f32[32,128,128]{2,1,0:T(8,128)} custom-call(s32[32]{0:T(128)S(1)} %fusion.1.list_ref, f32[32,128,128]{2,1,0:T(8,128)} %get-tuple-element.123.far_base, f32[32,128,128]{2,1,0:T(8,128)} %get-tuple-element.156.far_d, bf16[2,128,128]{2,1,0:T(8,128)(2,1)S(1)} %broadcast_select_fusion.col_diag_ref, ...), custom_call_target="tpu_custom_call" | custom-call | tf_op jit(solution)/shard_map/exchange/diagonal/pallas_call | solution.py:642
  179.6 3.7 %all-to-all-done.5 = f32[16,2,8,128]{3,2,1,0:T(8,128)S(1)} async-done(((f32[16,2,8,128]{3,2,1,0:T(8,128)}), f32[16,2,8,128]{3,2,1,0:T(8,128)S(1)}, u32[]{:S(2)}, u32[]{:S(2)}) %all-to-all-start.5) | async-done | bytes 131104 | tf_op jit(solution)/shard_map/exchange/all_to_all | solution.py:659
  183.4 1.3 exchange.5
  184.7 3.5 %all-to-all-start.6 = ((f32[16,2,8,128]{3,2,1,0:T(8,128)}), f32[16,2,8,128]{3,2,1,0:T(8,128)S(1)}, u32[]{:S(2)}, u32[]{:S(2)}) async-start(f32[16,2,8,128]{3,2,1,0:T(8,128)} %bitcast.14), calls=%async_computation.6 | async-start | bytes 262144 | tf_op jit(solution)/shard_map/exchange/all_to_all | solution.py:669
  188.2 4.2 %diagonal.11.far_t = f32[32,128,128]{2,1,0:T(8,128)} custom-call(s32[32]{0:T(128)S(1)} %fusion.1.list_ref, f32[32,128,128]{2,1,0:T(8,128)} %get-tuple-element.123.far_base, f32[32,128,128]{2,1,0:T(8,128)} %get-tuple-element.156.far_d, bf16[2,128,128]{2,1,0:T(8,128)(2,1)S(1)} %broadcast_select_fusion.col_diag_ref, ...), custom_call_target="tpu_custom_call", output_to_operand_aliasing={{}: (20, {})} | custom-call | tf_op jit(solution)/shard_map/exchange/diagonal/pallas_call | solution.py:642
  192.5 3.7 %all-to-all-done.6.q_ref = f32[16,2,8,128]{3,2,1,0:T(8,128)S(1)} async-done(((f32[16,2,8,128]{3,2,1,0:T(8,128)}), f32[16,2,8,128]{3,2,1,0:T(8,128)S(1)}, u32[]{:S(2)}, u32[]{:S(2)}) %all-to-all-start.6) | async-done | bytes 131104 | tf_op jit(solution)/shard_map/exchange/all_to_all | solution.py:669
  196.2 5.3 %sweep.5 = f32[32,128,128]{2,1,0:T(8,128)} custom-call(s32[32]{0:T(128)S(1)} %fusion.1.list_ref, s32[1]{0:T(128)} %bitcast.1.live_ref, f32[32,128,128]{2,1,0:T(8,128)} %diagonal.11.far_t, f32[32,128,128]{2,1,0:T(8,128)} %bitcast.29, bf16[32,128,256]{2,1,0:T(8,128)(2,1)} %split.1.far_pairs, f32[16,2,8,128]{3,2,1,0:T(8,128)S(1)} %all-to-all-done.6.q_ref), custom_call_target="tpu_custom_call" | custom-call | tf_op jit(solution)/shard_map/sweep/pallas_call | solution.py:675
  (70 shorter events, 0.2 us)
Async XLA Ops:
  6.5 52.8 %all-gather.2.cloned.1.call-start = ((), (), s32[]{:S(2)}) async-start(), calls=%async_computation.7 | async-start | bytes 4456448 | tf_op jit(solution)/shard_map/slices/all_gather | solution.py:506
  11.0 10.0 %copy-start.15 = (s32[16,16,2]{1,2,0:T(2,128)S(1)}, s32[16,16,2]{1,2,0:T(2,128)}, u32[]{:S(2)}) copy-start(s32[16,16,2]{1,2,0:T(2,128)} %param.14) | copy-start | bytes 6148
  15.2 20.0 %collective-permute-start = (bf16[2,640,128]{2,1,0:T(8,128)(2,1)}, bf16[2,640,128]{2,1,0:T(8,128)(2,1)S(1)}, u32[]{:S(2)}, u32[]{:S(2)}) collective-permute-start(bf16[2,640,128]{2,1,0:T(8,128)(2,1)} %get-tuple-element.84), channel_id=1, source_target_pairs={{0,1},{1,0},{2,3},{3,2},{4,5},{5,4},{6,7},{7,6},{8,9},{9,8},{10,11... | collective-permute-start | bytes 983048 | tf_op jit(solution)/shard_map/blocks/ppermute | solution.py:576
  15.3 12.6 %collective-permute-start.1 = (bf16[2,128,128]{2,1,0:T(8,128)(2,1)}, bf16[2,128,128]{2,1,0:T(8,128)(2,1)S(1)}, u32[]{:S(2)}, u32[]{:S(2)}) collective-permute-start(bf16[2,128,128]{2,1,0:T(8,128)(2,1)} %get-tuple-element.85), channel_id=1, source_target_pairs={{0,14},{1,15},{2,0},{3,1},{4,2},{5,3},{6,4},{7,5},{8,6},{9,7},{10,... | collective-permute-start | bytes 196616 | tf_op jit(solution)/shard_map/blocks/ppermute | solution.py:576
  17.2 15.2 %collective-permute-start.2 = (bf16[2,128,128]{2,1,0:T(8,128)(2,1)}, bf16[2,128,128]{2,1,0:T(8,128)(2,1)S(1)}, u32[]{:S(2)}, u32[]{:S(2)}) collective-permute-start(bf16[2,128,128]{2,1,0:T(8,128)(2,1)} %get-tuple-element.86), channel_id=1, source_target_pairs={{0,15},{1,14},{2,1},{3,0},{4,3},{5,2},{6,5},{7,4},{8,7},{9,6},{10,... | collective-permute-start | bytes 196616 | tf_op jit(solution)/shard_map/blocks/ppermute | solution.py:576
  21.0 11.5 %collective-permute-start.3 = (bf16[2,128,128]{2,1,0:T(8,128)(2,1)}, bf16[2,128,128]{2,1,0:T(8,128)(2,1)S(1)}, u32[]{:S(2)}, u32[]{:S(2)}) collective-permute-start(bf16[2,128,128]{2,1,0:T(8,128)(2,1)} %get-tuple-element.87), channel_id=1, source_target_pairs={{0,2},{1,3},{2,4},{3,5},{4,6},{5,7},{6,8},{7,9},{8,10},{9,11},{10,... | collective-permute-start | bytes 196616 | tf_op jit(solution)/shard_map/blocks/ppermute | solution.py:576
  21.0 19.6 %collective-permute-start.4 = (bf16[2,128,128]{2,1,0:T(8,128)(2,1)}, bf16[2,128,128]{2,1,0:T(8,128)(2,1)S(1)}, u32[]{:S(2)}, u32[]{:S(2)}) collective-permute-start(bf16[2,128,128]{2,1,0:T(8,128)(2,1)} %get-tuple-element.88), channel_id=1, source_target_pairs={{0,3},{1,2},{2,5},{3,4},{4,7},{5,6},{6,9},{7,8},{8,11},{9,10},{10,... | collective-permute-start | bytes 196616 | tf_op jit(solution)/shard_map/blocks/ppermute | solution.py:576
  23.0 4.9 %copy-start.25 = (bf16[2,128,128]{2,1,0:T(8,128)(2,1)S(1)}, bf16[2,128,128]{2,1,0:T(8,128)(2,1)}, u32[]{:S(2)}) copy-start(bf16[2,128,128]{2,1,0:T(8,128)(2,1)} %get-tuple-element.89) | copy-start | bytes 196612
  23.0 9.4 %copy-start.24 = (bf16[2,128,128]{2,1,0:T(8,128)(2,1)S(1)}, bf16[2,128,128]{2,1,0:T(8,128)(2,1)}, u32[]{:S(2)}) copy-start(bf16[2,128,128]{2,1,0:T(8,128)(2,1)} %get-tuple-element.90) | copy-start | bytes 196612
  23.0 9.5 %copy-start.23 = (bf16[2,128,128]{2,1,0:T(8,128)(2,1)S(1)}, bf16[2,128,128]{2,1,0:T(8,128)(2,1)}, u32[]{:S(2)}) copy-start(bf16[2,128,128]{2,1,0:T(8,128)(2,1)} %get-tuple-element.91) | copy-start | bytes 196612
  23.0 12.2 %copy-start.22 = (bf16[2,128,128]{2,1,0:T(8,128)(2,1)S(1)}, bf16[2,128,128]{2,1,0:T(8,128)(2,1)}, u32[]{:S(2)}) copy-start(bf16[2,128,128]{2,1,0:T(8,128)(2,1)} %get-tuple-element.92) | copy-start | bytes 196612
  27.9 41.2 %copy-start.1 = (bf16[2,128,128]{2,1,0:T(8,128)(2,1)}, bf16[2,128,128]{2,1,0:T(8,128)(2,1)S(1)}, u32[]{:S(2)}) copy-start(bf16[2,128,128]{2,1,0:T(8,128)(2,1)S(1)} %collective-permute-done.1.rest_2_) | copy-start | bytes 196612
  27.9 12.7 %collective-permute-start.5 = (bf16[2,128,128]{2,1,0:T(8,128)(2,1)S(1)}, bf16[2,128,128]{2,1,0:T(8,128)(2,1)S(1)}, u32[]{:S(2)}, u32[]{:S(2)}) collective-permute-start(bf16[2,128,128]{2,1,0:T(8,128)(2,1)S(1)} %copy-done.25), channel_id=1, source_target_pairs={{0,12},{1,13},{2,14},{3,15},{4,0},{5,1},{6,2},{7,3},{8,4},{9,5},{1... | collective-permute-start | bytes 196616 | tf_op jit(solution)/shard_map/blocks/ppermute | solution.py:576
  32.3 36.8 %copy-start.2 = (bf16[2,128,128]{2,1,0:T(8,128)(2,1)}, bf16[2,128,128]{2,1,0:T(8,128)(2,1)S(1)}, u32[]{:S(2)}) copy-start(bf16[2,128,128]{2,1,0:T(8,128)(2,1)S(1)} %collective-permute-done.2.rest_3_) | copy-start | bytes 196612
  32.3 8.4 %collective-permute-start.6 = (bf16[2,128,128]{2,1,0:T(8,128)(2,1)S(1)}, bf16[2,128,128]{2,1,0:T(8,128)(2,1)S(1)}, u32[]{:S(2)}, u32[]{:S(2)}) collective-permute-start(bf16[2,128,128]{2,1,0:T(8,128)(2,1)S(1)} %copy-done.24), channel_id=1, source_target_pairs={{0,13},{1,12},{2,15},{3,14},{4,1},{5,0},{6,3},{7,2},{8,5},{9,4},{1... | collective-permute-start | bytes 196616 | tf_op jit(solution)/shard_map/blocks/ppermute | solution.py:576
  32.5 36.6 %copy-start.3 = (bf16[2,128,128]{2,1,0:T(8,128)(2,1)}, bf16[2,128,128]{2,1,0:T(8,128)(2,1)S(1)}, u32[]{:S(2)}) copy-start(bf16[2,128,128]{2,1,0:T(8,128)(2,1)S(1)} %collective-permute-done.3.rest_4_) | copy-start | bytes 196612
  32.5 9.2 %collective-permute-start.7 = (bf16[2,128,128]{2,1,0:T(8,128)(2,1)S(1)}, bf16[2,128,128]{2,1,0:T(8,128)(2,1)S(1)}, u32[]{:S(2)}, u32[]{:S(2)}) collective-permute-start(bf16[2,128,128]{2,1,0:T(8,128)(2,1)S(1)} %copy-done.23), channel_id=1, source_target_pairs={{0,4},{1,5},{2,6},{3,7},{4,8},{5,9},{6,10},{7,11},{8,12},{9,13},{1... | collective-permute-start | bytes 196616 | tf_op jit(solution)/shard_map/blocks/ppermute | solution.py:576
  35.2 0.8 copy-start
  35.2 9.9 %collective-permute-start.8 = (bf16[2,128,128]{2,1,0:T(8,128)(2,1)S(1)}, bf16[2,128,128]{2,1,0:T(8,128)(2,1)S(1)}, u32[]{:S(2)}, u32[]{:S(2)}) collective-permute-start(bf16[2,128,128]{2,1,0:T(8,128)(2,1)S(1)} %copy-done.22), channel_id=1, source_target_pairs={{0,5},{1,4},{2,7},{3,6},{4,9},{5,8},{6,11},{7,10},{8,13},{9,12},{1... | collective-permute-start | bytes 196616 | tf_op jit(solution)/shard_map/blocks/ppermute | solution.py:576
  40.6 28.5 %copy-start.4 = (bf16[2,128,128]{2,1,0:T(8,128)(2,1)}, bf16[2,128,128]{2,1,0:T(8,128)(2,1)S(1)}, u32[]{:S(2)}) copy-start(bf16[2,128,128]{2,1,0:T(8,128)(2,1)S(1)} %collective-permute-done.4.rest_5_) | copy-start | bytes 196612
  40.6 28.5 %copy-start.5 = (bf16[2,128,128]{2,1,0:T(8,128)(2,1)}, bf16[2,128,128]{2,1,0:T(8,128)(2,1)S(1)}, u32[]{:S(2)}) copy-start(bf16[2,128,128]{2,1,0:T(8,128)(2,1)S(1)} %collective-permute-done.5.rest_6_) | copy-start | bytes 196612
  40.8 28.4 %copy-start.6 = (bf16[2,128,128]{2,1,0:T(8,128)(2,1)}, bf16[2,128,128]{2,1,0:T(8,128)(2,1)S(1)}, u32[]{:S(2)}) copy-start(bf16[2,128,128]{2,1,0:T(8,128)(2,1)S(1)} %collective-permute-done.6.rest_7_) | copy-start | bytes 196612
  41.7 27.4 %copy-start.7 = (bf16[2,128,128]{2,1,0:T(8,128)(2,1)}, bf16[2,128,128]{2,1,0:T(8,128)(2,1)S(1)}, u32[]{:S(2)}) copy-start(bf16[2,128,128]{2,1,0:T(8,128)(2,1)S(1)} %collective-permute-done.7.rest_8_) | copy-start | bytes 196612
  45.1 24.0 %copy-start.8 = (bf16[2,128,128]{2,1,0:T(8,128)(2,1)}, bf16[2,128,128]{2,1,0:T(8,128)(2,1)S(1)}, u32[]{:S(2)}) copy-start(bf16[2,128,128]{2,1,0:T(8,128)(2,1)S(1)} %collective-permute-done.8.rest_9_) | copy-start | bytes 196612
  69.2 7.0 %copy-start.21 = (bf16[2,128,128]{2,1,0:T(8,128)(2,1)S(1)}, bf16[2,128,128]{2,1,0:T(8,128)(2,1)}, u32[]{:S(2)}) copy-start(bf16[2,128,128]{2,1,0:T(8,128)(2,1)} %get-tuple-element.114) | copy-start | bytes 196612
  69.2 9.1 %copy-start.20 = (bf16[2,128,128]{2,1,0:T(8,128)(2,1)S(1)}, bf16[2,128,128]{2,1,0:T(8,128)(2,1)}, u32[]{:S(2)}) copy-start(bf16[2,128,128]{2,1,0:T(8,128)(2,1)} %get-tuple-element.115) | copy-start | bytes 196612
  69.2 12.2 %copy-start.19 = (bf16[2,128,128]{2,1,0:T(8,128)(2,1)S(1)}, bf16[2,128,128]{2,1,0:T(8,128)(2,1)}, u32[]{:S(2)}) copy-start(bf16[2,128,128]{2,1,0:T(8,128)(2,1)} %get-tuple-element.116) | copy-start | bytes 196612
  69.2 14.9 %copy-start.18 = (bf16[2,128,128]{2,1,0:T(8,128)(2,1)S(1)}, bf16[2,128,128]{2,1,0:T(8,128)(2,1)}, u32[]{:S(2)}) copy-start(bf16[2,128,128]{2,1,0:T(8,128)(2,1)} %get-tuple-element.117) | copy-start | bytes 196612
  69.2 17.5 %copy-start.17 = (bf16[2,128,128]{2,1,0:T(8,128)(2,1)S(1)}, bf16[2,128,128]{2,1,0:T(8,128)(2,1)}, u32[]{:S(2)}) copy-start(bf16[2,128,128]{2,1,0:T(8,128)(2,1)} %get-tuple-element.118) | copy-start | bytes 196612
  69.2 20.0 %copy-start.16 = (bf16[2,128,128]{2,1,0:T(8,128)(2,1)S(1)}, bf16[2,128,128]{2,1,0:T(8,128)(2,1)}, u32[]{:S(2)}) copy-start(bf16[2,128,128]{2,1,0:T(8,128)(2,1)} %get-tuple-element.113) | copy-start | bytes 196612
  69.2 36.2 %all-to-all-start = ((f32[16,28,8,128]{3,2,1,0:T(8,128)}), f32[16,28,8,128]{3,2,1,0:T(8,128)S(1)}, u32[]{:S(2)}, u32[]{:S(2)}) async-start(f32[16,28,8,128]{3,2,1,0:T(8,128)} %covariance.1), calls=%async_computation | async-start | bytes 3670016 | tf_op jit(solution)/shard_map/covariance/all_to_all | solution.py:616
  76.2 13.0 %collective-permute-start.10 = (bf16[2,128,128]{2,1,0:T(8,128)(2,1)S(1)}, bf16[2,128,128]{2,1,0:T(8,128)(2,1)S(1)}, u32[]{:S(2)}, u32[]{:S(2)}) collective-permute-start(bf16[2,128,128]{2,1,0:T(8,128)(2,1)S(1)} %copy-done.21), channel_id=1, source_target_pairs={{0,11},{1,10},{2,13},{3,12},{4,15},{5,14},{6,1},{7,0},{8,3},{9,2},... | collective-permute-start | bytes 196616 | tf_op jit(solution)/shard_map/diag/ppermute | solution.py:576
  78.3 15.1 %collective-permute-start.11 = (bf16[2,128,128]{2,1,0:T(8,128)(2,1)S(1)}, bf16[2,128,128]{2,1,0:T(8,128)(2,1)S(1)}, u32[]{:S(2)}, u32[]{:S(2)}) collective-permute-start(bf16[2,128,128]{2,1,0:T(8,128)(2,1)S(1)} %copy-done.20), channel_id=1, source_target_pairs={{0,8},{1,9},{2,10},{3,11},{4,12},{5,13},{6,14},{7,15},{8,0},{9,1},... | collective-permute-start | bytes 196616 | tf_op jit(solution)/shard_map/diag/ppermute | solution.py:576
  81.4 12.0 %collective-permute-start.12 = (bf16[2,128,128]{2,1,0:T(8,128)(2,1)S(1)}, bf16[2,128,128]{2,1,0:T(8,128)(2,1)S(1)}, u32[]{:S(2)}, u32[]{:S(2)}) collective-permute-start(bf16[2,128,128]{2,1,0:T(8,128)(2,1)S(1)} %copy-done.19), channel_id=1, source_target_pairs={{0,9},{1,8},{2,11},{3,10},{4,13},{5,12},{6,15},{7,14},{8,1},{9,0},... | collective-permute-start | bytes 196616 | tf_op jit(solution)/shard_map/diag/ppermute | solution.py:576
  84.1 10.5 %collective-permute-start.13 = (bf16[2,128,128]{2,1,0:T(8,128)(2,1)S(1)}, bf16[2,128,128]{2,1,0:T(8,128)(2,1)S(1)}, u32[]{:S(2)}, u32[]{:S(2)}) collective-permute-start(bf16[2,128,128]{2,1,0:T(8,128)(2,1)S(1)} %copy-done.18), channel_id=1, source_target_pairs={{0,6},{1,7},{2,8},{3,9},{4,10},{5,11},{6,12},{7,13},{8,14},{9,15},... | collective-permute-start | bytes 196616 | tf_op jit(solution)/shard_map/diag/ppermute | solution.py:576
  86.7 12.2 %collective-permute-start.14 = (bf16[2,128,128]{2,1,0:T(8,128)(2,1)S(1)}, bf16[2,128,128]{2,1,0:T(8,128)(2,1)S(1)}, u32[]{:S(2)}, u32[]{:S(2)}) collective-permute-start(bf16[2,128,128]{2,1,0:T(8,128)(2,1)S(1)} %copy-done.17), channel_id=1, source_target_pairs={{0,7},{1,6},{2,9},{3,8},{4,11},{5,10},{6,13},{7,12},{8,15},{9,14},... | collective-permute-start | bytes 196616 | tf_op jit(solution)/shard_map/diag/ppermute | solution.py:576
  89.3 21.8 %copy-start.9 = (bf16[2,128,128]{2,1,0:T(8,128)(2,1)}, bf16[2,128,128]{2,1,0:T(8,128)(2,1)S(1)}, u32[]{:S(2)}) copy-start(bf16[2,128,128]{2,1,0:T(8,128)(2,1)S(1)} %collective-permute-done.10.rest_11_) | copy-start | bytes 196612
  89.3 9.6 %collective-permute-start.9 = (bf16[2,128,128]{2,1,0:T(8,128)(2,1)S(1)}, bf16[2,128,128]{2,1,0:T(8,128)(2,1)S(1)}, u32[]{:S(2)}, u32[]{:S(2)}) collective-permute-start(bf16[2,128,128]{2,1,0:T(8,128)(2,1)S(1)} %copy-done.16), channel_id=1, source_target_pairs={{0,10},{1,11},{2,12},{3,13},{4,14},{5,15},{6,0},{7,1},{8,2},{9,3},... | collective-permute-start | bytes 196616 | tf_op jit(solution)/shard_map/diag/ppermute | solution.py:576
  93.4 17.7 %copy-start.10 = (bf16[2,128,128]{2,1,0:T(8,128)(2,1)}, bf16[2,128,128]{2,1,0:T(8,128)(2,1)S(1)}, u32[]{:S(2)}) copy-start(bf16[2,128,128]{2,1,0:T(8,128)(2,1)S(1)} %collective-permute-done.11.rest_12_) | copy-start | bytes 196612
  93.5 17.6 %copy-start.11 = (bf16[2,128,128]{2,1,0:T(8,128)(2,1)}, bf16[2,128,128]{2,1,0:T(8,128)(2,1)S(1)}, u32[]{:S(2)}) copy-start(bf16[2,128,128]{2,1,0:T(8,128)(2,1)S(1)} %collective-permute-done.12.rest_13_) | copy-start | bytes 196612
  94.6 16.5 %copy-start.12 = (bf16[2,128,128]{2,1,0:T(8,128)(2,1)}, bf16[2,128,128]{2,1,0:T(8,128)(2,1)S(1)}, u32[]{:S(2)}) copy-start(bf16[2,128,128]{2,1,0:T(8,128)(2,1)S(1)} %collective-permute-done.13.rest_14_) | copy-start | bytes 196612
  98.9 12.2 %copy-start.13 = (bf16[2,128,128]{2,1,0:T(8,128)(2,1)}, bf16[2,128,128]{2,1,0:T(8,128)(2,1)S(1)}, u32[]{:S(2)}) copy-start(bf16[2,128,128]{2,1,0:T(8,128)(2,1)S(1)} %collective-permute-done.14.rest_15_) | copy-start | bytes 196612
  98.9 12.2 %copy-start.14 = (bf16[2,128,128]{2,1,0:T(8,128)(2,1)}, bf16[2,128,128]{2,1,0:T(8,128)(2,1)S(1)}, u32[]{:S(2)}) copy-start(bf16[2,128,128]{2,1,0:T(8,128)(2,1)S(1)} %collective-permute-done.9.rest_10_) | copy-start | bytes 196612
  111.1 11.5 %all-to-all-start.1 = ((f32[16,2,8,128]{3,2,1,0:T(8,128)}), f32[16,2,8,128]{3,2,1,0:T(8,128)S(1)}, u32[]{:S(2)}, u32[]{:S(2)}) async-start(f32[16,2,8,128]{3,2,1,0:T(8,128)} %get-tuple-element.125), calls=%async_computation.1 | async-start | bytes 262144 | tf_op jit(solution)/shard_map/exchange/all_to_all | solution.py:659
  123.9 11.5 %all-to-all-start.2 = ((f32[16,2,8,128]{3,2,1,0:T(8,128)}), f32[16,2,8,128]{3,2,1,0:T(8,128)S(1)}, u32[]{:S(2)}, u32[]{:S(2)}) async-start(f32[16,2,8,128]{3,2,1,0:T(8,128)} %bitcast.10), calls=%async_computation.2 | async-start | bytes 262144 | tf_op jit(solution)/shard_map/exchange/all_to_all | solution.py:669
  141.5 11.5 %all-to-all-start.3 = ((f32[16,2,8,128]{3,2,1,0:T(8,128)}), f32[16,2,8,128]{3,2,1,0:T(8,128)S(1)}, u32[]{:S(2)}, u32[]{:S(2)}) async-start(f32[16,2,8,128]{3,2,1,0:T(8,128)} %get-tuple-element.148), calls=%async_computation.3 | async-start | bytes 262144 | tf_op jit(solution)/shard_map/exchange/all_to_all | solution.py:659
  154.3 11.5 %all-to-all-start.4 = ((f32[16,2,8,128]{3,2,1,0:T(8,128)}), f32[16,2,8,128]{3,2,1,0:T(8,128)S(1)}, u32[]{:S(2)}, u32[]{:S(2)}) async-start(f32[16,2,8,128]{3,2,1,0:T(8,128)} %bitcast.12), calls=%async_computation.4 | async-start | bytes 262144 | tf_op jit(solution)/shard_map/exchange/all_to_all | solution.py:669
  171.9 11.5 %all-to-all-start.5 = ((f32[16,2,8,128]{3,2,1,0:T(8,128)}), f32[16,2,8,128]{3,2,1,0:T(8,128)S(1)}, u32[]{:S(2)}, u32[]{:S(2)}) async-start(f32[16,2,8,128]{3,2,1,0:T(8,128)} %get-tuple-element.154), calls=%async_computation.5 | async-start | bytes 262144 | tf_op jit(solution)/shard_map/exchange/all_to_all | solution.py:659
  184.7 11.5 %all-to-all-start.6 = ((f32[16,2,8,128]{3,2,1,0:T(8,128)}), f32[16,2,8,128]{3,2,1,0:T(8,128)S(1)}, u32[]{:S(2)}, u32[]{:S(2)}) async-start(f32[16,2,8,128]{3,2,1,0:T(8,128)} %bitcast.14), calls=%async_computation.6 | async-start | bytes 262144 | tf_op jit(solution)/shard_map/exchange/all_to_all | solution.py:669
Sparse Core Ops, SparseCore 0:
  10.2 49.1 all-gather.1

commit v7 on v6

--- a/solution.py
+++ b/solution.py
@@ -70,32 +70,69 @@
         out_ref[s] = jnp.concatenate(split(tiles_ref[s]), axis=1)
 
 
-def gather_kernel(steps, wanted_ref, features, diag, *rest):
-    outs, (near_ref, far_ref, sems, out_sems) = rest[:-4], rest[-4:]
+def near_gather_kernel(wanted_ref, features, diag, own_out, other_out, swap_out, near_ref, swap_ref, sems, swap_sems, out_sems):
     c = lax.axis_index("col")
+    col_count = wanted_ref.shape[0]
     samples = features.shape[1]
     size = diag.shape[1]
-    near_count = near_ref.shape[0]
+    outs = (own_out, other_out)
+    first = []
+    for dk in range(CORES):
+        target = holder(c, 0, dk, col_count)
+        for p in range(own_out.shape[0]):
+            block = wanted_ref[target, p]
+            first.append(pltpu.make_async_copy(
+                features.at[block], near_ref.at[dk, p, pl.ds(0, samples)], sems.at[dk, p, 0]
+            ))
+            first.append(pltpu.make_async_copy(
+                diag.at[block], near_ref.at[dk, p, pl.ds(samples, size)], sems.at[dk, p, 1]
+            ))
+    second = [
+        pltpu.make_async_copy(
+            diag.at[wanted_ref[holder(c, -(n + 1), 1, col_count), p]],
+            swap_ref.at[n, p],
+            swap_sems.at[n, p],
+        )
+        for n in range(swap_ref.shape[0]) for p in range(swap_ref.shape[1])
+    ]
+    for copy in first + second:
+        copy.start()
+    backs = [
+        pltpu.make_async_copy(near_ref.at[dk], outs[dk], out_sems.at[dk]) for dk in range(CORES)
+    ]
+    backs.append(pltpu.make_async_copy(swap_ref, swap_out, out_sems.at[CORES]))
+    for copy in first:
+        copy.wait()
+    for back in backs[:-1]:
+        back.start()
+    for copy in second:
+        copy.wait()
+    backs[-1].start()
+    for back in backs:
+        back.wait()
+
+
+def far_gather_kernel(wanted_ref, diag, swapped, *rest):
+    outs, (near_ref, sems, out_sems) = rest[:-3], rest[-3:]
+    c = lax.axis_index("col")
+    count = swapped.shape[1]
+    backs = []
     copies = []
-    backs = []
-    for n, ((dz, dk), out) in enumerate(zip(steps, outs)):
-        target = holder(c, -dz, dk, wanted_ref.shape[0])
-        place = near_ref.at[n] if n < near_count else far_ref.at[n - near_count]
-        begin = samples if n < near_count else 0
-        mine = []
-        for p in range(out.shape[0]):
-            block = wanted_ref[target, p]
-            if n < near_count:
-                mine.append(pltpu.make_async_copy(
-                    features.at[block], place.at[p, pl.ds(0, samples)], sems.at[n, p, 0]
-                ))
-            mine.append(pltpu.make_async_copy(
-                diag.at[block], place.at[p, pl.ds(begin, size)], sems.at[n, p, 1]
-            ))
+    for n, out in enumerate(outs):
+        target = holder(c, -(n + 1), 0, wanted_ref.shape[0])
+        mine = [
+            pltpu.make_async_copy(
+                diag.at[wanted_ref[target, p]], near_ref.at[n, p], sems.at[n, p]
+            )
+            for p in range(count)
+        ]
+        mine.append(pltpu.make_async_copy(
+            swapped.at[n], near_ref.at[n, pl.ds(count, count)], sems.at[n, count]
+        ))
         for copy in mine:
             copy.start()
         copies.append(mine)
-        backs.append(pltpu.make_async_copy(place, out, out_sems.at[n]))
+        backs.append(pltpu.make_async_copy(near_ref.at[n], out, out_sems.at[n]))
     for mine, back in zip(copies, backs):
         for copy in mine:
             copy.wait()
@@ -162,38 +199,32 @@
     columns = owned_ref.shape[1]
     group = slices_ref.shape[1]
     _, samples, size = features.shape
-    part = far_slices.shape[0] * CORES // col_count
     slots = [chip_at(dz, col_count) * CHUNK + s for dz in far for s in range(CHUNK)]
 
-    def slice_copy(n):
-        here = pl.ds(chip_at(far[n], col_count) * part, part)
-        return pltpu.make_async_copy(
-            far_slices.at[here], slices_ref.at[here], slice_sem.at[n]
-        )
-
-    def right_copy(owner, a):
-        return pltpu.make_async_copy(
-            features.at[owned_ref[owner, a]], right_ref.at[owner, a], right_sem.at[owner, a]
-        )
+    def halves(source, target, sem):
+        count = source.shape[0] // 2
+        parts = [pl.ds(i * count, count) for i in range(2)]
+        return [
+            pltpu.make_async_copy(source.at[part], target.at[part], sem.at[i])
+            for i, part in enumerate(parts)
+        ]
 
     def out_copy(owner):
         return pltpu.make_async_copy(out_ref.at[owner], far_out.at[owner], out_sem.at[owner])
 
-    for n in range(len(far)):
-        slice_copy(n).start()
-    for owner in range(owners):
-        for a in range(columns):
-            right_copy(owner, a).start()
-    for n in range(len(far)):
-        slice_copy(n).wait()
+    copies = halves(far_slices, slices_ref, slice_sem) + halves(features, right_ref, right_sem)
+    for copy in copies:
+        copy.start()
+    for copy in copies:
+        copy.wait()
 
     def owner_step(owner, carry):
-        for a in range(columns):
-            right_copy(owner, a).wait()
         left = jnp.concatenate(
             [slices_ref[rows_ref[owner, slot]].astype(F32) for slot in slots], axis=0
         ).astype(BF)
-        right = jnp.concatenate([right_ref[owner, a] for a in range(columns)], axis=1)
+        right = jnp.concatenate(
+            [right_ref[owned_ref[owner, a]] for a in range(columns)], axis=1
+        )
         both = dot(left, right) * (1.0 / samples)
         for k, slot in enumerate(slots):
             rows = both[k * group:(k + 1) * group]
@@ -203,7 +234,7 @@
         out_copy(owner).start()
         return carry
 
-    lax.fori_loop(0, owners, owner_step, 0, unroll=2)
+    lax.fori_loop(0, owners, owner_step, 0, unroll=4)
     for owner in range(owners):
         out_copy(owner).wait()
 
@@ -344,14 +375,15 @@
             out.wait(chip_at(dz, col_count))
 
 
-def diagonal_kernel(steps, half, list_ref, far_base, far_d, col_diag_ref, *rest):
-    far_diag = rest[:len(steps)]
+def diagonal_kernel(half, list_ref, far_base, far_d, col_diag_ref, *rest):
     far_out, base_ref, d_ref, diag_ref, out_ref, diag_sem, sems = rest[-7:]
+    chips = diag_sem.shape[0] // CORES
+    near, far_diag = rest[:CORES], rest[CORES:CORES + chips - 1]
     slots, size, _ = d_ref.shape
     chunks = slots // MANY
     mine = range(half * chunks // 2, (half + 1) * chunks // 2)
     c = lax.axis_index("col")
-    per_source = slots // len(far_diag)
+    per_source = CHUNK // CORES
     arrays = [
         Tiles(far_d, d_ref, sems.at[1], count=MANY),
         Tiles(far_base, base_ref, sems.at[0], count=MANY),
@@ -359,23 +391,25 @@
     out = Tiles(far_out, out_ref, sems.at[2], True, count=MANY)
 
     def with_diag(n, use):
-        block = far_diag[n]
-        place = holder(c, *steps[n], len(far_diag)) * per_source
+        dz, dk = n // CORES, n % CORES
+        if dz == 0:
+            source = near[dk].at[:, pl.ds(near[dk].shape[1] - size, size)]
+        else:
+            source = far_diag[dz - 1].at[pl.ds(dk * per_source, per_source)]
+        place = holder(c, dz, dk, chips * CORES) * per_source
 
         @pl.when(place // (slots // 2) == half)
         def _():
             use(pltpu.make_async_copy(
-                block.at[:, pl.ds(block.shape[1] - size, size)],
-                diag_ref.at[pl.ds(place, per_source)],
-                diag_sem.at[n],
+                source, diag_ref.at[pl.ds(place, per_source)], diag_sem.at[n]
             ))
 
-    for n in range(len(far_diag)):
+    for n in range(chips * CORES):
         with_diag(n, lambda copy: copy.start())
     for i in mine:
         for array in arrays:
             array.start(i)
-    for n in range(len(far_diag)):
+    for n in range(chips * CORES):
         with_diag(n, lambda copy: copy.wait())
     for i in mine:
         for array in arrays:
@@ -540,42 +574,53 @@
         chips = col_count // CORES
         near = [0]
         far_chips = list(range(1, chips))
-        cores = range(CORES)
-        steps = [(dz, dk) for dz in near for dk in cores]
-        steps += [(dz, dk) for dz in (1, chips - 1, 2, chips - 2) for dk in cores]
-        early = len(steps)
-        steps += [(dz, dk) for dz in far_chips[2:-2] for dk in cores]
-        near_count = len(near) * CORES
-        block_shapes = [
-            (per_source, samples + size if n < near_count else size, size)
-            for n in range(len(steps))
-        ]
+        near_count = CORES
+        near_shape = (per_source, samples + size, size)
+        swap_shape = (chips - 1, per_source, size, size)
+        far_shape = (CORES * per_source, size, size)
         mine, wanted = lax.optimization_barrier((mine, wanted))
-        blocks_out = list(pl.pallas_call(
-            functools.partial(gather_kernel, steps),
+        own, other, swap = pl.pallas_call(
+            near_gather_kernel,
             in_specs=[SMEM, HBM, HBM],
-            out_specs=[HBM] * len(steps),
-            out_shape=[pltpu.HBM(dims, BF) for dims in block_shapes],
+            out_specs=[HBM] * 3,
+            out_shape=[
+                pltpu.HBM(near_shape, BF), pltpu.HBM(near_shape, BF), pltpu.HBM(swap_shape, BF)
+            ],
             scratch_shapes=[
-                pltpu.VMEM((near_count,) + block_shapes[0], BF),
-                pltpu.VMEM((len(steps) - near_count,) + block_shapes[-1], BF),
-                sems(len(steps), per_source, 2),
-                sems(len(steps)),
+                pltpu.VMEM((CORES,) + near_shape, BF),
+                pltpu.VMEM(swap_shape, BF),
+                sems(CORES, per_source, 2),
+                sems(chips - 1, per_source),
+                sems(CORES + 1),
             ],
             compiler_params=PARAMS,
-        )(wanted, far(features), far(diag_inverse)))
-
-        def send(n):
-            dz, dk = steps[n]
-            if dz == 0 and dk == 0:
-                return blocks_out[n]
-            pairs_of = [
-                (h, (h // CORES - dz) % chips * CORES + (h + dk) % CORES)
-                for h in range(col_count)
-            ]
-            return lax.ppermute(blocks_out[n], "col", pairs_of)
-
-        got_blocks = [send(n) for n in range(early)]
+        )(wanted, far(features), far(diag_inverse))
+        to_other = [
+            (i, i // CORES * CORES + (i + 1) % CORES) for i in range(col_count)
+        ]
+        swapped = lax.ppermute(swap, "col", to_other)
+        got_blocks = [own, lax.ppermute(other, "col", to_other)]
+        far_out = list(pl.pallas_call(
+            far_gather_kernel,
+            in_specs=[SMEM, HBM, HBM],
+            out_specs=[HBM] * (chips - 1),
+            out_shape=[pltpu.HBM(far_shape, BF)] * (chips - 1),
+            scratch_shapes=[
+                pltpu.VMEM((chips - 1,) + far_shape, BF),
+                sems(chips - 1, per_source + 1),
+                sems(chips - 1),
+            ],
+            compiler_params=PARAMS,
+        )(wanted, far(diag_inverse), far(swapped)))
+
+        def send(dz):
+            return lax.ppermute(far_out[dz - 1], "col", [
+                (h, (h // CORES - dz) % chips * CORES + h % CORES) for h in range(col_count)
+            ])
+
+        early = [1, chips - 1]
+        late = far_chips[1:-1]
+        sent = {dz: send(dz) for dz in early}
         base, d, near_sums = pl.pallas_call(
             functools.partial(near_kernel, near, col_count),
             in_specs=[SMEM, SMEM, SMEM] + [HBM] * (3 + near_count),
@@ -592,8 +637,8 @@
             my_list, live, my_owned, far(features), far(theta), far(tiles),
             *[far(block) for block in got_blocks[:near_count]],
         )
-        slices, pairs, got_blocks, base, d, near_sums = lax.optimization_barrier(
-            (slices, pairs, got_blocks, base, d, near_sums)
+        slices, pairs, got_blocks, base, d, near_sums, sent, far_out = lax.optimization_barrier(
+            (slices, pairs, got_blocks, base, d, near_sums, sent, far_out)
         )
 
     far_slots = len(far_chips) * CHUNK
@@ -605,10 +650,10 @@
             out_shape=pltpu.HBM((row_count, far_slots, group, size), F32),
             scratch_shapes=[
                 pltpu.VMEM(slices.shape, BF),
-                pltpu.VMEM((row_count, columns, samples, size), BF),
+                pltpu.VMEM(features.shape, BF),
                 pltpu.VMEM((row_count, far_slots, group, size), F32),
-                sems(len(far_chips)),
-                sems(row_count, columns),
+                sems(2),
+                sems(2),
                 sems(row_count),
             ],
             compiler_params=PARAMS,
@@ -616,9 +661,9 @@
         covariance = lax.all_to_all(partial, "row", split_axis=0, concat_axis=0, tiled=True)
 
     with jax.named_scope("diag"):
-        blocks_out[early:], _ = lax.optimization_barrier((blocks_out[early:], partial[0, 0]))
-        got_blocks = got_blocks + [send(n) for n in range(early, len(steps))]
-        covariance, got_blocks = lax.optimization_barrier((covariance, got_blocks))
+        far_out, _ = lax.optimization_barrier((far_out, partial[0, 0]))
+        sent.update({dz: send(dz) for dz in late})
+        got_blocks = got_blocks + [sent[dz] for dz in far_chips]
 
     with jax.named_scope("first"):
         base, d, pieces = pl.pallas_call(
@@ -640,7 +685,7 @@
         operands += [far(block) for block in got_blocks] + [far(x) for x in before]
         with jax.named_scope("diagonal"):
             return pl.pallas_call(
-                functools.partial(diagonal_kernel, steps, half),
+                functools.partial(diagonal_kernel, half),
                 in_specs=[SMEM, HBM, HBM, VMEM] + [HBM] * (len(operands) - 4),
                 out_specs=HBM,
                 out_shape=tile_out,

time: 210 us -> 205 us (0.976)
  starting transfers between devices: 56.7 us -> 43.5 us
  waiting for transfers between devices: 53.5 us -> 60.1 us
  local copies, waits for them, and re-layouts: 5.33 us -> 7.51 us
    ppermute x15 -> x9, starting transfers between devices: 28.4 us -> 14.3 us  [the longest x7 13.7 us: send(): lax.ppermute(far_out[dz - 1], 'col', [(h, (h // CORES - dz) % chips * COR...]
    all_to_all x1, waiting for transfers between devices: 6.57 us -> 15.6 us  [body(): lax.all_to_all(partial, 'row', split_axis=0, concat_axis=0, tiled=True)]
    ppermute x15 -> x9, waiting for transfers between devices: 9.9 us -> 1.12 us  [the longest x1 1.09 us: body(): swapped = lax.ppermute(swap, 'col', to_other)]
    all_gather x1, waiting for transfers between devices: 14.2 us -> 21.3 us  [body(): slices = lax.all_gather(mine, 'col', axis=0, tiled=True)]
    pallas_call x1, Pallas kernels: 9.72 us -> 7.38 us  [body(): pl.pallas_call(functools.partial(covariance_kernel, far_chips, col_count)...]
    unnamed x53 -> x31, local copies, waits for them, and re-layouts: 0.18 us -> 2.4 us
    pallas_call x7 -> x8, Pallas kernels: 28.7 us -> 30.7 us  [the longest x6 24.5 us: diagonal(): pl.pallas_call(functools.partial(diagonal_kernel, half), in_specs=[SMEM,...]
  transfers between devices with their start and end apart: 23 -> 17, of which waited for: 13 -> 9; matrix products, arithmetic and copies ran while one was open for 3% -> 3% of each run, Pallas kernels for 18% -> 22%
where the time goes in v7:
time: 205 us; the launch traced here: 204 us
  Pallas kernels  77.5 us (38%)
  waiting for transfers between devices  60.1 us (29%)
  starting transfers between devices  43.5 us (21%)
  between operations  13.8 us (7%)
  local copies, waits for them, and re-layouts  7.51 us (4%)
    pallas_call x6, Pallas kernels, diagonal(): pl.pallas_call(functools.partial(diagonal_kernel, half), in_specs=[SMEM,...  24.5 us
    all_gather x1, waiting for transfers between devices, body(): slices = lax.all_gather(mine, 'col', axis=0, tiled=True)  21.3 us
    pallas_call x3, Pallas kernels, body(): pl.pallas_call(functools.partial(sweep_kernel, last), in_specs=[SMEM, SME...  17.7 us
    all_to_all x1, waiting for transfers between devices, body(): lax.all_to_all(partial, 'row', split_axis=0, concat_axis=0, tiled=True)  15.6 us
    ppermute x7, starting transfers between devices, send(): lax.ppermute(far_out[dz - 1], 'col', [(h, (h // CORES - dz) % chips * COR...  13.7 us
    all_to_all x3, waiting for transfers between devices, body(): lax.all_to_all(summed.reshape(piece_shape), 'row', split_axis=0, concat_a...  12 us
    all_to_all x3, starting transfers between devices, body(): lax.all_to_all(summed.reshape(piece_shape), 'row', split_axis=0, concat_a...  11.4 us
    all_to_all x3, starting transfers between devices, body(): got = lax.all_to_all(pieces, 'row', split_axis=0, concat_axis=0, tiled=True)  10.7 us
  transfers between devices with their start and end apart: 17, of which 9 were waited for; matrix products, arithmetic and copies ran while one was open for 3% of the time, Pallas kernels for 22%

profile of v7, /device:TPU:32, one launch (start us, length us, event | category | flops | bytes accessed | tf_op | source)
XLA Modules:
  0.0 203.8 jit_solution(343445108425896502)
XLA Ops:
  6.5 3.5 %slices.1 = bf16[32,8,512]{2,1,0:T(8,128)(2,1)} custom-call(bf16[32,512,128]{2,1,0:T(8,128)(2,1)} %features.7), custom_call_target="tpu_custom_call" | custom-call | tf_op jit(solution)/shard_map/slices/pallas_call | solution.py:530
  10.1 0.8 dynamic-slice_subtract_fusion.1
  10.9 0.1 copy.35
  11.0 0.1 copy.31.wanted_ref
  11.1 3.2 %blocks.3 = (bf16[2,640,128]{2,1,0:T(8,128)(2,1)}, bf16[2,640,128]{2,1,0:T(8,128)(2,1)}, bf16[7,2,128,128]{3,2,1,0:T(8,128)(2,1)}) custom-call(s32[16,2]{1,0:T(8,128)S(1)} %copy.31.wanted_ref, bf16[32,512,128]{2,1,0:T(8,128)(2,1)} %features.7, bf16[32,128,128]{2,1,0:T(8,128)(2,1)} %diag.3), custom_call_target="tpu_custom_call" | custom-call | tf_op jit(solution)/shard_map/blocks/pallas_call | solution.py:582
  14.3 0.1 collective-permute-start.1
  14.4 0.5 collective-permute-start
  14.9 0.4 fusion.3
  15.3 1.1 collective-permute-done.1.swapped
  16.4 0.8 copy-done.8
  17.1 3.0 %blocks.5 = (bf16[4,128,128]{2,1,0:T(8,128)(2,1)}, bf16[4,128,128]{2,1,0:T(8,128)(2,1)}, bf16[4,128,128]{2,1,0:T(8,128)(2,1)}, bf16[4,128,128]{2,1,0:T(8,128)(2,...) custom-call(s32[16,2]{1,0:T(8,128)S(1)} %copy.31.wanted_ref, ...), custom_call_target="tpu_custom_call" | custom-call | tf_op jit(solution)/shard_map/blocks/pallas_call | solution.py:603
  20.1 2.0 collective-permute-start.2
  22.1 0.2 collective-permute-start.3
  22.3 0.7 fusion.1.list_ref
  23.0 0.1 fusion.owned_ref
  23.1 0.1 copy.29
  23.2 1.3 dynamic_slice.26
  24.4 3.9 %split.1.far_pairs = bf16[32,128,256]{2,1,0:T(8,128)(2,1)} custom-call(f32[32,128,128]{2,1,0:T(8,128)} %bitcast.30), custom_call_target="tpu_custom_call" | custom-call | tf_op jit(solution)/shard_map/split/pallas_call | solution.py:565
  28.3 0.1 copy.33.owned_ref
  28.4 0.9 constant_dynamic-slice_fusion.1
  29.3 0.7 copy-done
  30.0 4.6 %blocks.4 = (f32[32,128,128]{2,1,0:T(8,128)}, f32[32,128,128]{2,1,0:T(8,128)}, f32[2,128,256]{2,1,0:T(8,128)}) custom-call(s32[32]{0:T(128)S(1)} %fusion.1.list_ref, s32[1]{0:T(128)} %bitcast.1.live_ref, s32[2]{0:T(128)S(1)} %fusion.owned_ref, bf16[32,512,128]{2,1,0:T(8,128)(2,1)} %features.7, f32[32,128,128]{2,1,0:T(8,128)} %bitcast.25, ...), custom_call_target="tpu_custom_call" | custom-call | tf_op jit(solution)/shard_map/blocks/pallas_call | solution.py:624
  34.7 21.3 %all-gather.2.cloned.1.call-done.far_slices = bf16[512,8,512]{2,1,0:T(8,128)(2,1)} async-done(((bf16[32,8,512]{2,1,0:T(8,128)(2,1)}), bf16[512,8,512]{2,1,0:T(8,128)(2,1)}) %all-gather.2.cloned.1.call-update) | async-done | bytes 4194320 | tf_op jit(solution)/shard_map/slices/all_gather | solution.py:540
  56.0 7.4 %covariance.1 = f32[16,28,8,128]{3,2,1,0:T(8,128)} custom-call(s32[16,32]{1,0:T(8,128)S(1)} %bitcast.24, s32[16,32]{1,0:T(8,128)S(1)} %bitcast.23, s32[16,2]{1,0:T(8,128)S(1)} %copy.33.owned_ref, bf16[512,8,512]{2,1,0:T(8,128)(2,1)} %all-gather.2.cloned.1.call-done.far_slices, bf16[32,512,128]{2,1,0:T(8,128)(2,1)} %features.7), custom_call_target="tpu_custom_call" | custom-call | tf_op jit(solution)/shard_map/covariance/pallas_call | solution.py:646
  63.4 7.1 %all-to-all-start = ((f32[16,28,8,128]{3,2,1,0:T(8,128)}), f32[16,28,8,128]{3,2,1,0:T(8,128)S(1)}, u32[]{:S(2)}, u32[]{:S(2)}) async-start(f32[16,28,8,128]{3,2,1,0:T(8,128)} %covariance.1), calls=%async_computation | async-start | bytes 3670016 | tf_op jit(solution)/shard_map/covariance/all_to_all | solution.py:661
  70.5 1.8 gather_fusion
  72.3 0.1 sub.25
  72.4 0.1 broadcast_select_fusion.col_diag_ref
  72.5 2.8 %collective-permute-start.4 = (bf16[4,128,128]{2,1,0:T(8,128)(2,1)S(1)}, bf16[4,128,128]{2,1,0:T(8,128)(2,1)S(1)}, u32[]{:S(2)}, u32[]{:S(2)}) collective-permute-start(bf16[4,128,128]{2,1,0:T(8,128)(2,1)S(1)} %copy-done.14), channel_id=1, source_target_pairs={{0,12},{1,13},{2,14},{3,15},{4,0},{5,1},{6,2},{7,3},{8,4},{9,5},{1... | collective-permute-start | bytes 393224 | tf_op jit(solution)/shard_map/diag/ppermute | solution.py:617
  75.3 1.4 collective-permute-start.5
  76.7 2.9 %collective-permute-start.6 = (bf16[4,128,128]{2,1,0:T(8,128)(2,1)S(1)}, bf16[4,128,128]{2,1,0:T(8,128)(2,1)S(1)}, u32[]{:S(2)}, u32[]{:S(2)}) collective-permute-start(bf16[4,128,128]{2,1,0:T(8,128)(2,1)S(1)} %copy-done.12), channel_id=1, source_target_pairs={{0,8},{1,9},{2,10},{3,11},{4,12},{5,13},{6,14},{7,15},{8,0},{9,1},... | collective-permute-start | bytes 393224 | tf_op jit(solution)/shard_map/diag/ppermute | solution.py:617
  79.6 3.1 %collective-permute-start.7 = (bf16[4,128,128]{2,1,0:T(8,128)(2,1)S(1)}, bf16[4,128,128]{2,1,0:T(8,128)(2,1)S(1)}, u32[]{:S(2)}, u32[]{:S(2)}) collective-permute-start(bf16[4,128,128]{2,1,0:T(8,128)(2,1)S(1)} %copy-done.11), channel_id=1, source_target_pairs={{0,6},{1,7},{2,8},{3,9},{4,10},{5,11},{6,12},{7,13},{8,14},{9,15},... | collective-permute-start | bytes 393224 | tf_op jit(solution)/shard_map/diag/ppermute | solution.py:617
  82.8 1.4 collective-permute-start.8
  84.1 15.6 %all-to-all-done.cov_ref = f32[16,28,8,128]{3,2,1,0:T(8,128)S(1)} async-done(((f32[16,28,8,128]{3,2,1,0:T(8,128)}), f32[16,28,8,128]{3,2,1,0:T(8,128)S(1)}, u32[]{:S(2)}, u32[]{:S(2)}) %all-to-all-start) | async-done | bytes 1835040 | tf_op jit(solution)/shard_map/covariance/all_to_all | solution.py:661
  99.7 5.7 %first.1 = (f32[32,128,128]{2,1,0:T(8,128)}, f32[32,128,128]{2,1,0:T(8,128)}, f32[16,2,8,128]{3,2,1,0:T(8,128)}) custom-call(s32[32]{0:T(128)S(1)} %fusion.1.list_ref, s32[1]{0:T(128)} %bitcast.1.live_ref, f32[16,28,8,128]{3,2,1,0:T(8,128)S(1)} %all-to-all-done.cov_ref, ...), custom_call_target="tpu_custom_call", output_to_operand_aliasing={{0}: (6, {}), {1}: (7, {})} | custom-call | tf_op jit(solution)/shard_map/first/pallas_call | solution.py:669
  105.5 3.7 %all-to-all-start.1 = ((f32[16,2,8,128]{3,2,1,0:T(8,128)}), f32[16,2,8,128]{3,2,1,0:T(8,128)S(1)}, u32[]{:S(2)}, u32[]{:S(2)}) async-start(f32[16,2,8,128]{3,2,1,0:T(8,128)} %get-tuple-element.77), calls=%async_computation.1 | async-start | bytes 262144 | tf_op jit(solution)/shard_map/exchange/all_to_all | solution.py:704
  109.2 0.1 compare_convert_fusion.same_ref
  109.3 0.6 copy-done.3
  109.9 0.1 copy-done.5
  110.0 0.1 copy-done.6
  110.1 0.1 copy-done.7
  110.1 4.2 %diagonal.6.rest_9_ = f32[32,128,128]{2,1,0:T(8,128)} custom-call(s32[32]{0:T(128)S(1)} %fusion.1.list_ref, f32[32,128,128]{2,1,0:T(8,128)} %get-tuple-element.75.far_base, f32[32,128,128]{2,1,0:T(8,128)} %get-tuple-element.93.far_d, bf16[2,128,128]{2,1,0:T(8,128)(2,1)S(1)} %broadcast_select_fusion.col_diag_ref, ...), custom_call_target="tpu_custom_call" | custom-call | tf_op jit(solution)/shard_map/exchange/diagonal/pallas_call | solution.py:687
  114.3 2.6 %all-to-all-done.1 = f32[16,2,8,128]{3,2,1,0:T(8,128)S(1)} async-done(((f32[16,2,8,128]{3,2,1,0:T(8,128)}), f32[16,2,8,128]{3,2,1,0:T(8,128)S(1)}, u32[]{:S(2)}, u32[]{:S(2)}) %all-to-all-start.1) | async-done | bytes 131104 | tf_op jit(solution)/shard_map/exchange/all_to_all | solution.py:704
  117.0 1.3 exchange.3
  118.3 4.4 %all-to-all-start.2 = ((f32[16,2,8,128]{3,2,1,0:T(8,128)}), f32[16,2,8,128]{3,2,1,0:T(8,128)S(1)}, u32[]{:S(2)}, u32[]{:S(2)}) async-start(f32[16,2,8,128]{3,2,1,0:T(8,128)} %bitcast.10), calls=%async_computation.2 | async-start | bytes 262144 | tf_op jit(solution)/shard_map/exchange/all_to_all | solution.py:714
  122.7 4.0 %diagonal.7.far_t = f32[32,128,128]{2,1,0:T(8,128)} custom-call(s32[32]{0:T(128)S(1)} %fusion.1.list_ref, f32[32,128,128]{2,1,0:T(8,128)} %get-tuple-element.75.far_base, f32[32,128,128]{2,1,0:T(8,128)} %get-tuple-element.93.far_d, bf16[2,128,128]{2,1,0:T(8,128)(2,1)S(1)} %broadcast_select_fusion.col_diag_ref, ...), custom_call_target="tpu_custom_call", output_to_operand_aliasing={{}: (13, {})} | custom-call | tf_op jit(solution)/shard_map/exchange/diagonal/pallas_call | solution.py:687
  126.7 4.0 %all-to-all-done.2.q_ref = f32[16,2,8,128]{3,2,1,0:T(8,128)S(1)} async-done(((f32[16,2,8,128]{3,2,1,0:T(8,128)}), f32[16,2,8,128]{3,2,1,0:T(8,128)S(1)}, u32[]{:S(2)}, u32[]{:S(2)}) %all-to-all-start.2) | async-done | bytes 131104 | tf_op jit(solution)/shard_map/exchange/all_to_all | solution.py:714
  130.7 6.1 %sweep.3 = (f32[32,128,128]{2,1,0:T(8,128)}, f32[16,2,8,128]{3,2,1,0:T(8,128)}) custom-call(s32[32]{0:T(128)S(1)} %fusion.1.list_ref, s32[1]{0:T(128)} %bitcast.1.live_ref, f32[32,128,128]{2,1,0:T(8,128)} %diagonal.7.far_t, f32[32,128,128]{2,1,0:T(8,128)} %bitcast.27, bf16[32,128,256]{2,1,0:T(8,128)(2,1)} %split.1.far_pairs, ...), custom_call_target="tpu_custom_call" | custom-call | tf_op jit(solution)/shard_map/sweep/pallas_call | solution.py:720
  136.8 3.5 %all-to-all-start.3 = ((f32[16,2,8,128]{3,2,1,0:T(8,128)}), f32[16,2,8,128]{3,2,1,0:T(8,128)S(1)}, u32[]{:S(2)}, u32[]{:S(2)}) async-start(f32[16,2,8,128]{3,2,1,0:T(8,128)} %get-tuple-element.98), calls=%async_computation.3 | async-start | bytes 262144 | tf_op jit(solution)/shard_map/exchange/all_to_all | solution.py:704
  140.4 4.2 %diagonal.8.rest_9_ = f32[32,128,128]{2,1,0:T(8,128)} custom-call(s32[32]{0:T(128)S(1)} %fusion.1.list_ref, f32[32,128,128]{2,1,0:T(8,128)} %get-tuple-element.75.far_base, f32[32,128,128]{2,1,0:T(8,128)} %get-tuple-element.100.far_d, bf16[2,128,128]{2,1,0:T(8,128)(2,1)S(1)} %broadcast_select_fusion.col_diag_ref, ...), custom_call_target="tpu_custom_call" | custom-call | tf_op jit(solution)/shard_map/exchange/diagonal/pallas_call | solution.py:687
  144.6 3.7 %all-to-all-done.3 = f32[16,2,8,128]{3,2,1,0:T(8,128)S(1)} async-done(((f32[16,2,8,128]{3,2,1,0:T(8,128)}), f32[16,2,8,128]{3,2,1,0:T(8,128)S(1)}, u32[]{:S(2)}, u32[]{:S(2)}) %all-to-all-start.3) | async-done | bytes 131104 | tf_op jit(solution)/shard_map/exchange/all_to_all | solution.py:704
  148.3 1.3 exchange.4
  149.6 3.5 %all-to-all-start.4 = ((f32[16,2,8,128]{3,2,1,0:T(8,128)}), f32[16,2,8,128]{3,2,1,0:T(8,128)S(1)}, u32[]{:S(2)}, u32[]{:S(2)}) async-start(f32[16,2,8,128]{3,2,1,0:T(8,128)} %bitcast.12), calls=%async_computation.4 | async-start | bytes 262144 | tf_op jit(solution)/shard_map/exchange/all_to_all | solution.py:714
  153.2 4.0 %diagonal.9.far_t = f32[32,128,128]{2,1,0:T(8,128)} custom-call(s32[32]{0:T(128)S(1)} %fusion.1.list_ref, f32[32,128,128]{2,1,0:T(8,128)} %get-tuple-element.75.far_base, f32[32,128,128]{2,1,0:T(8,128)} %get-tuple-element.100.far_d, bf16[2,128,128]{2,1,0:T(8,128)(2,1)S(1)} %broadcast_select_fusion.col_diag_ref, ...), custom_call_target="tpu_custom_call", output_to_operand_aliasing={{}: (13, {})} | custom-call | tf_op jit(solution)/shard_map/exchange/diagonal/pallas_call | solution.py:687
  157.1 4.0 %all-to-all-done.4.q_ref = f32[16,2,8,128]{3,2,1,0:T(8,128)S(1)} async-done(((f32[16,2,8,128]{3,2,1,0:T(8,128)}), f32[16,2,8,128]{3,2,1,0:T(8,128)S(1)}, u32[]{:S(2)}, u32[]{:S(2)}) %all-to-all-start.4) | async-done | bytes 131104 | tf_op jit(solution)/shard_map/exchange/all_to_all | solution.py:714
  161.1 6.1 %sweep.4 = (f32[32,128,128]{2,1,0:T(8,128)}, f32[16,2,8,128]{3,2,1,0:T(8,128)}) custom-call(s32[32]{0:T(128)S(1)} %fusion.1.list_ref, s32[1]{0:T(128)} %bitcast.1.live_ref, f32[32,128,128]{2,1,0:T(8,128)} %diagonal.9.far_t, f32[32,128,128]{2,1,0:T(8,128)} %bitcast.28, bf16[32,128,256]{2,1,0:T(8,128)(2,1)} %split.1.far_pairs, ...), custom_call_target="tpu_custom_call" | custom-call | tf_op jit(solution)/shard_map/sweep/pallas_call | solution.py:720
  167.3 3.5 %all-to-all-start.5 = ((f32[16,2,8,128]{3,2,1,0:T(8,128)}), f32[16,2,8,128]{3,2,1,0:T(8,128)S(1)}, u32[]{:S(2)}, u32[]{:S(2)}) async-start(f32[16,2,8,128]{3,2,1,0:T(8,128)} %get-tuple-element.104), calls=%async_computation.5 | async-start | bytes 262144 | tf_op jit(solution)/shard_map/exchange/all_to_all | solution.py:704
  170.8 4.2 %diagonal.10.rest_9_ = f32[32,128,128]{2,1,0:T(8,128)} custom-call(s32[32]{0:T(128)S(1)} %fusion.1.list_ref, f32[32,128,128]{2,1,0:T(8,128)} %get-tuple-element.75.far_base, f32[32,128,128]{2,1,0:T(8,128)} %get-tuple-element.106.far_d, bf16[2,128,128]{2,1,0:T(8,128)(2,1)S(1)} %broadcast_select_fusion.col_diag_ref, ...), custom_call_target="tpu_custom_call" | custom-call | tf_op jit(solution)/shard_map/exchange/diagonal/pallas_call | solution.py:687
  175.0 3.7 %all-to-all-done.5 = f32[16,2,8,128]{3,2,1,0:T(8,128)S(1)} async-done(((f32[16,2,8,128]{3,2,1,0:T(8,128)}), f32[16,2,8,128]{3,2,1,0:T(8,128)S(1)}, u32[]{:S(2)}, u32[]{:S(2)}) %all-to-all-start.5) | async-done | bytes 131104 | tf_op jit(solution)/shard_map/exchange/all_to_all | solution.py:704
  178.7 1.3 exchange.5
  180.1 3.5 %all-to-all-start.6 = ((f32[16,2,8,128]{3,2,1,0:T(8,128)}), f32[16,2,8,128]{3,2,1,0:T(8,128)S(1)}, u32[]{:S(2)}, u32[]{:S(2)}) async-start(f32[16,2,8,128]{3,2,1,0:T(8,128)} %bitcast.14), calls=%async_computation.6 | async-start | bytes 262144 | tf_op jit(solution)/shard_map/exchange/all_to_all | solution.py:714
  183.6 4.0 %diagonal.11.far_t = f32[32,128,128]{2,1,0:T(8,128)} custom-call(s32[32]{0:T(128)S(1)} %fusion.1.list_ref, f32[32,128,128]{2,1,0:T(8,128)} %get-tuple-element.75.far_base, f32[32,128,128]{2,1,0:T(8,128)} %get-tuple-element.106.far_d, bf16[2,128,128]{2,1,0:T(8,128)(2,1)S(1)} %broadcast_select_fusion.col_diag_ref, ...), custom_call_target="tpu_custom_call", output_to_operand_aliasing={{}: (13, {})} | custom-call | tf_op jit(solution)/shard_map/exchange/diagonal/pallas_call | solution.py:687
  187.6 4.0 %all-to-all-done.6.q_ref = f32[16,2,8,128]{3,2,1,0:T(8,128)S(1)} async-done(((f32[16,2,8,128]{3,2,1,0:T(8,128)}), f32[16,2,8,128]{3,2,1,0:T(8,128)S(1)}, u32[]{:S(2)}, u32[]{:S(2)}) %all-to-all-start.6) | async-done | bytes 131104 | tf_op jit(solution)/shard_map/exchange/all_to_all | solution.py:714
  191.5 5.4 %sweep.5 = f32[32,128,128]{2,1,0:T(8,128)} custom-call(s32[32]{0:T(128)S(1)} %fusion.1.list_ref, s32[1]{0:T(128)} %bitcast.1.live_ref, f32[32,128,128]{2,1,0:T(8,128)} %diagonal.11.far_t, f32[32,128,128]{2,1,0:T(8,128)} %bitcast.29, bf16[32,128,256]{2,1,0:T(8,128)(2,1)} %split.1.far_pairs, f32[16,2,8,128]{3,2,1,0:T(8,128)S(1)} %all-to-all-done.6.q_ref), custom_call_target="tpu_custom_call" | custom-call | tf_op jit(solution)/shard_map/sweep/pallas_call | solution.py:720
  (37 shorter events, 0.2 us)
Async XLA Ops:
  6.5 49.4 %all-gather.2.cloned.1.call-start = ((), (), s32[]{:S(2)}) async-start(), calls=%async_computation.7 | async-start | bytes 4456448 | tf_op jit(solution)/shard_map/slices/all_gather | solution.py:540
  11.1 3.8 %copy-start.9 = (s32[16,16,2]{1,2,0:T(2,128)S(1)}, s32[16,16,2]{1,2,0:T(2,128)}, u32[]{:S(2)}) copy-start(s32[16,16,2]{1,2,0:T(2,128)} %param.14) | copy-start | bytes 6148
  14.3 2.1 %collective-permute-start.1 = (bf16[7,2,128,128]{3,2,1,0:T(8,128)(2,1)}, bf16[7,2,128,128]{3,2,1,0:T(8,128)(2,1)S(1)}, u32[]{:S(2)}, u32[]{:S(2)}) collective-permute-start(bf16[7,2,128,128]{3,2,1,0:T(8,128)(2,1)} %get-tuple-element.63), channel_id=1, source_target_pairs={{0,1},{1,0},{2,3},{3,2},{4,5},{5,4},{6,7},{7,6},{8,9},{9,8},{10,11... | collective-permute-start | bytes 1376264 | tf_op jit(solution)/shard_map/blocks/ppermute | solution.py:601
  14.4 14.9 %collective-permute-start = (bf16[2,640,128]{2,1,0:T(8,128)(2,1)}, bf16[2,640,128]{2,1,0:T(8,128)(2,1)S(1)}, u32[]{:S(2)}, u32[]{:S(2)}) collective-permute-start(bf16[2,640,128]{2,1,0:T(8,128)(2,1)} %get-tuple-element.59), channel_id=1, source_target_pairs={{0,1},{1,0},{2,3},{3,2},{4,5},{5,4},{6,7},{7,6},{8,9},{9,8},{10,11... | collective-permute-start | bytes 983048 | tf_op jit(solution)/shard_map/blocks/ppermute | solution.py:602
  16.4 0.8 copy-start.8
  20.1 14.5 %collective-permute-start.2 = (bf16[4,128,128]{2,1,0:T(8,128)(2,1)}, bf16[4,128,128]{2,1,0:T(8,128)(2,1)S(1)}, u32[]{:S(2)}, u32[]{:S(2)}) collective-permute-start(bf16[4,128,128]{2,1,0:T(8,128)(2,1)} %get-tuple-element.64), channel_id=1, source_target_pairs={{0,14},{1,15},{2,0},{3,1},{4,2},{5,3},{6,4},{7,5},{8,6},{9,7},{10,... | collective-permute-start | bytes 393224 | tf_op jit(solution)/shard_map/blocks/ppermute | solution.py:617
  22.1 12.6 %collective-permute-start.3 = (bf16[4,128,128]{2,1,0:T(8,128)(2,1)}, bf16[4,128,128]{2,1,0:T(8,128)(2,1)S(1)}, u32[]{:S(2)}, u32[]{:S(2)}) collective-permute-start(bf16[4,128,128]{2,1,0:T(8,128)(2,1)} %get-tuple-element.65), channel_id=1, source_target_pairs={{0,2},{1,3},{2,4},{3,5},{4,6},{5,7},{6,8},{7,9},{8,10},{9,11},{10,... | collective-permute-start | bytes 393224 | tf_op jit(solution)/shard_map/blocks/ppermute | solution.py:617
  29.3 0.7 copy-start
  34.7 28.7 %copy-start.1 = (bf16[4,128,128]{2,1,0:T(8,128)(2,1)}, bf16[4,128,128]{2,1,0:T(8,128)(2,1)S(1)}, u32[]{:S(2)}) copy-start(bf16[4,128,128]{2,1,0:T(8,128)(2,1)S(1)} %collective-permute-done.2.rest_2_) | copy-start | bytes 393220
  34.7 28.7 %copy-start.2 = (bf16[4,128,128]{2,1,0:T(8,128)(2,1)}, bf16[4,128,128]{2,1,0:T(8,128)(2,1)S(1)}, u32[]{:S(2)}) copy-start(bf16[4,128,128]{2,1,0:T(8,128)(2,1)S(1)} %collective-permute-done.3.rest_8_) | copy-start | bytes 393220
  63.4 9.1 %copy-start.14 = (bf16[4,128,128]{2,1,0:T(8,128)(2,1)S(1)}, bf16[4,128,128]{2,1,0:T(8,128)(2,1)}, u32[]{:S(2)}) copy-start(bf16[4,128,128]{2,1,0:T(8,128)(2,1)} %get-tuple-element.86) | copy-start | bytes 393220
  63.4 11.9 %copy-start.13 = (bf16[4,128,128]{2,1,0:T(8,128)(2,1)S(1)}, bf16[4,128,128]{2,1,0:T(8,128)(2,1)}, u32[]{:S(2)}) copy-start(bf16[4,128,128]{2,1,0:T(8,128)(2,1)} %get-tuple-element.87) | copy-start | bytes 393220
  63.4 13.3 %copy-start.12 = (bf16[4,128,128]{2,1,0:T(8,128)(2,1)S(1)}, bf16[4,128,128]{2,1,0:T(8,128)(2,1)}, u32[]{:S(2)}) copy-start(bf16[4,128,128]{2,1,0:T(8,128)(2,1)} %get-tuple-element.88) | copy-start | bytes 393220
  63.4 16.2 %copy-start.11 = (bf16[4,128,128]{2,1,0:T(8,128)(2,1)S(1)}, bf16[4,128,128]{2,1,0:T(8,128)(2,1)}, u32[]{:S(2)}) copy-start(bf16[4,128,128]{2,1,0:T(8,128)(2,1)} %get-tuple-element.89) | copy-start | bytes 393220
  63.4 19.3 %copy-start.10 = (bf16[4,128,128]{2,1,0:T(8,128)(2,1)S(1)}, bf16[4,128,128]{2,1,0:T(8,128)(2,1)}, u32[]{:S(2)}) copy-start(bf16[4,128,128]{2,1,0:T(8,128)(2,1)} %get-tuple-element.90) | copy-start | bytes 393220
  63.4 36.3 %all-to-all-start = ((f32[16,28,8,128]{3,2,1,0:T(8,128)}), f32[16,28,8,128]{3,2,1,0:T(8,128)S(1)}, u32[]{:S(2)}, u32[]{:S(2)}) async-start(f32[16,28,8,128]{3,2,1,0:T(8,128)} %covariance.1), calls=%async_computation | async-start | bytes 3670016 | tf_op jit(solution)/shard_map/covariance/all_to_all | solution.py:661
  72.5 36.7 %collective-permute-start.4 = (bf16[4,128,128]{2,1,0:T(8,128)(2,1)S(1)}, bf16[4,128,128]{2,1,0:T(8,128)(2,1)S(1)}, u32[]{:S(2)}, u32[]{:S(2)}) collective-permute-start(bf16[4,128,128]{2,1,0:T(8,128)(2,1)S(1)} %copy-done.14), channel_id=1, source_target_pairs={{0,12},{1,13},{2,14},{3,15},{4,0},{5,1},{6,2},{7,3},{8,4},{9,5},{1... | collective-permute-start | bytes 393224 | tf_op jit(solution)/shard_map/diag/ppermute | solution.py:617
  75.3 34.0 %collective-permute-start.5 = (bf16[4,128,128]{2,1,0:T(8,128)(2,1)S(1)}, bf16[4,128,128]{2,1,0:T(8,128)(2,1)S(1)}, u32[]{:S(2)}, u32[]{:S(2)}) collective-permute-start(bf16[4,128,128]{2,1,0:T(8,128)(2,1)S(1)} %copy-done.13), channel_id=1, source_target_pairs={{0,10},{1,11},{2,12},{3,13},{4,14},{5,15},{6,0},{7,1},{8,2},{9,3},... | collective-permute-start | bytes 393224 | tf_op jit(solution)/shard_map/diag/ppermute | solution.py:617
  76.7 32.6 %collective-permute-start.6 = (bf16[4,128,128]{2,1,0:T(8,128)(2,1)S(1)}, bf16[4,128,128]{2,1,0:T(8,128)(2,1)S(1)}, u32[]{:S(2)}, u32[]{:S(2)}) collective-permute-start(bf16[4,128,128]{2,1,0:T(8,128)(2,1)S(1)} %copy-done.12), channel_id=1, source_target_pairs={{0,8},{1,9},{2,10},{3,11},{4,12},{5,13},{6,14},{7,15},{8,0},{9,1},... | collective-permute-start | bytes 393224 | tf_op jit(solution)/shard_map/diag/ppermute | solution.py:617
  79.6 29.7 %collective-permute-start.7 = (bf16[4,128,128]{2,1,0:T(8,128)(2,1)S(1)}, bf16[4,128,128]{2,1,0:T(8,128)(2,1)S(1)}, u32[]{:S(2)}, u32[]{:S(2)}) collective-permute-start(bf16[4,128,128]{2,1,0:T(8,128)(2,1)S(1)} %copy-done.11), channel_id=1, source_target_pairs={{0,6},{1,7},{2,8},{3,9},{4,10},{5,11},{6,12},{7,13},{8,14},{9,15},... | collective-permute-start | bytes 393224 | tf_op jit(solution)/shard_map/diag/ppermute | solution.py:617
  82.8 26.5 %collective-permute-start.8 = (bf16[4,128,128]{2,1,0:T(8,128)(2,1)S(1)}, bf16[4,128,128]{2,1,0:T(8,128)(2,1)S(1)}, u32[]{:S(2)}, u32[]{:S(2)}) collective-permute-start(bf16[4,128,128]{2,1,0:T(8,128)(2,1)S(1)} %copy-done.10), channel_id=1, source_target_pairs={{0,4},{1,5},{2,6},{3,7},{4,8},{5,9},{6,10},{7,11},{8,12},{9,13},{1... | collective-permute-start | bytes 393224 | tf_op jit(solution)/shard_map/diag/ppermute | solution.py:617
  105.5 11.5 %all-to-all-start.1 = ((f32[16,2,8,128]{3,2,1,0:T(8,128)}), f32[16,2,8,128]{3,2,1,0:T(8,128)S(1)}, u32[]{:S(2)}, u32[]{:S(2)}) async-start(f32[16,2,8,128]{3,2,1,0:T(8,128)} %get-tuple-element.77), calls=%async_computation.1 | async-start | bytes 262144 | tf_op jit(solution)/shard_map/exchange/all_to_all | solution.py:704
  109.2 0.6 copy-start.3
  109.3 0.7 copy-start.4
  109.3 0.7 copy-start.5
  109.3 0.8 copy-start.6
  109.3 0.8 copy-start.7
  118.3 12.4 %all-to-all-start.2 = ((f32[16,2,8,128]{3,2,1,0:T(8,128)}), f32[16,2,8,128]{3,2,1,0:T(8,128)S(1)}, u32[]{:S(2)}, u32[]{:S(2)}) async-start(f32[16,2,8,128]{3,2,1,0:T(8,128)} %bitcast.10), calls=%async_computation.2 | async-start | bytes 262144 | tf_op jit(solution)/shard_map/exchange/all_to_all | solution.py:714
  136.8 11.5 %all-to-all-start.3 = ((f32[16,2,8,128]{3,2,1,0:T(8,128)}), f32[16,2,8,128]{3,2,1,0:T(8,128)S(1)}, u32[]{:S(2)}, u32[]{:S(2)}) async-start(f32[16,2,8,128]{3,2,1,0:T(8,128)} %get-tuple-element.98), calls=%async_computation.3 | async-start | bytes 262144 | tf_op jit(solution)/shard_map/exchange/all_to_all | solution.py:704
  149.6 11.5 %all-to-all-start.4 = ((f32[16,2,8,128]{3,2,1,0:T(8,128)}), f32[16,2,8,128]{3,2,1,0:T(8,128)S(1)}, u32[]{:S(2)}, u32[]{:S(2)}) async-start(f32[16,2,8,128]{3,2,1,0:T(8,128)} %bitcast.12), calls=%async_computation.4 | async-start | bytes 262144 | tf_op jit(solution)/shard_map/exchange/all_to_all | solution.py:714
  167.3 11.5 %all-to-all-start.5 = ((f32[16,2,8,128]{3,2,1,0:T(8,128)}), f32[16,2,8,128]{3,2,1,0:T(8,128)S(1)}, u32[]{:S(2)}, u32[]{:S(2)}) async-start(f32[16,2,8,128]{3,2,1,0:T(8,128)} %get-tuple-element.104), calls=%async_computation.5 | async-start | bytes 262144 | tf_op jit(solution)/shard_map/exchange/all_to_all | solution.py:704
  180.1 11.5 %all-to-all-start.6 = ((f32[16,2,8,128]{3,2,1,0:T(8,128)}), f32[16,2,8,128]{3,2,1,0:T(8,128)S(1)}, u32[]{:S(2)}, u32[]{:S(2)}) async-start(f32[16,2,8,128]{3,2,1,0:T(8,128)} %bitcast.14), calls=%async_computation.6 | async-start | bytes 262144 | tf_op jit(solution)/shard_map/exchange/all_to_all | solution.py:714
Sparse Core Ops, SparseCore 0:
  10.2 45.6 all-gather.1

commit v8 on v7

--- a/solution.py
+++ b/solution.py
@@ -618,9 +618,6 @@
                 (h, (h // CORES - dz) % chips * CORES + h % CORES) for h in range(col_count)
             ])
 
-        early = [1, chips - 1]
-        late = far_chips[1:-1]
-        sent = {dz: send(dz) for dz in early}
         base, d, near_sums = pl.pallas_call(
             functools.partial(near_kernel, near, col_count),
             in_specs=[SMEM, SMEM, SMEM] + [HBM] * (3 + near_count),
@@ -637,8 +634,8 @@
             my_list, live, my_owned, far(features), far(theta), far(tiles),
             *[far(block) for block in got_blocks[:near_count]],
         )
-        slices, pairs, got_blocks, base, d, near_sums, sent, far_out = lax.optimization_barrier(
-            (slices, pairs, got_blocks, base, d, near_sums, sent, far_out)
+        slices, pairs, got_blocks, base, d, near_sums, far_out = lax.optimization_barrier(
+            (slices, pairs, got_blocks, base, d, near_sums, far_out)
         )
 
     far_slots = len(far_chips) * CHUNK
@@ -662,7 +659,10 @@
 
     with jax.named_scope("diag"):
         far_out, _ = lax.optimization_barrier((far_out, partial[0, 0]))
-        sent.update({dz: send(dz) for dz in late})
+        soon = [1, chips - 1]
+        sent = {dz: send(dz) for dz in soon}
+        covariance, sent = lax.optimization_barrier((covariance, sent))
+        sent.update({dz: send(dz) for dz in far_chips if dz not in soon})
         got_blocks = got_blocks + [sent[dz] for dz in far_chips]
 
     with jax.named_scope("first"):

time: 205 us -> 204 us (level)
    all_to_all x1, waiting for transfers between devices: 15.6 us -> 12.9 us  [body(): lax.all_to_all(partial, 'row', split_axis=0, concat_axis=0, tiled=True)]
  transfers between devices with their start and end apart: 17 -> 17, of which waited for: 9 -> 8; matrix products, arithmetic and copies ran while one was open for 3% -> 3% of each run, Pallas kernels for 22% -> 22%
where the time goes in v8:
time: 204 us; the launch traced here: 202 us
  Pallas kernels  77.3 us (38%)
  waiting for transfers between devices  58.3 us (29%)
  starting transfers between devices  43.9 us (22%)
  between operations  13.8 us (7%)
  local copies, waits for them, and re-layouts  7.51 us (4%)
    pallas_call x6, Pallas kernels, diagonal(): pl.pallas_call(functools.partial(diagonal_kernel, half), in_specs=[SMEM,...  24.5 us
    all_gather x1, waiting for transfers between devices, body(): slices = lax.all_gather(mine, 'col', axis=0, tiled=True)  23.2 us
    pallas_call x3, Pallas kernels, body(): pl.pallas_call(functools.partial(sweep_kernel, last), in_specs=[SMEM, SME...  17.7 us
    ppermute x7, starting transfers between devices, send(): lax.ppermute(far_out[dz - 1], 'col', [(h, (h // CORES - dz) % chips * COR...  14.2 us
    all_to_all x1, waiting for transfers between devices, body(): lax.all_to_all(partial, 'row', split_axis=0, concat_axis=0, tiled=True)  12.9 us
    all_to_all x3, waiting for transfers between devices, body(): lax.all_to_all(summed.reshape(piece_shape), 'row', split_axis=0, concat_a...  12 us
    all_to_all x3, starting transfers between devices, body(): lax.all_to_all(summed.reshape(piece_shape), 'row', split_axis=0, concat_a...  11.4 us
    all_to_all x3, starting transfers between devices, body(): got = lax.all_to_all(pieces, 'row', split_axis=0, concat_axis=0, tiled=True)  10.7 us
  transfers between devices with their start and end apart: 17, of which 8 were waited for; matrix products, arithmetic and copies ran while one was open for 3% of the time, Pallas kernels for 22%

profile of v8, /device:TPU:32, one launch (start us, length us, event | category | flops | bytes accessed | tf_op | source)
XLA Modules:
  0.0 202.2 jit_solution(432218962687358366)
XLA Ops:
  6.5 3.5 %slices.1 = bf16[32,8,512]{2,1,0:T(8,128)(2,1)} custom-call(bf16[32,512,128]{2,1,0:T(8,128)(2,1)} %features.7), custom_call_target="tpu_custom_call" | custom-call | tf_op jit(solution)/shard_map/slices/pallas_call | solution.py:530
  10.1 0.8 dynamic-slice_subtract_fusion.1
  10.9 0.1 copy.35
  11.0 0.1 copy.31.wanted_ref
  11.0 3.2 %blocks.3 = (bf16[2,640,128]{2,1,0:T(8,128)(2,1)}, bf16[2,640,128]{2,1,0:T(8,128)(2,1)}, bf16[7,2,128,128]{3,2,1,0:T(8,128)(2,1)}) custom-call(s32[16,2]{1,0:T(8,128)S(1)} %copy.31.wanted_ref, bf16[32,512,128]{2,1,0:T(8,128)(2,1)} %features.7, bf16[32,128,128]{2,1,0:T(8,128)(2,1)} %diag.3), custom_call_target="tpu_custom_call" | custom-call | tf_op jit(solution)/shard_map/blocks/pallas_call | solution.py:582
  14.3 0.1 collective-permute-start.1
  14.4 0.5 collective-permute-start
  14.9 0.4 fusion.3
  15.3 0.1 fusion.owned_ref
  15.4 0.1 copy.29
  15.5 1.3 dynamic_slice.26
  16.8 3.8 %split.1.far_pairs = bf16[32,128,256]{2,1,0:T(8,128)(2,1)} custom-call(f32[32,128,128]{2,1,0:T(8,128)} %bitcast.30), custom_call_target="tpu_custom_call" | custom-call | tf_op jit(solution)/shard_map/split/pallas_call | solution.py:565
  20.6 0.1 copy.33.owned_ref
  20.7 0.7 fusion.1.list_ref
  21.4 0.9 constant_dynamic-slice_fusion.1
  22.3 0.7 copy-done
  23.0 4.7 %blocks.4 = (f32[32,128,128]{2,1,0:T(8,128)}, f32[32,128,128]{2,1,0:T(8,128)}, f32[2,128,256]{2,1,0:T(8,128)}) custom-call(s32[32]{0:T(128)S(1)} %fusion.1.list_ref, s32[1]{0:T(128)} %bitcast.1.live_ref, s32[2]{0:T(128)S(1)} %fusion.owned_ref, bf16[32,512,128]{2,1,0:T(8,128)(2,1)} %features.7, f32[32,128,128]{2,1,0:T(8,128)} %bitcast.25, ...), custom_call_target="tpu_custom_call" | custom-call | tf_op jit(solution)/shard_map/blocks/pallas_call | solution.py:621
  27.7 0.8 copy-done.8
  28.5 2.9 %blocks.5 = (bf16[4,128,128]{2,1,0:T(8,128)(2,1)}, bf16[4,128,128]{2,1,0:T(8,128)(2,1)}, bf16[4,128,128]{2,1,0:T(8,128)(2,1)}, bf16[4,128,128]{2,1,0:T(8,128)(2,...) custom-call(s32[16,2]{1,0:T(8,128)S(1)} %copy.31.wanted_ref, ...), custom_call_target="tpu_custom_call" | custom-call | tf_op jit(solution)/shard_map/blocks/pallas_call | solution.py:603
  31.4 23.2 %all-gather.2.cloned.1.call-done.far_slices = bf16[512,8,512]{2,1,0:T(8,128)(2,1)} async-done(((bf16[32,8,512]{2,1,0:T(8,128)(2,1)}), bf16[512,8,512]{2,1,0:T(8,128)(2,1)}) %all-gather.2.cloned.1.call-update) | async-done | bytes 4194320 | tf_op jit(solution)/shard_map/slices/all_gather | solution.py:540
  54.7 7.4 %covariance.1 = f32[16,28,8,128]{3,2,1,0:T(8,128)} custom-call(s32[16,32]{1,0:T(8,128)S(1)} %bitcast.24, s32[16,32]{1,0:T(8,128)S(1)} %bitcast.23, s32[16,2]{1,0:T(8,128)S(1)} %copy.33.owned_ref, bf16[512,8,512]{2,1,0:T(8,128)(2,1)} %all-gather.2.cloned.1.call-done.far_slices, bf16[32,512,128]{2,1,0:T(8,128)(2,1)} %features.7), custom_call_target="tpu_custom_call" | custom-call | tf_op jit(solution)/shard_map/covariance/pallas_call | solution.py:643
  62.1 7.0 %all-to-all-start = ((f32[16,28,8,128]{3,2,1,0:T(8,128)}), f32[16,28,8,128]{3,2,1,0:T(8,128)S(1)}, u32[]{:S(2)}, u32[]{:S(2)}) async-start(f32[16,28,8,128]{3,2,1,0:T(8,128)} %covariance.1), calls=%async_computation | async-start | bytes 3670016 | tf_op jit(solution)/shard_map/covariance/all_to_all | solution.py:658
  69.1 1.8 gather_fusion
  70.9 0.1 sub.25
  71.0 0.8 collective-permute-start.2
  71.9 1.3 collective-permute-start.3
  73.1 0.1 broadcast_select_fusion.col_diag_ref
  73.2 3.5 %collective-permute-start.4 = (bf16[4,128,128]{2,1,0:T(8,128)(2,1)S(1)}, bf16[4,128,128]{2,1,0:T(8,128)(2,1)S(1)}, u32[]{:S(2)}, u32[]{:S(2)}) collective-permute-start(bf16[4,128,128]{2,1,0:T(8,128)(2,1)S(1)} %copy-done.14), channel_id=1, source_target_pairs={{0,12},{1,13},{2,14},{3,15},{4,0},{5,1},{6,2},{7,3},{8,4},{9,5},{1... | collective-permute-start | bytes 393224 | tf_op jit(solution)/shard_map/diag/ppermute | solution.py:617
  76.7 0.8 collective-permute-start.5
  77.5 2.8 %collective-permute-start.6 = (bf16[4,128,128]{2,1,0:T(8,128)(2,1)S(1)}, bf16[4,128,128]{2,1,0:T(8,128)(2,1)S(1)}, u32[]{:S(2)}, u32[]{:S(2)}) collective-permute-start(bf16[4,128,128]{2,1,0:T(8,128)(2,1)S(1)} %copy-done.12), channel_id=1, source_target_pairs={{0,8},{1,9},{2,10},{3,11},{4,12},{5,13},{6,14},{7,15},{8,0},{9,1},... | collective-permute-start | bytes 393224 | tf_op jit(solution)/shard_map/diag/ppermute | solution.py:617
  80.2 5.0 %collective-permute-start.7 = (bf16[4,128,128]{2,1,0:T(8,128)(2,1)S(1)}, bf16[4,128,128]{2,1,0:T(8,128)(2,1)S(1)}, u32[]{:S(2)}, u32[]{:S(2)}) collective-permute-start(bf16[4,128,128]{2,1,0:T(8,128)(2,1)S(1)} %copy-done.11), channel_id=1, source_target_pairs={{0,6},{1,7},{2,8},{3,9},{4,10},{5,11},{6,12},{7,13},{8,14},{9,15},... | collective-permute-start | bytes 393224 | tf_op jit(solution)/shard_map/diag/ppermute | solution.py:617
  85.3 0.1 collective-permute-start.8
  85.3 12.9 %all-to-all-done.cov_ref = f32[16,28,8,128]{3,2,1,0:T(8,128)S(1)} async-done(((f32[16,28,8,128]{3,2,1,0:T(8,128)}), f32[16,28,8,128]{3,2,1,0:T(8,128)S(1)}, u32[]{:S(2)}, u32[]{:S(2)}) %all-to-all-start) | async-done | bytes 1835040 | tf_op jit(solution)/shard_map/covariance/all_to_all | solution.py:658
  98.2 5.7 %first.1 = (f32[32,128,128]{2,1,0:T(8,128)}, f32[32,128,128]{2,1,0:T(8,128)}, f32[16,2,8,128]{3,2,1,0:T(8,128)}) custom-call(s32[32]{0:T(128)S(1)} %fusion.1.list_ref, s32[1]{0:T(128)} %bitcast.1.live_ref, f32[16,28,8,128]{3,2,1,0:T(8,128)S(1)} %all-to-all-done.cov_ref, ...), custom_call_target="tpu_custom_call", output_to_operand_aliasing={{0}: (6, {}), {1}: (7, {})} | custom-call | tf_op jit(solution)/shard_map/first/pallas_call | solution.py:669
  103.9 3.7 %all-to-all-start.1 = ((f32[16,2,8,128]{3,2,1,0:T(8,128)}), f32[16,2,8,128]{3,2,1,0:T(8,128)S(1)}, u32[]{:S(2)}, u32[]{:S(2)}) async-start(f32[16,2,8,128]{3,2,1,0:T(8,128)} %get-tuple-element.92), calls=%async_computation.1 | async-start | bytes 262144 | tf_op jit(solution)/shard_map/exchange/all_to_all | solution.py:704
  107.7 0.1 compare_convert_fusion.same_ref
  107.8 0.6 copy-done.3
  108.4 0.1 copy-done.4
  108.4 0.1 copy-done.5
  108.5 0.1 copy-done.6
  108.5 0.0 copy-done.7
  108.6 4.2 %diagonal.6.rest_9_ = f32[32,128,128]{2,1,0:T(8,128)} custom-call(s32[32]{0:T(128)S(1)} %fusion.1.list_ref, f32[32,128,128]{2,1,0:T(8,128)} %get-tuple-element.90.far_base, f32[32,128,128]{2,1,0:T(8,128)} %get-tuple-element.103.far_d, bf16[2,128,128]{2,1,0:T(8,128)(2,1)S(1)} %broadcast_select_fusion.col_diag_ref, ...), custom_call_target="tpu_custom_call" | custom-call | tf_op jit(solution)/shard_map/exchange/diagonal/pallas_call | solution.py:687
  112.8 2.7 %all-to-all-done.1 = f32[16,2,8,128]{3,2,1,0:T(8,128)S(1)} async-done(((f32[16,2,8,128]{3,2,1,0:T(8,128)}), f32[16,2,8,128]{3,2,1,0:T(8,128)S(1)}, u32[]{:S(2)}, u32[]{:S(2)}) %all-to-all-start.1) | async-done | bytes 131104 | tf_op jit(solution)/shard_map/exchange/all_to_all | solution.py:704
  115.4 1.3 exchange.3
  116.8 4.4 %all-to-all-start.2 = ((f32[16,2,8,128]{3,2,1,0:T(8,128)}), f32[16,2,8,128]{3,2,1,0:T(8,128)S(1)}, u32[]{:S(2)}, u32[]{:S(2)}) async-start(f32[16,2,8,128]{3,2,1,0:T(8,128)} %bitcast.10), calls=%async_computation.2 | async-start | bytes 262144 | tf_op jit(solution)/shard_map/exchange/all_to_all | solution.py:714
  121.1 4.0 %diagonal.7.far_t = f32[32,128,128]{2,1,0:T(8,128)} custom-call(s32[32]{0:T(128)S(1)} %fusion.1.list_ref, f32[32,128,128]{2,1,0:T(8,128)} %get-tuple-element.90.far_base, f32[32,128,128]{2,1,0:T(8,128)} %get-tuple-element.103.far_d, bf16[2,128,128]{2,1,0:T(8,128)(2,1)S(1)} %broadcast_select_fusion.col_diag_ref, ...), custom_call_target="tpu_custom_call", output_to_operand_aliasing={{}: (13, {})} | custom-call | tf_op jit(solution)/shard_map/exchange/diagonal/pallas_call | solution.py:687
  125.1 4.0 %all-to-all-done.2.q_ref = f32[16,2,8,128]{3,2,1,0:T(8,128)S(1)} async-done(((f32[16,2,8,128]{3,2,1,0:T(8,128)}), f32[16,2,8,128]{3,2,1,0:T(8,128)S(1)}, u32[]{:S(2)}, u32[]{:S(2)}) %all-to-all-start.2) | async-done | bytes 131104 | tf_op jit(solution)/shard_map/exchange/all_to_all | solution.py:714
  129.1 6.2 %sweep.3 = (f32[32,128,128]{2,1,0:T(8,128)}, f32[16,2,8,128]{3,2,1,0:T(8,128)}) custom-call(s32[32]{0:T(128)S(1)} %fusion.1.list_ref, s32[1]{0:T(128)} %bitcast.1.live_ref, f32[32,128,128]{2,1,0:T(8,128)} %diagonal.7.far_t, f32[32,128,128]{2,1,0:T(8,128)} %bitcast.27, bf16[32,128,256]{2,1,0:T(8,128)(2,1)} %split.1.far_pairs, ...), custom_call_target="tpu_custom_call" | custom-call | tf_op jit(solution)/shard_map/sweep/pallas_call | solution.py:720
  135.3 3.5 %all-to-all-start.3 = ((f32[16,2,8,128]{3,2,1,0:T(8,128)}), f32[16,2,8,128]{3,2,1,0:T(8,128)S(1)}, u32[]{:S(2)}, u32[]{:S(2)}) async-start(f32[16,2,8,128]{3,2,1,0:T(8,128)} %get-tuple-element.108), calls=%async_computation.3 | async-start | bytes 262144 | tf_op jit(solution)/shard_map/exchange/all_to_all | solution.py:704
  138.8 4.2 %diagonal.8.rest_9_ = f32[32,128,128]{2,1,0:T(8,128)} custom-call(s32[32]{0:T(128)S(1)} %fusion.1.list_ref, f32[32,128,128]{2,1,0:T(8,128)} %get-tuple-element.90.far_base, f32[32,128,128]{2,1,0:T(8,128)} %get-tuple-element.110.far_d, bf16[2,128,128]{2,1,0:T(8,128)(2,1)S(1)} %broadcast_select_fusion.col_diag_ref, ...), custom_call_target="tpu_custom_call" | custom-call | tf_op jit(solution)/shard_map/exchange/diagonal/pallas_call | solution.py:687
  143.0 3.7 %all-to-all-done.3 = f32[16,2,8,128]{3,2,1,0:T(8,128)S(1)} async-done(((f32[16,2,8,128]{3,2,1,0:T(8,128)}), f32[16,2,8,128]{3,2,1,0:T(8,128)S(1)}, u32[]{:S(2)}, u32[]{:S(2)}) %all-to-all-start.3) | async-done | bytes 131104 | tf_op jit(solution)/shard_map/exchange/all_to_all | solution.py:704
  146.8 1.3 exchange.4
  148.1 3.5 %all-to-all-start.4 = ((f32[16,2,8,128]{3,2,1,0:T(8,128)}), f32[16,2,8,128]{3,2,1,0:T(8,128)S(1)}, u32[]{:S(2)}, u32[]{:S(2)}) async-start(f32[16,2,8,128]{3,2,1,0:T(8,128)} %bitcast.12), calls=%async_computation.4 | async-start | bytes 262144 | tf_op jit(solution)/shard_map/exchange/all_to_all | solution.py:714
  151.6 4.0 %diagonal.9.far_t = f32[32,128,128]{2,1,0:T(8,128)} custom-call(s32[32]{0:T(128)S(1)} %fusion.1.list_ref, f32[32,128,128]{2,1,0:T(8,128)} %get-tuple-element.90.far_base, f32[32,128,128]{2,1,0:T(8,128)} %get-tuple-element.110.far_d, bf16[2,128,128]{2,1,0:T(8,128)(2,1)S(1)} %broadcast_select_fusion.col_diag_ref, ...), custom_call_target="tpu_custom_call", output_to_operand_aliasing={{}: (13, {})} | custom-call | tf_op jit(solution)/shard_map/exchange/diagonal/pallas_call | solution.py:687
  155.6 4.0 %all-to-all-done.4.q_ref = f32[16,2,8,128]{3,2,1,0:T(8,128)S(1)} async-done(((f32[16,2,8,128]{3,2,1,0:T(8,128)}), f32[16,2,8,128]{3,2,1,0:T(8,128)S(1)}, u32[]{:S(2)}, u32[]{:S(2)}) %all-to-all-start.4) | async-done | bytes 131104 | tf_op jit(solution)/shard_map/exchange/all_to_all | solution.py:714
  159.6 6.2 %sweep.4 = (f32[32,128,128]{2,1,0:T(8,128)}, f32[16,2,8,128]{3,2,1,0:T(8,128)}) custom-call(s32[32]{0:T(128)S(1)} %fusion.1.list_ref, s32[1]{0:T(128)} %bitcast.1.live_ref, f32[32,128,128]{2,1,0:T(8,128)} %diagonal.9.far_t, f32[32,128,128]{2,1,0:T(8,128)} %bitcast.28, bf16[32,128,256]{2,1,0:T(8,128)(2,1)} %split.1.far_pairs, ...), custom_call_target="tpu_custom_call" | custom-call | tf_op jit(solution)/shard_map/sweep/pallas_call | solution.py:720
  165.7 3.5 %all-to-all-start.5 = ((f32[16,2,8,128]{3,2,1,0:T(8,128)}), f32[16,2,8,128]{3,2,1,0:T(8,128)S(1)}, u32[]{:S(2)}, u32[]{:S(2)}) async-start(f32[16,2,8,128]{3,2,1,0:T(8,128)} %get-tuple-element.114), calls=%async_computation.5 | async-start | bytes 262144 | tf_op jit(solution)/shard_map/exchange/all_to_all | solution.py:704
  169.3 4.2 %diagonal.10.rest_9_ = f32[32,128,128]{2,1,0:T(8,128)} custom-call(s32[32]{0:T(128)S(1)} %fusion.1.list_ref, f32[32,128,128]{2,1,0:T(8,128)} %get-tuple-element.90.far_base, f32[32,128,128]{2,1,0:T(8,128)} %get-tuple-element.116.far_d, bf16[2,128,128]{2,1,0:T(8,128)(2,1)S(1)} %broadcast_select_fusion.col_diag_ref, ...), custom_call_target="tpu_custom_call" | custom-call | tf_op jit(solution)/shard_map/exchange/diagonal/pallas_call | solution.py:687
  173.5 3.7 %all-to-all-done.5 = f32[16,2,8,128]{3,2,1,0:T(8,128)S(1)} async-done(((f32[16,2,8,128]{3,2,1,0:T(8,128)}), f32[16,2,8,128]{3,2,1,0:T(8,128)S(1)}, u32[]{:S(2)}, u32[]{:S(2)}) %all-to-all-start.5) | async-done | bytes 131104 | tf_op jit(solution)/shard_map/exchange/all_to_all | solution.py:704
  177.2 1.3 exchange.5
  178.5 3.5 %all-to-all-start.6 = ((f32[16,2,8,128]{3,2,1,0:T(8,128)}), f32[16,2,8,128]{3,2,1,0:T(8,128)S(1)}, u32[]{:S(2)}, u32[]{:S(2)}) async-start(f32[16,2,8,128]{3,2,1,0:T(8,128)} %bitcast.14), calls=%async_computation.6 | async-start | bytes 262144 | tf_op jit(solution)/shard_map/exchange/all_to_all | solution.py:714
  182.0 4.0 %diagonal.11.far_t = f32[32,128,128]{2,1,0:T(8,128)} custom-call(s32[32]{0:T(128)S(1)} %fusion.1.list_ref, f32[32,128,128]{2,1,0:T(8,128)} %get-tuple-element.90.far_base, f32[32,128,128]{2,1,0:T(8,128)} %get-tuple-element.116.far_d, bf16[2,128,128]{2,1,0:T(8,128)(2,1)S(1)} %broadcast_select_fusion.col_diag_ref, ...), custom_call_target="tpu_custom_call", output_to_operand_aliasing={{}: (13, {})} | custom-call | tf_op jit(solution)/shard_map/exchange/diagonal/pallas_call | solution.py:687
  186.0 4.0 %all-to-all-done.6.q_ref = f32[16,2,8,128]{3,2,1,0:T(8,128)S(1)} async-done(((f32[16,2,8,128]{3,2,1,0:T(8,128)}), f32[16,2,8,128]{3,2,1,0:T(8,128)S(1)}, u32[]{:S(2)}, u32[]{:S(2)}) %all-to-all-start.6) | async-done | bytes 131104 | tf_op jit(solution)/shard_map/exchange/all_to_all | solution.py:714
  190.0 5.4 %sweep.5 = f32[32,128,128]{2,1,0:T(8,128)} custom-call(s32[32]{0:T(128)S(1)} %fusion.1.list_ref, s32[1]{0:T(128)} %bitcast.1.live_ref, f32[32,128,128]{2,1,0:T(8,128)} %diagonal.11.far_t, f32[32,128,128]{2,1,0:T(8,128)} %bitcast.29, bf16[32,128,256]{2,1,0:T(8,128)(2,1)} %split.1.far_pairs, f32[16,2,8,128]{3,2,1,0:T(8,128)S(1)} %all-to-all-done.6.q_ref), custom_call_target="tpu_custom_call" | custom-call | tf_op jit(solution)/shard_map/sweep/pallas_call | solution.py:720
  (41 shorter events, 0.1 us)
Async XLA Ops:
  6.5 48.1 %all-gather.2.cloned.1.call-start = ((), (), s32[]{:S(2)}) async-start(), calls=%async_computation.7 | async-start | bytes 4456448 | tf_op jit(solution)/shard_map/slices/all_gather | solution.py:540
  11.0 3.9 %copy-start.9 = (s32[16,16,2]{1,2,0:T(2,128)S(1)}, s32[16,16,2]{1,2,0:T(2,128)}, u32[]{:S(2)}) copy-start(s32[16,16,2]{1,2,0:T(2,128)} %param.14) | copy-start | bytes 6148
  14.3 13.4 %collective-permute-start.1 = (bf16[7,2,128,128]{3,2,1,0:T(8,128)(2,1)}, bf16[7,2,128,128]{3,2,1,0:T(8,128)(2,1)S(1)}, u32[]{:S(2)}, u32[]{:S(2)}) collective-permute-start(bf16[7,2,128,128]{3,2,1,0:T(8,128)(2,1)} %get-tuple-element.68), channel_id=1, source_target_pairs={{0,1},{1,0},{2,3},{3,2},{4,5},{5,4},{6,7},{7,6},{8,9},{9,8},{10,11... | collective-permute-start | bytes 1376264 | tf_op jit(solution)/shard_map/blocks/ppermute | solution.py:601
  14.4 7.9 %collective-permute-start = (bf16[2,640,128]{2,1,0:T(8,128)(2,1)}, bf16[2,640,128]{2,1,0:T(8,128)(2,1)S(1)}, u32[]{:S(2)}, u32[]{:S(2)}) collective-permute-start(bf16[2,640,128]{2,1,0:T(8,128)(2,1)} %get-tuple-element.64), channel_id=1, source_target_pairs={{0,1},{1,0},{2,3},{3,2},{4,5},{5,4},{6,7},{7,6},{8,9},{9,8},{10,11... | collective-permute-start | bytes 983048 | tf_op jit(solution)/shard_map/blocks/ppermute | solution.py:602
  22.3 0.7 copy-start
  27.7 0.8 copy-start.8
  62.1 9.0 %copy-start.16 = (bf16[4,128,128]{2,1,0:T(8,128)(2,1)S(1)}, bf16[4,128,128]{2,1,0:T(8,128)(2,1)}, u32[]{:S(2)}) copy-start(bf16[4,128,128]{2,1,0:T(8,128)(2,1)} %get-tuple-element.84) | copy-start | bytes 393220
  62.1 9.8 %copy-start.15 = (bf16[4,128,128]{2,1,0:T(8,128)(2,1)S(1)}, bf16[4,128,128]{2,1,0:T(8,128)(2,1)}, u32[]{:S(2)}) copy-start(bf16[4,128,128]{2,1,0:T(8,128)(2,1)} %get-tuple-element.85) | copy-start | bytes 393220
  62.1 11.1 %copy-start.14 = (bf16[4,128,128]{2,1,0:T(8,128)(2,1)S(1)}, bf16[4,128,128]{2,1,0:T(8,128)(2,1)}, u32[]{:S(2)}) copy-start(bf16[4,128,128]{2,1,0:T(8,128)(2,1)} %get-tuple-element.96) | copy-start | bytes 393220
  62.1 14.6 %copy-start.13 = (bf16[4,128,128]{2,1,0:T(8,128)(2,1)S(1)}, bf16[4,128,128]{2,1,0:T(8,128)(2,1)}, u32[]{:S(2)}) copy-start(bf16[4,128,128]{2,1,0:T(8,128)(2,1)} %get-tuple-element.97) | copy-start | bytes 393220
  62.1 15.4 %copy-start.12 = (bf16[4,128,128]{2,1,0:T(8,128)(2,1)S(1)}, bf16[4,128,128]{2,1,0:T(8,128)(2,1)}, u32[]{:S(2)}) copy-start(bf16[4,128,128]{2,1,0:T(8,128)(2,1)} %get-tuple-element.98) | copy-start | bytes 393220
  62.1 18.1 %copy-start.11 = (bf16[4,128,128]{2,1,0:T(8,128)(2,1)S(1)}, bf16[4,128,128]{2,1,0:T(8,128)(2,1)}, u32[]{:S(2)}) copy-start(bf16[4,128,128]{2,1,0:T(8,128)(2,1)} %get-tuple-element.99) | copy-start | bytes 393220
  62.1 23.1 %copy-start.10 = (bf16[4,128,128]{2,1,0:T(8,128)(2,1)S(1)}, bf16[4,128,128]{2,1,0:T(8,128)(2,1)}, u32[]{:S(2)}) copy-start(bf16[4,128,128]{2,1,0:T(8,128)(2,1)} %get-tuple-element.100) | copy-start | bytes 393220
  62.1 36.1 %all-to-all-start = ((f32[16,28,8,128]{3,2,1,0:T(8,128)}), f32[16,28,8,128]{3,2,1,0:T(8,128)S(1)}, u32[]{:S(2)}, u32[]{:S(2)}) async-start(f32[16,28,8,128]{3,2,1,0:T(8,128)} %covariance.1), calls=%async_computation | async-start | bytes 3670016 | tf_op jit(solution)/shard_map/covariance/all_to_all | solution.py:658
  71.0 9.2 %collective-permute-start.2 = (bf16[4,128,128]{2,1,0:T(8,128)(2,1)S(1)}, bf16[4,128,128]{2,1,0:T(8,128)(2,1)S(1)}, u32[]{:S(2)}, u32[]{:S(2)}) collective-permute-start(bf16[4,128,128]{2,1,0:T(8,128)(2,1)S(1)} %copy-done.16), channel_id=1, source_target_pairs={{0,14},{1,15},{2,0},{3,1},{4,2},{5,3},{6,4},{7,5},{8,6},{9,7},{10,... | collective-permute-start | bytes 393224 | tf_op jit(solution)/shard_map/diag/ppermute | solution.py:617
  71.9 13.4 %collective-permute-start.3 = (bf16[4,128,128]{2,1,0:T(8,128)(2,1)S(1)}, bf16[4,128,128]{2,1,0:T(8,128)(2,1)S(1)}, u32[]{:S(2)}, u32[]{:S(2)}) collective-permute-start(bf16[4,128,128]{2,1,0:T(8,128)(2,1)S(1)} %copy-done.15), channel_id=1, source_target_pairs={{0,2},{1,3},{2,4},{3,5},{4,6},{5,7},{6,8},{7,9},{8,10},{9,11},{10,... | collective-permute-start | bytes 393224 | tf_op jit(solution)/shard_map/diag/ppermute | solution.py:617
  73.2 34.5 %collective-permute-start.4 = (bf16[4,128,128]{2,1,0:T(8,128)(2,1)S(1)}, bf16[4,128,128]{2,1,0:T(8,128)(2,1)S(1)}, u32[]{:S(2)}, u32[]{:S(2)}) collective-permute-start(bf16[4,128,128]{2,1,0:T(8,128)(2,1)S(1)} %copy-done.14), channel_id=1, source_target_pairs={{0,12},{1,13},{2,14},{3,15},{4,0},{5,1},{6,2},{7,3},{8,4},{9,5},{1... | collective-permute-start | bytes 393224 | tf_op jit(solution)/shard_map/diag/ppermute | solution.py:617
  76.7 31.0 %collective-permute-start.5 = (bf16[4,128,128]{2,1,0:T(8,128)(2,1)S(1)}, bf16[4,128,128]{2,1,0:T(8,128)(2,1)S(1)}, u32[]{:S(2)}, u32[]{:S(2)}) collective-permute-start(bf16[4,128,128]{2,1,0:T(8,128)(2,1)S(1)} %copy-done.13), channel_id=1, source_target_pairs={{0,10},{1,11},{2,12},{3,13},{4,14},{5,15},{6,0},{7,1},{8,2},{9,3},... | collective-permute-start | bytes 393224 | tf_op jit(solution)/shard_map/diag/ppermute | solution.py:617
  77.5 30.3 %collective-permute-start.6 = (bf16[4,128,128]{2,1,0:T(8,128)(2,1)S(1)}, bf16[4,128,128]{2,1,0:T(8,128)(2,1)S(1)}, u32[]{:S(2)}, u32[]{:S(2)}) collective-permute-start(bf16[4,128,128]{2,1,0:T(8,128)(2,1)S(1)} %copy-done.12), channel_id=1, source_target_pairs={{0,8},{1,9},{2,10},{3,11},{4,12},{5,13},{6,14},{7,15},{8,0},{9,1},... | collective-permute-start | bytes 393224 | tf_op jit(solution)/shard_map/diag/ppermute | solution.py:617
  80.2 23.7 %copy-start.1 = (bf16[4,128,128]{2,1,0:T(8,128)(2,1)}, bf16[4,128,128]{2,1,0:T(8,128)(2,1)S(1)}, u32[]{:S(2)}) copy-start(bf16[4,128,128]{2,1,0:T(8,128)(2,1)S(1)} %collective-permute-done.2.rest_2_) | copy-start | bytes 393220
  80.2 27.5 %collective-permute-start.7 = (bf16[4,128,128]{2,1,0:T(8,128)(2,1)S(1)}, bf16[4,128,128]{2,1,0:T(8,128)(2,1)S(1)}, u32[]{:S(2)}, u32[]{:S(2)}) collective-permute-start(bf16[4,128,128]{2,1,0:T(8,128)(2,1)S(1)} %copy-done.11), channel_id=1, source_target_pairs={{0,6},{1,7},{2,8},{3,9},{4,10},{5,11},{6,12},{7,13},{8,14},{9,15},... | collective-permute-start | bytes 393224 | tf_op jit(solution)/shard_map/diag/ppermute | solution.py:617
  85.2 18.7 %copy-start.2 = (bf16[4,128,128]{2,1,0:T(8,128)(2,1)}, bf16[4,128,128]{2,1,0:T(8,128)(2,1)S(1)}, u32[]{:S(2)}) copy-start(bf16[4,128,128]{2,1,0:T(8,128)(2,1)S(1)} %collective-permute-done.3.rest_8_) | copy-start | bytes 393220
  85.3 22.5 %collective-permute-start.8 = (bf16[4,128,128]{2,1,0:T(8,128)(2,1)S(1)}, bf16[4,128,128]{2,1,0:T(8,128)(2,1)S(1)}, u32[]{:S(2)}, u32[]{:S(2)}) collective-permute-start(bf16[4,128,128]{2,1,0:T(8,128)(2,1)S(1)} %copy-done.10), channel_id=1, source_target_pairs={{0,4},{1,5},{2,6},{3,7},{4,8},{5,9},{6,10},{7,11},{8,12},{9,13},{1... | collective-permute-start | bytes 393224 | tf_op jit(solution)/shard_map/diag/ppermute | solution.py:617
  103.9 11.5 %all-to-all-start.1 = ((f32[16,2,8,128]{3,2,1,0:T(8,128)}), f32[16,2,8,128]{3,2,1,0:T(8,128)S(1)}, u32[]{:S(2)}, u32[]{:S(2)}) async-start(f32[16,2,8,128]{3,2,1,0:T(8,128)} %get-tuple-element.92), calls=%async_computation.1 | async-start | bytes 262144 | tf_op jit(solution)/shard_map/exchange/all_to_all | solution.py:704
  107.7 0.6 copy-start.3
  107.7 0.7 copy-start.4
  107.8 0.7 copy-start.5
  107.8 0.8 copy-start.6
  107.8 0.8 copy-start.7
  116.8 12.4 %all-to-all-start.2 = ((f32[16,2,8,128]{3,2,1,0:T(8,128)}), f32[16,2,8,128]{3,2,1,0:T(8,128)S(1)}, u32[]{:S(2)}, u32[]{:S(2)}) async-start(f32[16,2,8,128]{3,2,1,0:T(8,128)} %bitcast.10), calls=%async_computation.2 | async-start | bytes 262144 | tf_op jit(solution)/shard_map/exchange/all_to_all | solution.py:714
  135.3 11.5 %all-to-all-start.3 = ((f32[16,2,8,128]{3,2,1,0:T(8,128)}), f32[16,2,8,128]{3,2,1,0:T(8,128)S(1)}, u32[]{:S(2)}, u32[]{:S(2)}) async-start(f32[16,2,8,128]{3,2,1,0:T(8,128)} %get-tuple-element.108), calls=%async_computation.3 | async-start | bytes 262144 | tf_op jit(solution)/shard_map/exchange/all_to_all | solution.py:704
  148.1 11.5 %all-to-all-start.4 = ((f32[16,2,8,128]{3,2,1,0:T(8,128)}), f32[16,2,8,128]{3,2,1,0:T(8,128)S(1)}, u32[]{:S(2)}, u32[]{:S(2)}) async-start(f32[16,2,8,128]{3,2,1,0:T(8,128)} %bitcast.12), calls=%async_computation.4 | async-start | bytes 262144 | tf_op jit(solution)/shard_map/exchange/all_to_all | solution.py:714
  165.7 11.5 %all-to-all-start.5 = ((f32[16,2,8,128]{3,2,1,0:T(8,128)}), f32[16,2,8,128]{3,2,1,0:T(8,128)S(1)}, u32[]{:S(2)}, u32[]{:S(2)}) async-start(f32[16,2,8,128]{3,2,1,0:T(8,128)} %get-tuple-element.114), calls=%async_computation.5 | async-start | bytes 262144 | tf_op jit(solution)/shard_map/exchange/all_to_all | solution.py:704
  178.5 11.5 %all-to-all-start.6 = ((f32[16,2,8,128]{3,2,1,0:T(8,128)}), f32[16,2,8,128]{3,2,1,0:T(8,128)S(1)}, u32[]{:S(2)}, u32[]{:S(2)}) async-start(f32[16,2,8,128]{3,2,1,0:T(8,128)} %bitcast.14), calls=%async_computation.6 | async-start | bytes 262144 | tf_op jit(solution)/shard_map/exchange/all_to_all | solution.py:714
Sparse Core Ops, SparseCore 0:
  10.2 44.4 all-gather.1

commit v9 on v8

--- a/solution.py
+++ b/solution.py
@@ -234,7 +234,7 @@
         out_copy(owner).start()
         return carry
 
-    lax.fori_loop(0, owners, owner_step, 0, unroll=4)
+    lax.fori_loop(0, owners, owner_step, 0, unroll=8)
     for owner in range(owners):
         out_copy(owner).wait()
 
@@ -352,8 +352,8 @@
         for array in arrays:
             array.start(chip_at(dz, col_count))
     bring.wait()
-    for begin in range(0, len(far), 2):
-        part = range(begin, min(begin + 2, len(far)))
+    for begin in range(0, len(far), 4):
+        part = range(begin, min(begin + 4, len(far)))
         chips = [chip_at(far[n], col_count) for n in part]
         for chip in chips:
             for array in arrays:

time: 204 us -> 204 us (level)
  no operation moved by 1% of the time
where the time goes in v9:
time: 204 us; the launch traced here: 203 us
  Pallas kernels  77.9 us (38%)
  waiting for transfers between devices  58.3 us (29%)
  starting transfers between devices  43.9 us (22%)
  between operations  13.8 us (7%)
  local copies, waits for them, and re-layouts  7.51 us (4%)
    pallas_call x6, Pallas kernels, diagonal(): pl.pallas_call(functools.partial(diagonal_kernel, half), in_specs=[SMEM,...  24.5 us
    all_gather x1, waiting for transfers between devices, body(): slices = lax.all_gather(mine, 'col', axis=0, tiled=True)  23.2 us
    pallas_call x3, Pallas kernels, body(): pl.pallas_call(functools.partial(sweep_kernel, last), in_specs=[SMEM, SME...  17.7 us
    ppermute x7, starting transfers between devices, send(): lax.ppermute(far_out[dz - 1], 'col', [(h, (h // CORES - dz) % chips * COR...  14.2 us
    all_to_all x1, waiting for transfers between devices, body(): lax.all_to_all(partial, 'row', split_axis=0, concat_axis=0, tiled=True)  12.9 us
    all_to_all x3, waiting for transfers between devices, body(): lax.all_to_all(summed.reshape(piece_shape), 'row', split_axis=0, concat_a...  12 us
    all_to_all x3, starting transfers between devices, body(): lax.all_to_all(summed.reshape(piece_shape), 'row', split_axis=0, concat_a...  11.4 us
    all_to_all x3, starting transfers between devices, body(): got = lax.all_to_all(pieces, 'row', split_axis=0, concat_axis=0, tiled=True)  10.7 us
  transfers between devices with their start and end apart: 17, of which 8 were waited for; matrix products, arithmetic and copies ran while one was open for 3% of the time, Pallas kernels for 22%

profile of v9, /device:TPU:32, one launch (start us, length us, event | category | flops | bytes accessed | tf_op | source)
XLA Modules:
  0.0 202.8 jit_solution(6813235410267113937)
XLA Ops:
  6.5 3.5 %slices.1 = bf16[32,8,512]{2,1,0:T(8,128)(2,1)} custom-call(bf16[32,512,128]{2,1,0:T(8,128)(2,1)} %features.7), custom_call_target="tpu_custom_call" | custom-call | tf_op jit(solution)/shard_map/slices/pallas_call | solution.py:530
  10.1 0.8 dynamic-slice_subtract_fusion.1
  10.9 0.1 copy.35
  11.0 0.1 copy.31.wanted_ref
  11.0 3.2 %blocks.3 = (bf16[2,640,128]{2,1,0:T(8,128)(2,1)}, bf16[2,640,128]{2,1,0:T(8,128)(2,1)}, bf16[7,2,128,128]{3,2,1,0:T(8,128)(2,1)}) custom-call(s32[16,2]{1,0:T(8,128)S(1)} %copy.31.wanted_ref, bf16[32,512,128]{2,1,0:T(8,128)(2,1)} %features.7, bf16[32,128,128]{2,1,0:T(8,128)(2,1)} %diag.3), custom_call_target="tpu_custom_call" | custom-call | tf_op jit(solution)/shard_map/blocks/pallas_call | solution.py:582
  14.3 0.1 collective-permute-start.1
  14.4 0.5 collective-permute-start
  14.9 0.4 fusion.3
  15.3 0.1 fusion.owned_ref
  15.4 0.1 copy.29
  15.5 1.3 dynamic_slice.26
  16.8 3.8 %split.1.far_pairs = bf16[32,128,256]{2,1,0:T(8,128)(2,1)} custom-call(f32[32,128,128]{2,1,0:T(8,128)} %bitcast.30), custom_call_target="tpu_custom_call" | custom-call | tf_op jit(solution)/shard_map/split/pallas_call | solution.py:565
  20.6 0.1 copy.33.owned_ref
  20.7 0.7 fusion.1.list_ref
  21.4 0.9 constant_dynamic-slice_fusion.1
  22.3 0.7 copy-done
  23.0 4.6 %blocks.4 = (f32[32,128,128]{2,1,0:T(8,128)}, f32[32,128,128]{2,1,0:T(8,128)}, f32[2,128,256]{2,1,0:T(8,128)}) custom-call(s32[32]{0:T(128)S(1)} %fusion.1.list_ref, s32[1]{0:T(128)} %bitcast.1.live_ref, s32[2]{0:T(128)S(1)} %fusion.owned_ref, bf16[32,512,128]{2,1,0:T(8,128)(2,1)} %features.7, f32[32,128,128]{2,1,0:T(8,128)} %bitcast.25, ...), custom_call_target="tpu_custom_call" | custom-call | tf_op jit(solution)/shard_map/blocks/pallas_call | solution.py:621
  27.7 0.8 copy-done.8
  28.5 3.0 %blocks.5 = (bf16[4,128,128]{2,1,0:T(8,128)(2,1)}, bf16[4,128,128]{2,1,0:T(8,128)(2,1)}, bf16[4,128,128]{2,1,0:T(8,128)(2,1)}, bf16[4,128,128]{2,1,0:T(8,128)(2,...) custom-call(s32[16,2]{1,0:T(8,128)S(1)} %copy.31.wanted_ref, ...), custom_call_target="tpu_custom_call" | custom-call | tf_op jit(solution)/shard_map/blocks/pallas_call | solution.py:603
  31.5 23.2 %all-gather.2.cloned.1.call-done.far_slices = bf16[512,8,512]{2,1,0:T(8,128)(2,1)} async-done(((bf16[32,8,512]{2,1,0:T(8,128)(2,1)}), bf16[512,8,512]{2,1,0:T(8,128)(2,1)}) %all-gather.2.cloned.1.call-update) | async-done | bytes 4194320 | tf_op jit(solution)/shard_map/slices/all_gather | solution.py:540
  54.7 7.4 %covariance.1 = f32[16,28,8,128]{3,2,1,0:T(8,128)} custom-call(s32[16,32]{1,0:T(8,128)S(1)} %bitcast.24, s32[16,32]{1,0:T(8,128)S(1)} %bitcast.23, s32[16,2]{1,0:T(8,128)S(1)} %copy.33.owned_ref, bf16[512,8,512]{2,1,0:T(8,128)(2,1)} %all-gather.2.cloned.1.call-done.far_slices, bf16[32,512,128]{2,1,0:T(8,128)(2,1)} %features.7), custom_call_target="tpu_custom_call" | custom-call | tf_op jit(solution)/shard_map/covariance/pallas_call | solution.py:643
  62.1 7.0 %all-to-all-start = ((f32[16,28,8,128]{3,2,1,0:T(8,128)}), f32[16,28,8,128]{3,2,1,0:T(8,128)S(1)}, u32[]{:S(2)}, u32[]{:S(2)}) async-start(f32[16,28,8,128]{3,2,1,0:T(8,128)} %covariance.1), calls=%async_computation | async-start | bytes 3670016 | tf_op jit(solution)/shard_map/covariance/all_to_all | solution.py:658
  69.1 1.8 gather_fusion
  70.9 0.1 sub.25
  71.0 0.9 collective-permute-start.2
  71.9 1.3 collective-permute-start.3
  73.1 0.1 broadcast_select_fusion.col_diag_ref
  73.2 3.5 %collective-permute-start.4 = (bf16[4,128,128]{2,1,0:T(8,128)(2,1)S(1)}, bf16[4,128,128]{2,1,0:T(8,128)(2,1)S(1)}, u32[]{:S(2)}, u32[]{:S(2)}) collective-permute-start(bf16[4,128,128]{2,1,0:T(8,128)(2,1)S(1)} %copy-done.14), channel_id=1, source_target_pairs={{0,12},{1,13},{2,14},{3,15},{4,0},{5,1},{6,2},{7,3},{8,4},{9,5},{1... | collective-permute-start | bytes 393224 | tf_op jit(solution)/shard_map/diag/ppermute | solution.py:617
  76.7 0.8 collective-permute-start.5
  77.5 2.8 %collective-permute-start.6 = (bf16[4,128,128]{2,1,0:T(8,128)(2,1)S(1)}, bf16[4,128,128]{2,1,0:T(8,128)(2,1)S(1)}, u32[]{:S(2)}, u32[]{:S(2)}) collective-permute-start(bf16[4,128,128]{2,1,0:T(8,128)(2,1)S(1)} %copy-done.12), channel_id=1, source_target_pairs={{0,8},{1,9},{2,10},{3,11},{4,12},{5,13},{6,14},{7,15},{8,0},{9,1},... | collective-permute-start | bytes 393224 | tf_op jit(solution)/shard_map/diag/ppermute | solution.py:617
  80.2 5.0 %collective-permute-start.7 = (bf16[4,128,128]{2,1,0:T(8,128)(2,1)S(1)}, bf16[4,128,128]{2,1,0:T(8,128)(2,1)S(1)}, u32[]{:S(2)}, u32[]{:S(2)}) collective-permute-start(bf16[4,128,128]{2,1,0:T(8,128)(2,1)S(1)} %copy-done.11), channel_id=1, source_target_pairs={{0,6},{1,7},{2,8},{3,9},{4,10},{5,11},{6,12},{7,13},{8,14},{9,15},... | collective-permute-start | bytes 393224 | tf_op jit(solution)/shard_map/diag/ppermute | solution.py:617
  85.3 0.1 collective-permute-start.8
  85.4 12.9 %all-to-all-done.cov_ref = f32[16,28,8,128]{3,2,1,0:T(8,128)S(1)} async-done(((f32[16,28,8,128]{3,2,1,0:T(8,128)}), f32[16,28,8,128]{3,2,1,0:T(8,128)S(1)}, u32[]{:S(2)}, u32[]{:S(2)}) %all-to-all-start) | async-done | bytes 1835040 | tf_op jit(solution)/shard_map/covariance/all_to_all | solution.py:658
  98.3 6.2 %first.1 = (f32[32,128,128]{2,1,0:T(8,128)}, f32[32,128,128]{2,1,0:T(8,128)}, f32[16,2,8,128]{3,2,1,0:T(8,128)}) custom-call(s32[32]{0:T(128)S(1)} %fusion.1.list_ref, s32[1]{0:T(128)} %bitcast.1.live_ref, f32[16,28,8,128]{3,2,1,0:T(8,128)S(1)} %all-to-all-done.cov_ref, ...), custom_call_target="tpu_custom_call", output_to_operand_aliasing={{0}: (6, {}), {1}: (7, {})} | custom-call | tf_op jit(solution)/shard_map/first/pallas_call | solution.py:669
  104.5 3.7 %all-to-all-start.1 = ((f32[16,2,8,128]{3,2,1,0:T(8,128)}), f32[16,2,8,128]{3,2,1,0:T(8,128)S(1)}, u32[]{:S(2)}, u32[]{:S(2)}) async-start(f32[16,2,8,128]{3,2,1,0:T(8,128)} %get-tuple-element.92), calls=%async_computation.1 | async-start | bytes 262144 | tf_op jit(solution)/shard_map/exchange/all_to_all | solution.py:704
  108.2 0.1 compare_convert_fusion.same_ref
  108.4 0.6 copy-done.3
  108.9 0.1 copy-done.4
  109.0 0.1 copy-done.5
  109.0 0.1 copy-done.6
  109.1 0.0 copy-done.7
  109.1 4.2 %diagonal.6.rest_9_ = f32[32,128,128]{2,1,0:T(8,128)} custom-call(s32[32]{0:T(128)S(1)} %fusion.1.list_ref, f32[32,128,128]{2,1,0:T(8,128)} %get-tuple-element.90.far_base, f32[32,128,128]{2,1,0:T(8,128)} %get-tuple-element.103.far_d, bf16[2,128,128]{2,1,0:T(8,128)(2,1)S(1)} %broadcast_select_fusion.col_diag_ref, ...), custom_call_target="tpu_custom_call" | custom-call | tf_op jit(solution)/shard_map/exchange/diagonal/pallas_call | solution.py:687
  113.3 2.7 %all-to-all-done.1 = f32[16,2,8,128]{3,2,1,0:T(8,128)S(1)} async-done(((f32[16,2,8,128]{3,2,1,0:T(8,128)}), f32[16,2,8,128]{3,2,1,0:T(8,128)S(1)}, u32[]{:S(2)}, u32[]{:S(2)}) %all-to-all-start.1) | async-done | bytes 131104 | tf_op jit(solution)/shard_map/exchange/all_to_all | solution.py:704
  116.0 1.3 exchange.3
  117.3 4.4 %all-to-all-start.2 = ((f32[16,2,8,128]{3,2,1,0:T(8,128)}), f32[16,2,8,128]{3,2,1,0:T(8,128)S(1)}, u32[]{:S(2)}, u32[]{:S(2)}) async-start(f32[16,2,8,128]{3,2,1,0:T(8,128)} %bitcast.10), calls=%async_computation.2 | async-start | bytes 262144 | tf_op jit(solution)/shard_map/exchange/all_to_all | solution.py:714
  121.7 4.0 %diagonal.7.far_t = f32[32,128,128]{2,1,0:T(8,128)} custom-call(s32[32]{0:T(128)S(1)} %fusion.1.list_ref, f32[32,128,128]{2,1,0:T(8,128)} %get-tuple-element.90.far_base, f32[32,128,128]{2,1,0:T(8,128)} %get-tuple-element.103.far_d, bf16[2,128,128]{2,1,0:T(8,128)(2,1)S(1)} %broadcast_select_fusion.col_diag_ref, ...), custom_call_target="tpu_custom_call", output_to_operand_aliasing={{}: (13, {})} | custom-call | tf_op jit(solution)/shard_map/exchange/diagonal/pallas_call | solution.py:687
  125.6 4.0 %all-to-all-done.2.q_ref = f32[16,2,8,128]{3,2,1,0:T(8,128)S(1)} async-done(((f32[16,2,8,128]{3,2,1,0:T(8,128)}), f32[16,2,8,128]{3,2,1,0:T(8,128)S(1)}, u32[]{:S(2)}, u32[]{:S(2)}) %all-to-all-start.2) | async-done | bytes 131104 | tf_op jit(solution)/shard_map/exchange/all_to_all | solution.py:714
  129.7 6.2 %sweep.3 = (f32[32,128,128]{2,1,0:T(8,128)}, f32[16,2,8,128]{3,2,1,0:T(8,128)}) custom-call(s32[32]{0:T(128)S(1)} %fusion.1.list_ref, s32[1]{0:T(128)} %bitcast.1.live_ref, f32[32,128,128]{2,1,0:T(8,128)} %diagonal.7.far_t, f32[32,128,128]{2,1,0:T(8,128)} %bitcast.27, bf16[32,128,256]{2,1,0:T(8,128)(2,1)} %split.1.far_pairs, ...), custom_call_target="tpu_custom_call" | custom-call | tf_op jit(solution)/shard_map/sweep/pallas_call | solution.py:720
  135.8 3.5 %all-to-all-start.3 = ((f32[16,2,8,128]{3,2,1,0:T(8,128)}), f32[16,2,8,128]{3,2,1,0:T(8,128)S(1)}, u32[]{:S(2)}, u32[]{:S(2)}) async-start(f32[16,2,8,128]{3,2,1,0:T(8,128)} %get-tuple-element.108), calls=%async_computation.3 | async-start | bytes 262144 | tf_op jit(solution)/shard_map/exchange/all_to_all | solution.py:704
  139.4 4.2 %diagonal.8.rest_9_ = f32[32,128,128]{2,1,0:T(8,128)} custom-call(s32[32]{0:T(128)S(1)} %fusion.1.list_ref, f32[32,128,128]{2,1,0:T(8,128)} %get-tuple-element.90.far_base, f32[32,128,128]{2,1,0:T(8,128)} %get-tuple-element.110.far_d, bf16[2,128,128]{2,1,0:T(8,128)(2,1)S(1)} %broadcast_select_fusion.col_diag_ref, ...), custom_call_target="tpu_custom_call" | custom-call | tf_op jit(solution)/shard_map/exchange/diagonal/pallas_call | solution.py:687
  143.6 3.7 %all-to-all-done.3 = f32[16,2,8,128]{3,2,1,0:T(8,128)S(1)} async-done(((f32[16,2,8,128]{3,2,1,0:T(8,128)}), f32[16,2,8,128]{3,2,1,0:T(8,128)S(1)}, u32[]{:S(2)}, u32[]{:S(2)}) %all-to-all-start.3) | async-done | bytes 131104 | tf_op jit(solution)/shard_map/exchange/all_to_all | solution.py:704
  147.3 1.3 exchange.4
  148.6 3.5 %all-to-all-start.4 = ((f32[16,2,8,128]{3,2,1,0:T(8,128)}), f32[16,2,8,128]{3,2,1,0:T(8,128)S(1)}, u32[]{:S(2)}, u32[]{:S(2)}) async-start(f32[16,2,8,128]{3,2,1,0:T(8,128)} %bitcast.12), calls=%async_computation.4 | async-start | bytes 262144 | tf_op jit(solution)/shard_map/exchange/all_to_all | solution.py:714
  152.1 4.0 %diagonal.9.far_t = f32[32,128,128]{2,1,0:T(8,128)} custom-call(s32[32]{0:T(128)S(1)} %fusion.1.list_ref, f32[32,128,128]{2,1,0:T(8,128)} %get-tuple-element.90.far_base, f32[32,128,128]{2,1,0:T(8,128)} %get-tuple-element.110.far_d, bf16[2,128,128]{2,1,0:T(8,128)(2,1)S(1)} %broadcast_select_fusion.col_diag_ref, ...), custom_call_target="tpu_custom_call", output_to_operand_aliasing={{}: (13, {})} | custom-call | tf_op jit(solution)/shard_map/exchange/diagonal/pallas_call | solution.py:687
  156.1 4.0 %all-to-all-done.4.q_ref = f32[16,2,8,128]{3,2,1,0:T(8,128)S(1)} async-done(((f32[16,2,8,128]{3,2,1,0:T(8,128)}), f32[16,2,8,128]{3,2,1,0:T(8,128)S(1)}, u32[]{:S(2)}, u32[]{:S(2)}) %all-to-all-start.4) | async-done | bytes 131104 | tf_op jit(solution)/shard_map/exchange/all_to_all | solution.py:714
  160.1 6.2 %sweep.4 = (f32[32,128,128]{2,1,0:T(8,128)}, f32[16,2,8,128]{3,2,1,0:T(8,128)}) custom-call(s32[32]{0:T(128)S(1)} %fusion.1.list_ref, s32[1]{0:T(128)} %bitcast.1.live_ref, f32[32,128,128]{2,1,0:T(8,128)} %diagonal.9.far_t, f32[32,128,128]{2,1,0:T(8,128)} %bitcast.28, bf16[32,128,256]{2,1,0:T(8,128)(2,1)} %split.1.far_pairs, ...), custom_call_target="tpu_custom_call" | custom-call | tf_op jit(solution)/shard_map/sweep/pallas_call | solution.py:720
  166.3 3.5 %all-to-all-start.5 = ((f32[16,2,8,128]{3,2,1,0:T(8,128)}), f32[16,2,8,128]{3,2,1,0:T(8,128)S(1)}, u32[]{:S(2)}, u32[]{:S(2)}) async-start(f32[16,2,8,128]{3,2,1,0:T(8,128)} %get-tuple-element.114), calls=%async_computation.5 | async-start | bytes 262144 | tf_op jit(solution)/shard_map/exchange/all_to_all | solution.py:704
  169.8 4.2 %diagonal.10.rest_9_ = f32[32,128,128]{2,1,0:T(8,128)} custom-call(s32[32]{0:T(128)S(1)} %fusion.1.list_ref, f32[32,128,128]{2,1,0:T(8,128)} %get-tuple-element.90.far_base, f32[32,128,128]{2,1,0:T(8,128)} %get-tuple-element.116.far_d, bf16[2,128,128]{2,1,0:T(8,128)(2,1)S(1)} %broadcast_select_fusion.col_diag_ref, ...), custom_call_target="tpu_custom_call" | custom-call | tf_op jit(solution)/shard_map/exchange/diagonal/pallas_call | solution.py:687
  174.0 3.7 %all-to-all-done.5 = f32[16,2,8,128]{3,2,1,0:T(8,128)S(1)} async-done(((f32[16,2,8,128]{3,2,1,0:T(8,128)}), f32[16,2,8,128]{3,2,1,0:T(8,128)S(1)}, u32[]{:S(2)}, u32[]{:S(2)}) %all-to-all-start.5) | async-done | bytes 131104 | tf_op jit(solution)/shard_map/exchange/all_to_all | solution.py:704
  177.7 1.3 exchange.5
  179.1 3.5 %all-to-all-start.6 = ((f32[16,2,8,128]{3,2,1,0:T(8,128)}), f32[16,2,8,128]{3,2,1,0:T(8,128)S(1)}, u32[]{:S(2)}, u32[]{:S(2)}) async-start(f32[16,2,8,128]{3,2,1,0:T(8,128)} %bitcast.14), calls=%async_computation.6 | async-start | bytes 262144 | tf_op jit(solution)/shard_map/exchange/all_to_all | solution.py:714
  182.6 4.0 %diagonal.11.far_t = f32[32,128,128]{2,1,0:T(8,128)} custom-call(s32[32]{0:T(128)S(1)} %fusion.1.list_ref, f32[32,128,128]{2,1,0:T(8,128)} %get-tuple-element.90.far_base, f32[32,128,128]{2,1,0:T(8,128)} %get-tuple-element.116.far_d, bf16[2,128,128]{2,1,0:T(8,128)(2,1)S(1)} %broadcast_select_fusion.col_diag_ref, ...), custom_call_target="tpu_custom_call", output_to_operand_aliasing={{}: (13, {})} | custom-call | tf_op jit(solution)/shard_map/exchange/diagonal/pallas_call | solution.py:687
  186.5 4.0 %all-to-all-done.6.q_ref = f32[16,2,8,128]{3,2,1,0:T(8,128)S(1)} async-done(((f32[16,2,8,128]{3,2,1,0:T(8,128)}), f32[16,2,8,128]{3,2,1,0:T(8,128)S(1)}, u32[]{:S(2)}, u32[]{:S(2)}) %all-to-all-start.6) | async-done | bytes 131104 | tf_op jit(solution)/shard_map/exchange/all_to_all | solution.py:714
  190.5 5.4 %sweep.5 = f32[32,128,128]{2,1,0:T(8,128)} custom-call(s32[32]{0:T(128)S(1)} %fusion.1.list_ref, s32[1]{0:T(128)} %bitcast.1.live_ref, f32[32,128,128]{2,1,0:T(8,128)} %diagonal.11.far_t, f32[32,128,128]{2,1,0:T(8,128)} %bitcast.29, bf16[32,128,256]{2,1,0:T(8,128)(2,1)} %split.1.far_pairs, f32[16,2,8,128]{3,2,1,0:T(8,128)S(1)} %all-to-all-done.6.q_ref), custom_call_target="tpu_custom_call" | custom-call | tf_op jit(solution)/shard_map/sweep/pallas_call | solution.py:720
  (41 shorter events, 0.1 us)
Async XLA Ops:
  6.5 48.1 %all-gather.2.cloned.1.call-start = ((), (), s32[]{:S(2)}) async-start(), calls=%async_computation.7 | async-start | bytes 4456448 | tf_op jit(solution)/shard_map/slices/all_gather | solution.py:540
  11.0 3.8 %copy-start.9 = (s32[16,16,2]{1,2,0:T(2,128)S(1)}, s32[16,16,2]{1,2,0:T(2,128)}, u32[]{:S(2)}) copy-start(s32[16,16,2]{1,2,0:T(2,128)} %param.14) | copy-start | bytes 6148
  14.3 13.4 %collective-permute-start.1 = (bf16[7,2,128,128]{3,2,1,0:T(8,128)(2,1)}, bf16[7,2,128,128]{3,2,1,0:T(8,128)(2,1)S(1)}, u32[]{:S(2)}, u32[]{:S(2)}) collective-permute-start(bf16[7,2,128,128]{3,2,1,0:T(8,128)(2,1)} %get-tuple-element.68), channel_id=1, source_target_pairs={{0,1},{1,0},{2,3},{3,2},{4,5},{5,4},{6,7},{7,6},{8,9},{9,8},{10,11... | collective-permute-start | bytes 1376264 | tf_op jit(solution)/shard_map/blocks/ppermute | solution.py:601
  14.4 7.9 %collective-permute-start = (bf16[2,640,128]{2,1,0:T(8,128)(2,1)}, bf16[2,640,128]{2,1,0:T(8,128)(2,1)S(1)}, u32[]{:S(2)}, u32[]{:S(2)}) collective-permute-start(bf16[2,640,128]{2,1,0:T(8,128)(2,1)} %get-tuple-element.64), channel_id=1, source_target_pairs={{0,1},{1,0},{2,3},{3,2},{4,5},{5,4},{6,7},{7,6},{8,9},{9,8},{10,11... | collective-permute-start | bytes 983048 | tf_op jit(solution)/shard_map/blocks/ppermute | solution.py:602
  22.3 0.7 copy-start
  27.7 0.8 copy-start.8
  62.1 9.0 %copy-start.16 = (bf16[4,128,128]{2,1,0:T(8,128)(2,1)S(1)}, bf16[4,128,128]{2,1,0:T(8,128)(2,1)}, u32[]{:S(2)}) copy-start(bf16[4,128,128]{2,1,0:T(8,128)(2,1)} %get-tuple-element.84) | copy-start | bytes 393220
  62.1 9.8 %copy-start.15 = (bf16[4,128,128]{2,1,0:T(8,128)(2,1)S(1)}, bf16[4,128,128]{2,1,0:T(8,128)(2,1)}, u32[]{:S(2)}) copy-start(bf16[4,128,128]{2,1,0:T(8,128)(2,1)} %get-tuple-element.85) | copy-start | bytes 393220
  62.1 11.1 %copy-start.14 = (bf16[4,128,128]{2,1,0:T(8,128)(2,1)S(1)}, bf16[4,128,128]{2,1,0:T(8,128)(2,1)}, u32[]{:S(2)}) copy-start(bf16[4,128,128]{2,1,0:T(8,128)(2,1)} %get-tuple-element.96) | copy-start | bytes 393220
  62.1 14.6 %copy-start.13 = (bf16[4,128,128]{2,1,0:T(8,128)(2,1)S(1)}, bf16[4,128,128]{2,1,0:T(8,128)(2,1)}, u32[]{:S(2)}) copy-start(bf16[4,128,128]{2,1,0:T(8,128)(2,1)} %get-tuple-element.97) | copy-start | bytes 393220
  62.1 15.4 %copy-start.12 = (bf16[4,128,128]{2,1,0:T(8,128)(2,1)S(1)}, bf16[4,128,128]{2,1,0:T(8,128)(2,1)}, u32[]{:S(2)}) copy-start(bf16[4,128,128]{2,1,0:T(8,128)(2,1)} %get-tuple-element.98) | copy-start | bytes 393220
  62.1 18.1 %copy-start.11 = (bf16[4,128,128]{2,1,0:T(8,128)(2,1)S(1)}, bf16[4,128,128]{2,1,0:T(8,128)(2,1)}, u32[]{:S(2)}) copy-start(bf16[4,128,128]{2,1,0:T(8,128)(2,1)} %get-tuple-element.99) | copy-start | bytes 393220
  62.1 23.1 %copy-start.10 = (bf16[4,128,128]{2,1,0:T(8,128)(2,1)S(1)}, bf16[4,128,128]{2,1,0:T(8,128)(2,1)}, u32[]{:S(2)}) copy-start(bf16[4,128,128]{2,1,0:T(8,128)(2,1)} %get-tuple-element.100) | copy-start | bytes 393220
  62.1 36.1 %all-to-all-start = ((f32[16,28,8,128]{3,2,1,0:T(8,128)}), f32[16,28,8,128]{3,2,1,0:T(8,128)S(1)}, u32[]{:S(2)}, u32[]{:S(2)}) async-start(f32[16,28,8,128]{3,2,1,0:T(8,128)} %covariance.1), calls=%async_computation | async-start | bytes 3670016 | tf_op jit(solution)/shard_map/covariance/all_to_all | solution.py:658
  71.0 9.2 %collective-permute-start.2 = (bf16[4,128,128]{2,1,0:T(8,128)(2,1)S(1)}, bf16[4,128,128]{2,1,0:T(8,128)(2,1)S(1)}, u32[]{:S(2)}, u32[]{:S(2)}) collective-permute-start(bf16[4,128,128]{2,1,0:T(8,128)(2,1)S(1)} %copy-done.16), channel_id=1, source_target_pairs={{0,14},{1,15},{2,0},{3,1},{4,2},{5,3},{6,4},{7,5},{8,6},{9,7},{10,... | collective-permute-start | bytes 393224 | tf_op jit(solution)/shard_map/diag/ppermute | solution.py:617
  71.9 13.4 %collective-permute-start.3 = (bf16[4,128,128]{2,1,0:T(8,128)(2,1)S(1)}, bf16[4,128,128]{2,1,0:T(8,128)(2,1)S(1)}, u32[]{:S(2)}, u32[]{:S(2)}) collective-permute-start(bf16[4,128,128]{2,1,0:T(8,128)(2,1)S(1)} %copy-done.15), channel_id=1, source_target_pairs={{0,2},{1,3},{2,4},{3,5},{4,6},{5,7},{6,8},{7,9},{8,10},{9,11},{10,... | collective-permute-start | bytes 393224 | tf_op jit(solution)/shard_map/diag/ppermute | solution.py:617
  73.2 35.0 %collective-permute-start.4 = (bf16[4,128,128]{2,1,0:T(8,128)(2,1)S(1)}, bf16[4,128,128]{2,1,0:T(8,128)(2,1)S(1)}, u32[]{:S(2)}, u32[]{:S(2)}) collective-permute-start(bf16[4,128,128]{2,1,0:T(8,128)(2,1)S(1)} %copy-done.14), channel_id=1, source_target_pairs={{0,12},{1,13},{2,14},{3,15},{4,0},{5,1},{6,2},{7,3},{8,4},{9,5},{1... | collective-permute-start | bytes 393224 | tf_op jit(solution)/shard_map/diag/ppermute | solution.py:617
  76.7 31.6 %collective-permute-start.5 = (bf16[4,128,128]{2,1,0:T(8,128)(2,1)S(1)}, bf16[4,128,128]{2,1,0:T(8,128)(2,1)S(1)}, u32[]{:S(2)}, u32[]{:S(2)}) collective-permute-start(bf16[4,128,128]{2,1,0:T(8,128)(2,1)S(1)} %copy-done.13), channel_id=1, source_target_pairs={{0,10},{1,11},{2,12},{3,13},{4,14},{5,15},{6,0},{7,1},{8,2},{9,3},... | collective-permute-start | bytes 393224 | tf_op jit(solution)/shard_map/diag/ppermute | solution.py:617
  77.5 30.8 %collective-permute-start.6 = (bf16[4,128,128]{2,1,0:T(8,128)(2,1)S(1)}, bf16[4,128,128]{2,1,0:T(8,128)(2,1)S(1)}, u32[]{:S(2)}, u32[]{:S(2)}) collective-permute-start(bf16[4,128,128]{2,1,0:T(8,128)(2,1)S(1)} %copy-done.12), channel_id=1, source_target_pairs={{0,8},{1,9},{2,10},{3,11},{4,12},{5,13},{6,14},{7,15},{8,0},{9,1},... | collective-permute-start | bytes 393224 | tf_op jit(solution)/shard_map/diag/ppermute | solution.py:617
  80.2 24.2 %copy-start.1 = (bf16[4,128,128]{2,1,0:T(8,128)(2,1)}, bf16[4,128,128]{2,1,0:T(8,128)(2,1)S(1)}, u32[]{:S(2)}) copy-start(bf16[4,128,128]{2,1,0:T(8,128)(2,1)S(1)} %collective-permute-done.2.rest_2_) | copy-start | bytes 393220
  80.2 28.1 %collective-permute-start.7 = (bf16[4,128,128]{2,1,0:T(8,128)(2,1)S(1)}, bf16[4,128,128]{2,1,0:T(8,128)(2,1)S(1)}, u32[]{:S(2)}, u32[]{:S(2)}) collective-permute-start(bf16[4,128,128]{2,1,0:T(8,128)(2,1)S(1)} %copy-done.11), channel_id=1, source_target_pairs={{0,6},{1,7},{2,8},{3,9},{4,10},{5,11},{6,12},{7,13},{8,14},{9,15},... | collective-permute-start | bytes 393224 | tf_op jit(solution)/shard_map/diag/ppermute | solution.py:617
  85.3 19.2 %copy-start.2 = (bf16[4,128,128]{2,1,0:T(8,128)(2,1)}, bf16[4,128,128]{2,1,0:T(8,128)(2,1)S(1)}, u32[]{:S(2)}) copy-start(bf16[4,128,128]{2,1,0:T(8,128)(2,1)S(1)} %collective-permute-done.3.rest_8_) | copy-start | bytes 393220
  85.3 23.1 %collective-permute-start.8 = (bf16[4,128,128]{2,1,0:T(8,128)(2,1)S(1)}, bf16[4,128,128]{2,1,0:T(8,128)(2,1)S(1)}, u32[]{:S(2)}, u32[]{:S(2)}) collective-permute-start(bf16[4,128,128]{2,1,0:T(8,128)(2,1)S(1)} %copy-done.10), channel_id=1, source_target_pairs={{0,4},{1,5},{2,6},{3,7},{4,8},{5,9},{6,10},{7,11},{8,12},{9,13},{1... | collective-permute-start | bytes 393224 | tf_op jit(solution)/shard_map/diag/ppermute | solution.py:617
  104.5 11.5 %all-to-all-start.1 = ((f32[16,2,8,128]{3,2,1,0:T(8,128)}), f32[16,2,8,128]{3,2,1,0:T(8,128)S(1)}, u32[]{:S(2)}, u32[]{:S(2)}) async-start(f32[16,2,8,128]{3,2,1,0:T(8,128)} %get-tuple-element.92), calls=%async_computation.1 | async-start | bytes 262144 | tf_op jit(solution)/shard_map/exchange/all_to_all | solution.py:704
  108.3 0.6 copy-start.3
  108.3 0.7 copy-start.4
  108.3 0.7 copy-start.5
  108.3 0.8 copy-start.6
  108.3 0.8 copy-start.7
  117.3 12.4 %all-to-all-start.2 = ((f32[16,2,8,128]{3,2,1,0:T(8,128)}), f32[16,2,8,128]{3,2,1,0:T(8,128)S(1)}, u32[]{:S(2)}, u32[]{:S(2)}) async-start(f32[16,2,8,128]{3,2,1,0:T(8,128)} %bitcast.10), calls=%async_computation.2 | async-start | bytes 262144 | tf_op jit(solution)/shard_map/exchange/all_to_all | solution.py:714
  135.8 11.5 %all-to-all-start.3 = ((f32[16,2,8,128]{3,2,1,0:T(8,128)}), f32[16,2,8,128]{3,2,1,0:T(8,128)S(1)}, u32[]{:S(2)}, u32[]{:S(2)}) async-start(f32[16,2,8,128]{3,2,1,0:T(8,128)} %get-tuple-element.108), calls=%async_computation.3 | async-start | bytes 262144 | tf_op jit(solution)/shard_map/exchange/all_to_all | solution.py:704
  148.6 11.5 %all-to-all-start.4 = ((f32[16,2,8,128]{3,2,1,0:T(8,128)}), f32[16,2,8,128]{3,2,1,0:T(8,128)S(1)}, u32[]{:S(2)}, u32[]{:S(2)}) async-start(f32[16,2,8,128]{3,2,1,0:T(8,128)} %bitcast.12), calls=%async_computation.4 | async-start | bytes 262144 | tf_op jit(solution)/shard_map/exchange/all_to_all | solution.py:714
  166.3 11.5 %all-to-all-start.5 = ((f32[16,2,8,128]{3,2,1,0:T(8,128)}), f32[16,2,8,128]{3,2,1,0:T(8,128)S(1)}, u32[]{:S(2)}, u32[]{:S(2)}) async-start(f32[16,2,8,128]{3,2,1,0:T(8,128)} %get-tuple-element.114), calls=%async_computation.5 | async-start | bytes 262144 | tf_op jit(solution)/shard_map/exchange/all_to_all | solution.py:704
  179.1 11.5 %all-to-all-start.6 = ((f32[16,2,8,128]{3,2,1,0:T(8,128)}), f32[16,2,8,128]{3,2,1,0:T(8,128)S(1)}, u32[]{:S(2)}, u32[]{:S(2)}) async-start(f32[16,2,8,128]{3,2,1,0:T(8,128)} %bitcast.14), calls=%async_computation.6 | async-start | bytes 262144 | tf_op jit(solution)/shard_map/exchange/all_to_all | solution.py:714
Sparse Core Ops, SparseCore 0:
  10.2 44.4 all-gather.1

commit v10 on v8

--- a/solution.py
+++ b/solution.py
@@ -533,7 +533,7 @@
             out_specs=VMEM,
             out_shape=shape((blocks, group, samples), BF),
             scratch_shapes=[
-                pltpu.VMEM(features.shape, BF), pltpu.SemaphoreType.DMA((4,))
+                pltpu.VMEM(features.shape, BF), pltpu.SemaphoreType.DMA((2,))
             ],
             compiler_params=PARAMS,
         )(far(features))

time: 204 us -> 204 us (level)
  no operation moved by 1% of the time
where the time goes in v10:
time: 204 us; the launch traced here: 202 us
  Pallas kernels  77.5 us (38%)
  waiting for transfers between devices  58.3 us (29%)
  starting transfers between devices  43.9 us (22%)
  between operations  13.8 us (7%)
  local copies, waits for them, and re-layouts  7.51 us (4%)
    pallas_call x6, Pallas kernels, diagonal(): pl.pallas_call(functools.partial(diagonal_kernel, half), in_specs=[SMEM,...  24.5 us
    all_gather x1, waiting for transfers between devices, body(): slices = lax.all_gather(mine, 'col', axis=0, tiled=True)  23.2 us
    pallas_call x3, Pallas kernels, body(): pl.pallas_call(functools.partial(sweep_kernel, last), in_specs=[SMEM, SME...  17.7 us
    ppermute x7, starting transfers between devices, send(): lax.ppermute(far_out[dz - 1], 'col', [(h, (h // CORES - dz) % chips * COR...  14.2 us
    all_to_all x1, waiting for transfers between devices, body(): lax.all_to_all(partial, 'row', split_axis=0, concat_axis=0, tiled=True)  12.9 us
    all_to_all x3, waiting for transfers between devices, body(): lax.all_to_all(summed.reshape(piece_shape), 'row', split_axis=0, concat_a...  12 us
    all_to_all x3, starting transfers between devices, body(): lax.all_to_all(summed.reshape(piece_shape), 'row', split_axis=0, concat_a...  11.4 us
    all_to_all x3, starting transfers between devices, body(): got = lax.all_to_all(pieces, 'row', split_axis=0, concat_axis=0, tiled=True)  10.7 us
  transfers between devices with their start and end apart: 17, of which 8 were waited for; matrix products, arithmetic and copies ran while one was open for 3% of the time, Pallas kernels for 22%

profile of v10, /device:TPU:32, one launch (start us, length us, event | category | flops | bytes accessed | tf_op | source)
XLA Modules:
  0.0 202.3 jit_solution(15884293554773483385)
XLA Ops:
  6.5 3.6 %slices.1 = bf16[32,8,512]{2,1,0:T(8,128)(2,1)} custom-call(bf16[32,512,128]{2,1,0:T(8,128)(2,1)} %features.7), custom_call_target="tpu_custom_call" | custom-call | tf_op jit(solution)/shard_map/slices/pallas_call | solution.py:530
  10.2 0.8 dynamic-slice_subtract_fusion.1
  11.0 0.1 copy.35
  11.1 0.1 copy.31.wanted_ref
  11.2 3.2 %blocks.3 = (bf16[2,640,128]{2,1,0:T(8,128)(2,1)}, bf16[2,640,128]{2,1,0:T(8,128)(2,1)}, bf16[7,2,128,128]{3,2,1,0:T(8,128)(2,1)}) custom-call(s32[16,2]{1,0:T(8,128)S(1)} %copy.31.wanted_ref, bf16[32,512,128]{2,1,0:T(8,128)(2,1)} %features.7, bf16[32,128,128]{2,1,0:T(8,128)(2,1)} %diag.3), custom_call_target="tpu_custom_call" | custom-call | tf_op jit(solution)/shard_map/blocks/pallas_call | solution.py:582
  14.4 0.1 collective-permute-start.1
  14.5 0.5 collective-permute-start
  15.0 0.4 fusion.3
  15.4 0.1 fusion.owned_ref
  15.5 0.1 copy.29
  15.6 1.3 dynamic_slice.26
  16.9 3.8 %split.1.far_pairs = bf16[32,128,256]{2,1,0:T(8,128)(2,1)} custom-call(f32[32,128,128]{2,1,0:T(8,128)} %bitcast.30), custom_call_target="tpu_custom_call" | custom-call | tf_op jit(solution)/shard_map/split/pallas_call | solution.py:565
  20.7 0.1 copy.33.owned_ref
  20.8 0.7 fusion.1.list_ref
  21.5 0.9 constant_dynamic-slice_fusion.1
  22.4 0.7 copy-done
  23.1 4.7 %blocks.4 = (f32[32,128,128]{2,1,0:T(8,128)}, f32[32,128,128]{2,1,0:T(8,128)}, f32[2,128,256]{2,1,0:T(8,128)}) custom-call(s32[32]{0:T(128)S(1)} %fusion.1.list_ref, s32[1]{0:T(128)} %bitcast.1.live_ref, s32[2]{0:T(128)S(1)} %fusion.owned_ref, bf16[32,512,128]{2,1,0:T(8,128)(2,1)} %features.7, f32[32,128,128]{2,1,0:T(8,128)} %bitcast.25, ...), custom_call_target="tpu_custom_call" | custom-call | tf_op jit(solution)/shard_map/blocks/pallas_call | solution.py:621
  27.8 0.8 copy-done.8
  28.6 3.0 %blocks.5 = (bf16[4,128,128]{2,1,0:T(8,128)(2,1)}, bf16[4,128,128]{2,1,0:T(8,128)(2,1)}, bf16[4,128,128]{2,1,0:T(8,128)(2,1)}, bf16[4,128,128]{2,1,0:T(8,128)(2,...) custom-call(s32[16,2]{1,0:T(8,128)S(1)} %copy.31.wanted_ref, ...), custom_call_target="tpu_custom_call" | custom-call | tf_op jit(solution)/shard_map/blocks/pallas_call | solution.py:603
  31.6 23.2 %all-gather.2.cloned.1.call-done.far_slices = bf16[512,8,512]{2,1,0:T(8,128)(2,1)} async-done(((bf16[32,8,512]{2,1,0:T(8,128)(2,1)}), bf16[512,8,512]{2,1,0:T(8,128)(2,1)}) %all-gather.2.cloned.1.call-update) | async-done | bytes 4194320 | tf_op jit(solution)/shard_map/slices/all_gather | solution.py:540
  54.8 7.4 %covariance.1 = f32[16,28,8,128]{3,2,1,0:T(8,128)} custom-call(s32[16,32]{1,0:T(8,128)S(1)} %bitcast.24, s32[16,32]{1,0:T(8,128)S(1)} %bitcast.23, s32[16,2]{1,0:T(8,128)S(1)} %copy.33.owned_ref, bf16[512,8,512]{2,1,0:T(8,128)(2,1)} %all-gather.2.cloned.1.call-done.far_slices, bf16[32,512,128]{2,1,0:T(8,128)(2,1)} %features.7), custom_call_target="tpu_custom_call" | custom-call | tf_op jit(solution)/shard_map/covariance/pallas_call | solution.py:643
  62.2 7.0 %all-to-all-start = ((f32[16,28,8,128]{3,2,1,0:T(8,128)}), f32[16,28,8,128]{3,2,1,0:T(8,128)S(1)}, u32[]{:S(2)}, u32[]{:S(2)}) async-start(f32[16,28,8,128]{3,2,1,0:T(8,128)} %covariance.1), calls=%async_computation | async-start | bytes 3670016 | tf_op jit(solution)/shard_map/covariance/all_to_all | solution.py:658
  69.2 1.8 gather_fusion
  71.0 0.1 sub.25
  71.1 0.8 collective-permute-start.2
  72.0 1.3 collective-permute-start.3
  73.2 0.1 broadcast_select_fusion.col_diag_ref
  73.3 3.5 %collective-permute-start.4 = (bf16[4,128,128]{2,1,0:T(8,128)(2,1)S(1)}, bf16[4,128,128]{2,1,0:T(8,128)(2,1)S(1)}, u32[]{:S(2)}, u32[]{:S(2)}) collective-permute-start(bf16[4,128,128]{2,1,0:T(8,128)(2,1)S(1)} %copy-done.14), channel_id=1, source_target_pairs={{0,12},{1,13},{2,14},{3,15},{4,0},{5,1},{6,2},{7,3},{8,4},{9,5},{1... | collective-permute-start | bytes 393224 | tf_op jit(solution)/shard_map/diag/ppermute | solution.py:617
  76.8 0.8 collective-permute-start.5
  77.6 2.8 %collective-permute-start.6 = (bf16[4,128,128]{2,1,0:T(8,128)(2,1)S(1)}, bf16[4,128,128]{2,1,0:T(8,128)(2,1)S(1)}, u32[]{:S(2)}, u32[]{:S(2)}) collective-permute-start(bf16[4,128,128]{2,1,0:T(8,128)(2,1)S(1)} %copy-done.12), channel_id=1, source_target_pairs={{0,8},{1,9},{2,10},{3,11},{4,12},{5,13},{6,14},{7,15},{8,0},{9,1},... | collective-permute-start | bytes 393224 | tf_op jit(solution)/shard_map/diag/ppermute | solution.py:617
  80.3 5.0 %collective-permute-start.7 = (bf16[4,128,128]{2,1,0:T(8,128)(2,1)S(1)}, bf16[4,128,128]{2,1,0:T(8,128)(2,1)S(1)}, u32[]{:S(2)}, u32[]{:S(2)}) collective-permute-start(bf16[4,128,128]{2,1,0:T(8,128)(2,1)S(1)} %copy-done.11), channel_id=1, source_target_pairs={{0,6},{1,7},{2,8},{3,9},{4,10},{5,11},{6,12},{7,13},{8,14},{9,15},... | collective-permute-start | bytes 393224 | tf_op jit(solution)/shard_map/diag/ppermute | solution.py:617
  85.4 0.1 collective-permute-start.8
  85.5 12.9 %all-to-all-done.cov_ref = f32[16,28,8,128]{3,2,1,0:T(8,128)S(1)} async-done(((f32[16,28,8,128]{3,2,1,0:T(8,128)}), f32[16,28,8,128]{3,2,1,0:T(8,128)S(1)}, u32[]{:S(2)}, u32[]{:S(2)}) %all-to-all-start) | async-done | bytes 1835040 | tf_op jit(solution)/shard_map/covariance/all_to_all | solution.py:658
  98.4 5.7 %first.1 = (f32[32,128,128]{2,1,0:T(8,128)}, f32[32,128,128]{2,1,0:T(8,128)}, f32[16,2,8,128]{3,2,1,0:T(8,128)}) custom-call(s32[32]{0:T(128)S(1)} %fusion.1.list_ref, s32[1]{0:T(128)} %bitcast.1.live_ref, f32[16,28,8,128]{3,2,1,0:T(8,128)S(1)} %all-to-all-done.cov_ref, ...), custom_call_target="tpu_custom_call", output_to_operand_aliasing={{0}: (6, {}), {1}: (7, {})} | custom-call | tf_op jit(solution)/shard_map/first/pallas_call | solution.py:669
  104.1 3.7 %all-to-all-start.1 = ((f32[16,2,8,128]{3,2,1,0:T(8,128)}), f32[16,2,8,128]{3,2,1,0:T(8,128)S(1)}, u32[]{:S(2)}, u32[]{:S(2)}) async-start(f32[16,2,8,128]{3,2,1,0:T(8,128)} %get-tuple-element.92), calls=%async_computation.1 | async-start | bytes 262144 | tf_op jit(solution)/shard_map/exchange/all_to_all | solution.py:704
  107.8 0.1 compare_convert_fusion.same_ref
  107.9 0.6 copy-done.3
  108.5 0.1 copy-done.4
  108.5 0.1 copy-done.5
  108.6 0.1 copy-done.6
  108.7 0.0 copy-done.7
  108.7 4.2 %diagonal.6.rest_9_ = f32[32,128,128]{2,1,0:T(8,128)} custom-call(s32[32]{0:T(128)S(1)} %fusion.1.list_ref, f32[32,128,128]{2,1,0:T(8,128)} %get-tuple-element.90.far_base, f32[32,128,128]{2,1,0:T(8,128)} %get-tuple-element.103.far_d, bf16[2,128,128]{2,1,0:T(8,128)(2,1)S(1)} %broadcast_select_fusion.col_diag_ref, ...), custom_call_target="tpu_custom_call" | custom-call | tf_op jit(solution)/shard_map/exchange/diagonal/pallas_call | solution.py:687
  112.9 2.7 %all-to-all-done.1 = f32[16,2,8,128]{3,2,1,0:T(8,128)S(1)} async-done(((f32[16,2,8,128]{3,2,1,0:T(8,128)}), f32[16,2,8,128]{3,2,1,0:T(8,128)S(1)}, u32[]{:S(2)}, u32[]{:S(2)}) %all-to-all-start.1) | async-done | bytes 131104 | tf_op jit(solution)/shard_map/exchange/all_to_all | solution.py:704
  115.6 1.3 exchange.3
  116.9 4.4 %all-to-all-start.2 = ((f32[16,2,8,128]{3,2,1,0:T(8,128)}), f32[16,2,8,128]{3,2,1,0:T(8,128)S(1)}, u32[]{:S(2)}, u32[]{:S(2)}) async-start(f32[16,2,8,128]{3,2,1,0:T(8,128)} %bitcast.10), calls=%async_computation.2 | async-start | bytes 262144 | tf_op jit(solution)/shard_map/exchange/all_to_all | solution.py:714
  121.3 4.0 %diagonal.7.far_t = f32[32,128,128]{2,1,0:T(8,128)} custom-call(s32[32]{0:T(128)S(1)} %fusion.1.list_ref, f32[32,128,128]{2,1,0:T(8,128)} %get-tuple-element.90.far_base, f32[32,128,128]{2,1,0:T(8,128)} %get-tuple-element.103.far_d, bf16[2,128,128]{2,1,0:T(8,128)(2,1)S(1)} %broadcast_select_fusion.col_diag_ref, ...), custom_call_target="tpu_custom_call", output_to_operand_aliasing={{}: (13, {})} | custom-call | tf_op jit(solution)/shard_map/exchange/diagonal/pallas_call | solution.py:687
  125.2 4.0 %all-to-all-done.2.q_ref = f32[16,2,8,128]{3,2,1,0:T(8,128)S(1)} async-done(((f32[16,2,8,128]{3,2,1,0:T(8,128)}), f32[16,2,8,128]{3,2,1,0:T(8,128)S(1)}, u32[]{:S(2)}, u32[]{:S(2)}) %all-to-all-start.2) | async-done | bytes 131104 | tf_op jit(solution)/shard_map/exchange/all_to_all | solution.py:714
  129.2 6.2 %sweep.3 = (f32[32,128,128]{2,1,0:T(8,128)}, f32[16,2,8,128]{3,2,1,0:T(8,128)}) custom-call(s32[32]{0:T(128)S(1)} %fusion.1.list_ref, s32[1]{0:T(128)} %bitcast.1.live_ref, f32[32,128,128]{2,1,0:T(8,128)} %diagonal.7.far_t, f32[32,128,128]{2,1,0:T(8,128)} %bitcast.27, bf16[32,128,256]{2,1,0:T(8,128)(2,1)} %split.1.far_pairs, ...), custom_call_target="tpu_custom_call" | custom-call | tf_op jit(solution)/shard_map/sweep/pallas_call | solution.py:720
  135.4 3.5 %all-to-all-start.3 = ((f32[16,2,8,128]{3,2,1,0:T(8,128)}), f32[16,2,8,128]{3,2,1,0:T(8,128)S(1)}, u32[]{:S(2)}, u32[]{:S(2)}) async-start(f32[16,2,8,128]{3,2,1,0:T(8,128)} %get-tuple-element.108), calls=%async_computation.3 | async-start | bytes 262144 | tf_op jit(solution)/shard_map/exchange/all_to_all | solution.py:704
  138.9 4.2 %diagonal.8.rest_9_ = f32[32,128,128]{2,1,0:T(8,128)} custom-call(s32[32]{0:T(128)S(1)} %fusion.1.list_ref, f32[32,128,128]{2,1,0:T(8,128)} %get-tuple-element.90.far_base, f32[32,128,128]{2,1,0:T(8,128)} %get-tuple-element.110.far_d, bf16[2,128,128]{2,1,0:T(8,128)(2,1)S(1)} %broadcast_select_fusion.col_diag_ref, ...), custom_call_target="tpu_custom_call" | custom-call | tf_op jit(solution)/shard_map/exchange/diagonal/pallas_call | solution.py:687
  143.2 3.7 %all-to-all-done.3 = f32[16,2,8,128]{3,2,1,0:T(8,128)S(1)} async-done(((f32[16,2,8,128]{3,2,1,0:T(8,128)}), f32[16,2,8,128]{3,2,1,0:T(8,128)S(1)}, u32[]{:S(2)}, u32[]{:S(2)}) %all-to-all-start.3) | async-done | bytes 131104 | tf_op jit(solution)/shard_map/exchange/all_to_all | solution.py:704
  146.9 1.3 exchange.4
  148.2 3.5 %all-to-all-start.4 = ((f32[16,2,8,128]{3,2,1,0:T(8,128)}), f32[16,2,8,128]{3,2,1,0:T(8,128)S(1)}, u32[]{:S(2)}, u32[]{:S(2)}) async-start(f32[16,2,8,128]{3,2,1,0:T(8,128)} %bitcast.12), calls=%async_computation.4 | async-start | bytes 262144 | tf_op jit(solution)/shard_map/exchange/all_to_all | solution.py:714
  151.7 4.0 %diagonal.9.far_t = f32[32,128,128]{2,1,0:T(8,128)} custom-call(s32[32]{0:T(128)S(1)} %fusion.1.list_ref, f32[32,128,128]{2,1,0:T(8,128)} %get-tuple-element.90.far_base, f32[32,128,128]{2,1,0:T(8,128)} %get-tuple-element.110.far_d, bf16[2,128,128]{2,1,0:T(8,128)(2,1)S(1)} %broadcast_select_fusion.col_diag_ref, ...), custom_call_target="tpu_custom_call", output_to_operand_aliasing={{}: (13, {})} | custom-call | tf_op jit(solution)/shard_map/exchange/diagonal/pallas_call | solution.py:687
  155.7 4.0 %all-to-all-done.4.q_ref = f32[16,2,8,128]{3,2,1,0:T(8,128)S(1)} async-done(((f32[16,2,8,128]{3,2,1,0:T(8,128)}), f32[16,2,8,128]{3,2,1,0:T(8,128)S(1)}, u32[]{:S(2)}, u32[]{:S(2)}) %all-to-all-start.4) | async-done | bytes 131104 | tf_op jit(solution)/shard_map/exchange/all_to_all | solution.py:714
  159.7 6.2 %sweep.4 = (f32[32,128,128]{2,1,0:T(8,128)}, f32[16,2,8,128]{3,2,1,0:T(8,128)}) custom-call(s32[32]{0:T(128)S(1)} %fusion.1.list_ref, s32[1]{0:T(128)} %bitcast.1.live_ref, f32[32,128,128]{2,1,0:T(8,128)} %diagonal.9.far_t, f32[32,128,128]{2,1,0:T(8,128)} %bitcast.28, bf16[32,128,256]{2,1,0:T(8,128)(2,1)} %split.1.far_pairs, ...), custom_call_target="tpu_custom_call" | custom-call | tf_op jit(solution)/shard_map/sweep/pallas_call | solution.py:720
  165.8 3.5 %all-to-all-start.5 = ((f32[16,2,8,128]{3,2,1,0:T(8,128)}), f32[16,2,8,128]{3,2,1,0:T(8,128)S(1)}, u32[]{:S(2)}, u32[]{:S(2)}) async-start(f32[16,2,8,128]{3,2,1,0:T(8,128)} %get-tuple-element.114), calls=%async_computation.5 | async-start | bytes 262144 | tf_op jit(solution)/shard_map/exchange/all_to_all | solution.py:704
  169.4 4.2 %diagonal.10.rest_9_ = f32[32,128,128]{2,1,0:T(8,128)} custom-call(s32[32]{0:T(128)S(1)} %fusion.1.list_ref, f32[32,128,128]{2,1,0:T(8,128)} %get-tuple-element.90.far_base, f32[32,128,128]{2,1,0:T(8,128)} %get-tuple-element.116.far_d, bf16[2,128,128]{2,1,0:T(8,128)(2,1)S(1)} %broadcast_select_fusion.col_diag_ref, ...), custom_call_target="tpu_custom_call" | custom-call | tf_op jit(solution)/shard_map/exchange/diagonal/pallas_call | solution.py:687
  173.6 3.7 %all-to-all-done.5 = f32[16,2,8,128]{3,2,1,0:T(8,128)S(1)} async-done(((f32[16,2,8,128]{3,2,1,0:T(8,128)}), f32[16,2,8,128]{3,2,1,0:T(8,128)S(1)}, u32[]{:S(2)}, u32[]{:S(2)}) %all-to-all-start.5) | async-done | bytes 131104 | tf_op jit(solution)/shard_map/exchange/all_to_all | solution.py:704
  177.3 1.3 exchange.5
  178.6 3.5 %all-to-all-start.6 = ((f32[16,2,8,128]{3,2,1,0:T(8,128)}), f32[16,2,8,128]{3,2,1,0:T(8,128)S(1)}, u32[]{:S(2)}, u32[]{:S(2)}) async-start(f32[16,2,8,128]{3,2,1,0:T(8,128)} %bitcast.14), calls=%async_computation.6 | async-start | bytes 262144 | tf_op jit(solution)/shard_map/exchange/all_to_all | solution.py:714
  182.2 4.0 %diagonal.11.far_t = f32[32,128,128]{2,1,0:T(8,128)} custom-call(s32[32]{0:T(128)S(1)} %fusion.1.list_ref, f32[32,128,128]{2,1,0:T(8,128)} %get-tuple-element.90.far_base, f32[32,128,128]{2,1,0:T(8,128)} %get-tuple-element.116.far_d, bf16[2,128,128]{2,1,0:T(8,128)(2,1)S(1)} %broadcast_select_fusion.col_diag_ref, ...), custom_call_target="tpu_custom_call", output_to_operand_aliasing={{}: (13, {})} | custom-call | tf_op jit(solution)/shard_map/exchange/diagonal/pallas_call | solution.py:687
  186.1 4.0 %all-to-all-done.6.q_ref = f32[16,2,8,128]{3,2,1,0:T(8,128)S(1)} async-done(((f32[16,2,8,128]{3,2,1,0:T(8,128)}), f32[16,2,8,128]{3,2,1,0:T(8,128)S(1)}, u32[]{:S(2)}, u32[]{:S(2)}) %all-to-all-start.6) | async-done | bytes 131104 | tf_op jit(solution)/shard_map/exchange/all_to_all | solution.py:714
  190.1 5.4 %sweep.5 = f32[32,128,128]{2,1,0:T(8,128)} custom-call(s32[32]{0:T(128)S(1)} %fusion.1.list_ref, s32[1]{0:T(128)} %bitcast.1.live_ref, f32[32,128,128]{2,1,0:T(8,128)} %diagonal.11.far_t, f32[32,128,128]{2,1,0:T(8,128)} %bitcast.29, bf16[32,128,256]{2,1,0:T(8,128)(2,1)} %split.1.far_pairs, f32[16,2,8,128]{3,2,1,0:T(8,128)S(1)} %all-to-all-done.6.q_ref), custom_call_target="tpu_custom_call" | custom-call | tf_op jit(solution)/shard_map/sweep/pallas_call | solution.py:720
  (41 shorter events, 0.1 us)
Async XLA Ops:
  6.5 48.2 %all-gather.2.cloned.1.call-start = ((), (), s32[]{:S(2)}) async-start(), calls=%async_computation.7 | async-start | bytes 4456448 | tf_op jit(solution)/shard_map/slices/all_gather | solution.py:540
  11.2 3.8 %copy-start.9 = (s32[16,16,2]{1,2,0:T(2,128)S(1)}, s32[16,16,2]{1,2,0:T(2,128)}, u32[]{:S(2)}) copy-start(s32[16,16,2]{1,2,0:T(2,128)} %param.14) | copy-start | bytes 6148
  14.4 13.4 %collective-permute-start.1 = (bf16[7,2,128,128]{3,2,1,0:T(8,128)(2,1)}, bf16[7,2,128,128]{3,2,1,0:T(8,128)(2,1)S(1)}, u32[]{:S(2)}, u32[]{:S(2)}) collective-permute-start(bf16[7,2,128,128]{3,2,1,0:T(8,128)(2,1)} %get-tuple-element.68), channel_id=1, source_target_pairs={{0,1},{1,0},{2,3},{3,2},{4,5},{5,4},{6,7},{7,6},{8,9},{9,8},{10,11... | collective-permute-start | bytes 1376264 | tf_op jit(solution)/shard_map/blocks/ppermute | solution.py:601
  14.5 7.9 %collective-permute-start = (bf16[2,640,128]{2,1,0:T(8,128)(2,1)}, bf16[2,640,128]{2,1,0:T(8,128)(2,1)S(1)}, u32[]{:S(2)}, u32[]{:S(2)}) collective-permute-start(bf16[2,640,128]{2,1,0:T(8,128)(2,1)} %get-tuple-element.64), channel_id=1, source_target_pairs={{0,1},{1,0},{2,3},{3,2},{4,5},{5,4},{6,7},{7,6},{8,9},{9,8},{10,11... | collective-permute-start | bytes 983048 | tf_op jit(solution)/shard_map/blocks/ppermute | solution.py:602
  22.4 0.7 copy-start
  27.8 0.8 copy-start.8
  62.2 9.0 %copy-start.16 = (bf16[4,128,128]{2,1,0:T(8,128)(2,1)S(1)}, bf16[4,128,128]{2,1,0:T(8,128)(2,1)}, u32[]{:S(2)}) copy-start(bf16[4,128,128]{2,1,0:T(8,128)(2,1)} %get-tuple-element.84) | copy-start | bytes 393220
  62.2 9.8 %copy-start.15 = (bf16[4,128,128]{2,1,0:T(8,128)(2,1)S(1)}, bf16[4,128,128]{2,1,0:T(8,128)(2,1)}, u32[]{:S(2)}) copy-start(bf16[4,128,128]{2,1,0:T(8,128)(2,1)} %get-tuple-element.85) | copy-start | bytes 393220
  62.2 11.1 %copy-start.14 = (bf16[4,128,128]{2,1,0:T(8,128)(2,1)S(1)}, bf16[4,128,128]{2,1,0:T(8,128)(2,1)}, u32[]{:S(2)}) copy-start(bf16[4,128,128]{2,1,0:T(8,128)(2,1)} %get-tuple-element.96) | copy-start | bytes 393220
  62.2 14.6 %copy-start.13 = (bf16[4,128,128]{2,1,0:T(8,128)(2,1)S(1)}, bf16[4,128,128]{2,1,0:T(8,128)(2,1)}, u32[]{:S(2)}) copy-start(bf16[4,128,128]{2,1,0:T(8,128)(2,1)} %get-tuple-element.97) | copy-start | bytes 393220
  62.2 15.4 %copy-start.12 = (bf16[4,128,128]{2,1,0:T(8,128)(2,1)S(1)}, bf16[4,128,128]{2,1,0:T(8,128)(2,1)}, u32[]{:S(2)}) copy-start(bf16[4,128,128]{2,1,0:T(8,128)(2,1)} %get-tuple-element.98) | copy-start | bytes 393220
  62.2 18.1 %copy-start.11 = (bf16[4,128,128]{2,1,0:T(8,128)(2,1)S(1)}, bf16[4,128,128]{2,1,0:T(8,128)(2,1)}, u32[]{:S(2)}) copy-start(bf16[4,128,128]{2,1,0:T(8,128)(2,1)} %get-tuple-element.99) | copy-start | bytes 393220
  62.2 23.1 %copy-start.10 = (bf16[4,128,128]{2,1,0:T(8,128)(2,1)S(1)}, bf16[4,128,128]{2,1,0:T(8,128)(2,1)}, u32[]{:S(2)}) copy-start(bf16[4,128,128]{2,1,0:T(8,128)(2,1)} %get-tuple-element.100) | copy-start | bytes 393220
  62.2 36.1 %all-to-all-start = ((f32[16,28,8,128]{3,2,1,0:T(8,128)}), f32[16,28,8,128]{3,2,1,0:T(8,128)S(1)}, u32[]{:S(2)}, u32[]{:S(2)}) async-start(f32[16,28,8,128]{3,2,1,0:T(8,128)} %covariance.1), calls=%async_computation | async-start | bytes 3670016 | tf_op jit(solution)/shard_map/covariance/all_to_all | solution.py:658
  71.1 9.2 %collective-permute-start.2 = (bf16[4,128,128]{2,1,0:T(8,128)(2,1)S(1)}, bf16[4,128,128]{2,1,0:T(8,128)(2,1)S(1)}, u32[]{:S(2)}, u32[]{:S(2)}) collective-permute-start(bf16[4,128,128]{2,1,0:T(8,128)(2,1)S(1)} %copy-done.16), channel_id=1, source_target_pairs={{0,14},{1,15},{2,0},{3,1},{4,2},{5,3},{6,4},{7,5},{8,6},{9,7},{10,... | collective-permute-start | bytes 393224 | tf_op jit(solution)/shard_map/diag/ppermute | solution.py:617
  72.0 13.4 %collective-permute-start.3 = (bf16[4,128,128]{2,1,0:T(8,128)(2,1)S(1)}, bf16[4,128,128]{2,1,0:T(8,128)(2,1)S(1)}, u32[]{:S(2)}, u32[]{:S(2)}) collective-permute-start(bf16[4,128,128]{2,1,0:T(8,128)(2,1)S(1)} %copy-done.15), channel_id=1, source_target_pairs={{0,2},{1,3},{2,4},{3,5},{4,6},{5,7},{6,8},{7,9},{8,10},{9,11},{10,... | collective-permute-start | bytes 393224 | tf_op jit(solution)/shard_map/diag/ppermute | solution.py:617
  73.3 34.5 %collective-permute-start.4 = (bf16[4,128,128]{2,1,0:T(8,128)(2,1)S(1)}, bf16[4,128,128]{2,1,0:T(8,128)(2,1)S(1)}, u32[]{:S(2)}, u32[]{:S(2)}) collective-permute-start(bf16[4,128,128]{2,1,0:T(8,128)(2,1)S(1)} %copy-done.14), channel_id=1, source_target_pairs={{0,12},{1,13},{2,14},{3,15},{4,0},{5,1},{6,2},{7,3},{8,4},{9,5},{1... | collective-permute-start | bytes 393224 | tf_op jit(solution)/shard_map/diag/ppermute | solution.py:617
  76.8 31.0 %collective-permute-start.5 = (bf16[4,128,128]{2,1,0:T(8,128)(2,1)S(1)}, bf16[4,128,128]{2,1,0:T(8,128)(2,1)S(1)}, u32[]{:S(2)}, u32[]{:S(2)}) collective-permute-start(bf16[4,128,128]{2,1,0:T(8,128)(2,1)S(1)} %copy-done.13), channel_id=1, source_target_pairs={{0,10},{1,11},{2,12},{3,13},{4,14},{5,15},{6,0},{7,1},{8,2},{9,3},... | collective-permute-start | bytes 393224 | tf_op jit(solution)/shard_map/diag/ppermute | solution.py:617
  77.6 30.3 %collective-permute-start.6 = (bf16[4,128,128]{2,1,0:T(8,128)(2,1)S(1)}, bf16[4,128,128]{2,1,0:T(8,128)(2,1)S(1)}, u32[]{:S(2)}, u32[]{:S(2)}) collective-permute-start(bf16[4,128,128]{2,1,0:T(8,128)(2,1)S(1)} %copy-done.12), channel_id=1, source_target_pairs={{0,8},{1,9},{2,10},{3,11},{4,12},{5,13},{6,14},{7,15},{8,0},{9,1},... | collective-permute-start | bytes 393224 | tf_op jit(solution)/shard_map/diag/ppermute | solution.py:617
  80.3 23.7 %copy-start.1 = (bf16[4,128,128]{2,1,0:T(8,128)(2,1)}, bf16[4,128,128]{2,1,0:T(8,128)(2,1)S(1)}, u32[]{:S(2)}) copy-start(bf16[4,128,128]{2,1,0:T(8,128)(2,1)S(1)} %collective-permute-done.2.rest_2_) | copy-start | bytes 393220
  80.3 27.5 %collective-permute-start.7 = (bf16[4,128,128]{2,1,0:T(8,128)(2,1)S(1)}, bf16[4,128,128]{2,1,0:T(8,128)(2,1)S(1)}, u32[]{:S(2)}, u32[]{:S(2)}) collective-permute-start(bf16[4,128,128]{2,1,0:T(8,128)(2,1)S(1)} %copy-done.11), channel_id=1, source_target_pairs={{0,6},{1,7},{2,8},{3,9},{4,10},{5,11},{6,12},{7,13},{8,14},{9,15},... | collective-permute-start | bytes 393224 | tf_op jit(solution)/shard_map/diag/ppermute | solution.py:617
  85.4 18.7 %copy-start.2 = (bf16[4,128,128]{2,1,0:T(8,128)(2,1)}, bf16[4,128,128]{2,1,0:T(8,128)(2,1)S(1)}, u32[]{:S(2)}) copy-start(bf16[4,128,128]{2,1,0:T(8,128)(2,1)S(1)} %collective-permute-done.3.rest_8_) | copy-start | bytes 393220
  85.4 22.5 %collective-permute-start.8 = (bf16[4,128,128]{2,1,0:T(8,128)(2,1)S(1)}, bf16[4,128,128]{2,1,0:T(8,128)(2,1)S(1)}, u32[]{:S(2)}, u32[]{:S(2)}) collective-permute-start(bf16[4,128,128]{2,1,0:T(8,128)(2,1)S(1)} %copy-done.10), channel_id=1, source_target_pairs={{0,4},{1,5},{2,6},{3,7},{4,8},{5,9},{6,10},{7,11},{8,12},{9,13},{1... | collective-permute-start | bytes 393224 | tf_op jit(solution)/shard_map/diag/ppermute | solution.py:617
  104.1 11.5 %all-to-all-start.1 = ((f32[16,2,8,128]{3,2,1,0:T(8,128)}), f32[16,2,8,128]{3,2,1,0:T(8,128)S(1)}, u32[]{:S(2)}, u32[]{:S(2)}) async-start(f32[16,2,8,128]{3,2,1,0:T(8,128)} %get-tuple-element.92), calls=%async_computation.1 | async-start | bytes 262144 | tf_op jit(solution)/shard_map/exchange/all_to_all | solution.py:704
  107.8 0.6 copy-start.3
  107.9 0.7 copy-start.4
  107.9 0.7 copy-start.5
  107.9 0.8 copy-start.6
  107.9 0.8 copy-start.7
  116.9 12.4 %all-to-all-start.2 = ((f32[16,2,8,128]{3,2,1,0:T(8,128)}), f32[16,2,8,128]{3,2,1,0:T(8,128)S(1)}, u32[]{:S(2)}, u32[]{:S(2)}) async-start(f32[16,2,8,128]{3,2,1,0:T(8,128)} %bitcast.10), calls=%async_computation.2 | async-start | bytes 262144 | tf_op jit(solution)/shard_map/exchange/all_to_all | solution.py:714
  135.4 11.5 %all-to-all-start.3 = ((f32[16,2,8,128]{3,2,1,0:T(8,128)}), f32[16,2,8,128]{3,2,1,0:T(8,128)S(1)}, u32[]{:S(2)}, u32[]{:S(2)}) async-start(f32[16,2,8,128]{3,2,1,0:T(8,128)} %get-tuple-element.108), calls=%async_computation.3 | async-start | bytes 262144 | tf_op jit(solution)/shard_map/exchange/all_to_all | solution.py:704
  148.2 11.5 %all-to-all-start.4 = ((f32[16,2,8,128]{3,2,1,0:T(8,128)}), f32[16,2,8,128]{3,2,1,0:T(8,128)S(1)}, u32[]{:S(2)}, u32[]{:S(2)}) async-start(f32[16,2,8,128]{3,2,1,0:T(8,128)} %bitcast.12), calls=%async_computation.4 | async-start | bytes 262144 | tf_op jit(solution)/shard_map/exchange/all_to_all | solution.py:714
  165.8 11.5 %all-to-all-start.5 = ((f32[16,2,8,128]{3,2,1,0:T(8,128)}), f32[16,2,8,128]{3,2,1,0:T(8,128)S(1)}, u32[]{:S(2)}, u32[]{:S(2)}) async-start(f32[16,2,8,128]{3,2,1,0:T(8,128)} %get-tuple-element.114), calls=%async_computation.5 | async-start | bytes 262144 | tf_op jit(solution)/shard_map/exchange/all_to_all | solution.py:704
  178.6 11.5 %all-to-all-start.6 = ((f32[16,2,8,128]{3,2,1,0:T(8,128)}), f32[16,2,8,128]{3,2,1,0:T(8,128)S(1)}, u32[]{:S(2)}, u32[]{:S(2)}) async-start(f32[16,2,8,128]{3,2,1,0:T(8,128)} %bitcast.14), calls=%async_computation.6 | async-start | bytes 262144 | tf_op jit(solution)/shard_map/exchange/all_to_all | solution.py:714
Sparse Core Ops, SparseCore 0:
  10.3 44.4 all-gather.1
